TPU v7x, 512 devices: a whole 4x4x16 slice. The times are simulated.
512 devices in a mesh: dp: 16 (over x_hi, y, core), factor: 32 (over x_lo, z).
Axes of the slice: x: 4 (x_hi: 2, x_lo: 2; x = x_hi * 2 + x_lo), y: 4, z: 16, core: 2. Of those that a mesh axis runs over, the one named last changes fastest.
Arguments:
- activations: bfloat16 [2048, 8192], P('dp', 'factor'), may hold values from -12 to 12
- gradients: bfloat16 [2048, 8192], P('dp', 'factor'), may hold values from -12 to 12
- act_basis: bfloat16 [8192, 8192], P('dp', 'factor'), may hold values from -0.0625 to 0.0625
- grad_basis: bfloat16 [8192, 8192], P('dp', 'factor'), may hold values from -0.0625 to 0.0625
Outputs:
- corrected: float32 [8192, 8192], P('factor', 'dp')
All inputs are finite; a program needn't handle non-finite values.
Results may differ from a plain program's by a relative error of at most 0.00062.
Values may be sent and summed in bfloat16 or wider, within the bound.
No kernel may reach another device: no remote copies, remote signals or barrier semaphores. Data moves between devices by JAX's collectives and lax.ppermute only.
A program may use at most 64 MiB of HBM per device.

v0:
```python
import jax
import jax.numpy as jnp
from jax import lax
from jax.sharding import PartitionSpec as P


def on_device(activations, gradients, act_basis, grad_basis):
    act_full, grad_full = (
        lax.all_gather(activations, "factor", axis=1, tiled=True),
        lax.all_gather(gradients, "factor", axis=1, tiled=True),
    )
    columns = act_full
    rotated_act = jnp.dot(
        columns,
        lax.all_gather(act_basis, "dp", axis=0, tiled=True),
        preferred_element_type=jnp.float32,
    )
    columns = grad_full
    rotated_grad = jnp.dot(
        columns,
        lax.all_gather(grad_basis, "dp", axis=0, tiled=True),
        preferred_element_type=jnp.float32,
    )
    act_square = (rotated_act * rotated_act).astype(jnp.bfloat16)
    grad_square = (rotated_grad * rotated_grad).astype(jnp.bfloat16)
    act_every = lax.all_gather(act_square, "dp", axis=0, tiled=True)
    grad_wide = lax.all_gather(grad_square, "factor", axis=1, tiled=True)
    grad_block = lax.all_to_all(grad_wide, "dp", split_axis=1, concat_axis=0, tiled=True)
    total = lax.dot_general(
        act_every, grad_block, (((0,), (0,)), ((), ())), preferred_element_type=jnp.float32
    )
    return total * (1.0 / act_every.shape[0])


def solution(mesh):
    return jax.shard_map(
        on_device,
        mesh=mesh,
        in_specs=(P("dp", "factor"), P("dp", "factor"), P("dp", "factor"), P("dp", "factor")),
        out_specs=P("factor", "dp"),
        check_vma=False,
    )
```

profile of v0, /device:TPU:1, one launch (start us, length us, event | category | flops | bytes accessed | tf_op | source)
XLA Modules:
  0.0 617.3 jit_solution(8077619885345062295)
XLA Ops:
  6.5 0.0 all-gather.13.cloned.1.call-start
  6.5 0.7 all-gather.13.cloned.1.call-update
  7.3 0.0 all-gather.15.cloned.1.call-start
  7.3 0.7 all-gather.15.cloned.1.call-update
  8.0 0.0 all-gather.7.cloned.1.call-start
  8.1 0.7 all-gather.7.cloned.1.call-update
  8.7 0.0 all-gather.9.cloned.1.call-start
  8.8 0.5 all-gather.9.cloned.1.call-update
  9.3 0.0 all-gather.17.cloned.1.call-start
  9.4 111.3 %all-gather.13.cloned.1.call-done = bf16[128,8192]{1,0:T(8,128)(2,1)} async-done(((bf16[128,256]{1,0:T(8,128)(2,1)}), bf16[128,8192]{1,0:T(8,128)(2,1)}) %all-gather.13.cloned.1.call-update) | async-done | bytes 2097168 | tf_op jit(solution)/shard_map/all_gather | solution.py:10
  120.7 92.8 %all-gather.15.cloned.1.call-done = bf16[8192,256]{1,0:T(8,128)(2,1)} async-done(((bf16[512,256]{1,0:T(8,128)(2,1)}), bf16[8192,256]{1,0:T(8,128)(2,1)}) %all-gather.15.cloned.1.call-update) | async-done | bytes 4194320 | tf_op jit(solution)/shard_map/all_gather | solution.py:21
  213.5 4.2 fusion.1
  217.6 0.0 all-gather.17.cloned.1.call-update
  217.6 0.0 all-gather.11.cloned.1.call-start
  217.7 101.3 %all-gather.7.cloned.1.call-done = bf16[128,8192]{1,0:T(8,128)(2,1)} async-done(((bf16[128,256]{1,0:T(8,128)(2,1)}), bf16[128,8192]{1,0:T(8,128)(2,1)}) %all-gather.7.cloned.1.call-update) | async-done | bytes 2097168 | tf_op jit(solution)/shard_map/all_gather | solution.py:9
  319.0 92.6 %all-gather.9.cloned.1.call-done = bf16[8192,256]{1,0:T(8,128)(2,1)} async-done(((bf16[512,256]{1,0:T(8,128)(2,1)}), bf16[8192,256]{1,0:T(8,128)(2,1)}) %all-gather.9.cloned.1.call-update) | async-done | bytes 4194320 | tf_op jit(solution)/shard_map/all_gather | solution.py:15
  411.7 4.2 fusion
  415.8 0.0 all-gather.11.cloned.1.call-update
  415.8 101.2 %all-gather.17.cloned.1.call-done = bf16[128,8192]{1,0:T(8,128)(2,1)} async-done(((bf16[128,256]{1,0:T(8,128)(2,1)}), bf16[128,8192]{1,0:T(8,128)(2,1)}) %all-gather.17.cloned.1.call-update) | async-done | bytes 2097168 | tf_op jit(solution)/shard_map/all_gather | solution.py:27
  517.1 3.2 copy.8
  520.2 29.6 %all-to-all-start = ((bf16[128,16,512]{2,0,1:T(8,128)(2,1)}), bf16[128,16,512]{2,0,1:T(8,128)(2,1)S(1)}, u32[]{:S(2)}, u32[]{:S(2)}) async-start(bf16[128,16,512]{2,0,1:T(8,128)(2,1)} %bitcast.12), calls=%async_computation | async-start | bytes 4194304 | tf_op jit(solution)/shard_map/all_to_all | solution.py:28
  549.8 57.8 %all-gather.11.cloned.1.call-done = bf16[2048,256]{1,0:T(8,128)(2,1)} async-done(((bf16[128,256]{1,0:T(8,128)(2,1)}), bf16[2048,256]{1,0:T(8,128)(2,1)}) %all-gather.11.cloned.1.call-update) | async-done | bytes 1048592 | tf_op jit(solution)/shard_map/all_gather | solution.py:26
  607.7 0.0 all-to-all-done
  607.7 2.7 convolution_multiply_fusion
Async XLA Ops:
  6.5 114.2 %all-gather.13.cloned.1.call-start = ((), (), s32[]{:S(2)}) async-start(), calls=%async_computation.4 | async-start | bytes 2162688 | tf_op jit(solution)/shard_map/all_gather | solution.py:10
  7.3 206.2 %all-gather.15.cloned.1.call-start = ((), (), s32[]{:S(2)}) async-start(), calls=%async_computation.5 | async-start | bytes 4456448 | tf_op jit(solution)/shard_map/all_gather | solution.py:21
  8.0 311.0 %all-gather.7.cloned.1.call-start = ((), (), s32[]{:S(2)}) async-start(), calls=%async_computation.1 | async-start | bytes 2162688 | tf_op jit(solution)/shard_map/all_gather | solution.py:9
  8.7 402.9 %all-gather.9.cloned.1.call-start = ((), (), s32[]{:S(2)}) async-start(), calls=%async_computation.2 | async-start | bytes 4456448 | tf_op jit(solution)/shard_map/all_gather | solution.py:15
  9.3 507.7 %all-gather.17.cloned.1.call-start = ((), (), s32[]{:S(2)}) async-start(), calls=%async_computation.6 | async-start | bytes 2162688 | tf_op jit(solution)/shard_map/all_gather | solution.py:27
  217.6 390.0 %all-gather.11.cloned.1.call-start = ((), (), s32[]{:S(2)}) async-start(), calls=%async_computation.3 | async-start | bytes 1114112 | tf_op jit(solution)/shard_map/all_gather | solution.py:26
  520.2 87.5 %all-to-all-start = ((bf16[128,16,512]{2,0,1:T(8,128)(2,1)}), bf16[128,16,512]{2,0,1:T(8,128)(2,1)S(1)}, u32[]{:S(2)}, u32[]{:S(2)}) async-start(bf16[128,16,512]{2,0,1:T(8,128)(2,1)} %bitcast.12), calls=%async_computation | async-start | bytes 4194304 | tf_op jit(solution)/shard_map/all_to_all | solution.py:28
Sparse Core Ops, SparseCore 0:
  9.4 111.2 all-gather.12
  124.0 89.3 all-gather.14
  215.5 103.5 all-gather.6
  322.2 89.3 all-gather.8
  413.5 103.5 all-gather.16
  520.3 87.3 all-gather.10
where the time goes:
time: 617 us
  waiting for transfers between devices  560 us (91%)
  starting transfers between devices  29.8 us (5%)
  between operations  13.5 us (2%)
  matrix products  11.1 us (2%)
    all_gather x1, waiting for transfers between devices, on_device(): lax.all_gather(gradients, 'factor', axis=1, tiled=True)  111 us
    all_gather x1, waiting for transfers between devices, on_device(): lax.all_gather(activations, 'factor', axis=1, tiled=True)  101 us
    all_gather x1, waiting for transfers between devices, on_device(): grad_wide = lax.all_gather(grad_square, 'factor', axis=1, tiled=True)  101 us
    all_gather x1, waiting for transfers between devices, on_device(): lax.all_gather(grad_basis, 'dp', axis=0, tiled=True)  92.8 us
    all_gather x1, waiting for transfers between devices, on_device(): lax.all_gather(act_basis, 'dp', axis=0, tiled=True)  92.6 us
    all_gather x1, waiting for transfers between devices, on_device(): act_every = lax.all_gather(act_square, 'dp', axis=0, tiled=True)  57.8 us
    all_to_all x1, starting transfers between devices, on_device(): lax.all_to_all(grad_wide, 'dp', split_axis=1, concat_axis=0, tiled=True)  29.6 us
  transfers between devices with their start and end apart: 7, of which 6 were waited for; matrix products, arithmetic and copies ran while one was open for 2% of the time, Pallas kernels for 0%

commit v1 on v0

v1 whole, which is shorter than its diff:
```python
import functools
import jax
import jax.numpy as jnp
from jax import lax
from jax.experimental import pallas as pl
from jax.experimental.pallas import tpu as pltpu
from jax.sharding import Mesh, PartitionSpec as P

AXES = ("xh", "y", "c", "xl", "zh", "zl")
SIZES = (2, 4, 2, 2, 4, 4)
VMEM = pl.BlockSpec(memory_space=pltpu.VMEM)
SMEM = pl.BlockSpec(memory_space=pltpu.SMEM)
PARAMS = pltpu.CompilerParams(vmem_limit_bytes=40 * 1024 * 1024)


def to_all(x, axes, n):
    spread = jnp.broadcast_to(x[None], (n,) + x.shape)
    return lax.all_to_all(spread, axes, split_axis=0, concat_axis=0, tiled=True)


def move(x, axes, target):
    sizes = [SIZES[AXES.index(a)] for a in axes]

    def flat(coords):
        out = 0
        for c, s in zip(coords, sizes):
            out = out * s + c
        return out

    total = 1
    for s in sizes:
        total *= s
    pairs = []
    for i in range(total):
        rest, coords = i, []
        for s in reversed(sizes):
            coords.insert(0, rest % s)
            rest //= s
        pairs.append((i, flat(target(*coords))))
    return lax.ppermute(x, axes, pairs)


def dot(a, b):
    return jnp.dot(a, b, preferred_element_type=jnp.float32)


def grad_kernel(at_ref, g_ref, near_ref, far_ref, near_other_ref, far_other_ref, mine_ref, theirs_ref):
    y, c, turned = at_ref[0], at_ref[1], at_ref[2]
    sums = []
    for own, other in ((near_ref, near_other_ref), (far_ref, far_other_ref)):
        acc = jnp.zeros(mine_ref.shape, jnp.float32)
        for j in range(4):
            at = 4 * lax.rem(y + 4 - j, 4)
            for h in range(2):
                rows = slice(256 * h, 256 * h + 256)
                acc += dot(g_ref[at + 2 * c + h], own[j, rows, :])
                acc += dot(g_ref[at + 2 * (1 - c) + h], other[j, rows, :])
        sums.append(acc)
    near, far = sums
    mine_ref[...] = jnp.where(turned == 0, near, far)
    theirs_ref[...] = jnp.where(turned == 0, far, near)


def act_kernel(at_ref, a_ref, near_ref, far_ref, out_ref):
    c, xl = at_ref[0], at_ref[1]
    for y in range(4):
        for basis, x in ((near_ref, xl), (far_ref, 1 - xl)):
            acc = jnp.zeros(out_ref.shape[1:], jnp.float32)
            for k, core in ((0, c), (1, 1 - c)):
                for h in range(2):
                    rows = slice(256 * h, 256 * h + 256)
                    acc += dot(a_ref[4 * y + 2 * core + h], basis[k, rows, :])
            out_ref[2 * y + x] = acc


def corrected_kernel(x_ref, r_ref, s_ref, out_ref):
    x = x_ref[0]
    for h in range(2):
        acc = jnp.zeros((256, 256), jnp.float32)
        for y in range(4):
            for c in range(2):
                acc += lax.dot_general(
                    r_ref[4 * y + 2 * x + c], s_ref[4 * y + 2 * c + h],
                    (((0,), (0,)), ((), ())), preferred_element_type=jnp.float32,
                )
        out_ref[:, 256 * h:256 * h + 256] = acc


def call(kernel, shapes, *args):
    single = not isinstance(shapes, list)
    out = pl.pallas_call(
        kernel,
        out_shape=[jax.ShapeDtypeStruct(s, jnp.float32) for s in ([shapes] if single else shapes)],
        in_specs=[SMEM] + [VMEM] * (len(args) - 1),
        out_specs=[VMEM] * (1 if single else len(shapes)),
        compiler_params=PARAMS,
    )(*args)
    return out[0] if single else out


def swap(x, axis):
    return move(x, (axis,), lambda i: (1 - i,))


def on_device(activations, gradients, act_basis, grad_basis):
    tokens = activations.shape[0] * 16
    xh, y, c, xl = (lax.axis_index(a) for a in ("xh", "y", "c", "xl"))

    grad_half = to_all(gradients, ("zh", "zl"), 16)
    act_moved = move(activations, ("xh", "y", "xl", "zh"), lambda a, b, p, q: (p, q, a, b))

    grad_basis, act_basis, act_moved = lax.optimization_barrier((grad_basis, act_basis, act_moved))
    act_every = lax.all_gather(act_moved, ("zh", "zl"), axis=0, tiled=False)
    turned = move(grad_basis, ("xh", "xl"), lambda a, b: (b, a))
    near = jnp.stack(
        [turned] + [move(turned, ("y",), lambda b, j=j: ((b + j) % 4,)) for j in (1, 2, 3)]
    )
    far = swap(near, "xh")
    near_other, far_other = swap(near, "c"), swap(far, "c")

    act_near = jnp.stack([act_basis, swap(act_basis, "c")])
    act_far = swap(act_near, "xl")

    mine, theirs = call(
        grad_kernel, [(128, 256), (128, 256)],
        jnp.stack([y, c, (xh + xl) % 2]), grad_half, near, far, near_other, far_other,
    )
    rotated_grad = mine + swap(theirs, "xl")
    grad_square = (rotated_grad * rotated_grad).astype(jnp.bfloat16)
    grad_square = move(
        grad_square, AXES, lambda a, b, e, p, q, r: (p, q, r // 2, a, b, 2 * e + r % 2)
    )

    act_every, mine = lax.optimization_barrier((act_every, mine))
    part = call(act_kernel, (8, 128, 256), jnp.stack([c, xl]), act_every, act_near, act_far)
    part = lax.all_to_all(part, ("xh", "y"), split_axis=0, concat_axis=0, tiled=True)
    rotated_act = jnp.sum(part, axis=0)
    act_square = (rotated_act * rotated_act).astype(jnp.bfloat16)
    act_block = lax.all_gather(act_square, ("xh", "y", "c"), axis=0, tiled=False)
    grad_block = to_all(grad_square, ("zh", "zl"), 16)

    theirs = call(corrected_kernel, (256, 512), (1 - xl)[None], act_block, grad_block)
    theirs = swap(theirs, "xl")
    mine = call(corrected_kernel, (256, 512), xl[None], act_block, grad_block)
    return (mine + theirs) * (1.0 / tokens)


def solution(mesh):
    fine = Mesh(mesh.devices.reshape(SIZES), AXES)
    spec = P(("xh", "y", "c"), ("xl", "zh", "zl"))
    return jax.shard_map(
        on_device,
        mesh=fine,
        in_specs=(spec, spec, spec, spec),
        out_specs=P(("xl", "zh", "zl"), ("xh", "y", "c")),
        check_vma=False,
    )
```

time: 617 us -> 321 us (0.52)
  waiting for transfers between devices: 560 us -> 143 us
  starting transfers between devices: 29.8 us -> 151 us
  matrix products: 11.1 us -> 0 us
  Pallas kernels: 0 us -> 6.32 us
    all_gather x6 -> x2, waiting for transfers between devices: 557 us -> 97.5 us  [the longest x1 71.5 us: on_device(): lax.all_gather(act_square, ('xh', 'y', 'c'), axis=0, tiled=False)]
    ppermute x0 -> x13, starting transfers between devices: none -> 115 us  [move(): return lax.ppermute(x, axes, pairs)]
    ppermute x0 -> x13, waiting for transfers between devices: none -> 45.1 us  [move(): return lax.ppermute(x, axes, pairs)]
    dot_general x3 -> x0, matrix products: 11.1 us -> none  [the longest x1 4.17 us: on_device(): jnp.dot(columns, lax.all_gather(act_basis, 'dp', axis=0, tiled=True), pre...]
    pallas_call x0 -> x4, Pallas kernels: none -> 6.32 us  [call(): pl.pallas_call(kernel, out_shape=[jax.ShapeDtypeStruct(s, jnp.float32) fo...]
    all_to_all x1 -> x3, starting transfers between devices: 29.6 us -> 35.3 us  [the longest x2 28.9 us: to_all(): return lax.all_to_all(spread, axes, split_axis=0, concat_axis=0, tiled=True)]
  transfers between devices with their start and end apart: 7 -> 18, of which waited for: 6 -> 9; matrix products, arithmetic and copies ran while one was open for 2% -> 0% of each run, Pallas kernels for 0% -> 1%
where the time goes in v1:
time: 321 us
  starting transfers between devices  151 us (47%)
  waiting for transfers between devices  143 us (45%)
  between operations  13.7 us (4%)
  Pallas kernels  6.32 us (2%)
  local copies, waits for them, and re-layouts  5.45 us (2%)
    ppermute x13, starting transfers between devices, move(): return lax.ppermute(x, axes, pairs)  115 us
    all_gather x1, waiting for transfers between devices, on_device(): lax.all_gather(act_square, ('xh', 'y', 'c'), axis=0, tiled=False)  71.5 us
    ppermute x13, waiting for transfers between devices, move(): return lax.ppermute(x, axes, pairs)  45.1 us
    all_to_all x2, starting transfers between devices, to_all(): return lax.all_to_all(spread, axes, split_axis=0, concat_axis=0, tiled=True)  28.9 us
    all_gather x1, waiting for transfers between devices, on_device(): act_every = lax.all_gather(act_moved, ('zh', 'zl'), axis=0, tiled=False)  26 us
    all_to_all x1, starting transfers between devices, on_device(): lax.all_to_all(part, ('xh', 'y'), split_axis=0, concat_axis=0, tiled=True)  6.46 us
  transfers between devices with their start and end apart: 18, of which 9 were waited for; matrix products, arithmetic and copies ran while one was open for 0% of the time, Pallas kernels for 1%

profile of v1, /device:TPU:1, one launch (start us, length us, event | category | flops | bytes accessed | tf_op | source)
XLA Modules:
  0.0 320.7 jit_solution(8475887462512567639)
XLA Ops:
  6.5 1.9 broadcast_in_dim.9
  8.4 0.0 copy-start.6
  8.4 0.0 copy-start.5
  8.4 15.9 %all-to-all-start = ((bf16[16,128,256]{2,1,0:T(8,128)(2,1)}), bf16[16,128,256]{2,1,0:T(8,128)(2,1)S(1)}, u32[]{:S(2)}, u32[]{:S(2)}) async-start(bf16[16,128,256]{2,1,0:T(8,128)(2,1)} %broadcast_in_dim.9), calls=%async_computation | async-start | bytes 2097152 | tf_op jit(solution)/shard_map/all_to_all | solution.py:18
  24.3 0.0 all-gather.5.cloned.1.call-start
  24.4 0.0 copy-done.6
  24.4 0.7 collective-permute-start
  25.1 0.0 collective-permute-done
  25.1 0.0 copy-start.4
  25.1 0.0 copy-done.5
  25.1 0.7 collective-permute-start.1
  25.8 0.0 collective-permute-done.1
  25.8 55.9 %collective-permute-start.2 = (bf16[512,256]{1,0:T(8,128)(2,1)S(1)}, bf16[512,256]{1,0:T(8,128)(2,1)S(1)}, u32[]{:S(2)}, u32[]{:S(2)}) collective-permute-start(bf16[512,256]{1,0:T(8,128)(2,1)S(1)} %collective-permute-done.1), channel_id=1, source_target_pairs={{0,64},{64,128},{128,192},{192,0},{1,65},{65,129},{129,193},{193,1... | collective-permute-start | bytes 786440 | tf_op jit(solution)/shard_map/ppermute | solution.py:40
  81.7 7.1 %collective-permute-start.3 = (bf16[512,256]{1,0:T(8,128)(2,1)S(1)}, bf16[512,256]{1,0:T(8,128)(2,1)S(1)}, u32[]{:S(2)}, u32[]{:S(2)}) collective-permute-start(bf16[512,256]{1,0:T(8,128)(2,1)S(1)} %collective-permute-done.1), channel_id=1, source_target_pairs={{0,128},{64,192},{128,0},{192,64},{1,129},{65,193},{129,1},{193,65... | collective-permute-start | bytes 786440 | tf_op jit(solution)/shard_map/ppermute | solution.py:40
  88.8 4.0 %collective-permute-start.4 = (bf16[512,256]{1,0:T(8,128)(2,1)S(1)}, bf16[512,256]{1,0:T(8,128)(2,1)S(1)}, u32[]{:S(2)}, u32[]{:S(2)}) collective-permute-start(bf16[512,256]{1,0:T(8,128)(2,1)S(1)} %collective-permute-done.1), channel_id=1, source_target_pairs={{0,192},{64,0},{128,64},{192,128},{1,193},{65,1},{129,65},{193,129... | collective-permute-start | bytes 786440 | tf_op jit(solution)/shard_map/ppermute | solution.py:40
  92.8 0.0 collective-permute-done.2
  92.8 4.5 %collective-permute-done.3 = bf16[512,256]{1,0:T(8,128)(2,1)S(1)} collective-permute-done((bf16[512,256]{1,0:T(8,128)(2,1)S(1)}, bf16[512,256]{1,0:T(8,128)(2,1)S(1)}, u32[]{:S(2)}, u32[]{:S(2)}) %collective-permute-start.3) | collective-permute-done | bytes 262176 | tf_op jit(solution)/shard_map/ppermute | solution.py:40
  97.3 1.7 collective-permute-done.4
  99.1 0.0 copy-start.3
  99.1 0.1 pad_maximum_fusion.near_ref
  99.2 0.0 copy-done.4
  99.2 12.6 %collective-permute-start.5 = (bf16[4,512,256]{2,1,0:T(8,128)(2,1)S(1)}, bf16[4,512,256]{2,1,0:T(8,128)(2,1)}, u32[]{:S(2)}, u32[]{:S(2)}) collective-permute-start(bf16[4,512,256]{2,1,0:T(8,128)(2,1)S(1)} %pad_maximum_fusion.near_ref), channel_id=1, source_target_pairs={{0,256},{256,0},{1,257},{257,1},{2,258},{258,2},{3,259},{259,3},{4... | collective-permute-start | bytes 3145736 | tf_op jit(solution)/shard_map/ppermute | solution.py:40
  111.9 0.0 all-gather.5.cloned.1.call-update
  111.9 4.5 %collective-permute-start.6 = (bf16[4,512,256]{2,1,0:T(8,128)(2,1)S(1)}, bf16[4,512,256]{2,1,0:T(8,128)(2,1)}, u32[]{:S(2)}, u32[]{:S(2)}) collective-permute-start(bf16[4,512,256]{2,1,0:T(8,128)(2,1)S(1)} %pad_maximum_fusion.near_ref), channel_id=1, source_target_pairs={{0,32},{32,0},{1,33},{33,1},{2,34},{34,2},{3,35},{35,3},{4,36},{36... | collective-permute-start | bytes 3145736 | tf_op jit(solution)/shard_map/ppermute | solution.py:40
  116.3 16.8 %collective-permute-done.5.far_ref = bf16[4,512,256]{2,1,0:T(8,128)(2,1)} collective-permute-done((bf16[4,512,256]{2,1,0:T(8,128)(2,1)S(1)}, bf16[4,512,256]{2,1,0:T(8,128)(2,1)}, u32[]{:S(2)}, u32[]{:S(2)}) %collective-permute-start.5) | collective-permute-done | bytes 1048608 | tf_op jit(solution)/shard_map/ppermute | solution.py:40
  133.2 4.8 %collective-permute-start.7 = (bf16[4,512,256]{2,1,0:T(8,128)(2,1)}, bf16[4,512,256]{2,1,0:T(8,128)(2,1)}, u32[]{:S(2)}, u32[]{:S(2)}) collective-permute-start(bf16[4,512,256]{2,1,0:T(8,128)(2,1)} %collective-permute-done.5.far_ref), channel_id=1, source_target_pairs={{0,32},{32,0},{1,33},{33,1},{2,34},{34,2},{3,35},{35,3},{4,36},{36... | collective-permute-start | bytes 3145736 | tf_op jit(solution)/shard_map/ppermute | solution.py:40
  138.0 0.0 copy-done.3
  138.0 1.9 collective-permute-start.8
  139.9 1.5 collective-permute-done.8
  141.4 0.1 pad_maximum_fusion.1.near_ref
  141.5 4.3 %collective-permute-start.9 = (bf16[2,512,256]{2,1,0:T(8,128)(2,1)S(1)}, bf16[2,512,256]{2,1,0:T(8,128)(2,1)S(1)}, u32[]{:S(2)}, u32[]{:S(2)}) collective-permute-start(bf16[2,512,256]{2,1,0:T(8,128)(2,1)S(1)} %pad_maximum_fusion.1.near_ref), channel_id=1, source_target_pairs={{0,16},{16,0},{1,17},{17,1},{2,18},{18,2},{3,19},{19,3},{4,20},{20... | collective-permute-start | bytes 1572872 | tf_op jit(solution)/shard_map/ppermute | solution.py:40
  145.8 0.1 pad_add_fusion.at_ref
  145.9 0.1 pad_add_fusion.1.at_ref
  145.9 0.0 collective-permute-done.6.near_other_ref
  145.9 0.0 collective-permute-done.7.far_other_ref
  145.9 0.0 all-to-all-done.g_ref
  145.9 2.6 shard_map.46
  148.5 26.0 %all-gather.5.cloned.1.call-done = bf16[2048,256]{1,0:T(8,128)(2,1)} async-done(((bf16[128,256]{1,0:T(8,128)(2,1)}), bf16[2048,256]{1,0:T(8,128)(2,1)}) %all-gather.5.cloned.1.call-update) | async-done | bytes 1048592 | tf_op jit(solution)/shard_map/all_gather | solution.py:113
  174.6 0.0 collective-permute-done.9.far_ref
  174.6 0.0 copy-start.2
  174.6 1.2 copy-done.2
  175.8 2.3 shard_map.47
  178.1 6.5 %all-to-all-start.1 = ((f32[8,128,256]{2,1,0:T(8,128)}), f32[8,128,256]{2,1,0:T(8,128)S(1)}, u32[]{:S(2)}, u32[]{:S(2)}) async-start(f32[8,128,256]{2,1,0:T(8,128)} %shard_map.47), calls=%async_computation.1 | async-start | bytes 2097152 | tf_op jit(solution)/shard_map/all_to_all | solution.py:136
  184.6 2.3 collective-permute-start.10
  186.8 6.3 %collective-permute-done.10 = f32[128,256]{1,0:T(8,128)S(1)} collective-permute-done((f32[128,256]{1,0:T(8,128)S(1)}, f32[128,256]{1,0:T(8,128)S(1)}, u32[]{:S(2)}, u32[]{:S(2)}) %collective-permute-start.10) | collective-permute-done | bytes 131104 | tf_op jit(solution)/shard_map/ppermute | solution.py:40
  193.2 14.4 %collective-permute-start.11 = (bf16[128,256]{1,0:T(8,128)(2,1)S(1)}, bf16[128,256]{1,0:T(8,128)(2,1)S(1)}, u32[]{:S(2)}, u32[]{:S(2)}) collective-permute-start(bf16[128,256]{1,0:T(8,128)(2,1)S(1)} %multiply_convert_fusion), channel_id=1, source_target_pairs={{0,0},{1,1},{2,32},{3,33},{4,64},{5,65},{6,96},{7,97},{8,128},{9,1... | collective-permute-start | bytes 196616 | tf_op jit(solution)/shard_map/ppermute | solution.py:40
  207.5 1.9 collective-permute-done.11
  209.5 0.0 all-to-all-done.1
  209.5 1.1 broadcast_in_dim.20
  210.5 13.0 %all-to-all-start.2 = ((bf16[16,128,256]{2,1,0:T(8,128)(2,1)}), bf16[16,128,256]{2,1,0:T(8,128)(2,1)S(1)}, u32[]{:S(2)}, u32[]{:S(2)}) async-start(bf16[16,128,256]{2,1,0:T(8,128)(2,1)} %broadcast_in_dim.20), calls=%async_computation.2 | async-start | bytes 2097152 | tf_op jit(solution)/shard_map/all_to_all | solution.py:18
  223.5 0.0 all-gather.7.cloned.1.call-start
  223.6 0.1 reduce_sum.9
  223.7 0.6 multiply_convert_fusion.1
  224.3 0.0 all-gather.7.cloned.1.call-update
  224.3 71.5 %all-gather.7.cloned.1.call-done = bf16[2048,256]{1,0:T(8,128)(2,1)} async-done(((bf16[128,256]{1,0:T(8,128)(2,1)}), bf16[2048,256]{1,0:T(8,128)(2,1)}) %all-gather.7.cloned.1.call-update) | async-done | bytes 1048592 | tf_op jit(solution)/shard_map/all_gather | solution.py:139
  295.8 0.0 all-to-all-done.2.s_ref
  295.8 0.0 copy-start
  295.8 1.2 copy-done
  297.1 0.7 shard_map.49
  297.8 2.2 collective-permute-start.12
  300.0 0.0 copy-done.1
  300.0 0.7 shard_map.48
  300.7 12.2 %collective-permute-done.12 = f32[256,512]{1,0:T(8,128)S(1)} collective-permute-done((f32[256,512]{1,0:T(8,128)S(1)}, f32[256,512]{1,0:T(8,128)S(1)}, u32[]{:S(2)}, u32[]{:S(2)}) %collective-permute-start.12) | collective-permute-done | bytes 524320 | tf_op jit(solution)/shard_map/ppermute | solution.py:40
  313.0 0.9 add_multiply_fusion
  (2 shorter events, 0.0 us)
Async XLA Ops:
  8.4 15.9 %copy-start.6 = (bf16[128,256]{1,0:T(8,128)(2,1)S(1)}, bf16[128,256]{1,0:T(8,128)(2,1)}, u32[]{:S(2)}) copy-start(bf16[128,256]{1,0:T(8,128)(2,1)} %param.4) | copy-start | bytes 196612
  8.4 16.6 %copy-start.5 = (bf16[512,256]{1,0:T(8,128)(2,1)S(1)}, bf16[512,256]{1,0:T(8,128)(2,1)}, u32[]{:S(2)}) copy-start(bf16[512,256]{1,0:T(8,128)(2,1)} %param.7) | copy-start | bytes 786436
  8.4 137.5 %all-to-all-start = ((bf16[16,128,256]{2,1,0:T(8,128)(2,1)}), bf16[16,128,256]{2,1,0:T(8,128)(2,1)S(1)}, u32[]{:S(2)}, u32[]{:S(2)}) async-start(bf16[16,128,256]{2,1,0:T(8,128)(2,1)} %broadcast_in_dim.9), calls=%async_computation | async-start | bytes 2097152 | tf_op jit(solution)/shard_map/all_to_all | solution.py:18
  24.3 150.2 %all-gather.5.cloned.1.call-start = ((), (), s32[]{:S(2)}) async-start(), calls=%async_computation.3 | async-start | bytes 1114112 | tf_op jit(solution)/shard_map/all_gather | solution.py:113
  24.4 0.7 collective-permute-start
  25.1 74.1 %copy-start.4 = (bf16[128,256]{1,0:T(8,128)(2,1)}, bf16[128,256]{1,0:T(8,128)(2,1)S(1)}, u32[]{:S(2)}) copy-start(bf16[128,256]{1,0:T(8,128)(2,1)S(1)} %collective-permute-done) | copy-start | bytes 196612
  25.1 0.7 collective-permute-start.1
  25.8 67.0 %collective-permute-start.2 = (bf16[512,256]{1,0:T(8,128)(2,1)S(1)}, bf16[512,256]{1,0:T(8,128)(2,1)S(1)}, u32[]{:S(2)}, u32[]{:S(2)}) collective-permute-start(bf16[512,256]{1,0:T(8,128)(2,1)S(1)} %collective-permute-done.1), channel_id=1, source_target_pairs={{0,64},{64,128},{128,192},{192,0},{1,65},{65,129},{129,193},{193,1... | collective-permute-start | bytes 786440 | tf_op jit(solution)/shard_map/ppermute | solution.py:40
  81.7 15.7 %collective-permute-start.3 = (bf16[512,256]{1,0:T(8,128)(2,1)S(1)}, bf16[512,256]{1,0:T(8,128)(2,1)S(1)}, u32[]{:S(2)}, u32[]{:S(2)}) collective-permute-start(bf16[512,256]{1,0:T(8,128)(2,1)S(1)} %collective-permute-done.1), channel_id=1, source_target_pairs={{0,128},{64,192},{128,0},{192,64},{1,129},{65,193},{129,1},{193,65... | collective-permute-start | bytes 786440 | tf_op jit(solution)/shard_map/ppermute | solution.py:40
  88.8 10.3 %collective-permute-start.4 = (bf16[512,256]{1,0:T(8,128)(2,1)S(1)}, bf16[512,256]{1,0:T(8,128)(2,1)S(1)}, u32[]{:S(2)}, u32[]{:S(2)}) collective-permute-start(bf16[512,256]{1,0:T(8,128)(2,1)S(1)} %collective-permute-done.1), channel_id=1, source_target_pairs={{0,192},{64,0},{128,64},{192,128},{1,193},{65,1},{129,65},{193,129... | collective-permute-start | bytes 786440 | tf_op jit(solution)/shard_map/ppermute | solution.py:40
  99.1 38.9 %copy-start.3 = (bf16[512,256]{1,0:T(8,128)(2,1)S(1)}, bf16[512,256]{1,0:T(8,128)(2,1)}, u32[]{:S(2)}) copy-start(bf16[512,256]{1,0:T(8,128)(2,1)} %param.6) | copy-start | bytes 786436
  99.2 33.9 %collective-permute-start.5 = (bf16[4,512,256]{2,1,0:T(8,128)(2,1)S(1)}, bf16[4,512,256]{2,1,0:T(8,128)(2,1)}, u32[]{:S(2)}, u32[]{:S(2)}) collective-permute-start(bf16[4,512,256]{2,1,0:T(8,128)(2,1)S(1)} %pad_maximum_fusion.near_ref), channel_id=1, source_target_pairs={{0,256},{256,0},{1,257},{257,1},{2,258},{258,2},{3,259},{259,3},{4... | collective-permute-start | bytes 3145736 | tf_op jit(solution)/shard_map/ppermute | solution.py:40
  111.9 34.0 %collective-permute-start.6 = (bf16[4,512,256]{2,1,0:T(8,128)(2,1)S(1)}, bf16[4,512,256]{2,1,0:T(8,128)(2,1)}, u32[]{:S(2)}, u32[]{:S(2)}) collective-permute-start(bf16[4,512,256]{2,1,0:T(8,128)(2,1)S(1)} %pad_maximum_fusion.near_ref), channel_id=1, source_target_pairs={{0,32},{32,0},{1,33},{33,1},{2,34},{34,2},{3,35},{35,3},{4,36},{36... | collective-permute-start | bytes 3145736 | tf_op jit(solution)/shard_map/ppermute | solution.py:40
  133.2 12.8 %collective-permute-start.7 = (bf16[4,512,256]{2,1,0:T(8,128)(2,1)}, bf16[4,512,256]{2,1,0:T(8,128)(2,1)}, u32[]{:S(2)}, u32[]{:S(2)}) collective-permute-start(bf16[4,512,256]{2,1,0:T(8,128)(2,1)} %collective-permute-done.5.far_ref), channel_id=1, source_target_pairs={{0,32},{32,0},{1,33},{33,1},{2,34},{34,2},{3,35},{35,3},{4,36},{36... | collective-permute-start | bytes 3145736 | tf_op jit(solution)/shard_map/ppermute | solution.py:40
  138.0 3.4 %collective-permute-start.8 = (bf16[512,256]{1,0:T(8,128)(2,1)S(1)}, bf16[512,256]{1,0:T(8,128)(2,1)S(1)}, u32[]{:S(2)}, u32[]{:S(2)}) collective-permute-start(bf16[512,256]{1,0:T(8,128)(2,1)S(1)} %copy-done.3), channel_id=1, source_target_pairs={{0,32},{32,0},{1,33},{33,1},{2,34},{34,2},{3,35},{35,3},{4,36},{36... | collective-permute-start | bytes 786440 | tf_op jit(solution)/shard_map/ppermute | solution.py:40
  141.5 33.1 %collective-permute-start.9 = (bf16[2,512,256]{2,1,0:T(8,128)(2,1)S(1)}, bf16[2,512,256]{2,1,0:T(8,128)(2,1)S(1)}, u32[]{:S(2)}, u32[]{:S(2)}) collective-permute-start(bf16[2,512,256]{2,1,0:T(8,128)(2,1)S(1)} %pad_maximum_fusion.1.near_ref), channel_id=1, source_target_pairs={{0,16},{16,0},{1,17},{17,1},{2,18},{18,2},{3,19},{19,3},{4,20},{20... | collective-permute-start | bytes 1572872 | tf_op jit(solution)/shard_map/ppermute | solution.py:40
  174.6 1.2 copy-start.2
  178.1 31.4 %all-to-all-start.1 = ((f32[8,128,256]{2,1,0:T(8,128)}), f32[8,128,256]{2,1,0:T(8,128)S(1)}, u32[]{:S(2)}, u32[]{:S(2)}) async-start(f32[8,128,256]{2,1,0:T(8,128)} %shard_map.47), calls=%async_computation.1 | async-start | bytes 2097152 | tf_op jit(solution)/shard_map/all_to_all | solution.py:136
  184.6 8.6 %collective-permute-start.10 = (f32[128,256]{1,0:T(8,128)S(1)}, f32[128,256]{1,0:T(8,128)S(1)}, u32[]{:S(2)}, u32[]{:S(2)}) collective-permute-start(f32[128,256]{1,0:T(8,128)S(1)} %get-tuple-element.16), channel_id=1, source_target_pairs={{0,16},{16,0},{1,17},{17,1},{2,18},{18,2},{3,19},{19,3},{4,20},{20... | collective-permute-start | bytes 393224 | tf_op jit(solution)/shard_map/ppermute | solution.py:40
  193.2 16.3 %collective-permute-start.11 = (bf16[128,256]{1,0:T(8,128)(2,1)S(1)}, bf16[128,256]{1,0:T(8,128)(2,1)S(1)}, u32[]{:S(2)}, u32[]{:S(2)}) collective-permute-start(bf16[128,256]{1,0:T(8,128)(2,1)S(1)} %multiply_convert_fusion), channel_id=1, source_target_pairs={{0,0},{1,1},{2,32},{3,33},{4,64},{5,65},{6,96},{7,97},{8,128},{9,1... | collective-permute-start | bytes 196616 | tf_op jit(solution)/shard_map/ppermute | solution.py:40
  210.5 85.3 %all-to-all-start.2 = ((bf16[16,128,256]{2,1,0:T(8,128)(2,1)}), bf16[16,128,256]{2,1,0:T(8,128)(2,1)S(1)}, u32[]{:S(2)}, u32[]{:S(2)}) async-start(bf16[16,128,256]{2,1,0:T(8,128)(2,1)} %broadcast_in_dim.20), calls=%async_computation.2 | async-start | bytes 2097152 | tf_op jit(solution)/shard_map/all_to_all | solution.py:18
  223.5 72.3 %all-gather.7.cloned.1.call-start = ((), (), s32[]{:S(2)}) async-start(), calls=%async_computation.4 | async-start | bytes 1114112 | tf_op jit(solution)/shard_map/all_gather | solution.py:139
  295.8 1.2 copy-start
  297.0 2.9 copy-start.1
  297.8 15.2 %collective-permute-start.12 = (f32[256,512]{1,0:T(8,128)S(1)}, f32[256,512]{1,0:T(8,128)S(1)}, u32[]{:S(2)}, u32[]{:S(2)}) collective-permute-start(f32[256,512]{1,0:T(8,128)S(1)} %shard_map.49), channel_id=1, source_target_pairs={{0,16},{16,0},{1,17},{17,1},{2,18},{18,2},{3,19},{19,3},{4,20},{20... | collective-permute-start | bytes 1572872 | tf_op jit(solution)/shard_map/ppermute | solution.py:40
Sparse Core Ops, SparseCore 0:
  112.0 62.5 all-gather.4
  227.7 68.0 all-gather.6

commit v2 on v1

--- a/solution.py
+++ b/solution.py
@@ -53,8 +53,8 @@
             at = 4 * lax.rem(y + 4 - j, 4)
             for h in range(2):
                 rows = slice(256 * h, 256 * h + 256)
-                acc += dot(g_ref[at + 2 * c + h], own[j, rows, :])
-                acc += dot(g_ref[at + 2 * (1 - c) + h], other[j, rows, :])
+                acc += dot(g_ref[at + 2 * c + h, 1], own[j, rows, :])
+                acc += dot(g_ref[at + 2 * (1 - c) + h, 1], other[j, rows, :])
         sums.append(acc)
     near, far = sums
     mine_ref[...] = jnp.where(turned == 0, near, far)
@@ -69,20 +69,22 @@
             for k, core in ((0, c), (1, 1 - c)):
                 for h in range(2):
                     rows = slice(256 * h, 256 * h + 256)
-                    acc += dot(a_ref[4 * y + 2 * core + h], basis[k, rows, :])
+                    acc += dot(a_ref[4 * y + 2 * core + h, 0], basis[k, rows, :])
             out_ref[2 * y + x] = acc
 
 
-def corrected_kernel(x_ref, r_ref, s_ref, out_ref):
-    x = x_ref[0]
+def corrected_kernel(at_ref, near_ref, far_ref, s_ref, out_ref):
+    x, xh, y, c = at_ref[0], at_ref[1], at_ref[2], at_ref[3]
     for h in range(2):
         acc = jnp.zeros((256, 256), jnp.float32)
-        for y in range(4):
-            for c in range(2):
-                acc += lax.dot_general(
-                    r_ref[4 * y + 2 * x + c], s_ref[4 * y + 2 * c + h],
-                    (((0,), (0,)), ((), ())), preferred_element_type=jnp.float32,
-                )
+        for act, high in ((near_ref, xh), (far_ref, 1 - xh)):
+            for low in range(2):
+                shift = lax.rem(y + 4 - x - 2 * low, 4)
+                for k, core in ((0, c), (1, 1 - c)):
+                    acc += lax.dot_general(
+                        act[2 * shift + k], s_ref[8 * high + 4 * low + 2 * core + h],
+                        (((0,), (0,)), ((), ())), preferred_element_type=jnp.float32,
+                    )
         out_ref[:, 256 * h:256 * h + 256] = acc
 
 
@@ -102,19 +104,21 @@
     return move(x, (axis,), lambda i: (1 - i,))
 
 
+def shift_y(x, j):
+    return move(x, ("y",), lambda b: ((b + j) % 4,))
+
+
 def on_device(activations, gradients, act_basis, grad_basis):
     tokens = activations.shape[0] * 16
     xh, y, c, xl = (lax.axis_index(a) for a in ("xh", "y", "c", "xl"))
 
-    grad_half = to_all(gradients, ("zh", "zl"), 16)
     act_moved = move(activations, ("xh", "y", "xl", "zh"), lambda a, b, p, q: (p, q, a, b))
+    both = jnp.stack([act_moved, gradients])
+    both, grad_basis, act_basis = lax.optimization_barrier((both, grad_basis, act_basis))
+    every = lax.all_gather(both, ("zh", "zl"), axis=0, tiled=False)
 
-    grad_basis, act_basis, act_moved = lax.optimization_barrier((grad_basis, act_basis, act_moved))
-    act_every = lax.all_gather(act_moved, ("zh", "zl"), axis=0, tiled=False)
     turned = move(grad_basis, ("xh", "xl"), lambda a, b: (b, a))
-    near = jnp.stack(
-        [turned] + [move(turned, ("y",), lambda b, j=j: ((b + j) % 4,)) for j in (1, 2, 3)]
-    )
+    near = jnp.stack([turned] + [shift_y(turned, j) for j in (1, 2, 3)])
     far = swap(near, "xh")
     near_other, far_other = swap(near, "c"), swap(far, "c")
 
@@ -123,7 +127,7 @@
 
     mine, theirs = call(
         grad_kernel, [(128, 256), (128, 256)],
-        jnp.stack([y, c, (xh + xl) % 2]), grad_half, near, far, near_other, far_other,
+        jnp.stack([y, c, (xh + xl) % 2]), every, near, far, near_other, far_other,
     )
     rotated_grad = mine + swap(theirs, "xl")
     grad_square = (rotated_grad * rotated_grad).astype(jnp.bfloat16)
@@ -131,17 +135,21 @@
         grad_square, AXES, lambda a, b, e, p, q, r: (p, q, r // 2, a, b, 2 * e + r % 2)
     )
 
-    act_every, mine = lax.optimization_barrier((act_every, mine))
-    part = call(act_kernel, (8, 128, 256), jnp.stack([c, xl]), act_every, act_near, act_far)
+    every, mine = lax.optimization_barrier((every, mine))
+    part = call(act_kernel, (8, 128, 256), jnp.stack([c, xl]), every, act_near, act_far)
     part = lax.all_to_all(part, ("xh", "y"), split_axis=0, concat_axis=0, tiled=True)
     rotated_act = jnp.sum(part, axis=0)
     act_square = (rotated_act * rotated_act).astype(jnp.bfloat16)
-    act_block = lax.all_gather(act_square, ("xh", "y", "c"), axis=0, tiled=False)
+    grad_square, act_square = lax.optimization_barrier((grad_square, act_square))
     grad_block = to_all(grad_square, ("zh", "zl"), 16)
 
-    theirs = call(corrected_kernel, (256, 512), (1 - xl)[None], act_block, grad_block)
+    pair = jnp.stack([act_square, swap(act_square, "c")])
+    near = jnp.concatenate([pair] + [shift_y(pair, j) for j in (1, 2, 3)])
+    far = swap(near, "xh")
+
+    theirs = call(corrected_kernel, (256, 512), jnp.stack([1 - xl, xh, y, c]), near, far, grad_block)
     theirs = swap(theirs, "xl")
-    mine = call(corrected_kernel, (256, 512), xl[None], act_block, grad_block)
+    mine = call(corrected_kernel, (256, 512), jnp.stack([xl, xh, y, c]), near, far, grad_block)
     return (mine + theirs) * (1.0 / tokens)
 
 

time: 321 us -> 228 us (0.71)
  the two profiles are of different devices: /device:TPU:1 before, /device:TPU:98 now
where the time goes in v2:
time: 228 us
  waiting for transfers between devices  113 us (50%)
  starting transfers between devices  87.9 us (39%)
  between operations  13.7 us (6%)
  Pallas kernels  7.25 us (3%)
  other arithmetic  2.99 us (1%)
  local copies, waits for them, and re-layouts  2.76 us (1%)
    ppermute x18, waiting for transfers between devices, move(): return lax.ppermute(x, axes, pairs)  86.9 us
    ppermute x18, starting transfers between devices, move(): return lax.ppermute(x, axes, pairs)  59.9 us
    all_to_all x1, starting transfers between devices, to_all(): return lax.all_to_all(spread, axes, split_axis=0, concat_axis=0, tiled=True)  22.1 us
    all_to_all x1, waiting for transfers between devices, to_all(): return lax.all_to_all(spread, axes, split_axis=0, concat_axis=0, tiled=True)  13.7 us
    all_gather x1, waiting for transfers between devices, on_device(): every = lax.all_gather(both, ('zh', 'zl'), axis=0, tiled=False)  12.4 us
    pallas_call x4, Pallas kernels, call(): pl.pallas_call(kernel, out_shape=[jax.ShapeDtypeStruct(s, jnp.float32) fo...  7.25 us
    all_to_all x1, starting transfers between devices, on_device(): lax.all_to_all(part, ('xh', 'y'), split_axis=0, concat_axis=0, tiled=True)  5.83 us
  transfers between devices with their start and end apart: 21, of which 15 were waited for; matrix products, arithmetic and copies ran while one was open for 0% of the time, Pallas kernels for 2%

profile of v2, /device:TPU:98, one launch (start us, length us, event | category | flops | bytes accessed | tf_op | source)
XLA Modules:
  0.0 227.6 jit_solution(3848909012053178371)
XLA Ops:
  6.5 0.0 copy-start.2
  6.5 0.0 all-gather.3.cloned.1.call-start
  6.5 3.5 %collective-permute-start = (bf16[128,256]{1,0:T(8,128)(2,1)}, bf16[128,256]{1,0:T(8,128)(2,1)S(1)}, u32[]{:S(2)}, u32[]{:S(2)}) collective-permute-start(bf16[128,256]{1,0:T(8,128)(2,1)} %param.4), channel_id=1, source_target_pairs={{0,0},{4,64},{8,128},{12,192},{16,256},{20,320},{24,384},{28,448},... | collective-permute-start | bytes 196616 | tf_op jit(solution)/shard_map/ppermute | solution.py:40
  10.1 3.0 %collective-permute-done = bf16[128,256]{1,0:T(8,128)(2,1)S(1)} collective-permute-done((bf16[128,256]{1,0:T(8,128)(2,1)}, bf16[128,256]{1,0:T(8,128)(2,1)S(1)}, u32[]{:S(2)}, u32[]{:S(2)}) %collective-permute-start) | collective-permute-done | bytes 65568 | tf_op jit(solution)/shard_map/ppermute | solution.py:40
  13.0 1.5 pad_maximum_fusion.2
  14.5 0.0 all-gather.3.cloned.1.call-update
  14.6 3.4 %collective-permute-start.1 = (bf16[512,256]{1,0:T(8,128)(2,1)}, bf16[512,256]{1,0:T(8,128)(2,1)S(1)}, u32[]{:S(2)}, u32[]{:S(2)}) collective-permute-start(bf16[512,256]{1,0:T(8,128)(2,1)} %param.7), channel_id=1, source_target_pairs={{0,0},{16,256},{256,16},{272,272},{1,1},{17,257},{257,17},{273,273... | collective-permute-start | bytes 786440 | tf_op jit(solution)/shard_map/ppermute | solution.py:40
  18.0 9.5 %collective-permute-done.1 = bf16[512,256]{1,0:T(8,128)(2,1)S(1)} collective-permute-done((bf16[512,256]{1,0:T(8,128)(2,1)}, bf16[512,256]{1,0:T(8,128)(2,1)S(1)}, u32[]{:S(2)}, u32[]{:S(2)}) %collective-permute-start.1) | collective-permute-done | bytes 262176 | tf_op jit(solution)/shard_map/ppermute | solution.py:40
  27.5 13.3 %collective-permute-start.3 = (bf16[512,256]{1,0:T(8,128)(2,1)S(1)}, bf16[512,256]{1,0:T(8,128)(2,1)S(1)}, u32[]{:S(2)}, u32[]{:S(2)}) collective-permute-start(bf16[512,256]{1,0:T(8,128)(2,1)S(1)} %collective-permute-done.1), channel_id=1, source_target_pairs={{0,128},{64,192},{128,0},{192,64},{1,129},{65,193},{129,1},{193,65... | collective-permute-start | bytes 786440 | tf_op jit(solution)/shard_map/ppermute | solution.py:40
  40.8 4.1 %collective-permute-start.4 = (bf16[512,256]{1,0:T(8,128)(2,1)S(1)}, bf16[512,256]{1,0:T(8,128)(2,1)S(1)}, u32[]{:S(2)}, u32[]{:S(2)}) collective-permute-start(bf16[512,256]{1,0:T(8,128)(2,1)S(1)} %collective-permute-done.1), channel_id=1, source_target_pairs={{0,192},{64,0},{128,64},{192,128},{1,193},{65,1},{129,65},{193,129... | collective-permute-start | bytes 786440 | tf_op jit(solution)/shard_map/ppermute | solution.py:40
  44.9 2.8 %collective-permute-start.2 = (bf16[512,256]{1,0:T(8,128)(2,1)S(1)}, bf16[512,256]{1,0:T(8,128)(2,1)S(1)}, u32[]{:S(2)}, u32[]{:S(2)}) collective-permute-start(bf16[512,256]{1,0:T(8,128)(2,1)S(1)} %collective-permute-done.1), channel_id=1, source_target_pairs={{0,64},{64,128},{128,192},{192,0},{1,65},{65,129},{129,193},{193,1... | collective-permute-start | bytes 786440 | tf_op jit(solution)/shard_map/ppermute | solution.py:40
  47.6 0.0 collective-permute-done.3
  47.6 6.4 %collective-permute-done.4 = bf16[512,256]{1,0:T(8,128)(2,1)S(1)} collective-permute-done((bf16[512,256]{1,0:T(8,128)(2,1)S(1)}, bf16[512,256]{1,0:T(8,128)(2,1)S(1)}, u32[]{:S(2)}, u32[]{:S(2)}) %collective-permute-start.4) | collective-permute-done | bytes 262176 | tf_op jit(solution)/shard_map/ppermute | solution.py:40
  54.1 0.3 collective-permute-done.2
  54.4 0.1 pad_maximum_fusion.near_ref
  54.5 1.9 collective-permute-start.5
  56.5 1.9 collective-permute-start.6
  58.4 22.8 %collective-permute-done.5.far_ref = bf16[4,512,256]{2,1,0:T(8,128)(2,1)S(1)} collective-permute-done((bf16[4,512,256]{2,1,0:T(8,128)(2,1)S(1)}, bf16[4,512,256]{2,1,0:T(8,128)(2,1)S(1)}, u32[]{:S(2)}, u32[]{:S(2)}) %collective-permute-start.5) | collective-permute-done | bytes 1048608 | tf_op jit(solution)/shard_map/ppermute | solution.py:40
  81.2 1.9 collective-permute-start.7
  83.1 0.0 copy-done.2
  83.1 2.4 %collective-permute-start.10 = (bf16[512,256]{1,0:T(8,128)(2,1)S(1)}, bf16[512,256]{1,0:T(8,128)(2,1)S(1)}, u32[]{:S(2)}, u32[]{:S(2)}) collective-permute-start(bf16[512,256]{1,0:T(8,128)(2,1)S(1)} %copy-done.2), channel_id=1, source_target_pairs={{0,32},{32,0},{1,33},{33,1},{2,34},{34,2},{3,35},{35,3},{4,36},{36... | collective-permute-start | bytes 786440 | tf_op jit(solution)/shard_map/ppermute | solution.py:40
  85.5 1.1 collective-permute-done.10
  86.7 0.1 pad_maximum_fusion.1.near_ref
  86.7 3.1 %collective-permute-start.11 = (bf16[2,512,256]{2,1,0:T(8,128)(2,1)S(1)}, bf16[2,512,256]{2,1,0:T(8,128)(2,1)S(1)}, u32[]{:S(2)}, u32[]{:S(2)}) collective-permute-start(bf16[2,512,256]{2,1,0:T(8,128)(2,1)S(1)} %pad_maximum_fusion.1.near_ref), channel_id=1, source_target_pairs={{0,16},{16,0},{1,17},{17,1},{2,18},{18,2},{3,19},{19,3},{4,20},{20... | collective-permute-start | bytes 1572872 | tf_op jit(solution)/shard_map/ppermute | solution.py:40
  89.8 0.1 pad_add_fusion.1.at_ref
  89.9 0.1 pad_add_fusion.at_ref
  90.0 0.0 collective-permute-done.6.near_other_ref
  90.0 0.0 collective-permute-done.7.far_other_ref
  90.0 12.4 %all-gather.3.cloned.1.call-done = bf16[32,128,256]{2,1,0:T(8,128)(2,1)} async-done(((bf16[2,128,256]{2,1,0:T(8,128)(2,1)}), bf16[32,128,256]{2,1,0:T(8,128)(2,1)}) %all-gather.3.cloned.1.call-update) | async-done | bytes 2097168 | tf_op jit(solution)/shard_map/all_gather | solution.py:118
  102.4 0.0 copy-start
  102.4 1.6 copy-done
  104.0 0.0 copy-start.1
  104.0 2.4 %shard_map.46 = (f32[128,256]{1,0:T(8,128)S(1)}, f32[128,256]{1,0:T(8,128)S(1)}) custom-call(s32[3]{0:T(128)S(1)} %pad_add_fusion.at_ref, bf16[16,2,128,256]{3,2,1,0:T(8,128)(2,1)S(1)} %bitcast.19, bf16[4,512,256]{2,1,0:T(8,128)(2,1)S(1)} %pad_maximum_fusion.near_ref, bf16[4,512,256]{2,1,0:T(8,128)(2,1)S(1)} %collective-permute-done.5.far_ref, ...), custom_call_target="tpu_custom_call" | custom-call | tf_op jit(solution)/shard_map/pallas_call | solution.py:93
  106.4 0.0 collective-permute-done.11.far_ref
  106.4 0.0 copy-done.1
  106.4 2.3 %shard_map.47 = f32[8,128,256]{2,1,0:T(8,128)} custom-call(s32[2]{0:T(128)S(1)} %pad_add_fusion.1.at_ref, bf16[16,2,128,256]{3,2,1,0:T(8,128)(2,1)S(1)} %bitcast.20, bf16[2,512,256]{2,1,0:T(8,128)(2,1)S(1)} %pad_maximum_fusion.1.near_ref, bf16[2,512,256]{2,1,0:T(8,128)(2,1)S(1)} %collective-permute-done.11.far_ref), custom_call_target="tpu_custom_call" | custom-call | tf_op jit(solution)/shard_map/pallas_call | solution.py:93
  108.7 5.8 %all-to-all-start = ((f32[8,128,256]{2,1,0:T(8,128)}), f32[8,128,256]{2,1,0:T(8,128)S(1)}, u32[]{:S(2)}, u32[]{:S(2)}) async-start(f32[8,128,256]{2,1,0:T(8,128)} %shard_map.47), calls=%async_computation | async-start | bytes 2097152 | tf_op jit(solution)/shard_map/all_to_all | solution.py:140
  114.6 3.2 %collective-permute-start.8 = (f32[128,256]{1,0:T(8,128)S(1)}, f32[128,256]{1,0:T(8,128)S(1)}, u32[]{:S(2)}, u32[]{:S(2)}) collective-permute-start(f32[128,256]{1,0:T(8,128)S(1)} %get-tuple-element.16), channel_id=1, source_target_pairs={{0,16},{16,0},{1,17},{17,1},{2,18},{18,2},{3,19},{19,3},{4,20},{20... | collective-permute-start | bytes 393224 | tf_op jit(solution)/shard_map/ppermute | solution.py:40
  117.8 10.6 %collective-permute-done.8 = f32[128,256]{1,0:T(8,128)S(1)} collective-permute-done((f32[128,256]{1,0:T(8,128)S(1)}, f32[128,256]{1,0:T(8,128)S(1)}, u32[]{:S(2)}, u32[]{:S(2)}) %collective-permute-start.8) | collective-permute-done | bytes 131104 | tf_op jit(solution)/shard_map/ppermute | solution.py:40
  128.5 1.9 collective-permute-start.9
  130.4 0.0 all-to-all-done
  130.4 0.1 reduce_sum.9
  130.5 6.1 %collective-permute-done.9 = bf16[128,256]{1,0:T(8,128)(2,1)S(1)} collective-permute-done((bf16[128,256]{1,0:T(8,128)(2,1)S(1)}, bf16[128,256]{1,0:T(8,128)(2,1)S(1)}, u32[]{:S(2)}, u32[]{:S(2)}) %collective-permute-start.9) | collective-permute-done | bytes 65568 | tf_op jit(solution)/shard_map/ppermute | solution.py:40
  136.6 1.1 broadcast_in_dim.2
  137.7 22.1 %all-to-all-start.1 = ((bf16[16,128,256]{2,1,0:T(8,128)(2,1)}), bf16[16,128,256]{2,1,0:T(8,128)(2,1)S(1)}, u32[]{:S(2)}, u32[]{:S(2)}) async-start(bf16[16,128,256]{2,1,0:T(8,128)(2,1)} %broadcast_in_dim.2), calls=%async_computation.1 | async-start | bytes 2097152 | tf_op jit(solution)/shard_map/all_to_all | solution.py:18
  159.8 1.9 collective-permute-start.12
  161.8 1.2 collective-permute-done.12
  163.0 1.9 collective-permute-start.13
  164.9 1.9 collective-permute-start.14
  166.8 5.1 %collective-permute-start.15 = (bf16[2,128,256]{2,1,0:T(8,128)(2,1)S(1)}, bf16[2,128,256]{2,1,0:T(8,128)(2,1)S(1)}, u32[]{:S(2)}, u32[]{:S(2)}) collective-permute-start(bf16[2,128,256]{2,1,0:T(8,128)(2,1)S(1)} %pad_maximum_fusion.3), channel_id=1, source_target_pairs={{0,192},{64,0},{128,64},{192,128},{1,193},{65,1},{129,65},{193,129... | collective-permute-start | bytes 393224 | tf_op jit(solution)/shard_map/ppermute | solution.py:40
  172.0 2.5 %collective-permute-done.13 = bf16[2,128,256]{2,1,0:T(8,128)(2,1)S(1)} collective-permute-done((bf16[2,128,256]{2,1,0:T(8,128)(2,1)S(1)}, bf16[2,128,256]{2,1,0:T(8,128)(2,1)S(1)}, u32[]{:S(2)}, u32[]{:S(2)}) %collective-permute-start.13) | collective-permute-done | bytes 131104 | tf_op jit(solution)/shard_map/ppermute | solution.py:40
  174.5 0.0 collective-permute-done.14
  174.5 2.5 %collective-permute-done.15 = bf16[2,128,256]{2,1,0:T(8,128)(2,1)S(1)} collective-permute-done((bf16[2,128,256]{2,1,0:T(8,128)(2,1)S(1)}, bf16[2,128,256]{2,1,0:T(8,128)(2,1)S(1)}, u32[]{:S(2)}, u32[]{:S(2)}) %collective-permute-start.15) | collective-permute-done | bytes 131104 | tf_op jit(solution)/shard_map/ppermute | solution.py:40
  177.0 3.7 %collective-permute-start.16 = (bf16[8,128,256]{2,1,0:T(8,128)(2,1)S(1)}, bf16[8,128,256]{2,1,0:T(8,128)(2,1)S(1)}, u32[]{:S(2)}, u32[]{:S(2)}) collective-permute-start(bf16[8,128,256]{2,1,0:T(8,128)(2,1)S(1)} %constant_dynamic-update-slice_fusion.near_ref), channel_id=1, source_target_pairs={{0,256},{256,0},{1,257},{257,1},{2,258},{258,2},{3,259},{259,3},{4... | collective-permute-start | bytes 1572872 | tf_op jit(solution)/shard_map/ppermute | solution.py:40
  180.6 0.1 add_add_fusion.1.at_ref
  180.7 12.7 %collective-permute-done.16.far_ref = bf16[8,128,256]{2,1,0:T(8,128)(2,1)S(1)} collective-permute-done((bf16[8,128,256]{2,1,0:T(8,128)(2,1)S(1)}, bf16[8,128,256]{2,1,0:T(8,128)(2,1)S(1)}, u32[]{:S(2)}, u32[]{:S(2)}) %collective-permute-start.16) | collective-permute-done | bytes 524320 | tf_op jit(solution)/shard_map/ppermute | solution.py:40
  193.4 13.7 %all-to-all-done.1.s_ref = bf16[16,128,256]{2,1,0:T(8,128)(2,1)S(1)} async-done(((bf16[16,128,256]{2,1,0:T(8,128)(2,1)}), bf16[16,128,256]{2,1,0:T(8,128)(2,1)S(1)}, u32[]{:S(2)}, u32[]{:S(2)}) %all-to-all-start.1) | async-done | bytes 1048608 | tf_op jit(solution)/shard_map/all_to_all | solution.py:18
  207.1 1.3 shard_map.49
  208.3 1.9 collective-permute-start.17
  210.3 0.1 add_add_fusion.at_ref
  210.3 1.3 shard_map.48
  211.6 8.3 %collective-permute-done.17 = f32[256,512]{1,0:T(8,128)S(1)} collective-permute-done((f32[256,512]{1,0:T(8,128)S(1)}, f32[256,512]{1,0:T(8,128)S(1)}, u32[]{:S(2)}, u32[]{:S(2)}) %collective-permute-start.17) | collective-permute-done | bytes 524320 | tf_op jit(solution)/shard_map/ppermute | solution.py:40
  219.9 0.9 add_multiply_fusion
  (8 shorter events, 0.1 us)
Async XLA Ops:
  6.5 76.6 %copy-start.2 = (bf16[512,256]{1,0:T(8,128)(2,1)S(1)}, bf16[512,256]{1,0:T(8,128)(2,1)}, u32[]{:S(2)}) copy-start(bf16[512,256]{1,0:T(8,128)(2,1)} %param.6) | copy-start | bytes 786436
  6.5 95.9 %all-gather.3.cloned.1.call-start = ((), (), s32[]{:S(2)}) async-start(), calls=%async_computation.2 | async-start | bytes 2228224 | tf_op jit(solution)/shard_map/all_gather | solution.py:118
  6.5 6.5 %collective-permute-start = (bf16[128,256]{1,0:T(8,128)(2,1)}, bf16[128,256]{1,0:T(8,128)(2,1)S(1)}, u32[]{:S(2)}, u32[]{:S(2)}) collective-permute-start(bf16[128,256]{1,0:T(8,128)(2,1)} %param.4), channel_id=1, source_target_pairs={{0,0},{4,64},{8,128},{12,192},{16,256},{20,320},{24,384},{28,448},... | collective-permute-start | bytes 196616 | tf_op jit(solution)/shard_map/ppermute | solution.py:40
  14.6 12.9 %collective-permute-start.1 = (bf16[512,256]{1,0:T(8,128)(2,1)}, bf16[512,256]{1,0:T(8,128)(2,1)S(1)}, u32[]{:S(2)}, u32[]{:S(2)}) collective-permute-start(bf16[512,256]{1,0:T(8,128)(2,1)} %param.7), channel_id=1, source_target_pairs={{0,0},{16,256},{256,16},{272,272},{1,1},{17,257},{257,17},{273,273... | collective-permute-start | bytes 786440 | tf_op jit(solution)/shard_map/ppermute | solution.py:40
  27.5 20.1 %collective-permute-start.3 = (bf16[512,256]{1,0:T(8,128)(2,1)S(1)}, bf16[512,256]{1,0:T(8,128)(2,1)S(1)}, u32[]{:S(2)}, u32[]{:S(2)}) collective-permute-start(bf16[512,256]{1,0:T(8,128)(2,1)S(1)} %collective-permute-done.1), channel_id=1, source_target_pairs={{0,128},{64,192},{128,0},{192,64},{1,129},{65,193},{129,1},{193,65... | collective-permute-start | bytes 786440 | tf_op jit(solution)/shard_map/ppermute | solution.py:40
  40.8 13.3 %collective-permute-start.4 = (bf16[512,256]{1,0:T(8,128)(2,1)S(1)}, bf16[512,256]{1,0:T(8,128)(2,1)S(1)}, u32[]{:S(2)}, u32[]{:S(2)}) collective-permute-start(bf16[512,256]{1,0:T(8,128)(2,1)S(1)} %collective-permute-done.1), channel_id=1, source_target_pairs={{0,192},{64,0},{128,64},{192,128},{1,193},{65,1},{129,65},{193,129... | collective-permute-start | bytes 786440 | tf_op jit(solution)/shard_map/ppermute | solution.py:40
  44.9 9.5 %collective-permute-start.2 = (bf16[512,256]{1,0:T(8,128)(2,1)S(1)}, bf16[512,256]{1,0:T(8,128)(2,1)S(1)}, u32[]{:S(2)}, u32[]{:S(2)}) collective-permute-start(bf16[512,256]{1,0:T(8,128)(2,1)S(1)} %collective-permute-done.1), channel_id=1, source_target_pairs={{0,64},{64,128},{128,192},{192,0},{1,65},{65,129},{129,193},{193,1... | collective-permute-start | bytes 786440 | tf_op jit(solution)/shard_map/ppermute | solution.py:40
  54.5 26.6 %collective-permute-start.5 = (bf16[4,512,256]{2,1,0:T(8,128)(2,1)S(1)}, bf16[4,512,256]{2,1,0:T(8,128)(2,1)S(1)}, u32[]{:S(2)}, u32[]{:S(2)}) collective-permute-start(bf16[4,512,256]{2,1,0:T(8,128)(2,1)S(1)} %pad_maximum_fusion.near_ref), channel_id=1, source_target_pairs={{0,256},{256,0},{1,257},{257,1},{2,258},{258,2},{3,259},{259,3},{4... | collective-permute-start | bytes 3145736 | tf_op jit(solution)/shard_map/ppermute | solution.py:40
  56.5 33.5 %collective-permute-start.6 = (bf16[4,512,256]{2,1,0:T(8,128)(2,1)S(1)}, bf16[4,512,256]{2,1,0:T(8,128)(2,1)}, u32[]{:S(2)}, u32[]{:S(2)}) collective-permute-start(bf16[4,512,256]{2,1,0:T(8,128)(2,1)S(1)} %pad_maximum_fusion.near_ref), channel_id=1, source_target_pairs={{0,32},{32,0},{1,33},{33,1},{2,34},{34,2},{3,35},{35,3},{4,36},{36... | collective-permute-start | bytes 3145736 | tf_op jit(solution)/shard_map/ppermute | solution.py:40
  81.2 8.8 %collective-permute-start.7 = (bf16[4,512,256]{2,1,0:T(8,128)(2,1)S(1)}, bf16[4,512,256]{2,1,0:T(8,128)(2,1)}, u32[]{:S(2)}, u32[]{:S(2)}) collective-permute-start(bf16[4,512,256]{2,1,0:T(8,128)(2,1)S(1)} %collective-permute-done.5.far_ref), channel_id=1, source_target_pairs={{0,32},{32,0},{1,33},{33,1},{2,34},{34,2},{3,35},{35,3},{4,36},{36... | collective-permute-start | bytes 3145736 | tf_op jit(solution)/shard_map/ppermute | solution.py:40
  83.1 3.6 %collective-permute-start.10 = (bf16[512,256]{1,0:T(8,128)(2,1)S(1)}, bf16[512,256]{1,0:T(8,128)(2,1)S(1)}, u32[]{:S(2)}, u32[]{:S(2)}) collective-permute-start(bf16[512,256]{1,0:T(8,128)(2,1)S(1)} %copy-done.2), channel_id=1, source_target_pairs={{0,32},{32,0},{1,33},{33,1},{2,34},{34,2},{3,35},{35,3},{4,36},{36... | collective-permute-start | bytes 786440 | tf_op jit(solution)/shard_map/ppermute | solution.py:40
  86.7 19.7 %collective-permute-start.11 = (bf16[2,512,256]{2,1,0:T(8,128)(2,1)S(1)}, bf16[2,512,256]{2,1,0:T(8,128)(2,1)S(1)}, u32[]{:S(2)}, u32[]{:S(2)}) collective-permute-start(bf16[2,512,256]{2,1,0:T(8,128)(2,1)S(1)} %pad_maximum_fusion.1.near_ref), channel_id=1, source_target_pairs={{0,16},{16,0},{1,17},{17,1},{2,18},{18,2},{3,19},{19,3},{4,20},{20... | collective-permute-start | bytes 1572872 | tf_op jit(solution)/shard_map/ppermute | solution.py:40
  102.4 1.6 copy-start
  104.0 2.4 %copy-start.1 = (bf16[32,128,256]{2,1,0:T(8,128)(2,1)S(1)}, bf16[32,128,256]{2,1,0:T(8,128)(2,1)}, u32[]{:S(2)}) copy-start(bf16[32,128,256]{2,1,0:T(8,128)(2,1)} %all-gather.3.cloned.1.call-done) | copy-start | bytes 6291460
  108.7 21.7 %all-to-all-start = ((f32[8,128,256]{2,1,0:T(8,128)}), f32[8,128,256]{2,1,0:T(8,128)S(1)}, u32[]{:S(2)}, u32[]{:S(2)}) async-start(f32[8,128,256]{2,1,0:T(8,128)} %shard_map.47), calls=%async_computation | async-start | bytes 2097152 | tf_op jit(solution)/shard_map/all_to_all | solution.py:140
  114.6 13.9 %collective-permute-start.8 = (f32[128,256]{1,0:T(8,128)S(1)}, f32[128,256]{1,0:T(8,128)S(1)}, u32[]{:S(2)}, u32[]{:S(2)}) collective-permute-start(f32[128,256]{1,0:T(8,128)S(1)} %get-tuple-element.16), channel_id=1, source_target_pairs={{0,16},{16,0},{1,17},{17,1},{2,18},{18,2},{3,19},{19,3},{4,20},{20... | collective-permute-start | bytes 393224 | tf_op jit(solution)/shard_map/ppermute | solution.py:40
  128.5 8.1 %collective-permute-start.9 = (bf16[128,256]{1,0:T(8,128)(2,1)S(1)}, bf16[128,256]{1,0:T(8,128)(2,1)S(1)}, u32[]{:S(2)}, u32[]{:S(2)}) collective-permute-start(bf16[128,256]{1,0:T(8,128)(2,1)S(1)} %multiply_convert_fusion.1), channel_id=1, source_target_pairs={{0,0},{1,1},{2,32},{3,33},{4,64},{5,65},{6,96},{7,97},{8,128},{9,1... | collective-permute-start | bytes 196616 | tf_op jit(solution)/shard_map/ppermute | solution.py:40
  137.7 69.4 %all-to-all-start.1 = ((bf16[16,128,256]{2,1,0:T(8,128)(2,1)}), bf16[16,128,256]{2,1,0:T(8,128)(2,1)S(1)}, u32[]{:S(2)}, u32[]{:S(2)}) async-start(bf16[16,128,256]{2,1,0:T(8,128)(2,1)} %broadcast_in_dim.2), calls=%async_computation.1 | async-start | bytes 2097152 | tf_op jit(solution)/shard_map/all_to_all | solution.py:18
  159.8 3.1 %collective-permute-start.12 = (bf16[128,256]{1,0:T(8,128)(2,1)S(1)}, bf16[128,256]{1,0:T(8,128)(2,1)S(1)}, u32[]{:S(2)}, u32[]{:S(2)}) collective-permute-start(bf16[128,256]{1,0:T(8,128)(2,1)S(1)} %multiply_convert_fusion), channel_id=1, source_target_pairs={{0,32},{32,0},{1,33},{33,1},{2,34},{34,2},{3,35},{35,3},{4,36},{36... | collective-permute-start | bytes 196616 | tf_op jit(solution)/shard_map/ppermute | solution.py:40
  163.0 11.5 %collective-permute-start.13 = (bf16[2,128,256]{2,1,0:T(8,128)(2,1)S(1)}, bf16[2,128,256]{2,1,0:T(8,128)(2,1)S(1)}, u32[]{:S(2)}, u32[]{:S(2)}) collective-permute-start(bf16[2,128,256]{2,1,0:T(8,128)(2,1)S(1)} %pad_maximum_fusion.3), channel_id=1, source_target_pairs={{0,64},{64,128},{128,192},{192,0},{1,65},{65,129},{129,193},{193,1... | collective-permute-start | bytes 393224 | tf_op jit(solution)/shard_map/ppermute | solution.py:40
  164.9 9.6 %collective-permute-start.14 = (bf16[2,128,256]{2,1,0:T(8,128)(2,1)S(1)}, bf16[2,128,256]{2,1,0:T(8,128)(2,1)S(1)}, u32[]{:S(2)}, u32[]{:S(2)}) collective-permute-start(bf16[2,128,256]{2,1,0:T(8,128)(2,1)S(1)} %pad_maximum_fusion.3), channel_id=1, source_target_pairs={{0,128},{64,192},{128,0},{192,64},{1,129},{65,193},{129,1},{193,65... | collective-permute-start | bytes 393224 | tf_op jit(solution)/shard_map/ppermute | solution.py:40
  166.8 10.1 %collective-permute-start.15 = (bf16[2,128,256]{2,1,0:T(8,128)(2,1)S(1)}, bf16[2,128,256]{2,1,0:T(8,128)(2,1)S(1)}, u32[]{:S(2)}, u32[]{:S(2)}) collective-permute-start(bf16[2,128,256]{2,1,0:T(8,128)(2,1)S(1)} %pad_maximum_fusion.3), channel_id=1, source_target_pairs={{0,192},{64,0},{128,64},{192,128},{1,193},{65,1},{129,65},{193,129... | collective-permute-start | bytes 393224 | tf_op jit(solution)/shard_map/ppermute | solution.py:40
  177.0 16.4 %collective-permute-start.16 = (bf16[8,128,256]{2,1,0:T(8,128)(2,1)S(1)}, bf16[8,128,256]{2,1,0:T(8,128)(2,1)S(1)}, u32[]{:S(2)}, u32[]{:S(2)}) collective-permute-start(bf16[8,128,256]{2,1,0:T(8,128)(2,1)S(1)} %constant_dynamic-update-slice_fusion.near_ref), channel_id=1, source_target_pairs={{0,256},{256,0},{1,257},{257,1},{2,258},{258,2},{3,259},{259,3},{4... | collective-permute-start | bytes 1572872 | tf_op jit(solution)/shard_map/ppermute | solution.py:40
  208.3 11.5 %collective-permute-start.17 = (f32[256,512]{1,0:T(8,128)S(1)}, f32[256,512]{1,0:T(8,128)S(1)}, u32[]{:S(2)}, u32[]{:S(2)}) collective-permute-start(f32[256,512]{1,0:T(8,128)S(1)} %shard_map.49), channel_id=1, source_target_pairs={{0,16},{16,0},{1,17},{17,1},{2,18},{18,2},{3,19},{19,3},{4,20},{20... | collective-permute-start | bytes 1572872 | tf_op jit(solution)/shard_map/ppermute | solution.py:40
Sparse Core Ops, SparseCore 0:
  14.7 87.6 all-gather.2

commit v3 on v1

v3 whole, which is shorter than its diff:
```python
import functools
import jax
import jax.numpy as jnp
from jax import lax
from jax.experimental import pallas as pl
from jax.experimental.pallas import tpu as pltpu
from jax.sharding import Mesh, PartitionSpec as P

AXES = ("xh", "y", "c", "xl", "zh", "zl")
SIZES = (2, 4, 2, 2, 4, 4)
VMEM = pl.BlockSpec(memory_space=pltpu.VMEM)
SMEM = pl.BlockSpec(memory_space=pltpu.SMEM)
PARAMS = pltpu.CompilerParams(vmem_limit_bytes=40 * 1024 * 1024)


def to_all(x, axes, n):
    spread = jnp.broadcast_to(x[None], (n,) + x.shape)
    return lax.all_to_all(spread, axes, split_axis=0, concat_axis=0, tiled=True)


def move(x, axes, target):
    sizes = [SIZES[AXES.index(a)] for a in axes]

    def flat(coords):
        out = 0
        for c, s in zip(coords, sizes):
            out = out * s + c
        return out

    total = 1
    for s in sizes:
        total *= s
    pairs = []
    for i in range(total):
        rest, coords = i, []
        for s in reversed(sizes):
            coords.insert(0, rest % s)
            rest //= s
        pairs.append((i, flat(target(*coords))))
    return lax.ppermute(x, axes, pairs)


def dot(a, b):
    return jnp.dot(a, b, preferred_element_type=jnp.float32)


def rotate_kernel(at_ref, x_ref, near_ref, far_ref, near_other_ref, far_other_ref, mine_ref, theirs_ref):
    y, c, turned = at_ref[0], at_ref[1], at_ref[2]
    sums = []
    for own, other in ((near_ref, near_other_ref), (far_ref, far_other_ref)):
        acc = jnp.zeros(mine_ref.shape, jnp.float32)
        for j in range(4):
            at = 4 * lax.rem(y + 4 - j, 4)
            for h in range(2):
                rows = slice(256 * h, 256 * h + 256)
                acc += dot(x_ref[at + 2 * c + h, 0], own[j, 0, rows, :])
                acc += dot(x_ref[at + 2 * (1 - c) + h, 0], other[j, 0, rows, :])
        sums.append(acc)
    near, far = sums
    mine_ref[...] = jnp.where(turned == 0, near, far)
    theirs_ref[...] = jnp.where(turned == 0, far, near)


def corrected_kernel(at_ref, near_ref, far_ref, near_other_ref, far_other_ref, s_ref, out_ref):
    y, c, which = at_ref[0], at_ref[1], at_ref[2]

    def contract(own, other):
        for h in range(2):
            acc = jnp.zeros((256, 256), jnp.float32)
            for j in range(4):
                at = 4 * lax.rem(y + 4 - j, 4) + h
                for act, core in ((own, c), (other, 1 - c)):
                    acc += lax.dot_general(
                        act[j], s_ref[at + 2 * core],
                        (((0,), (0,)), ((), ())), preferred_element_type=jnp.float32,
                    )
            out_ref[:, 256 * h:256 * h + 256] = acc

    @pl.when(which == 0)
    def _():
        contract(near_ref, near_other_ref)

    @pl.when(which != 0)
    def _():
        contract(far_ref, far_other_ref)


def rotate(at, x, part, bases, basis_part):
    one = lambda shape, part: pl.BlockSpec(
        (shape[0], 1) + shape[2:], lambda i: (0, part, 0, 0), pipeline_mode=pl.Buffered(1)
    )
    out = jax.ShapeDtypeStruct(x.shape[2:], jnp.float32)
    return pl.pallas_call(
        rotate_kernel,
        grid=(1,),
        out_shape=[out, out],
        in_specs=[SMEM, one(x.shape, part)] + [one(b.shape, basis_part) for b in bases],
        out_specs=[pl.BlockSpec(out.shape, lambda i: (0, 0))] * 2,
        compiler_params=PARAMS,
    )(at, x, *bases)


def correct(at, acts, grads):
    return pl.pallas_call(
        corrected_kernel,
        out_shape=jax.ShapeDtypeStruct((256, 512), jnp.float32),
        in_specs=[SMEM] + [VMEM] * 5,
        out_specs=VMEM,
        compiler_params=PARAMS,
    )(at, *acts, grads)


def swap(x, axis):
    return move(x, (axis,), lambda i: (1 - i,))


def plane_gather(x):
    own = []
    for k in range(2):
        blocks = [
            move(x, ("xh", "y", "xl"), lambda a, b, p, j=j: (p ^ k, (b + j) % 4, a)) for j in range(4)
        ]
        own.append(jnp.stack(blocks))
    return own + [swap(o, "c") for o in own]


def square(mine, theirs):
    total = mine + swap(theirs, "xl")
    return (total * total).astype(jnp.bfloat16)


def on_device(activations, gradients, act_basis, grad_basis):
    tokens = activations.shape[0] * 16
    xh, y, c, xl = (lax.axis_index(a) for a in ("xh", "y", "c", "xl"))
    turned = (xh + xl) % 2
    at = jnp.stack([y, c, turned])

    both = jnp.stack([activations, gradients])
    act_every = grad_every = lax.all_gather(both, ("zh", "zl"), axis=0, tiled=False)
    bases = plane_gather(jnp.stack([act_basis, grad_basis]))

    mine, theirs = rotate(at, grad_every, 1, bases, 1)
    grad_square = square(mine, theirs)
    grad_square = move(
        grad_square, AXES, lambda a, b, e, p, q, r: (p, q, r // 2, a, b, 2 * e + r % 2)
    )

    act_every, mine = lax.optimization_barrier((act_every, mine))
    act_square = square(*rotate(at, act_every, 0, bases, 0))
    grad_square, act_square = lax.optimization_barrier((grad_square, act_square))
    grad_block = to_all(grad_square, ("zh", "zl"), 16)
    acts = plane_gather(act_square)

    theirs = swap(correct(jnp.stack([y, c, 1 - turned]), acts, grad_block), "xl")
    mine = correct(at, acts, grad_block)
    return (mine + theirs) * (1.0 / tokens)


def solution(mesh):
    fine = Mesh(mesh.devices.reshape(SIZES), AXES)
    spec = P(("xh", "y", "c"), ("xl", "zh", "zl"))
    return jax.shard_map(
        on_device,
        mesh=fine,
        in_specs=(spec, spec, spec, spec),
        out_specs=P(("xl", "zh", "zl"), ("xh", "y", "c")),
        check_vma=False,
    )
```

time: 321 us -> 236 us (0.74)
  the two profiles are of different devices: /device:TPU:1 before, /device:TPU:8 now
where the time goes in v3:
time: 236 us
  starting transfers between devices  139 us (59%)
  waiting for transfers between devices  66.9 us (28%)
  between operations  13.8 us (6%)
  Pallas kernels  7.98 us (3%)
  other arithmetic  5.6 us (2%)
  local copies, waits for them, and re-layouts  2.68 us (1%)
    ppermute x24, starting transfers between devices, move(): return lax.ppermute(x, axes, pairs)  119 us
    ppermute x24, waiting for transfers between devices, move(): return lax.ppermute(x, axes, pairs)  55.5 us
    all_to_all x1, starting transfers between devices, to_all(): return lax.all_to_all(spread, axes, split_axis=0, concat_axis=0, tiled=True)  19.3 us
    all_to_all x1, waiting for transfers between devices, to_all(): return lax.all_to_all(spread, axes, split_axis=0, concat_axis=0, tiled=True)  11.3 us
    pallas_call x2, Pallas kernels, rotate(): pl.pallas_call(rotate_kernel, grid=(1,), out_shape=[out, out], in_specs=[...  5.43 us
  transfers between devices with their start and end apart: 26, of which 9 were waited for; matrix products, arithmetic and copies ran while one was open for 1% of the time, Pallas kernels for 2%

profile of v3, /device:TPU:8, one launch (start us, length us, event | category | flops | bytes accessed | tf_op | source)
XLA Modules:
  0.0 235.6 jit_solution(6961413976618941638)
XLA Ops:
  6.5 1.5 pad_maximum_fusion.5
  8.1 0.0 all-gather.3.cloned.1.call-update
  8.1 1.1 pad_maximum_fusion.2
  9.2 7.7 %collective-permute-start.3 = (bf16[2,512,256]{2,1,0:T(8,128)(2,1)S(1)}, bf16[2,512,256]{2,1,0:T(8,128)(2,1)S(1)}, u32[]{:S(2)}, u32[]{:S(2)}) collective-permute-start(bf16[2,512,256]{2,1,0:T(8,128)(2,1)S(1)} %pad_maximum_fusion.2), channel_id=1, source_target_pairs={{0,192},{16,448},{64,0},{80,256},{128,64},{144,320},{192,128},{208... | collective-permute-start | bytes 1572872 | tf_op jit(solution)/shard_map/ppermute | solution.py:40
  16.9 1.9 collective-permute-start.2
  18.9 3.4 %collective-permute-start.1 = (bf16[2,512,256]{2,1,0:T(8,128)(2,1)S(1)}, bf16[2,512,256]{2,1,0:T(8,128)(2,1)S(1)}, u32[]{:S(2)}, u32[]{:S(2)}) collective-permute-start(bf16[2,512,256]{2,1,0:T(8,128)(2,1)S(1)} %pad_maximum_fusion.2), channel_id=1, source_target_pairs={{0,64},{16,320},{64,128},{80,384},{128,192},{144,448},{192,0},{208... | collective-permute-start | bytes 1572872 | tf_op jit(solution)/shard_map/ppermute | solution.py:40
  22.2 0.7 collective-permute-start
  22.9 5.7 %collective-permute-start.7 = (bf16[2,512,256]{2,1,0:T(8,128)(2,1)S(1)}, bf16[2,512,256]{2,1,0:T(8,128)(2,1)S(1)}, u32[]{:S(2)}, u32[]{:S(2)}) collective-permute-start(bf16[2,512,256]{2,1,0:T(8,128)(2,1)S(1)} %pad_maximum_fusion.2), channel_id=1, source_target_pairs={{0,448},{16,192},{64,256},{80,0},{128,320},{144,64},{192,384},{208... | collective-permute-start | bytes 1572872 | tf_op jit(solution)/shard_map/ppermute | solution.py:40
  28.7 10.8 %collective-permute-done.3 = bf16[2,512,256]{2,1,0:T(8,128)(2,1)S(1)} collective-permute-done((bf16[2,512,256]{2,1,0:T(8,128)(2,1)S(1)}, bf16[2,512,256]{2,1,0:T(8,128)(2,1)S(1)}, u32[]{:S(2)}, u32[]{:S(2)}) %collective-permute-start.3) | collective-permute-done | bytes 524320 | tf_op jit(solution)/shard_map/ppermute | solution.py:40
  39.5 1.9 collective-permute-start.6
  41.4 18.1 %collective-permute-done.2 = bf16[2,512,256]{2,1,0:T(8,128)(2,1)S(1)} collective-permute-done((bf16[2,512,256]{2,1,0:T(8,128)(2,1)S(1)}, bf16[2,512,256]{2,1,0:T(8,128)(2,1)S(1)}, u32[]{:S(2)}, u32[]{:S(2)}) %collective-permute-start.2) | collective-permute-done | bytes 524320 | tf_op jit(solution)/shard_map/ppermute | solution.py:40
  59.5 12.0 %collective-permute-start.5 = (bf16[2,512,256]{2,1,0:T(8,128)(2,1)S(1)}, bf16[2,512,256]{2,1,0:T(8,128)(2,1)S(1)}, u32[]{:S(2)}, u32[]{:S(2)}) collective-permute-start(bf16[2,512,256]{2,1,0:T(8,128)(2,1)S(1)} %pad_maximum_fusion.2), channel_id=1, source_target_pairs={{0,320},{16,64},{64,384},{80,128},{128,448},{144,192},{192,256},{2... | collective-permute-start | bytes 1572872 | tf_op jit(solution)/shard_map/ppermute | solution.py:40
  71.5 0.0 collective-permute-done.1
  71.5 18.6 %collective-permute-start.4 = (bf16[2,512,256]{2,1,0:T(8,128)(2,1)S(1)}, bf16[2,512,256]{2,1,0:T(8,128)(2,1)S(1)}, u32[]{:S(2)}, u32[]{:S(2)}) collective-permute-start(bf16[2,512,256]{2,1,0:T(8,128)(2,1)S(1)} %pad_maximum_fusion.2), channel_id=1, source_target_pairs={{0,256},{16,0},{64,320},{80,64},{128,384},{144,128},{192,448},{208... | collective-permute-start | bytes 1572872 | tf_op jit(solution)/shard_map/ppermute | solution.py:40
  90.2 0.0 collective-permute-done
  90.2 0.3 pad_maximum_fusion.near_ref
  90.5 1.9 collective-permute-start.8
  92.4 0.0 collective-permute-done.7
  92.4 0.0 collective-permute-done.6
  92.4 0.0 collective-permute-done.5
  92.4 6.9 %collective-permute-done.4 = bf16[2,512,256]{2,1,0:T(8,128)(2,1)S(1)} collective-permute-done((bf16[2,512,256]{2,1,0:T(8,128)(2,1)S(1)}, bf16[2,512,256]{2,1,0:T(8,128)(2,1)S(1)}, u32[]{:S(2)}, u32[]{:S(2)}) %collective-permute-start.4) | collective-permute-done | bytes 524320 | tf_op jit(solution)/shard_map/ppermute | solution.py:40
  99.4 1.6 pad_maximum_fusion.1.far_ref
  100.9 1.9 collective-permute-start.9
  102.9 0.1 pad_add_fusion.at_ref
  102.9 0.0 collective-permute-done.8.near_other_ref
  102.9 4.4 %collective-permute-done.9.far_other_ref = bf16[4,2,512,256]{3,2,1,0:T(8,128)(2,1)} collective-permute-done((bf16[4,2,512,256]{3,2,1,0:T(8,128)(2,1)}, bf16[4,2,512,256]{3,2,1,0:T(8,128)(2,1)}, u32[]{:S(2)}, u32[]{:S(2)}) %collective-permute-start.9) | collective-permute-done | bytes 2097184 | tf_op jit(solution)/shard_map/ppermute | solution.py:40
  107.3 1.6 copy-done
  108.9 2.7 %shard_map.46 = (f32[128,256]{1,0:T(8,128)S(1)}, f32[128,256]{1,0:T(8,128)S(1)}) custom-call(s32[3]{0:T(128)S(1)} %pad_add_fusion.at_ref, bf16[16,2,128,256]{3,2,1,0:T(8,128)(2,1)S(1)} %bitcast.25, bf16[4,2,512,256]{3,2,1,0:T(8,128)(2,1)S(1)} %pad_maximum_fusion.near_ref, bf16[4,2,512,256]{3,2,1,0:T(8,128)(2,1)} %pad_maximum_fusion.1.far_ref, ...), custom_call_target="tpu_custom_call" | custom-call | tf_op jit(solution)/shard_map/pallas_call | solution.py:93
  111.6 14.2 %collective-permute-start.10 = (f32[128,256]{1,0:T(8,128)S(1)}, f32[128,256]{1,0:T(8,128)S(1)}, u32[]{:S(2)}, u32[]{:S(2)}) collective-permute-start(f32[128,256]{1,0:T(8,128)S(1)} %get-tuple-element.13), channel_id=1, source_target_pairs={{0,16},{16,0},{1,17},{17,1},{2,18},{18,2},{3,19},{19,3},{4,20},{20... | collective-permute-start | bytes 393224 | tf_op jit(solution)/shard_map/ppermute | solution.py:40
  125.8 2.7 %shard_map.47 = (f32[128,256]{1,0:T(8,128)S(1)}, f32[128,256]{1,0:T(8,128)S(1)}) custom-call(s32[3]{0:T(128)S(1)} %pad_add_fusion.at_ref, bf16[16,2,128,256]{3,2,1,0:T(8,128)(2,1)S(1)} %bitcast.26, bf16[4,2,512,256]{3,2,1,0:T(8,128)(2,1)S(1)} %pad_maximum_fusion.near_ref, bf16[4,2,512,256]{3,2,1,0:T(8,128)(2,1)} %pad_maximum_fusion.1.far_ref, ...), custom_call_target="tpu_custom_call" | custom-call | tf_op jit(solution)/shard_map/pallas_call | solution.py:93
  128.5 1.9 collective-permute-start.12
  130.5 0.0 collective-permute-done.10
  130.5 7.4 %collective-permute-start.11 = (bf16[128,256]{1,0:T(8,128)(2,1)S(1)}, bf16[128,256]{1,0:T(8,128)(2,1)S(1)}, u32[]{:S(2)}, u32[]{:S(2)}) collective-permute-start(bf16[128,256]{1,0:T(8,128)(2,1)S(1)} %multiply_convert_fusion.1), channel_id=1, source_target_pairs={{0,0},{1,1},{2,32},{3,33},{4,64},{5,65},{6,96},{7,97},{8,128},{9,1... | collective-permute-start | bytes 196616 | tf_op jit(solution)/shard_map/ppermute | solution.py:40
  137.9 0.0 collective-permute-done.12
  138.0 3.9 %collective-permute-done.11 = bf16[128,256]{1,0:T(8,128)(2,1)S(1)} collective-permute-done((bf16[128,256]{1,0:T(8,128)(2,1)S(1)}, bf16[128,256]{1,0:T(8,128)(2,1)S(1)}, u32[]{:S(2)}, u32[]{:S(2)}) %collective-permute-start.11) | collective-permute-done | bytes 65568 | tf_op jit(solution)/shard_map/ppermute | solution.py:40
  141.8 1.1 broadcast_in_dim.2
  142.9 19.3 %all-to-all-start = ((bf16[16,128,256]{2,1,0:T(8,128)(2,1)}), bf16[16,128,256]{2,1,0:T(8,128)(2,1)S(1)}, u32[]{:S(2)}, u32[]{:S(2)}) async-start(bf16[16,128,256]{2,1,0:T(8,128)(2,1)} %broadcast_in_dim.2), calls=%async_computation | async-start | bytes 2097152 | tf_op jit(solution)/shard_map/all_to_all | solution.py:18
  162.2 3.0 %collective-permute-start.16 = (bf16[128,256]{1,0:T(8,128)(2,1)S(1)}, bf16[128,256]{1,0:T(8,128)(2,1)S(1)}, u32[]{:S(2)}, u32[]{:S(2)}) collective-permute-start(bf16[128,256]{1,0:T(8,128)(2,1)S(1)} %multiply_convert_fusion), channel_id=1, source_target_pairs={{0,192},{16,448},{64,0},{80,256},{128,64},{144,320},{192,128},{208... | collective-permute-start | bytes 196616 | tf_op jit(solution)/shard_map/ppermute | solution.py:40
  165.2 4.6 %collective-permute-start.15 = (bf16[128,256]{1,0:T(8,128)(2,1)S(1)}, bf16[128,256]{1,0:T(8,128)(2,1)S(1)}, u32[]{:S(2)}, u32[]{:S(2)}) collective-permute-start(bf16[128,256]{1,0:T(8,128)(2,1)S(1)} %multiply_convert_fusion), channel_id=1, source_target_pairs={{0,128},{16,384},{64,192},{80,448},{128,0},{144,256},{192,64},{208... | collective-permute-start | bytes 196616 | tf_op jit(solution)/shard_map/ppermute | solution.py:40
  169.8 4.5 %collective-permute-start.14 = (bf16[128,256]{1,0:T(8,128)(2,1)S(1)}, bf16[128,256]{1,0:T(8,128)(2,1)S(1)}, u32[]{:S(2)}, u32[]{:S(2)}) collective-permute-start(bf16[128,256]{1,0:T(8,128)(2,1)S(1)} %multiply_convert_fusion), channel_id=1, source_target_pairs={{0,64},{16,320},{64,128},{80,384},{128,192},{144,448},{192,0},{208... | collective-permute-start | bytes 196616 | tf_op jit(solution)/shard_map/ppermute | solution.py:40
  174.3 0.7 collective-permute-start.13
  175.0 7.8 %collective-permute-start.20 = (bf16[128,256]{1,0:T(8,128)(2,1)S(1)}, bf16[128,256]{1,0:T(8,128)(2,1)S(1)}, u32[]{:S(2)}, u32[]{:S(2)}) collective-permute-start(bf16[128,256]{1,0:T(8,128)(2,1)S(1)} %multiply_convert_fusion), channel_id=1, source_target_pairs={{0,448},{16,192},{64,256},{80,0},{128,320},{144,64},{192,384},{208... | collective-permute-start | bytes 196616 | tf_op jit(solution)/shard_map/ppermute | solution.py:40
  182.8 0.0 collective-permute-done.16
  182.8 3.1 %collective-permute-start.19 = (bf16[128,256]{1,0:T(8,128)(2,1)S(1)}, bf16[128,256]{1,0:T(8,128)(2,1)S(1)}, u32[]{:S(2)}, u32[]{:S(2)}) collective-permute-start(bf16[128,256]{1,0:T(8,128)(2,1)S(1)} %multiply_convert_fusion), channel_id=1, source_target_pairs={{0,384},{16,128},{64,448},{80,192},{128,256},{144,0},{192,320},{20... | collective-permute-start | bytes 196616 | tf_op jit(solution)/shard_map/ppermute | solution.py:40
  186.0 0.0 collective-permute-done.15
  186.0 6.2 %collective-permute-start.18 = (bf16[128,256]{1,0:T(8,128)(2,1)S(1)}, bf16[128,256]{1,0:T(8,128)(2,1)S(1)}, u32[]{:S(2)}, u32[]{:S(2)}) collective-permute-start(bf16[128,256]{1,0:T(8,128)(2,1)S(1)} %multiply_convert_fusion), channel_id=1, source_target_pairs={{0,320},{16,64},{64,384},{80,128},{128,448},{144,192},{192,256},{2... | collective-permute-start | bytes 196616 | tf_op jit(solution)/shard_map/ppermute | solution.py:40
  192.2 0.0 collective-permute-done.14
  192.2 2.0 collective-permute-start.17
  194.2 0.0 collective-permute-done.13
  194.3 1.9 collective-permute-start.21
  196.2 0.0 collective-permute-done.20
  196.2 0.0 collective-permute-done.19
  196.2 0.0 collective-permute-done.18
  196.2 2.1 collective-permute-done.17
  198.4 1.9 collective-permute-start.22
  200.3 0.1 pad_add_fusion.2.at_ref
  200.4 0.0 collective-permute-done.21.near_other_ref
  200.4 1.4 collective-permute-done.22.far_other_ref
  201.8 11.3 %all-to-all-done.s_ref = bf16[16,128,256]{2,1,0:T(8,128)(2,1)S(1)} async-done(((bf16[16,128,256]{2,1,0:T(8,128)(2,1)}), bf16[16,128,256]{2,1,0:T(8,128)(2,1)S(1)}, u32[]{:S(2)}, u32[]{:S(2)}) %all-to-all-start) | async-done | bytes 1048608 | tf_op jit(solution)/shard_map/all_to_all | solution.py:18
  213.1 1.3 shard_map.49
  214.4 4.2 %collective-permute-start.23 = (f32[256,512]{1,0:T(8,128)S(1)}, f32[256,512]{1,0:T(8,128)S(1)}, u32[]{:S(2)}, u32[]{:S(2)}) collective-permute-start(f32[256,512]{1,0:T(8,128)S(1)} %shard_map.49), channel_id=1, source_target_pairs={{0,16},{16,0},{1,17},{17,1},{2,18},{18,2},{3,19},{19,3},{4,20},{20... | collective-permute-start | bytes 1572872 | tf_op jit(solution)/shard_map/ppermute | solution.py:40
  218.7 1.3 shard_map.48
  219.9 7.9 %collective-permute-done.23 = f32[256,512]{1,0:T(8,128)S(1)} collective-permute-done((f32[256,512]{1,0:T(8,128)S(1)}, f32[256,512]{1,0:T(8,128)S(1)}, u32[]{:S(2)}, u32[]{:S(2)}) %collective-permute-start.23) | collective-permute-done | bytes 524320 | tf_op jit(solution)/shard_map/ppermute | solution.py:40
  227.8 0.9 add_multiply_fusion
  (7 shorter events, 0.1 us)
Async XLA Ops:
  6.5 100.8 %all-gather.3.cloned.1.call-start = ((), (), s32[]{:S(2)}) async-start(), calls=%async_computation.1 | async-start | bytes 2228224 | tf_op jit(solution)/shard_map/all_gather | solution.py:139
  9.2 30.3 %collective-permute-start.3 = (bf16[2,512,256]{2,1,0:T(8,128)(2,1)S(1)}, bf16[2,512,256]{2,1,0:T(8,128)(2,1)S(1)}, u32[]{:S(2)}, u32[]{:S(2)}) collective-permute-start(bf16[2,512,256]{2,1,0:T(8,128)(2,1)S(1)} %pad_maximum_fusion.2), channel_id=1, source_target_pairs={{0,192},{16,448},{64,0},{80,256},{128,64},{144,320},{192,128},{208... | collective-permute-start | bytes 1572872 | tf_op jit(solution)/shard_map/ppermute | solution.py:40
  16.9 42.5 %collective-permute-start.2 = (bf16[2,512,256]{2,1,0:T(8,128)(2,1)S(1)}, bf16[2,512,256]{2,1,0:T(8,128)(2,1)S(1)}, u32[]{:S(2)}, u32[]{:S(2)}) collective-permute-start(bf16[2,512,256]{2,1,0:T(8,128)(2,1)S(1)} %pad_maximum_fusion.2), channel_id=1, source_target_pairs={{0,128},{16,384},{64,192},{80,448},{128,0},{144,256},{192,64},{208... | collective-permute-start | bytes 1572872 | tf_op jit(solution)/shard_map/ppermute | solution.py:40
  18.9 52.7 %collective-permute-start.1 = (bf16[2,512,256]{2,1,0:T(8,128)(2,1)S(1)}, bf16[2,512,256]{2,1,0:T(8,128)(2,1)S(1)}, u32[]{:S(2)}, u32[]{:S(2)}) collective-permute-start(bf16[2,512,256]{2,1,0:T(8,128)(2,1)S(1)} %pad_maximum_fusion.2), channel_id=1, source_target_pairs={{0,64},{16,320},{64,128},{80,384},{128,192},{144,448},{192,0},{208... | collective-permute-start | bytes 1572872 | tf_op jit(solution)/shard_map/ppermute | solution.py:40
  22.2 67.9 %collective-permute-start = (bf16[2,512,256]{2,1,0:T(8,128)(2,1)S(1)}, bf16[2,512,256]{2,1,0:T(8,128)(2,1)S(1)}, u32[]{:S(2)}, u32[]{:S(2)}) collective-permute-start(bf16[2,512,256]{2,1,0:T(8,128)(2,1)S(1)} %pad_maximum_fusion.2), channel_id=1, source_target_pairs={{0,0},{16,256},{64,64},{80,320},{128,128},{144,384},{192,192},{208... | collective-permute-start | bytes 1572872 | tf_op jit(solution)/shard_map/ppermute | solution.py:40
  22.9 69.5 %collective-permute-start.7 = (bf16[2,512,256]{2,1,0:T(8,128)(2,1)S(1)}, bf16[2,512,256]{2,1,0:T(8,128)(2,1)S(1)}, u32[]{:S(2)}, u32[]{:S(2)}) collective-permute-start(bf16[2,512,256]{2,1,0:T(8,128)(2,1)S(1)} %pad_maximum_fusion.2), channel_id=1, source_target_pairs={{0,448},{16,192},{64,256},{80,0},{128,320},{144,64},{192,384},{208... | collective-permute-start | bytes 1572872 | tf_op jit(solution)/shard_map/ppermute | solution.py:40
  39.5 52.9 %collective-permute-start.6 = (bf16[2,512,256]{2,1,0:T(8,128)(2,1)S(1)}, bf16[2,512,256]{2,1,0:T(8,128)(2,1)S(1)}, u32[]{:S(2)}, u32[]{:S(2)}) collective-permute-start(bf16[2,512,256]{2,1,0:T(8,128)(2,1)S(1)} %pad_maximum_fusion.2), channel_id=1, source_target_pairs={{0,384},{16,128},{64,448},{80,192},{128,256},{144,0},{192,320},{20... | collective-permute-start | bytes 1572872 | tf_op jit(solution)/shard_map/ppermute | solution.py:40
  59.5 32.9 %collective-permute-start.5 = (bf16[2,512,256]{2,1,0:T(8,128)(2,1)S(1)}, bf16[2,512,256]{2,1,0:T(8,128)(2,1)S(1)}, u32[]{:S(2)}, u32[]{:S(2)}) collective-permute-start(bf16[2,512,256]{2,1,0:T(8,128)(2,1)S(1)} %pad_maximum_fusion.2), channel_id=1, source_target_pairs={{0,320},{16,64},{64,384},{80,128},{128,448},{144,192},{192,256},{2... | collective-permute-start | bytes 1572872 | tf_op jit(solution)/shard_map/ppermute | solution.py:40
  71.5 27.8 %collective-permute-start.4 = (bf16[2,512,256]{2,1,0:T(8,128)(2,1)S(1)}, bf16[2,512,256]{2,1,0:T(8,128)(2,1)S(1)}, u32[]{:S(2)}, u32[]{:S(2)}) collective-permute-start(bf16[2,512,256]{2,1,0:T(8,128)(2,1)S(1)} %pad_maximum_fusion.2), channel_id=1, source_target_pairs={{0,256},{16,0},{64,320},{80,64},{128,384},{144,128},{192,448},{208... | collective-permute-start | bytes 1572872 | tf_op jit(solution)/shard_map/ppermute | solution.py:40
  90.5 12.5 %collective-permute-start.8 = (bf16[4,2,512,256]{3,2,1,0:T(8,128)(2,1)S(1)}, bf16[4,2,512,256]{3,2,1,0:T(8,128)(2,1)}, u32[]{:S(2)}, u32[]{:S(2)}) collective-permute-start(bf16[4,2,512,256]{3,2,1,0:T(8,128)(2,1)S(1)} %pad_maximum_fusion.near_ref), channel_id=1, source_target_pairs={{0,32},{32,0},{1,33},{33,1},{2,34},{34,2},{3,35},{35,3},{4,36},{36... | collective-permute-start | bytes 6291464 | tf_op jit(solution)/shard_map/ppermute | solution.py:40
  100.9 6.4 %collective-permute-start.9 = (bf16[4,2,512,256]{3,2,1,0:T(8,128)(2,1)}, bf16[4,2,512,256]{3,2,1,0:T(8,128)(2,1)}, u32[]{:S(2)}, u32[]{:S(2)}) collective-permute-start(bf16[4,2,512,256]{3,2,1,0:T(8,128)(2,1)} %pad_maximum_fusion.1.far_ref), channel_id=1, source_target_pairs={{0,32},{32,0},{1,33},{33,1},{2,34},{34,2},{3,35},{35,3},{4,36},{36... | collective-permute-start | bytes 6291464 | tf_op jit(solution)/shard_map/ppermute | solution.py:40
  107.3 1.6 copy-start
  111.6 18.8 %collective-permute-start.10 = (f32[128,256]{1,0:T(8,128)S(1)}, f32[128,256]{1,0:T(8,128)S(1)}, u32[]{:S(2)}, u32[]{:S(2)}) collective-permute-start(f32[128,256]{1,0:T(8,128)S(1)} %get-tuple-element.13), channel_id=1, source_target_pairs={{0,16},{16,0},{1,17},{17,1},{2,18},{18,2},{3,19},{19,3},{4,20},{20... | collective-permute-start | bytes 393224 | tf_op jit(solution)/shard_map/ppermute | solution.py:40
  128.5 9.4 %collective-permute-start.12 = (f32[128,256]{1,0:T(8,128)S(1)}, f32[128,256]{1,0:T(8,128)S(1)}, u32[]{:S(2)}, u32[]{:S(2)}) collective-permute-start(f32[128,256]{1,0:T(8,128)S(1)} %get-tuple-element.16), channel_id=1, source_target_pairs={{0,16},{16,0},{1,17},{17,1},{2,18},{18,2},{3,19},{19,3},{4,20},{20... | collective-permute-start | bytes 393224 | tf_op jit(solution)/shard_map/ppermute | solution.py:40
  130.5 11.3 %collective-permute-start.11 = (bf16[128,256]{1,0:T(8,128)(2,1)S(1)}, bf16[128,256]{1,0:T(8,128)(2,1)S(1)}, u32[]{:S(2)}, u32[]{:S(2)}) collective-permute-start(bf16[128,256]{1,0:T(8,128)(2,1)S(1)} %multiply_convert_fusion.1), channel_id=1, source_target_pairs={{0,0},{1,1},{2,32},{3,33},{4,64},{5,65},{6,96},{7,97},{8,128},{9,1... | collective-permute-start | bytes 196616 | tf_op jit(solution)/shard_map/ppermute | solution.py:40
  142.9 70.2 %all-to-all-start = ((bf16[16,128,256]{2,1,0:T(8,128)(2,1)}), bf16[16,128,256]{2,1,0:T(8,128)(2,1)S(1)}, u32[]{:S(2)}, u32[]{:S(2)}) async-start(bf16[16,128,256]{2,1,0:T(8,128)(2,1)} %broadcast_in_dim.2), calls=%async_computation | async-start | bytes 2097152 | tf_op jit(solution)/shard_map/all_to_all | solution.py:18
  162.2 20.6 %collective-permute-start.16 = (bf16[128,256]{1,0:T(8,128)(2,1)S(1)}, bf16[128,256]{1,0:T(8,128)(2,1)S(1)}, u32[]{:S(2)}, u32[]{:S(2)}) collective-permute-start(bf16[128,256]{1,0:T(8,128)(2,1)S(1)} %multiply_convert_fusion), channel_id=1, source_target_pairs={{0,192},{16,448},{64,0},{80,256},{128,64},{144,320},{192,128},{208... | collective-permute-start | bytes 196616 | tf_op jit(solution)/shard_map/ppermute | solution.py:40
  165.2 20.7 %collective-permute-start.15 = (bf16[128,256]{1,0:T(8,128)(2,1)S(1)}, bf16[128,256]{1,0:T(8,128)(2,1)S(1)}, u32[]{:S(2)}, u32[]{:S(2)}) collective-permute-start(bf16[128,256]{1,0:T(8,128)(2,1)S(1)} %multiply_convert_fusion), channel_id=1, source_target_pairs={{0,128},{16,384},{64,192},{80,448},{128,0},{144,256},{192,64},{208... | collective-permute-start | bytes 196616 | tf_op jit(solution)/shard_map/ppermute | solution.py:40
  169.8 22.4 %collective-permute-start.14 = (bf16[128,256]{1,0:T(8,128)(2,1)S(1)}, bf16[128,256]{1,0:T(8,128)(2,1)S(1)}, u32[]{:S(2)}, u32[]{:S(2)}) collective-permute-start(bf16[128,256]{1,0:T(8,128)(2,1)S(1)} %multiply_convert_fusion), channel_id=1, source_target_pairs={{0,64},{16,320},{64,128},{80,384},{128,192},{144,448},{192,0},{208... | collective-permute-start | bytes 196616 | tf_op jit(solution)/shard_map/ppermute | solution.py:40
  174.3 19.9 %collective-permute-start.13 = (bf16[128,256]{1,0:T(8,128)(2,1)S(1)}, bf16[128,256]{1,0:T(8,128)(2,1)S(1)}, u32[]{:S(2)}, u32[]{:S(2)}) collective-permute-start(bf16[128,256]{1,0:T(8,128)(2,1)S(1)} %multiply_convert_fusion), channel_id=1, source_target_pairs={{0,0},{16,256},{64,64},{80,320},{128,128},{144,384},{192,192},{208... | collective-permute-start | bytes 196616 | tf_op jit(solution)/shard_map/ppermute | solution.py:40
  175.0 21.2 %collective-permute-start.20 = (bf16[128,256]{1,0:T(8,128)(2,1)S(1)}, bf16[128,256]{1,0:T(8,128)(2,1)S(1)}, u32[]{:S(2)}, u32[]{:S(2)}) collective-permute-start(bf16[128,256]{1,0:T(8,128)(2,1)S(1)} %multiply_convert_fusion), channel_id=1, source_target_pairs={{0,448},{16,192},{64,256},{80,0},{128,320},{144,64},{192,384},{208... | collective-permute-start | bytes 196616 | tf_op jit(solution)/shard_map/ppermute | solution.py:40
  182.8 13.4 %collective-permute-start.19 = (bf16[128,256]{1,0:T(8,128)(2,1)S(1)}, bf16[128,256]{1,0:T(8,128)(2,1)S(1)}, u32[]{:S(2)}, u32[]{:S(2)}) collective-permute-start(bf16[128,256]{1,0:T(8,128)(2,1)S(1)} %multiply_convert_fusion), channel_id=1, source_target_pairs={{0,384},{16,128},{64,448},{80,192},{128,256},{144,0},{192,320},{20... | collective-permute-start | bytes 196616 | tf_op jit(solution)/shard_map/ppermute | solution.py:40
  186.0 10.2 %collective-permute-start.18 = (bf16[128,256]{1,0:T(8,128)(2,1)S(1)}, bf16[128,256]{1,0:T(8,128)(2,1)S(1)}, u32[]{:S(2)}, u32[]{:S(2)}) collective-permute-start(bf16[128,256]{1,0:T(8,128)(2,1)S(1)} %multiply_convert_fusion), channel_id=1, source_target_pairs={{0,320},{16,64},{64,384},{80,128},{128,448},{144,192},{192,256},{2... | collective-permute-start | bytes 196616 | tf_op jit(solution)/shard_map/ppermute | solution.py:40
  192.2 6.2 %collective-permute-start.17 = (bf16[128,256]{1,0:T(8,128)(2,1)S(1)}, bf16[128,256]{1,0:T(8,128)(2,1)S(1)}, u32[]{:S(2)}, u32[]{:S(2)}) collective-permute-start(bf16[128,256]{1,0:T(8,128)(2,1)S(1)} %multiply_convert_fusion), channel_id=1, source_target_pairs={{0,256},{16,0},{64,320},{80,64},{128,384},{144,128},{192,448},{208... | collective-permute-start | bytes 196616 | tf_op jit(solution)/shard_map/ppermute | solution.py:40
  194.3 6.1 %collective-permute-start.21 = (bf16[4,128,256]{2,1,0:T(8,128)(2,1)S(1)}, bf16[4,128,256]{2,1,0:T(8,128)(2,1)S(1)}, u32[]{:S(2)}, u32[]{:S(2)}) collective-permute-start(bf16[4,128,256]{2,1,0:T(8,128)(2,1)S(1)} %pad_maximum_fusion.3.near_ref), channel_id=1, source_target_pairs={{0,32},{32,0},{1,33},{33,1},{2,34},{34,2},{3,35},{35,3},{4,36},{36... | collective-permute-start | bytes 786440 | tf_op jit(solution)/shard_map/ppermute | solution.py:40
  198.4 3.4 %collective-permute-start.22 = (bf16[4,128,256]{2,1,0:T(8,128)(2,1)S(1)}, bf16[4,128,256]{2,1,0:T(8,128)(2,1)S(1)}, u32[]{:S(2)}, u32[]{:S(2)}) collective-permute-start(bf16[4,128,256]{2,1,0:T(8,128)(2,1)S(1)} %pad_maximum_fusion.4.far_ref), channel_id=1, source_target_pairs={{0,32},{32,0},{1,33},{33,1},{2,34},{34,2},{3,35},{35,3},{4,36},{36... | collective-permute-start | bytes 786440 | tf_op jit(solution)/shard_map/ppermute | solution.py:40
  214.4 13.4 %collective-permute-start.23 = (f32[256,512]{1,0:T(8,128)S(1)}, f32[256,512]{1,0:T(8,128)S(1)}, u32[]{:S(2)}, u32[]{:S(2)}) collective-permute-start(f32[256,512]{1,0:T(8,128)S(1)} %shard_map.49), channel_id=1, source_target_pairs={{0,16},{16,0},{1,17},{17,1},{2,18},{18,2},{3,19},{19,3},{4,20},{20... | collective-permute-start | bytes 1572872 | tf_op jit(solution)/shard_map/ppermute | solution.py:40
Sparse Core Ops, SparseCore 0:
  9.4 77.6 all-gather.2

commit v4 on v3

v4 whole, which is shorter than its diff:
```python
import functools
import jax
import jax.numpy as jnp
from jax import lax
from jax.experimental import pallas as pl
from jax.experimental.pallas import tpu as pltpu
from jax.sharding import Mesh, PartitionSpec as P

AXES = ("xh", "y", "c", "xl", "zh", "zl")
SIZES = (2, 4, 2, 2, 4, 4)
VMEM = pl.BlockSpec(memory_space=pltpu.VMEM)
SMEM = pl.BlockSpec(memory_space=pltpu.SMEM)
PARAMS = pltpu.CompilerParams(vmem_limit_bytes=40 * 1024 * 1024)


def to_all(x, axes, n):
    spread = jnp.broadcast_to(x[None], (n,) + x.shape)
    return lax.all_to_all(spread, axes, split_axis=0, concat_axis=0, tiled=True)


def move(x, axes, target):
    sizes = [SIZES[AXES.index(a)] for a in axes]

    def flat(coords):
        out = 0
        for c, s in zip(coords, sizes):
            out = out * s + c
        return out

    total = 1
    for s in sizes:
        total *= s
    pairs = []
    for i in range(total):
        rest, coords = i, []
        for s in reversed(sizes):
            coords.insert(0, rest % s)
            rest //= s
        pairs.append((i, flat(target(*coords))))
    return lax.ppermute(x, axes, pairs)


def dot(a, b):
    return jnp.dot(a, b, preferred_element_type=jnp.float32)


def rotate_kernel(at_ref, x_ref, own_ref, other_ref, mine_ref, theirs_ref):
    y, c, turned = at_ref[0], at_ref[1], at_ref[2]
    sums = []
    for k in range(2):
        acc = jnp.zeros(mine_ref.shape, jnp.float32)
        for j in range(4):
            at = 4 * lax.rem(y + 4 - j, 4)
            for h in range(2):
                rows = slice(256 * h, 256 * h + 256)
                acc += dot(x_ref[at + 2 * c + h, 0], own_ref[j, k, rows, :])
                acc += dot(x_ref[at + 2 * (1 - c) + h, 0], other_ref[j, k, rows, :])
        sums.append(acc)
    near, far = sums
    mine_ref[...] = jnp.where(turned == 0, near, far)
    theirs_ref[...] = jnp.where(turned == 0, far, near)


def corrected_kernel(at_ref, own_ref, other_ref, s_ref, out_ref):
    y, c, k = at_ref[0], at_ref[1], at_ref[2]
    for h in range(2):
        acc = jnp.zeros((256, 256), jnp.float32)
        for j in range(4):
            at = 4 * lax.rem(y + 4 - j, 4) + h
            for act, core in ((own_ref, c), (other_ref, 1 - c)):
                acc += lax.dot_general(
                    act[j, k], s_ref[at + 2 * core],
                    (((0,), (0,)), ((), ())), preferred_element_type=jnp.float32,
                )
        out_ref[:, 256 * h:256 * h + 256] = acc


def rotate(at, x, part, basis):
    out = jax.ShapeDtypeStruct(x.shape[2:], jnp.float32)
    return pl.pallas_call(
        rotate_kernel,
        grid=(1,),
        out_shape=[out, out],
        in_specs=[SMEM, pl.BlockSpec((16, 1) + out.shape, lambda i: (0, part, 0, 0)), VMEM, VMEM],
        out_specs=[VMEM, VMEM],
        compiler_params=PARAMS,
    )(at, x, *basis)


def correct(at, acts, grads):
    return pl.pallas_call(
        corrected_kernel,
        out_shape=jax.ShapeDtypeStruct((256, 512), jnp.float32),
        in_specs=[SMEM] + [VMEM] * 3,
        out_specs=VMEM,
        compiler_params=PARAMS,
    )(at, *acts, grads)


def swap(x, axis):
    return move(x, (axis,), lambda i: (1 - i,))


def plane_gather(x):
    pair = jnp.stack([move(x, ("xh", "xl"), lambda a, p, k=k: (p ^ k, a)) for k in range(2)])
    shifted = [move(pair, ("y",), lambda b, j=j: ((b + j) % 4,)) for j in (1, 2, 3)]
    own = jnp.stack([pair] + shifted)
    return own, swap(own, "c")


def square(mine, theirs):
    total = mine + swap(theirs, "xl")
    return (total * total).astype(jnp.bfloat16)


def on_device(activations, gradients, act_basis, grad_basis):
    tokens = activations.shape[0] * 16
    xh, y, c, xl = (lax.axis_index(a) for a in ("xh", "y", "c", "xl"))
    turned = (xh + xl) % 2
    at = jnp.stack([y, c, turned])

    both = jnp.stack([activations, gradients])
    both, grad_basis = lax.optimization_barrier((both, grad_basis))
    act_every = grad_every = lax.all_gather(both, ("zh", "zl"), axis=0, tiled=False)
    grad_panels = plane_gather(grad_basis)
    act_basis, grad_own = lax.optimization_barrier((act_basis, grad_panels[0]))
    act_panels = plane_gather(act_basis)

    mine, theirs = rotate(at, grad_every, 1, grad_panels)
    grad_square = square(mine, theirs)
    grad_square = move(
        grad_square, AXES, lambda a, b, e, p, q, r: (p, q, r // 2, a, b, 2 * e + r % 2)
    )

    act_every, mine = lax.optimization_barrier((act_every, mine))
    act_square = square(*rotate(at, act_every, 0, act_panels))
    act_square, grad_square = lax.optimization_barrier((act_square, grad_square))
    grad_block = to_all(grad_square, ("zh", "zl"), 16)
    acts = plane_gather(act_square)

    theirs = swap(correct(jnp.stack([y, c, 1 - turned]), acts, grad_block), "xl")
    mine = correct(at, acts, grad_block)
    return (mine + theirs) * (1.0 / tokens)


def solution(mesh):
    fine = Mesh(mesh.devices.reshape(SIZES), AXES)
    spec = P(("xh", "y", "c"), ("xl", "zh", "zl"))
    return jax.shard_map(
        on_device,
        mesh=fine,
        in_specs=(spec, spec, spec, spec),
        out_specs=P(("xl", "zh", "zl"), ("xh", "y", "c")),
        check_vma=False,
    )
```

time: 236 us -> 221 us (0.936)
  starting transfers between devices: 139 us -> 98.4 us
  waiting for transfers between devices: 66.9 us -> 91.9 us
    ppermute x24 -> x22, starting transfers between devices: 119 us -> 83.8 us  [move(): return lax.ppermute(x, axes, pairs)]
    ppermute x24 -> x22, waiting for transfers between devices: 55.5 us -> 69.9 us  [move(): return lax.ppermute(x, axes, pairs)]
    all_to_all x1, waiting for transfers between devices: 11.3 us -> 22 us  [to_all(): return lax.all_to_all(spread, axes, split_axis=0, concat_axis=0, tiled=True)]
    all_to_all x1, starting transfers between devices: 19.3 us -> 14.6 us  [to_all(): return lax.all_to_all(spread, axes, split_axis=0, concat_axis=0, tiled=True)]
  transfers between devices with their start and end apart: 26 -> 24, of which waited for: 9 -> 14; matrix products, arithmetic and copies ran while one was open for 1% -> 1% of each run, Pallas kernels for 2% -> 3%
where the time goes in v4:
time: 221 us; the launch traced here: 220 us
  starting transfers between devices  98.4 us (45%)
  waiting for transfers between devices  91.9 us (42%)
  between operations  13.7 us (6%)
  Pallas kernels  7.91 us (4%)
  other arithmetic  4.68 us (2%)
  local copies, waits for them, and re-layouts  3.35 us (2%)
    ppermute x22, starting transfers between devices, move(): return lax.ppermute(x, axes, pairs)  83.8 us
    ppermute x22, waiting for transfers between devices, move(): return lax.ppermute(x, axes, pairs)  69.9 us
    all_to_all x1, waiting for transfers between devices, to_all(): return lax.all_to_all(spread, axes, split_axis=0, concat_axis=0, tiled=True)  22 us
    all_to_all x1, starting transfers between devices, to_all(): return lax.all_to_all(spread, axes, split_axis=0, concat_axis=0, tiled=True)  14.6 us
    pallas_call x2, Pallas kernels, rotate(): pl.pallas_call(rotate_kernel, grid=(1,), out_shape=[out, out], in_specs=[...  5.38 us
  transfers between devices with their start and end apart: 24, of which 14 were waited for; matrix products, arithmetic and copies ran while one was open for 1% of the time, Pallas kernels for 3%

profile of v4, /device:TPU:8, one launch (start us, length us, event | category | flops | bytes accessed | tf_op | source)
XLA Modules:
  0.0 220.0 jit_solution(580473898722305860)
XLA Ops:
  6.5 0.0 all-gather.3.cloned.1.call-start
  6.5 1.5 pad_maximum_fusion.5
  8.1 1.6 collective-permute-start
  9.7 5.8 %collective-permute-start.1 = (bf16[512,256]{1,0:T(8,128)(2,1)}, bf16[512,256]{1,0:T(8,128)(2,1)S(1)}, u32[]{:S(2)}, u32[]{:S(2)}) collective-permute-start(bf16[512,256]{1,0:T(8,128)(2,1)} %param.7), channel_id=1, source_target_pairs={{0,256},{16,0},{256,272},{272,16},{1,257},{17,1},{257,273},{273,17... | collective-permute-start | bytes 786440 | tf_op jit(solution)/shard_map/ppermute | solution.py:40
  15.5 0.0 all-gather.3.cloned.1.call-update
  15.5 0.0 collective-permute-done
  15.5 5.6 %collective-permute-done.1 = bf16[512,256]{1,0:T(8,128)(2,1)S(1)} collective-permute-done((bf16[512,256]{1,0:T(8,128)(2,1)}, bf16[512,256]{1,0:T(8,128)(2,1)S(1)}, u32[]{:S(2)}, u32[]{:S(2)}) %collective-permute-start.1) | collective-permute-done | bytes 262176 | tf_op jit(solution)/shard_map/ppermute | solution.py:40
  21.1 0.1 fusion.2
  21.2 4.2 %collective-permute-start.3 = (bf16[2,512,256]{2,1,0:T(8,128)(2,1)S(1)}, bf16[2,512,256]{2,1,0:T(8,128)(2,1)S(1)}, u32[]{:S(2)}, u32[]{:S(2)}) collective-permute-start(bf16[2,512,256]{2,1,0:T(8,128)(2,1)S(1)} %get-tuple-element.28), channel_id=1, source_target_pairs={{0,128},{64,192},{128,0},{192,64},{1,129},{65,193},{129,1},{193,65... | collective-permute-start | bytes 1572872 | tf_op jit(solution)/shard_map/ppermute | solution.py:40
  25.4 3.3 %collective-permute-start.4 = (bf16[2,512,256]{2,1,0:T(8,128)(2,1)S(1)}, bf16[2,512,256]{2,1,0:T(8,128)(2,1)S(1)}, u32[]{:S(2)}, u32[]{:S(2)}) collective-permute-start(bf16[2,512,256]{2,1,0:T(8,128)(2,1)S(1)} %get-tuple-element.28), channel_id=1, source_target_pairs={{0,192},{64,0},{128,64},{192,128},{1,193},{65,1},{129,65},{193,129... | collective-permute-start | bytes 1572872 | tf_op jit(solution)/shard_map/ppermute | solution.py:40
  28.7 2.6 %collective-permute-start.2 = (bf16[2,512,256]{2,1,0:T(8,128)(2,1)S(1)}, bf16[2,512,256]{2,1,0:T(8,128)(2,1)S(1)}, u32[]{:S(2)}, u32[]{:S(2)}) collective-permute-start(bf16[2,512,256]{2,1,0:T(8,128)(2,1)S(1)} %get-tuple-element.28), channel_id=1, source_target_pairs={{0,64},{64,128},{128,192},{192,0},{1,65},{65,129},{129,193},{193,1... | collective-permute-start | bytes 1572872 | tf_op jit(solution)/shard_map/ppermute | solution.py:40
  31.3 8.2 %collective-permute-done.3 = bf16[2,512,256]{2,1,0:T(8,128)(2,1)S(1)} collective-permute-done((bf16[2,512,256]{2,1,0:T(8,128)(2,1)S(1)}, bf16[2,512,256]{2,1,0:T(8,128)(2,1)S(1)}, u32[]{:S(2)}, u32[]{:S(2)}) %collective-permute-start.3) | collective-permute-done | bytes 524320 | tf_op jit(solution)/shard_map/ppermute | solution.py:40
  39.5 9.1 %collective-permute-done.4 = bf16[2,512,256]{2,1,0:T(8,128)(2,1)S(1)} collective-permute-done((bf16[2,512,256]{2,1,0:T(8,128)(2,1)S(1)}, bf16[2,512,256]{2,1,0:T(8,128)(2,1)S(1)}, u32[]{:S(2)}, u32[]{:S(2)}) %collective-permute-start.4) | collective-permute-done | bytes 524320 | tf_op jit(solution)/shard_map/ppermute | solution.py:40
  48.6 0.2 collective-permute-done.2
  48.8 0.3 pad_maximum_fusion.own_ref
  49.0 0.7 copy-done.1
  49.7 0.7 collective-permute-start.6
  50.4 8.9 %collective-permute-start.7 = (bf16[512,256]{1,0:T(8,128)(2,1)S(1)}, bf16[512,256]{1,0:T(8,128)(2,1)S(1)}, u32[]{:S(2)}, u32[]{:S(2)}) collective-permute-start(bf16[512,256]{1,0:T(8,128)(2,1)S(1)} %copy-done.1), channel_id=1, source_target_pairs={{0,256},{16,0},{256,272},{272,16},{1,257},{17,1},{257,273},{273,17... | collective-permute-start | bytes 786440 | tf_op jit(solution)/shard_map/ppermute | solution.py:40
  59.3 0.0 collective-permute-done.6
  59.3 6.1 %collective-permute-done.7 = bf16[512,256]{1,0:T(8,128)(2,1)S(1)} collective-permute-done((bf16[512,256]{1,0:T(8,128)(2,1)S(1)}, bf16[512,256]{1,0:T(8,128)(2,1)S(1)}, u32[]{:S(2)}, u32[]{:S(2)}) %collective-permute-start.7) | collective-permute-done | bytes 262176 | tf_op jit(solution)/shard_map/ppermute | solution.py:40
  65.4 0.1 fusion.1
  65.5 3.5 %collective-permute-start.8 = (bf16[2,512,256]{2,1,0:T(8,128)(2,1)S(1)}, bf16[2,512,256]{2,1,0:T(8,128)(2,1)S(1)}, u32[]{:S(2)}, u32[]{:S(2)}) collective-permute-start(bf16[2,512,256]{2,1,0:T(8,128)(2,1)S(1)} %get-tuple-element.26), channel_id=1, source_target_pairs={{0,64},{64,128},{128,192},{192,0},{1,65},{65,129},{129,193},{193,1... | collective-permute-start | bytes 1572872 | tf_op jit(solution)/shard_map/ppermute | solution.py:40
  69.0 2.6 %collective-permute-start.9 = (bf16[2,512,256]{2,1,0:T(8,128)(2,1)S(1)}, bf16[2,512,256]{2,1,0:T(8,128)(2,1)S(1)}, u32[]{:S(2)}, u32[]{:S(2)}) collective-permute-start(bf16[2,512,256]{2,1,0:T(8,128)(2,1)S(1)} %get-tuple-element.26), channel_id=1, source_target_pairs={{0,128},{64,192},{128,0},{192,64},{1,129},{65,193},{129,1},{193,65... | collective-permute-start | bytes 1572872 | tf_op jit(solution)/shard_map/ppermute | solution.py:40
  71.6 4.5 %collective-permute-start.10 = (bf16[2,512,256]{2,1,0:T(8,128)(2,1)S(1)}, bf16[2,512,256]{2,1,0:T(8,128)(2,1)S(1)}, u32[]{:S(2)}, u32[]{:S(2)}) collective-permute-start(bf16[2,512,256]{2,1,0:T(8,128)(2,1)S(1)} %get-tuple-element.26), channel_id=1, source_target_pairs={{0,192},{64,0},{128,64},{192,128},{1,193},{65,1},{129,65},{193,129... | collective-permute-start | bytes 1572872 | tf_op jit(solution)/shard_map/ppermute | solution.py:40
  76.1 1.9 collective-permute-start.5
  78.1 12.8 %collective-permute-done.8 = bf16[2,512,256]{2,1,0:T(8,128)(2,1)S(1)} collective-permute-done((bf16[2,512,256]{2,1,0:T(8,128)(2,1)S(1)}, bf16[2,512,256]{2,1,0:T(8,128)(2,1)S(1)}, u32[]{:S(2)}, u32[]{:S(2)}) %collective-permute-start.8) | collective-permute-done | bytes 524320 | tf_op jit(solution)/shard_map/ppermute | solution.py:40
  90.8 0.0 collective-permute-done.9
  90.8 5.6 %collective-permute-done.10 = bf16[2,512,256]{2,1,0:T(8,128)(2,1)S(1)} collective-permute-done((bf16[2,512,256]{2,1,0:T(8,128)(2,1)S(1)}, bf16[2,512,256]{2,1,0:T(8,128)(2,1)S(1)}, u32[]{:S(2)}, u32[]{:S(2)}) %collective-permute-start.10) | collective-permute-done | bytes 524320 | tf_op jit(solution)/shard_map/ppermute | solution.py:40
  96.4 1.6 pad_maximum_fusion.1.own_ref
  98.0 1.9 collective-permute-start.11
  99.9 0.1 pad_add_fusion.at_ref
  100.0 0.0 collective-permute-done.5.other_ref
  100.0 1.6 copy-done
  101.6 2.4 %shard_map.46 = (f32[128,256]{1,0:T(8,128)S(1)}, f32[128,256]{1,0:T(8,128)S(1)}) custom-call(s32[3]{0:T(128)S(1)} %pad_add_fusion.at_ref, bf16[16,2,128,256]{3,2,1,0:T(8,128)(2,1)S(1)} %bitcast.28, bf16[4,2,512,256]{3,2,1,0:T(8,128)(2,1)S(1)} %pad_maximum_fusion.own_ref, bf16[4,2,512,256]{3,2,1,0:T(8,128)(2,1)} %collective-permute-done.5.other_ref), custom_call_target="tpu_custom_call" | custom-call | tf_op jit(solution)/shard_map/pallas_call | solution.py:80
  104.0 6.2 %collective-permute-start.13 = (f32[128,256]{1,0:T(8,128)S(1)}, f32[128,256]{1,0:T(8,128)S(1)}, u32[]{:S(2)}, u32[]{:S(2)}) collective-permute-start(f32[128,256]{1,0:T(8,128)S(1)} %get-tuple-element.22), channel_id=1, source_target_pairs={{0,16},{16,0},{1,17},{17,1},{2,18},{18,2},{3,19},{19,3},{4,20},{20... | collective-permute-start | bytes 393224 | tf_op jit(solution)/shard_map/ppermute | solution.py:40
  110.2 0.0 collective-permute-done.11.other_ref
  110.2 3.0 %shard_map.47 = (f32[128,256]{1,0:T(8,128)S(1)}, f32[128,256]{1,0:T(8,128)S(1)}) custom-call(s32[3]{0:T(128)S(1)} %pad_add_fusion.at_ref, bf16[16,2,128,256]{3,2,1,0:T(8,128)(2,1)S(1)} %bitcast.29, bf16[4,2,512,256]{3,2,1,0:T(8,128)(2,1)} %pad_maximum_fusion.1.own_ref, bf16[4,2,512,256]{3,2,1,0:T(8,128)(2,1)} %collective-permute-done.11.other_ref), custom_call_target="tpu_custom_call" | custom-call | tf_op jit(solution)/shard_map/pallas_call | solution.py:80
  113.2 1.9 collective-permute-start.12
  115.2 0.0 collective-permute-done.13
  115.2 8.2 %collective-permute-start.14 = (bf16[128,256]{1,0:T(8,128)(2,1)S(1)}, bf16[128,256]{1,0:T(8,128)(2,1)S(1)}, u32[]{:S(2)}, u32[]{:S(2)}) collective-permute-start(bf16[128,256]{1,0:T(8,128)(2,1)S(1)} %multiply_convert_fusion), channel_id=1, source_target_pairs={{0,0},{1,1},{2,32},{3,33},{4,64},{5,65},{6,96},{7,97},{8,128},{9,1... | collective-permute-start | bytes 196616 | tf_op jit(solution)/shard_map/ppermute | solution.py:40
  123.4 0.0 collective-permute-done.12
  123.5 7.7 %collective-permute-done.14 = bf16[128,256]{1,0:T(8,128)(2,1)S(1)} collective-permute-done((bf16[128,256]{1,0:T(8,128)(2,1)S(1)}, bf16[128,256]{1,0:T(8,128)(2,1)S(1)}, u32[]{:S(2)}, u32[]{:S(2)}) %collective-permute-start.14) | collective-permute-done | bytes 65568 | tf_op jit(solution)/shard_map/ppermute | solution.py:40
  131.2 1.1 broadcast_in_dim.2
  132.2 14.6 %all-to-all-start = ((bf16[16,128,256]{2,1,0:T(8,128)(2,1)}), bf16[16,128,256]{2,1,0:T(8,128)(2,1)S(1)}, u32[]{:S(2)}, u32[]{:S(2)}) async-start(bf16[16,128,256]{2,1,0:T(8,128)(2,1)} %broadcast_in_dim.2), calls=%async_computation | async-start | bytes 2097152 | tf_op jit(solution)/shard_map/all_to_all | solution.py:18
  146.9 0.7 collective-permute-start.15
  147.5 8.0 %collective-permute-start.16 = (bf16[128,256]{1,0:T(8,128)(2,1)S(1)}, bf16[128,256]{1,0:T(8,128)(2,1)S(1)}, u32[]{:S(2)}, u32[]{:S(2)}) collective-permute-start(bf16[128,256]{1,0:T(8,128)(2,1)S(1)} %multiply_convert_fusion.1), channel_id=1, source_target_pairs={{0,256},{16,0},{256,272},{272,16},{1,257},{17,1},{257,273},{273,17... | collective-permute-start | bytes 196616 | tf_op jit(solution)/shard_map/ppermute | solution.py:40
  155.5 0.0 collective-permute-done.15
  155.6 1.9 collective-permute-done.16
  157.4 1.9 collective-permute-start.17
  159.4 5.7 %collective-permute-start.18 = (bf16[2,128,256]{2,1,0:T(8,128)(2,1)S(1)}, bf16[2,128,256]{2,1,0:T(8,128)(2,1)S(1)}, u32[]{:S(2)}, u32[]{:S(2)}) collective-permute-start(bf16[2,128,256]{2,1,0:T(8,128)(2,1)S(1)} %get-tuple-element.30), channel_id=1, source_target_pairs={{0,128},{64,192},{128,0},{192,64},{1,129},{65,193},{129,1},{193,65... | collective-permute-start | bytes 393224 | tf_op jit(solution)/shard_map/ppermute | solution.py:40
  165.1 3.5 %collective-permute-start.19 = (bf16[2,128,256]{2,1,0:T(8,128)(2,1)S(1)}, bf16[2,128,256]{2,1,0:T(8,128)(2,1)S(1)}, u32[]{:S(2)}, u32[]{:S(2)}) collective-permute-start(bf16[2,128,256]{2,1,0:T(8,128)(2,1)S(1)} %get-tuple-element.30), channel_id=1, source_target_pairs={{0,192},{64,0},{128,64},{192,128},{1,193},{65,1},{129,65},{193,129... | collective-permute-start | bytes 393224 | tf_op jit(solution)/shard_map/ppermute | solution.py:40
  168.6 0.0 collective-permute-done.17
  168.6 0.4 collective-permute-done.18
  169.0 2.9 %collective-permute-done.19 = bf16[2,128,256]{2,1,0:T(8,128)(2,1)S(1)} collective-permute-done((bf16[2,128,256]{2,1,0:T(8,128)(2,1)S(1)}, bf16[2,128,256]{2,1,0:T(8,128)(2,1)S(1)}, u32[]{:S(2)}, u32[]{:S(2)}) %collective-permute-start.19) | collective-permute-done | bytes 131104 | tf_op jit(solution)/shard_map/ppermute | solution.py:40
  171.9 0.1 pad_maximum_fusion.4.own_ref
  172.0 1.9 collective-permute-start.20
  173.9 0.1 pad_add_fusion.2.at_ref
  174.0 1.8 collective-permute-done.20.other_ref
  175.8 22.0 %all-to-all-done.s_ref = bf16[16,128,256]{2,1,0:T(8,128)(2,1)S(1)} async-done(((bf16[16,128,256]{2,1,0:T(8,128)(2,1)}), bf16[16,128,256]{2,1,0:T(8,128)(2,1)S(1)}, u32[]{:S(2)}, u32[]{:S(2)}) %all-to-all-start) | async-done | bytes 1048608 | tf_op jit(solution)/shard_map/all_to_all | solution.py:18
  197.8 1.3 shard_map.49
  199.0 4.3 %collective-permute-start.21 = (f32[256,512]{1,0:T(8,128)S(1)}, f32[256,512]{1,0:T(8,128)S(1)}, u32[]{:S(2)}, u32[]{:S(2)}) collective-permute-start(f32[256,512]{1,0:T(8,128)S(1)} %shard_map.49), channel_id=1, source_target_pairs={{0,16},{16,0},{1,17},{17,1},{2,18},{18,2},{3,19},{19,3},{4,20},{20... | collective-permute-start | bytes 1572872 | tf_op jit(solution)/shard_map/ppermute | solution.py:40
  203.3 1.3 shard_map.48
  204.6 7.7 %collective-permute-done.21 = f32[256,512]{1,0:T(8,128)S(1)} collective-permute-done((f32[256,512]{1,0:T(8,128)S(1)}, f32[256,512]{1,0:T(8,128)S(1)}, u32[]{:S(2)}, u32[]{:S(2)}) %collective-permute-start.21) | collective-permute-done | bytes 524320 | tf_op jit(solution)/shard_map/ppermute | solution.py:40
  212.2 0.9 add_multiply_fusion
  (6 shorter events, 0.1 us)
Async XLA Ops:
  6.5 93.5 %all-gather.3.cloned.1.call-start = ((), (), s32[]{:S(2)}) async-start(), calls=%async_computation.1 | async-start | bytes 2228224 | tf_op jit(solution)/shard_map/all_gather | solution.py:124
  8.1 7.4 %collective-permute-start = (bf16[512,256]{1,0:T(8,128)(2,1)}, bf16[512,256]{1,0:T(8,128)(2,1)S(1)}, u32[]{:S(2)}, u32[]{:S(2)}) collective-permute-start(bf16[512,256]{1,0:T(8,128)(2,1)} %param.7), channel_id=1, source_target_pairs={{0,0},{16,256},{256,16},{272,272},{1,1},{17,257},{257,17},{273,273... | collective-permute-start | bytes 786440 | tf_op jit(solution)/shard_map/ppermute | solution.py:40
  9.7 11.4 %collective-permute-start.1 = (bf16[512,256]{1,0:T(8,128)(2,1)}, bf16[512,256]{1,0:T(8,128)(2,1)S(1)}, u32[]{:S(2)}, u32[]{:S(2)}) collective-permute-start(bf16[512,256]{1,0:T(8,128)(2,1)} %param.7), channel_id=1, source_target_pairs={{0,256},{16,0},{256,272},{272,16},{1,257},{17,1},{257,273},{273,17... | collective-permute-start | bytes 786440 | tf_op jit(solution)/shard_map/ppermute | solution.py:40
  21.2 18.3 %collective-permute-start.3 = (bf16[2,512,256]{2,1,0:T(8,128)(2,1)S(1)}, bf16[2,512,256]{2,1,0:T(8,128)(2,1)S(1)}, u32[]{:S(2)}, u32[]{:S(2)}) collective-permute-start(bf16[2,512,256]{2,1,0:T(8,128)(2,1)S(1)} %get-tuple-element.28), channel_id=1, source_target_pairs={{0,128},{64,192},{128,0},{192,64},{1,129},{65,193},{129,1},{193,65... | collective-permute-start | bytes 1572872 | tf_op jit(solution)/shard_map/ppermute | solution.py:40
  25.4 23.2 %collective-permute-start.4 = (bf16[2,512,256]{2,1,0:T(8,128)(2,1)S(1)}, bf16[2,512,256]{2,1,0:T(8,128)(2,1)S(1)}, u32[]{:S(2)}, u32[]{:S(2)}) collective-permute-start(bf16[2,512,256]{2,1,0:T(8,128)(2,1)S(1)} %get-tuple-element.28), channel_id=1, source_target_pairs={{0,192},{64,0},{128,64},{192,128},{1,193},{65,1},{129,65},{193,129... | collective-permute-start | bytes 1572872 | tf_op jit(solution)/shard_map/ppermute | solution.py:40
  28.7 20.1 %collective-permute-start.2 = (bf16[2,512,256]{2,1,0:T(8,128)(2,1)S(1)}, bf16[2,512,256]{2,1,0:T(8,128)(2,1)S(1)}, u32[]{:S(2)}, u32[]{:S(2)}) collective-permute-start(bf16[2,512,256]{2,1,0:T(8,128)(2,1)S(1)} %get-tuple-element.28), channel_id=1, source_target_pairs={{0,64},{64,128},{128,192},{192,0},{1,65},{65,129},{129,193},{193,1... | collective-permute-start | bytes 1572872 | tf_op jit(solution)/shard_map/ppermute | solution.py:40
  48.8 1.0 copy-start.1
  49.7 9.6 %collective-permute-start.6 = (bf16[512,256]{1,0:T(8,128)(2,1)S(1)}, bf16[512,256]{1,0:T(8,128)(2,1)S(1)}, u32[]{:S(2)}, u32[]{:S(2)}) collective-permute-start(bf16[512,256]{1,0:T(8,128)(2,1)S(1)} %copy-done.1), channel_id=1, source_target_pairs={{0,0},{16,256},{256,16},{272,272},{1,1},{17,257},{257,17},{273,273... | collective-permute-start | bytes 786440 | tf_op jit(solution)/shard_map/ppermute | solution.py:40
  50.4 15.0 %collective-permute-start.7 = (bf16[512,256]{1,0:T(8,128)(2,1)S(1)}, bf16[512,256]{1,0:T(8,128)(2,1)S(1)}, u32[]{:S(2)}, u32[]{:S(2)}) collective-permute-start(bf16[512,256]{1,0:T(8,128)(2,1)S(1)} %copy-done.1), channel_id=1, source_target_pairs={{0,256},{16,0},{256,272},{272,16},{1,257},{17,1},{257,273},{273,17... | collective-permute-start | bytes 786440 | tf_op jit(solution)/shard_map/ppermute | solution.py:40
  65.5 25.4 %collective-permute-start.8 = (bf16[2,512,256]{2,1,0:T(8,128)(2,1)S(1)}, bf16[2,512,256]{2,1,0:T(8,128)(2,1)S(1)}, u32[]{:S(2)}, u32[]{:S(2)}) collective-permute-start(bf16[2,512,256]{2,1,0:T(8,128)(2,1)S(1)} %get-tuple-element.26), channel_id=1, source_target_pairs={{0,64},{64,128},{128,192},{192,0},{1,65},{65,129},{129,193},{193,1... | collective-permute-start | bytes 1572872 | tf_op jit(solution)/shard_map/ppermute | solution.py:40
  69.0 21.9 %collective-permute-start.9 = (bf16[2,512,256]{2,1,0:T(8,128)(2,1)S(1)}, bf16[2,512,256]{2,1,0:T(8,128)(2,1)S(1)}, u32[]{:S(2)}, u32[]{:S(2)}) collective-permute-start(bf16[2,512,256]{2,1,0:T(8,128)(2,1)S(1)} %get-tuple-element.26), channel_id=1, source_target_pairs={{0,128},{64,192},{128,0},{192,64},{1,129},{65,193},{129,1},{193,65... | collective-permute-start | bytes 1572872 | tf_op jit(solution)/shard_map/ppermute | solution.py:40
  71.6 24.8 %collective-permute-start.10 = (bf16[2,512,256]{2,1,0:T(8,128)(2,1)S(1)}, bf16[2,512,256]{2,1,0:T(8,128)(2,1)S(1)}, u32[]{:S(2)}, u32[]{:S(2)}) collective-permute-start(bf16[2,512,256]{2,1,0:T(8,128)(2,1)S(1)} %get-tuple-element.26), channel_id=1, source_target_pairs={{0,192},{64,0},{128,64},{192,128},{1,193},{65,1},{129,65},{193,129... | collective-permute-start | bytes 1572872 | tf_op jit(solution)/shard_map/ppermute | solution.py:40
  76.1 23.9 %collective-permute-start.5 = (bf16[4,2,512,256]{3,2,1,0:T(8,128)(2,1)S(1)}, bf16[4,2,512,256]{3,2,1,0:T(8,128)(2,1)}, u32[]{:S(2)}, u32[]{:S(2)}) collective-permute-start(bf16[4,2,512,256]{3,2,1,0:T(8,128)(2,1)S(1)} %pad_maximum_fusion.own_ref), channel_id=1, source_target_pairs={{0,32},{32,0},{1,33},{33,1},{2,34},{34,2},{3,35},{35,3},{4,36},{36... | collective-permute-start | bytes 6291464 | tf_op jit(solution)/shard_map/ppermute | solution.py:40
  98.0 12.2 %collective-permute-start.11 = (bf16[4,2,512,256]{3,2,1,0:T(8,128)(2,1)}, bf16[4,2,512,256]{3,2,1,0:T(8,128)(2,1)}, u32[]{:S(2)}, u32[]{:S(2)}) collective-permute-start(bf16[4,2,512,256]{3,2,1,0:T(8,128)(2,1)} %pad_maximum_fusion.1.own_ref), channel_id=1, source_target_pairs={{0,32},{32,0},{1,33},{33,1},{2,34},{34,2},{3,35},{35,3},{4,36},{36... | collective-permute-start | bytes 6291464 | tf_op jit(solution)/shard_map/ppermute | solution.py:40
  100.0 1.6 copy-start
  104.0 11.2 %collective-permute-start.13 = (f32[128,256]{1,0:T(8,128)S(1)}, f32[128,256]{1,0:T(8,128)S(1)}, u32[]{:S(2)}, u32[]{:S(2)}) collective-permute-start(f32[128,256]{1,0:T(8,128)S(1)} %get-tuple-element.22), channel_id=1, source_target_pairs={{0,16},{16,0},{1,17},{17,1},{2,18},{18,2},{3,19},{19,3},{4,20},{20... | collective-permute-start | bytes 393224 | tf_op jit(solution)/shard_map/ppermute | solution.py:40
  113.2 10.2 %collective-permute-start.12 = (f32[128,256]{1,0:T(8,128)S(1)}, f32[128,256]{1,0:T(8,128)S(1)}, u32[]{:S(2)}, u32[]{:S(2)}) collective-permute-start(f32[128,256]{1,0:T(8,128)S(1)} %get-tuple-element.21), channel_id=1, source_target_pairs={{0,16},{16,0},{1,17},{17,1},{2,18},{18,2},{3,19},{19,3},{4,20},{20... | collective-permute-start | bytes 393224 | tf_op jit(solution)/shard_map/ppermute | solution.py:40
  115.2 15.9 %collective-permute-start.14 = (bf16[128,256]{1,0:T(8,128)(2,1)S(1)}, bf16[128,256]{1,0:T(8,128)(2,1)S(1)}, u32[]{:S(2)}, u32[]{:S(2)}) collective-permute-start(bf16[128,256]{1,0:T(8,128)(2,1)S(1)} %multiply_convert_fusion), channel_id=1, source_target_pairs={{0,0},{1,1},{2,32},{3,33},{4,64},{5,65},{6,96},{7,97},{8,128},{9,1... | collective-permute-start | bytes 196616 | tf_op jit(solution)/shard_map/ppermute | solution.py:40
  132.2 65.5 %all-to-all-start = ((bf16[16,128,256]{2,1,0:T(8,128)(2,1)}), bf16[16,128,256]{2,1,0:T(8,128)(2,1)S(1)}, u32[]{:S(2)}, u32[]{:S(2)}) async-start(bf16[16,128,256]{2,1,0:T(8,128)(2,1)} %broadcast_in_dim.2), calls=%async_computation | async-start | bytes 2097152 | tf_op jit(solution)/shard_map/all_to_all | solution.py:18
  146.9 8.7 %collective-permute-start.15 = (bf16[128,256]{1,0:T(8,128)(2,1)S(1)}, bf16[128,256]{1,0:T(8,128)(2,1)S(1)}, u32[]{:S(2)}, u32[]{:S(2)}) collective-permute-start(bf16[128,256]{1,0:T(8,128)(2,1)S(1)} %multiply_convert_fusion.1), channel_id=1, source_target_pairs={{0,0},{16,256},{256,16},{272,272},{1,1},{17,257},{257,17},{273,273... | collective-permute-start | bytes 196616 | tf_op jit(solution)/shard_map/ppermute | solution.py:40
  147.5 9.9 %collective-permute-start.16 = (bf16[128,256]{1,0:T(8,128)(2,1)S(1)}, bf16[128,256]{1,0:T(8,128)(2,1)S(1)}, u32[]{:S(2)}, u32[]{:S(2)}) collective-permute-start(bf16[128,256]{1,0:T(8,128)(2,1)S(1)} %multiply_convert_fusion.1), channel_id=1, source_target_pairs={{0,256},{16,0},{256,272},{272,16},{1,257},{17,1},{257,273},{273,17... | collective-permute-start | bytes 196616 | tf_op jit(solution)/shard_map/ppermute | solution.py:40
  157.4 11.2 %collective-permute-start.17 = (bf16[2,128,256]{2,1,0:T(8,128)(2,1)S(1)}, bf16[2,128,256]{2,1,0:T(8,128)(2,1)S(1)}, u32[]{:S(2)}, u32[]{:S(2)}) collective-permute-start(bf16[2,128,256]{2,1,0:T(8,128)(2,1)S(1)} %get-tuple-element.30), channel_id=1, source_target_pairs={{0,64},{64,128},{128,192},{192,0},{1,65},{65,129},{129,193},{193,1... | collective-permute-start | bytes 393224 | tf_op jit(solution)/shard_map/ppermute | solution.py:40
  159.4 9.6 %collective-permute-start.18 = (bf16[2,128,256]{2,1,0:T(8,128)(2,1)S(1)}, bf16[2,128,256]{2,1,0:T(8,128)(2,1)S(1)}, u32[]{:S(2)}, u32[]{:S(2)}) collective-permute-start(bf16[2,128,256]{2,1,0:T(8,128)(2,1)S(1)} %get-tuple-element.30), channel_id=1, source_target_pairs={{0,128},{64,192},{128,0},{192,64},{1,129},{65,193},{129,1},{193,65... | collective-permute-start | bytes 393224 | tf_op jit(solution)/shard_map/ppermute | solution.py:40
  165.1 6.9 %collective-permute-start.19 = (bf16[2,128,256]{2,1,0:T(8,128)(2,1)S(1)}, bf16[2,128,256]{2,1,0:T(8,128)(2,1)S(1)}, u32[]{:S(2)}, u32[]{:S(2)}) collective-permute-start(bf16[2,128,256]{2,1,0:T(8,128)(2,1)S(1)} %get-tuple-element.30), channel_id=1, source_target_pairs={{0,192},{64,0},{128,64},{192,128},{1,193},{65,1},{129,65},{193,129... | collective-permute-start | bytes 393224 | tf_op jit(solution)/shard_map/ppermute | solution.py:40
  172.0 3.8 %collective-permute-start.20 = (bf16[4,2,128,256]{3,2,1,0:T(8,128)(2,1)S(1)}, bf16[4,2,128,256]{3,2,1,0:T(8,128)(2,1)S(1)}, u32[]{:S(2)}, u32[]{:S(2)}) collective-permute-start(bf16[4,2,128,256]{3,2,1,0:T(8,128)(2,1)S(1)} %pad_maximum_fusion.4.own_ref), channel_id=1, source_target_pairs={{0,32},{32,0},{1,33},{33,1},{2,34},{34,2},{3,35},{35,3},{4,36},{36... | collective-permute-start | bytes 1572872 | tf_op jit(solution)/shard_map/ppermute | solution.py:40
  199.0 13.2 %collective-permute-start.21 = (f32[256,512]{1,0:T(8,128)S(1)}, f32[256,512]{1,0:T(8,128)S(1)}, u32[]{:S(2)}, u32[]{:S(2)}) collective-permute-start(f32[256,512]{1,0:T(8,128)S(1)} %shard_map.49), channel_id=1, source_target_pairs={{0,16},{16,0},{1,17},{17,1},{2,18},{18,2},{3,19},{19,3},{4,20},{20... | collective-permute-start | bytes 1572872 | tf_op jit(solution)/shard_map/ppermute | solution.py:40
Sparse Core Ops, SparseCore 0:
  15.6 76.6 all-gather.2

commit v5 on v4

--- a/solution.py
+++ b/solution.py
@@ -101,10 +101,16 @@
     return move(x, (axis,), lambda i: (1 - i,))
 
 
-def plane_gather(x):
-    pair = jnp.stack([move(x, ("xh", "xl"), lambda a, p, k=k: (p ^ k, a)) for k in range(2)])
-    shifted = [move(pair, ("y",), lambda b, j=j: ((b + j) % 4,)) for j in (1, 2, 3)]
-    own = jnp.stack([pair] + shifted)
+def cross(x):
+    return jnp.stack([move(x, ("xh", "xl"), lambda a, p, k=k: (p ^ k, a)) for k in range(2)])
+
+
+def shifts(pair):
+    return [pair] + [move(pair, ("y",), lambda b, j=j: ((b + j) % 4,)) for j in (1, 2, 3)]
+
+
+def both_cores(blocks):
+    own = jnp.stack(blocks)
     return own, swap(own, "c")
 
 
@@ -121,22 +127,24 @@
 
     both = jnp.stack([activations, gradients])
     both, grad_basis = lax.optimization_barrier((both, grad_basis))
-    act_every = grad_every = lax.all_gather(both, ("zh", "zl"), axis=0, tiled=False)
-    grad_panels = plane_gather(grad_basis)
-    act_basis, grad_own = lax.optimization_barrier((act_basis, grad_panels[0]))
-    act_panels = plane_gather(act_basis)
+    every = lax.all_gather(both, ("zh", "zl"), axis=0, tiled=False)
+    grad_pair = cross(grad_basis)
+    act_basis, grad_pair = lax.optimization_barrier((act_basis, grad_pair))
+    grad_panels = both_cores(shifts(grad_pair))
+    act_pair, grad_own = lax.optimization_barrier((cross(act_basis), grad_panels[0]))
+    act_shifts = shifts(act_pair)
 
-    mine, theirs = rotate(at, grad_every, 1, grad_panels)
+    mine, theirs = rotate(at, every, 1, grad_panels)
+    act_shifts, mine = lax.optimization_barrier((act_shifts, mine))
     grad_square = square(mine, theirs)
     grad_square = move(
         grad_square, AXES, lambda a, b, e, p, q, r: (p, q, r // 2, a, b, 2 * e + r % 2)
     )
+    grad_block = to_all(grad_square, ("zh", "zl"), 16)
 
-    act_every, mine = lax.optimization_barrier((act_every, mine))
-    act_square = square(*rotate(at, act_every, 0, act_panels))
-    act_square, grad_square = lax.optimization_barrier((act_square, grad_square))
-    grad_block = to_all(grad_square, ("zh", "zl"), 16)
-    acts = plane_gather(act_square)
+    act_panels = both_cores(act_shifts)
+    act_square = square(*rotate(at, every, 0, act_panels))
+    acts = both_cores(shifts(cross(act_square)))
 
     theirs = swap(correct(jnp.stack([y, c, 1 - turned]), acts, grad_block), "xl")
     mine = correct(at, acts, grad_block)

time: 221 us -> 210 us (0.950)
  the two profiles are of different devices: /device:TPU:8 before, /device:TPU:1 now
where the time goes in v5:
time: 210 us; the launch traced here: 208 us
  starting transfers between devices  116 us (55%)
  waiting for transfers between devices  65.2 us (31%)
  between operations  13.7 us (7%)
  Pallas kernels  6.18 us (3%)
  other arithmetic  4.67 us (2%)
  local copies, waits for them, and re-layouts  2.69 us (1%)
    ppermute x22, starting transfers between devices, move(): return lax.ppermute(x, axes, pairs)  93 us
    ppermute x22, waiting for transfers between devices, move(): return lax.ppermute(x, axes, pairs)  65.2 us
    all_to_all x1, starting transfers between devices, to_all(): return lax.all_to_all(spread, axes, split_axis=0, concat_axis=0, tiled=True)  22.6 us
  transfers between devices with their start and end apart: 24, of which 15 were waited for; matrix products, arithmetic and copies ran while one was open for 1% of the time, Pallas kernels for 2%

profile of v5, /device:TPU:1, one launch (start us, length us, event | category | flops | bytes accessed | tf_op | source)
XLA Modules:
  0.0 208.1 jit_solution(7357798290679921789)
XLA Ops:
  6.5 0.0 all-gather.3.cloned.1.call-start
  6.5 1.5 pad_maximum_fusion.5
  8.1 0.0 all-gather.3.cloned.1.call-update
  8.1 1.6 collective-permute-start
  9.7 6.0 %collective-permute-start.1 = (bf16[512,256]{1,0:T(8,128)(2,1)}, bf16[512,256]{1,0:T(8,128)(2,1)S(1)}, u32[]{:S(2)}, u32[]{:S(2)}) collective-permute-start(bf16[512,256]{1,0:T(8,128)(2,1)} %param.7), channel_id=1, source_target_pairs={{0,256},{16,0},{256,272},{272,16},{1,257},{17,1},{257,273},{273,17... | collective-permute-start | bytes 786440 | tf_op jit(solution)/shard_map/ppermute | solution.py:40
  15.8 0.0 collective-permute-done
  15.8 3.6 %collective-permute-done.1 = bf16[512,256]{1,0:T(8,128)(2,1)S(1)} collective-permute-done((bf16[512,256]{1,0:T(8,128)(2,1)}, bf16[512,256]{1,0:T(8,128)(2,1)S(1)}, u32[]{:S(2)}, u32[]{:S(2)}) %collective-permute-start.1) | collective-permute-done | bytes 262176 | tf_op jit(solution)/shard_map/ppermute | solution.py:40
  19.4 0.1 pad_maximum_fusion.2
  19.5 4.9 %collective-permute-start.4 = (bf16[2,512,256]{2,1,0:T(8,128)(2,1)S(1)}, bf16[2,512,256]{2,1,0:T(8,128)(2,1)S(1)}, u32[]{:S(2)}, u32[]{:S(2)}) collective-permute-start(bf16[2,512,256]{2,1,0:T(8,128)(2,1)S(1)} %pad_maximum_fusion.2), channel_id=1, source_target_pairs={{0,64},{64,128},{128,192},{192,0},{1,65},{65,129},{129,193},{193,1... | collective-permute-start | bytes 1572872 | tf_op jit(solution)/shard_map/ppermute | solution.py:40
  24.4 4.5 %collective-permute-start.5 = (bf16[2,512,256]{2,1,0:T(8,128)(2,1)S(1)}, bf16[2,512,256]{2,1,0:T(8,128)(2,1)S(1)}, u32[]{:S(2)}, u32[]{:S(2)}) collective-permute-start(bf16[2,512,256]{2,1,0:T(8,128)(2,1)S(1)} %pad_maximum_fusion.2), channel_id=1, source_target_pairs={{0,128},{64,192},{128,0},{192,64},{1,129},{65,193},{129,1},{193,65... | collective-permute-start | bytes 1572872 | tf_op jit(solution)/shard_map/ppermute | solution.py:40
  28.9 3.0 %collective-permute-start.6 = (bf16[2,512,256]{2,1,0:T(8,128)(2,1)S(1)}, bf16[2,512,256]{2,1,0:T(8,128)(2,1)S(1)}, u32[]{:S(2)}, u32[]{:S(2)}) collective-permute-start(bf16[2,512,256]{2,1,0:T(8,128)(2,1)S(1)} %pad_maximum_fusion.2), channel_id=1, source_target_pairs={{0,192},{64,0},{128,64},{192,128},{1,193},{65,1},{129,65},{193,129... | collective-permute-start | bytes 1572872 | tf_op jit(solution)/shard_map/ppermute | solution.py:40
  31.9 2.0 collective-permute-done.4
  33.9 14.7 %collective-permute-done.5 = bf16[2,512,256]{2,1,0:T(8,128)(2,1)S(1)} collective-permute-done((bf16[2,512,256]{2,1,0:T(8,128)(2,1)S(1)}, bf16[2,512,256]{2,1,0:T(8,128)(2,1)S(1)}, u32[]{:S(2)}, u32[]{:S(2)}) %collective-permute-start.5) | collective-permute-done | bytes 524320 | tf_op jit(solution)/shard_map/ppermute | solution.py:40
  48.6 2.3 %collective-permute-done.6 = bf16[2,512,256]{2,1,0:T(8,128)(2,1)S(1)} collective-permute-done((bf16[2,512,256]{2,1,0:T(8,128)(2,1)S(1)}, bf16[2,512,256]{2,1,0:T(8,128)(2,1)S(1)}, u32[]{:S(2)}, u32[]{:S(2)}) %collective-permute-start.6) | collective-permute-done | bytes 524320 | tf_op jit(solution)/shard_map/ppermute | solution.py:40
  50.9 0.3 pad_maximum_fusion.own_ref
  51.1 3.5 %collective-permute-start.10 = (bf16[4,2,512,256]{3,2,1,0:T(8,128)(2,1)S(1)}, bf16[4,2,512,256]{3,2,1,0:T(8,128)(2,1)}, u32[]{:S(2)}, u32[]{:S(2)}) collective-permute-start(bf16[4,2,512,256]{3,2,1,0:T(8,128)(2,1)S(1)} %pad_maximum_fusion.own_ref), channel_id=1, source_target_pairs={{0,32},{32,0},{1,33},{33,1},{2,34},{34,2},{3,35},{35,3},{4,36},{36... | collective-permute-start | bytes 6291464 | tf_op jit(solution)/shard_map/ppermute | solution.py:40
  54.6 0.0 copy-done.2
  54.6 0.7 collective-permute-start.2
  55.3 8.6 %collective-permute-start.3 = (bf16[512,256]{1,0:T(8,128)(2,1)S(1)}, bf16[512,256]{1,0:T(8,128)(2,1)S(1)}, u32[]{:S(2)}, u32[]{:S(2)}) collective-permute-start(bf16[512,256]{1,0:T(8,128)(2,1)S(1)} %copy-done.2), channel_id=1, source_target_pairs={{0,256},{16,0},{256,272},{272,16},{1,257},{17,1},{257,273},{273,17... | collective-permute-start | bytes 786440 | tf_op jit(solution)/shard_map/ppermute | solution.py:40
  64.0 0.0 collective-permute-done.2
  64.0 6.2 %collective-permute-done.3 = bf16[512,256]{1,0:T(8,128)(2,1)S(1)} collective-permute-done((bf16[512,256]{1,0:T(8,128)(2,1)S(1)}, bf16[512,256]{1,0:T(8,128)(2,1)S(1)}, u32[]{:S(2)}, u32[]{:S(2)}) %collective-permute-start.3) | collective-permute-done | bytes 262176 | tf_op jit(solution)/shard_map/ppermute | solution.py:40
  70.2 0.1 pad_maximum_fusion.3
  70.2 4.0 %collective-permute-start.7 = (bf16[2,512,256]{2,1,0:T(8,128)(2,1)S(1)}, bf16[2,512,256]{2,1,0:T(8,128)(2,1)S(1)}, u32[]{:S(2)}, u32[]{:S(2)}) collective-permute-start(bf16[2,512,256]{2,1,0:T(8,128)(2,1)S(1)} %pad_maximum_fusion.3), channel_id=1, source_target_pairs={{0,64},{64,128},{128,192},{192,0},{1,65},{65,129},{129,193},{193,1... | collective-permute-start | bytes 1572872 | tf_op jit(solution)/shard_map/ppermute | solution.py:40
  74.2 3.4 %collective-permute-start.8 = (bf16[2,512,256]{2,1,0:T(8,128)(2,1)S(1)}, bf16[2,512,256]{2,1,0:T(8,128)(2,1)}, u32[]{:S(2)}, u32[]{:S(2)}) collective-permute-start(bf16[2,512,256]{2,1,0:T(8,128)(2,1)S(1)} %pad_maximum_fusion.3), channel_id=1, source_target_pairs={{0,128},{64,192},{128,0},{192,64},{1,129},{65,193},{129,1},{193,65... | collective-permute-start | bytes 1572872 | tf_op jit(solution)/shard_map/ppermute | solution.py:40
  77.6 3.3 %collective-permute-start.9 = (bf16[2,512,256]{2,1,0:T(8,128)(2,1)S(1)}, bf16[2,512,256]{2,1,0:T(8,128)(2,1)}, u32[]{:S(2)}, u32[]{:S(2)}) collective-permute-start(bf16[2,512,256]{2,1,0:T(8,128)(2,1)S(1)} %pad_maximum_fusion.3), channel_id=1, source_target_pairs={{0,192},{64,0},{128,64},{192,128},{1,193},{65,1},{129,65},{193,129... | collective-permute-start | bytes 1572872 | tf_op jit(solution)/shard_map/ppermute | solution.py:40
  80.9 0.1 pad_add_fusion.at_ref
  81.0 0.0 collective-permute-done.10.other_ref
  81.0 1.6 copy-done
  82.6 2.4 %shard_map.46 = (f32[128,256]{1,0:T(8,128)S(1)}, f32[128,256]{1,0:T(8,128)S(1)}) custom-call(s32[3]{0:T(128)S(1)} %pad_add_fusion.at_ref, bf16[16,2,128,256]{3,2,1,0:T(8,128)(2,1)S(1)} %bitcast.26, bf16[4,2,512,256]{3,2,1,0:T(8,128)(2,1)S(1)} %pad_maximum_fusion.own_ref, bf16[4,2,512,256]{3,2,1,0:T(8,128)(2,1)} %collective-permute-done.10.other_ref), custom_call_target="tpu_custom_call" | custom-call | tf_op jit(solution)/shard_map/pallas_call | solution.py:80
  85.0 5.8 %collective-permute-start.19 = (f32[128,256]{1,0:T(8,128)S(1)}, f32[128,256]{1,0:T(8,128)S(1)}, u32[]{:S(2)}, u32[]{:S(2)}) collective-permute-start(f32[128,256]{1,0:T(8,128)S(1)} %get-tuple-element.32), channel_id=1, source_target_pairs={{0,16},{16,0},{1,17},{17,1},{2,18},{18,2},{3,19},{19,3},{4,20},{20... | collective-permute-start | bytes 393224 | tf_op jit(solution)/shard_map/ppermute | solution.py:40
  90.8 0.0 collective-permute-done.7
  90.8 7.5 %collective-permute-done.8 = bf16[2,512,256]{2,1,0:T(8,128)(2,1)} collective-permute-done((bf16[2,512,256]{2,1,0:T(8,128)(2,1)S(1)}, bf16[2,512,256]{2,1,0:T(8,128)(2,1)}, u32[]{:S(2)}, u32[]{:S(2)}) %collective-permute-start.8) | collective-permute-done | bytes 524320 | tf_op jit(solution)/shard_map/ppermute | solution.py:40
  98.3 1.6 collective-permute-done.9
  99.9 0.0 collective-permute-done.19
  99.9 6.3 %collective-permute-start.20 = (bf16[128,256]{1,0:T(8,128)(2,1)S(1)}, bf16[128,256]{1,0:T(8,128)(2,1)S(1)}, u32[]{:S(2)}, u32[]{:S(2)}) collective-permute-start(bf16[128,256]{1,0:T(8,128)(2,1)S(1)} %multiply_convert_fusion), channel_id=1, source_target_pairs={{0,0},{1,1},{2,32},{3,33},{4,64},{5,65},{6,96},{7,97},{8,128},{9,1... | collective-permute-start | bytes 196616 | tf_op jit(solution)/shard_map/ppermute | solution.py:40
  106.3 1.9 collective-permute-done.20
  108.2 1.1 broadcast_in_dim.2
  109.3 22.6 %all-to-all-start = ((bf16[16,128,256]{2,1,0:T(8,128)(2,1)}), bf16[16,128,256]{2,1,0:T(8,128)(2,1)S(1)}, u32[]{:S(2)}, u32[]{:S(2)}) async-start(bf16[16,128,256]{2,1,0:T(8,128)(2,1)} %broadcast_in_dim.2), calls=%async_computation | async-start | bytes 2097152 | tf_op jit(solution)/shard_map/all_to_all | solution.py:18
  131.9 1.6 pad_maximum_fusion.1.own_ref
  133.5 5.2 %collective-permute-start.11 = (bf16[4,2,512,256]{3,2,1,0:T(8,128)(2,1)S(1)}, bf16[4,2,512,256]{3,2,1,0:T(8,128)(2,1)S(1)}, u32[]{:S(2)}, u32[]{:S(2)}) collective-permute-start(bf16[4,2,512,256]{3,2,1,0:T(8,128)(2,1)S(1)} %pad_maximum_fusion.1.own_ref), channel_id=1, source_target_pairs={{0,32},{32,0},{1,33},{33,1},{2,34},{34,2},{3,35},{35,3},{4,36},{36... | collective-permute-start | bytes 6291464 | tf_op jit(solution)/shard_map/ppermute | solution.py:40
  138.7 3.8 %collective-permute-done.11.other_ref = bf16[4,2,512,256]{3,2,1,0:T(8,128)(2,1)S(1)} collective-permute-done((bf16[4,2,512,256]{3,2,1,0:T(8,128)(2,1)S(1)}, bf16[4,2,512,256]{3,2,1,0:T(8,128)(2,1)S(1)}, u32[]{:S(2)}, u32[]{:S(2)}) %collective-permute-start.11) | collective-permute-done | bytes 2097184 | tf_op jit(solution)/shard_map/ppermute | solution.py:40
  142.5 1.3 shard_map.47
  143.7 6.7 %collective-permute-start.12 = (f32[128,256]{1,0:T(8,128)S(1)}, f32[128,256]{1,0:T(8,128)S(1)}, u32[]{:S(2)}, u32[]{:S(2)}) collective-permute-start(f32[128,256]{1,0:T(8,128)S(1)} %get-tuple-element.30), channel_id=1, source_target_pairs={{0,16},{16,0},{1,17},{17,1},{2,18},{18,2},{3,19},{19,3},{4,20},{20... | collective-permute-start | bytes 393224 | tf_op jit(solution)/shard_map/ppermute | solution.py:40
  150.5 3.6 %collective-permute-done.12 = f32[128,256]{1,0:T(8,128)S(1)} collective-permute-done((f32[128,256]{1,0:T(8,128)S(1)}, f32[128,256]{1,0:T(8,128)S(1)}, u32[]{:S(2)}, u32[]{:S(2)}) %collective-permute-start.12) | collective-permute-done | bytes 131104 | tf_op jit(solution)/shard_map/ppermute | solution.py:40
  154.1 0.7 collective-permute-start.13
  154.7 6.1 %collective-permute-start.14 = (bf16[128,256]{1,0:T(8,128)(2,1)S(1)}, bf16[128,256]{1,0:T(8,128)(2,1)S(1)}, u32[]{:S(2)}, u32[]{:S(2)}) collective-permute-start(bf16[128,256]{1,0:T(8,128)(2,1)S(1)} %multiply_convert_fusion.1), channel_id=1, source_target_pairs={{0,256},{16,0},{256,272},{272,16},{1,257},{17,1},{257,273},{273,17... | collective-permute-start | bytes 196616 | tf_op jit(solution)/shard_map/ppermute | solution.py:40
  160.8 0.0 collective-permute-done.13
  160.8 1.4 collective-permute-done.14
  162.2 2.3 %collective-permute-start.15 = (bf16[2,128,256]{2,1,0:T(8,128)(2,1)S(1)}, bf16[2,128,256]{2,1,0:T(8,128)(2,1)S(1)}, u32[]{:S(2)}, u32[]{:S(2)}) collective-permute-start(bf16[2,128,256]{2,1,0:T(8,128)(2,1)S(1)} %get-tuple-element.34), channel_id=1, source_target_pairs={{0,64},{64,128},{128,192},{192,0},{1,65},{65,129},{129,193},{193,1... | collective-permute-start | bytes 393224 | tf_op jit(solution)/shard_map/ppermute | solution.py:40
  164.6 4.9 %collective-permute-start.16 = (bf16[2,128,256]{2,1,0:T(8,128)(2,1)S(1)}, bf16[2,128,256]{2,1,0:T(8,128)(2,1)S(1)}, u32[]{:S(2)}, u32[]{:S(2)}) collective-permute-start(bf16[2,128,256]{2,1,0:T(8,128)(2,1)S(1)} %get-tuple-element.34), channel_id=1, source_target_pairs={{0,128},{64,192},{128,0},{192,64},{1,129},{65,193},{129,1},{193,65... | collective-permute-start | bytes 393224 | tf_op jit(solution)/shard_map/ppermute | solution.py:40
  169.4 1.9 collective-permute-start.17
  171.4 0.0 collective-permute-done.15
  171.4 1.3 collective-permute-done.16
  172.7 3.7 %collective-permute-done.17 = bf16[2,128,256]{2,1,0:T(8,128)(2,1)S(1)} collective-permute-done((bf16[2,128,256]{2,1,0:T(8,128)(2,1)S(1)}, bf16[2,128,256]{2,1,0:T(8,128)(2,1)S(1)}, u32[]{:S(2)}, u32[]{:S(2)}) %collective-permute-start.17) | collective-permute-done | bytes 131104 | tf_op jit(solution)/shard_map/ppermute | solution.py:40
  176.3 0.1 pad_maximum_fusion.4.own_ref
  176.4 4.8 %collective-permute-start.18 = (bf16[4,2,128,256]{3,2,1,0:T(8,128)(2,1)S(1)}, bf16[4,2,128,256]{3,2,1,0:T(8,128)(2,1)S(1)}, u32[]{:S(2)}, u32[]{:S(2)}) collective-permute-start(bf16[4,2,128,256]{3,2,1,0:T(8,128)(2,1)S(1)} %pad_maximum_fusion.4.own_ref), channel_id=1, source_target_pairs={{0,32},{32,0},{1,33},{33,1},{2,34},{34,2},{3,35},{35,3},{4,36},{36... | collective-permute-start | bytes 1572872 | tf_op jit(solution)/shard_map/ppermute | solution.py:40
  181.2 0.1 pad_add_fusion.2.at_ref
  181.3 1.4 collective-permute-done.18.other_ref
  182.7 0.0 all-to-all-done.s_ref
  182.7 1.3 shard_map.49
  184.0 4.9 %collective-permute-start.21 = (f32[256,512]{1,0:T(8,128)S(1)}, f32[256,512]{1,0:T(8,128)S(1)}, u32[]{:S(2)}, u32[]{:S(2)}) collective-permute-start(f32[256,512]{1,0:T(8,128)S(1)} %shard_map.49), channel_id=1, source_target_pairs={{0,16},{16,0},{1,17},{17,1},{2,18},{18,2},{3,19},{19,3},{4,20},{20... | collective-permute-start | bytes 1572872 | tf_op jit(solution)/shard_map/ppermute | solution.py:40
  188.9 1.3 shard_map.48
  190.1 10.3 %collective-permute-done.21 = f32[256,512]{1,0:T(8,128)S(1)} collective-permute-done((f32[256,512]{1,0:T(8,128)S(1)}, f32[256,512]{1,0:T(8,128)S(1)}, u32[]{:S(2)}, u32[]{:S(2)}) %collective-permute-start.21) | collective-permute-done | bytes 524320 | tf_op jit(solution)/shard_map/ppermute | solution.py:40
  200.4 0.9 add_multiply_fusion
  (8 shorter events, 0.1 us)
Async XLA Ops:
  6.5 74.5 %all-gather.3.cloned.1.call-start = ((), (), s32[]{:S(2)}) async-start(), calls=%async_computation.1 | async-start | bytes 2228224 | tf_op jit(solution)/shard_map/all_gather | solution.py:130
  8.1 7.7 %collective-permute-start = (bf16[512,256]{1,0:T(8,128)(2,1)}, bf16[512,256]{1,0:T(8,128)(2,1)S(1)}, u32[]{:S(2)}, u32[]{:S(2)}) collective-permute-start(bf16[512,256]{1,0:T(8,128)(2,1)} %param.7), channel_id=1, source_target_pairs={{0,0},{16,256},{256,16},{272,272},{1,1},{17,257},{257,17},{273,273... | collective-permute-start | bytes 786440 | tf_op jit(solution)/shard_map/ppermute | solution.py:40
  9.7 9.7 %collective-permute-start.1 = (bf16[512,256]{1,0:T(8,128)(2,1)}, bf16[512,256]{1,0:T(8,128)(2,1)S(1)}, u32[]{:S(2)}, u32[]{:S(2)}) collective-permute-start(bf16[512,256]{1,0:T(8,128)(2,1)} %param.7), channel_id=1, source_target_pairs={{0,256},{16,0},{256,272},{272,16},{1,257},{17,1},{257,273},{273,17... | collective-permute-start | bytes 786440 | tf_op jit(solution)/shard_map/ppermute | solution.py:40
  19.5 14.4 %collective-permute-start.4 = (bf16[2,512,256]{2,1,0:T(8,128)(2,1)S(1)}, bf16[2,512,256]{2,1,0:T(8,128)(2,1)S(1)}, u32[]{:S(2)}, u32[]{:S(2)}) collective-permute-start(bf16[2,512,256]{2,1,0:T(8,128)(2,1)S(1)} %pad_maximum_fusion.2), channel_id=1, source_target_pairs={{0,64},{64,128},{128,192},{192,0},{1,65},{65,129},{129,193},{193,1... | collective-permute-start | bytes 1572872 | tf_op jit(solution)/shard_map/ppermute | solution.py:40
  24.4 24.2 %collective-permute-start.5 = (bf16[2,512,256]{2,1,0:T(8,128)(2,1)S(1)}, bf16[2,512,256]{2,1,0:T(8,128)(2,1)S(1)}, u32[]{:S(2)}, u32[]{:S(2)}) collective-permute-start(bf16[2,512,256]{2,1,0:T(8,128)(2,1)S(1)} %pad_maximum_fusion.2), channel_id=1, source_target_pairs={{0,128},{64,192},{128,0},{192,64},{1,129},{65,193},{129,1},{193,65... | collective-permute-start | bytes 1572872 | tf_op jit(solution)/shard_map/ppermute | solution.py:40
  28.9 22.0 %collective-permute-start.6 = (bf16[2,512,256]{2,1,0:T(8,128)(2,1)S(1)}, bf16[2,512,256]{2,1,0:T(8,128)(2,1)S(1)}, u32[]{:S(2)}, u32[]{:S(2)}) collective-permute-start(bf16[2,512,256]{2,1,0:T(8,128)(2,1)S(1)} %pad_maximum_fusion.2), channel_id=1, source_target_pairs={{0,192},{64,0},{128,64},{192,128},{1,193},{65,1},{129,65},{193,129... | collective-permute-start | bytes 1572872 | tf_op jit(solution)/shard_map/ppermute | solution.py:40
  50.9 3.7 %copy-start.2 = (bf16[512,256]{1,0:T(8,128)(2,1)S(1)}, bf16[512,256]{1,0:T(8,128)(2,1)}, u32[]{:S(2)}) copy-start(bf16[512,256]{1,0:T(8,128)(2,1)} %param.6) | copy-start | bytes 786436
  51.1 29.8 %collective-permute-start.10 = (bf16[4,2,512,256]{3,2,1,0:T(8,128)(2,1)S(1)}, bf16[4,2,512,256]{3,2,1,0:T(8,128)(2,1)}, u32[]{:S(2)}, u32[]{:S(2)}) collective-permute-start(bf16[4,2,512,256]{3,2,1,0:T(8,128)(2,1)S(1)} %pad_maximum_fusion.own_ref), channel_id=1, source_target_pairs={{0,32},{32,0},{1,33},{33,1},{2,34},{34,2},{3,35},{35,3},{4,36},{36... | collective-permute-start | bytes 6291464 | tf_op jit(solution)/shard_map/ppermute | solution.py:40
  54.6 9.3 %collective-permute-start.2 = (bf16[512,256]{1,0:T(8,128)(2,1)S(1)}, bf16[512,256]{1,0:T(8,128)(2,1)S(1)}, u32[]{:S(2)}, u32[]{:S(2)}) collective-permute-start(bf16[512,256]{1,0:T(8,128)(2,1)S(1)} %copy-done.2), channel_id=1, source_target_pairs={{0,0},{16,256},{256,16},{272,272},{1,1},{17,257},{257,17},{273,273... | collective-permute-start | bytes 786440 | tf_op jit(solution)/shard_map/ppermute | solution.py:40
  55.3 14.9 %collective-permute-start.3 = (bf16[512,256]{1,0:T(8,128)(2,1)S(1)}, bf16[512,256]{1,0:T(8,128)(2,1)S(1)}, u32[]{:S(2)}, u32[]{:S(2)}) collective-permute-start(bf16[512,256]{1,0:T(8,128)(2,1)S(1)} %copy-done.2), channel_id=1, source_target_pairs={{0,256},{16,0},{256,272},{272,16},{1,257},{17,1},{257,273},{273,17... | collective-permute-start | bytes 786440 | tf_op jit(solution)/shard_map/ppermute | solution.py:40
  70.2 20.6 %collective-permute-start.7 = (bf16[2,512,256]{2,1,0:T(8,128)(2,1)S(1)}, bf16[2,512,256]{2,1,0:T(8,128)(2,1)S(1)}, u32[]{:S(2)}, u32[]{:S(2)}) collective-permute-start(bf16[2,512,256]{2,1,0:T(8,128)(2,1)S(1)} %pad_maximum_fusion.3), channel_id=1, source_target_pairs={{0,64},{64,128},{128,192},{192,0},{1,65},{65,129},{129,193},{193,1... | collective-permute-start | bytes 1572872 | tf_op jit(solution)/shard_map/ppermute | solution.py:40
  74.2 24.1 %collective-permute-start.8 = (bf16[2,512,256]{2,1,0:T(8,128)(2,1)S(1)}, bf16[2,512,256]{2,1,0:T(8,128)(2,1)}, u32[]{:S(2)}, u32[]{:S(2)}) collective-permute-start(bf16[2,512,256]{2,1,0:T(8,128)(2,1)S(1)} %pad_maximum_fusion.3), channel_id=1, source_target_pairs={{0,128},{64,192},{128,0},{192,64},{1,129},{65,193},{129,1},{193,65... | collective-permute-start | bytes 1572872 | tf_op jit(solution)/shard_map/ppermute | solution.py:40
  77.6 22.3 %collective-permute-start.9 = (bf16[2,512,256]{2,1,0:T(8,128)(2,1)S(1)}, bf16[2,512,256]{2,1,0:T(8,128)(2,1)}, u32[]{:S(2)}, u32[]{:S(2)}) collective-permute-start(bf16[2,512,256]{2,1,0:T(8,128)(2,1)S(1)} %pad_maximum_fusion.3), channel_id=1, source_target_pairs={{0,192},{64,0},{128,64},{192,128},{1,193},{65,1},{129,65},{193,129... | collective-permute-start | bytes 1572872 | tf_op jit(solution)/shard_map/ppermute | solution.py:40
  81.0 1.6 copy-start
  85.0 14.9 %collective-permute-start.19 = (f32[128,256]{1,0:T(8,128)S(1)}, f32[128,256]{1,0:T(8,128)S(1)}, u32[]{:S(2)}, u32[]{:S(2)}) collective-permute-start(f32[128,256]{1,0:T(8,128)S(1)} %get-tuple-element.32), channel_id=1, source_target_pairs={{0,16},{16,0},{1,17},{17,1},{2,18},{18,2},{3,19},{19,3},{4,20},{20... | collective-permute-start | bytes 393224 | tf_op jit(solution)/shard_map/ppermute | solution.py:40
  99.9 8.3 %collective-permute-start.20 = (bf16[128,256]{1,0:T(8,128)(2,1)S(1)}, bf16[128,256]{1,0:T(8,128)(2,1)S(1)}, u32[]{:S(2)}, u32[]{:S(2)}) collective-permute-start(bf16[128,256]{1,0:T(8,128)(2,1)S(1)} %multiply_convert_fusion), channel_id=1, source_target_pairs={{0,0},{1,1},{2,32},{3,33},{4,64},{5,65},{6,96},{7,97},{8,128},{9,1... | collective-permute-start | bytes 196616 | tf_op jit(solution)/shard_map/ppermute | solution.py:40
  109.3 73.4 %all-to-all-start = ((bf16[16,128,256]{2,1,0:T(8,128)(2,1)}), bf16[16,128,256]{2,1,0:T(8,128)(2,1)S(1)}, u32[]{:S(2)}, u32[]{:S(2)}) async-start(bf16[16,128,256]{2,1,0:T(8,128)(2,1)} %broadcast_in_dim.2), calls=%async_computation | async-start | bytes 2097152 | tf_op jit(solution)/shard_map/all_to_all | solution.py:18
  131.9 10.6 %copy-start.1 = (bf16[32,128,256]{2,1,0:T(8,128)(2,1)S(1)}, bf16[32,128,256]{2,1,0:T(8,128)(2,1)}, u32[]{:S(2)}) copy-start(bf16[32,128,256]{2,1,0:T(8,128)(2,1)} %all-gather.3.cloned.1.call-done) | copy-start | bytes 6291460
  133.5 8.9 %collective-permute-start.11 = (bf16[4,2,512,256]{3,2,1,0:T(8,128)(2,1)S(1)}, bf16[4,2,512,256]{3,2,1,0:T(8,128)(2,1)S(1)}, u32[]{:S(2)}, u32[]{:S(2)}) collective-permute-start(bf16[4,2,512,256]{3,2,1,0:T(8,128)(2,1)S(1)} %pad_maximum_fusion.1.own_ref), channel_id=1, source_target_pairs={{0,32},{32,0},{1,33},{33,1},{2,34},{34,2},{3,35},{35,3},{4,36},{36... | collective-permute-start | bytes 6291464 | tf_op jit(solution)/shard_map/ppermute | solution.py:40
  143.7 10.3 %collective-permute-start.12 = (f32[128,256]{1,0:T(8,128)S(1)}, f32[128,256]{1,0:T(8,128)S(1)}, u32[]{:S(2)}, u32[]{:S(2)}) collective-permute-start(f32[128,256]{1,0:T(8,128)S(1)} %get-tuple-element.30), channel_id=1, source_target_pairs={{0,16},{16,0},{1,17},{17,1},{2,18},{18,2},{3,19},{19,3},{4,20},{20... | collective-permute-start | bytes 393224 | tf_op jit(solution)/shard_map/ppermute | solution.py:40
  154.1 6.8 %collective-permute-start.13 = (bf16[128,256]{1,0:T(8,128)(2,1)S(1)}, bf16[128,256]{1,0:T(8,128)(2,1)S(1)}, u32[]{:S(2)}, u32[]{:S(2)}) collective-permute-start(bf16[128,256]{1,0:T(8,128)(2,1)S(1)} %multiply_convert_fusion.1), channel_id=1, source_target_pairs={{0,0},{16,256},{256,16},{272,272},{1,1},{17,257},{257,17},{273,273... | collective-permute-start | bytes 196616 | tf_op jit(solution)/shard_map/ppermute | solution.py:40
  154.7 7.5 %collective-permute-start.14 = (bf16[128,256]{1,0:T(8,128)(2,1)S(1)}, bf16[128,256]{1,0:T(8,128)(2,1)S(1)}, u32[]{:S(2)}, u32[]{:S(2)}) collective-permute-start(bf16[128,256]{1,0:T(8,128)(2,1)S(1)} %multiply_convert_fusion.1), channel_id=1, source_target_pairs={{0,256},{16,0},{256,272},{272,16},{1,257},{17,1},{257,273},{273,17... | collective-permute-start | bytes 196616 | tf_op jit(solution)/shard_map/ppermute | solution.py:40
  162.2 9.2 %collective-permute-start.15 = (bf16[2,128,256]{2,1,0:T(8,128)(2,1)S(1)}, bf16[2,128,256]{2,1,0:T(8,128)(2,1)S(1)}, u32[]{:S(2)}, u32[]{:S(2)}) collective-permute-start(bf16[2,128,256]{2,1,0:T(8,128)(2,1)S(1)} %get-tuple-element.34), channel_id=1, source_target_pairs={{0,64},{64,128},{128,192},{192,0},{1,65},{65,129},{129,193},{193,1... | collective-permute-start | bytes 393224 | tf_op jit(solution)/shard_map/ppermute | solution.py:40
  164.6 8.1 %collective-permute-start.16 = (bf16[2,128,256]{2,1,0:T(8,128)(2,1)S(1)}, bf16[2,128,256]{2,1,0:T(8,128)(2,1)S(1)}, u32[]{:S(2)}, u32[]{:S(2)}) collective-permute-start(bf16[2,128,256]{2,1,0:T(8,128)(2,1)S(1)} %get-tuple-element.34), channel_id=1, source_target_pairs={{0,128},{64,192},{128,0},{192,64},{1,129},{65,193},{129,1},{193,65... | collective-permute-start | bytes 393224 | tf_op jit(solution)/shard_map/ppermute | solution.py:40
  169.4 6.9 %collective-permute-start.17 = (bf16[2,128,256]{2,1,0:T(8,128)(2,1)S(1)}, bf16[2,128,256]{2,1,0:T(8,128)(2,1)S(1)}, u32[]{:S(2)}, u32[]{:S(2)}) collective-permute-start(bf16[2,128,256]{2,1,0:T(8,128)(2,1)S(1)} %get-tuple-element.34), channel_id=1, source_target_pairs={{0,192},{64,0},{128,64},{192,128},{1,193},{65,1},{129,65},{193,129... | collective-permute-start | bytes 393224 | tf_op jit(solution)/shard_map/ppermute | solution.py:40
  176.4 6.3 %collective-permute-start.18 = (bf16[4,2,128,256]{3,2,1,0:T(8,128)(2,1)S(1)}, bf16[4,2,128,256]{3,2,1,0:T(8,128)(2,1)S(1)}, u32[]{:S(2)}, u32[]{:S(2)}) collective-permute-start(bf16[4,2,128,256]{3,2,1,0:T(8,128)(2,1)S(1)} %pad_maximum_fusion.4.own_ref), channel_id=1, source_target_pairs={{0,32},{32,0},{1,33},{33,1},{2,34},{34,2},{3,35},{35,3},{4,36},{36... | collective-permute-start | bytes 1572872 | tf_op jit(solution)/shard_map/ppermute | solution.py:40
  184.0 16.4 %collective-permute-start.21 = (f32[256,512]{1,0:T(8,128)S(1)}, f32[256,512]{1,0:T(8,128)S(1)}, u32[]{:S(2)}, u32[]{:S(2)}) collective-permute-start(f32[256,512]{1,0:T(8,128)S(1)} %shard_map.49), channel_id=1, source_target_pairs={{0,16},{16,0},{1,17},{17,1},{2,18},{18,2},{3,19},{19,3},{4,20},{20... | collective-permute-start | bytes 1572872 | tf_op jit(solution)/shard_map/ppermute | solution.py:40
Sparse Core Ops, SparseCore 0:
  9.4 69.9 all-gather.2

commit v6 on v5

--- a/solution.py
+++ b/solution.py
@@ -44,11 +44,11 @@
     return jnp.dot(a, b, preferred_element_type=jnp.float32)
 
 
-def rotate_kernel(at_ref, x_ref, own_ref, other_ref, mine_ref, theirs_ref):
+def rotate_kernel(at_ref, x_ref, own_ref, other_ref, first_ref, second_ref):
     y, c, turned = at_ref[0], at_ref[1], at_ref[2]
     sums = []
     for k in range(2):
-        acc = jnp.zeros(mine_ref.shape, jnp.float32)
+        acc = jnp.zeros(x_ref.shape[2:], jnp.float32)
         for j in range(4):
             at = 4 * lax.rem(y + 4 - j, 4)
             for h in range(2):
@@ -57,8 +57,12 @@
                 acc += dot(x_ref[at + 2 * (1 - c) + h, 0], other_ref[j, k, rows, :])
         sums.append(acc)
     near, far = sums
-    mine_ref[...] = jnp.where(turned == 0, near, far)
-    theirs_ref[...] = jnp.where(turned == 0, far, near)
+    mine, theirs = jnp.where(turned == 0, near, far), jnp.where(turned == 0, far, near)
+    if len(first_ref.shape) == 2:
+        first_ref[...], second_ref[...] = mine, theirs
+    else:
+        first_ref[0], first_ref[1] = mine, theirs
+        second_ref[0], second_ref[1] = theirs, mine
 
 
 def corrected_kernel(at_ref, own_ref, other_ref, s_ref, out_ref):
@@ -75,13 +79,13 @@
         out_ref[:, 256 * h:256 * h + 256] = acc
 
 
-def rotate(at, x, part, basis):
-    out = jax.ShapeDtypeStruct(x.shape[2:], jnp.float32)
+def rotate(at, x, part, basis, paired):
+    out = jax.ShapeDtypeStruct((2,) * paired + x.shape[2:], jnp.float32)
     return pl.pallas_call(
         rotate_kernel,
         grid=(1,),
         out_shape=[out, out],
-        in_specs=[SMEM, pl.BlockSpec((16, 1) + out.shape, lambda i: (0, part, 0, 0)), VMEM, VMEM],
+        in_specs=[SMEM, pl.BlockSpec((16, 1) + x.shape[2:], lambda i: (0, part, 0, 0)), VMEM, VMEM],
         out_specs=[VMEM, VMEM],
         compiler_params=PARAMS,
     )(at, x, *basis)
@@ -114,11 +118,6 @@
     return own, swap(own, "c")
 
 
-def square(mine, theirs):
-    total = mine + swap(theirs, "xl")
-    return (total * total).astype(jnp.bfloat16)
-
-
 def on_device(activations, gradients, act_basis, grad_basis):
     tokens = activations.shape[0] * 16
     xh, y, c, xl = (lax.axis_index(a) for a in ("xh", "y", "c", "xl"))
@@ -130,21 +129,26 @@
     every = lax.all_gather(both, ("zh", "zl"), axis=0, tiled=False)
     grad_pair = cross(grad_basis)
     act_basis, grad_pair = lax.optimization_barrier((act_basis, grad_pair))
-    grad_panels = both_cores(shifts(grad_pair))
-    act_pair, grad_own = lax.optimization_barrier((cross(act_basis), grad_panels[0]))
+    grad_shifts, act_pair = lax.optimization_barrier((shifts(grad_pair), cross(act_basis)))
+    grad_panels = both_cores(grad_shifts)
+    act_pair, grad_own = lax.optimization_barrier((act_pair, grad_panels[0]))
     act_shifts = shifts(act_pair)
 
-    mine, theirs = rotate(at, every, 1, grad_panels)
-    act_shifts, mine = lax.optimization_barrier((act_shifts, mine))
-    grad_square = square(mine, theirs)
+    mine, theirs = rotate(at, every, 1, grad_panels, 0)
+    rotated_grad = mine + swap(theirs, "xl")
+    grad_square = (rotated_grad * rotated_grad).astype(jnp.bfloat16)
+    act_shifts, grad_square = lax.optimization_barrier((act_shifts, grad_square))
     grad_square = move(
         grad_square, AXES, lambda a, b, e, p, q, r: (p, q, r // 2, a, b, 2 * e + r % 2)
     )
+
+    parts = rotate(at, every, 0, both_cores(act_shifts), 1)
+    grad_square, parts = lax.optimization_barrier((grad_square, parts))
     grad_block = to_all(grad_square, ("zh", "zl"), 16)
-
-    act_panels = both_cores(act_shifts)
-    act_square = square(*rotate(at, every, 0, act_panels))
-    acts = both_cores(shifts(cross(act_square)))
+    parts = [move(parts[k], ("xh", "xl"), lambda a, p, k=k: (p ^ k, a)) for k in range(2)]
+    rotated_act = parts[0] + parts[1]
+    act_square = (rotated_act * rotated_act).astype(jnp.bfloat16)
+    acts = both_cores(shifts(act_square))
 
     theirs = swap(correct(jnp.stack([y, c, 1 - turned]), acts, grad_block), "xl")
     mine = correct(at, acts, grad_block)

time: 210 us -> 202 us (0.962)
  the two profiles are of different devices: /device:TPU:1 before, /device:TPU:13 now
where the time goes in v6:
time: 202 us; the launch traced here: 201 us
  waiting for transfers between devices  95.9 us (47%)
  starting transfers between devices  77.6 us (38%)
  between operations  13.7 us (7%)
  Pallas kernels  6.19 us (3%)
  other arithmetic  4.53 us (2%)
  local copies, waits for them, and re-layouts  2.7 us (1%)
    ppermute x21, starting transfers between devices, move(): return lax.ppermute(x, axes, pairs)  68 us
    ppermute x21, waiting for transfers between devices, move(): return lax.ppermute(x, axes, pairs)  67.3 us
    all_to_all x1, waiting for transfers between devices, to_all(): return lax.all_to_all(spread, axes, split_axis=0, concat_axis=0, tiled=True)  16.1 us
    all_gather x1, waiting for transfers between devices, on_device(): every = lax.all_gather(both, ('zh', 'zl'), axis=0, tiled=False)  12.5 us
    all_to_all x1, starting transfers between devices, to_all(): return lax.all_to_all(spread, axes, split_axis=0, concat_axis=0, tiled=True)  9.57 us
  transfers between devices with their start and end apart: 23, of which 13 were waited for; matrix products, arithmetic and copies ran while one was open for 0% of the time, Pallas kernels for 2%

profile of v6, /device:TPU:13, one launch (start us, length us, event | category | flops | bytes accessed | tf_op | source)
XLA Modules:
  0.0 200.7 jit_solution(4339025946464132284)
XLA Ops:
  6.5 0.0 all-gather.3.cloned.1.call-start
  6.5 1.5 pad_maximum_fusion.5
  8.1 0.0 all-gather.3.cloned.1.call-update
  8.1 2.2 %collective-permute-start = (bf16[512,256]{1,0:T(8,128)(2,1)}, bf16[512,256]{1,0:T(8,128)(2,1)S(1)}, u32[]{:S(2)}, u32[]{:S(2)}) collective-permute-start(bf16[512,256]{1,0:T(8,128)(2,1)} %param.7), channel_id=1, source_target_pairs={{0,0},{16,256},{256,16},{272,272},{1,1},{17,257},{257,17},{273,273... | collective-permute-start | bytes 786440 | tf_op jit(solution)/shard_map/ppermute | solution.py:40
  10.3 2.3 %collective-permute-start.1 = (bf16[512,256]{1,0:T(8,128)(2,1)}, bf16[512,256]{1,0:T(8,128)(2,1)S(1)}, u32[]{:S(2)}, u32[]{:S(2)}) collective-permute-start(bf16[512,256]{1,0:T(8,128)(2,1)} %param.7), channel_id=1, source_target_pairs={{0,256},{16,0},{256,272},{272,16},{1,257},{17,1},{257,273},{273,17... | collective-permute-start | bytes 786440 | tf_op jit(solution)/shard_map/ppermute | solution.py:40
  12.5 10.5 %collective-permute-done = bf16[512,256]{1,0:T(8,128)(2,1)S(1)} collective-permute-done((bf16[512,256]{1,0:T(8,128)(2,1)}, bf16[512,256]{1,0:T(8,128)(2,1)S(1)}, u32[]{:S(2)}, u32[]{:S(2)}) %collective-permute-start) | collective-permute-done | bytes 262176 | tf_op jit(solution)/shard_map/ppermute | solution.py:40
  23.0 0.0 collective-permute-done.1
  23.0 0.1 pad_maximum_fusion.2
  23.1 3.2 %collective-permute-start.2 = (bf16[2,512,256]{2,1,0:T(8,128)(2,1)S(1)}, bf16[2,512,256]{2,1,0:T(8,128)(2,1)S(1)}, u32[]{:S(2)}, u32[]{:S(2)}) collective-permute-start(bf16[2,512,256]{2,1,0:T(8,128)(2,1)S(1)} %pad_maximum_fusion.2), channel_id=1, source_target_pairs={{0,64},{64,128},{128,192},{192,0},{1,65},{65,129},{129,193},{193,1... | collective-permute-start | bytes 1572872 | tf_op jit(solution)/shard_map/ppermute | solution.py:40
  26.3 2.6 %collective-permute-start.3 = (bf16[2,512,256]{2,1,0:T(8,128)(2,1)S(1)}, bf16[2,512,256]{2,1,0:T(8,128)(2,1)S(1)}, u32[]{:S(2)}, u32[]{:S(2)}) collective-permute-start(bf16[2,512,256]{2,1,0:T(8,128)(2,1)S(1)} %pad_maximum_fusion.2), channel_id=1, source_target_pairs={{0,128},{64,192},{128,0},{192,64},{1,129},{65,193},{129,1},{193,65... | collective-permute-start | bytes 1572872 | tf_op jit(solution)/shard_map/ppermute | solution.py:40
  28.9 4.0 %collective-permute-start.4 = (bf16[2,512,256]{2,1,0:T(8,128)(2,1)S(1)}, bf16[2,512,256]{2,1,0:T(8,128)(2,1)S(1)}, u32[]{:S(2)}, u32[]{:S(2)}) collective-permute-start(bf16[2,512,256]{2,1,0:T(8,128)(2,1)S(1)} %pad_maximum_fusion.2), channel_id=1, source_target_pairs={{0,192},{64,0},{128,64},{192,128},{1,193},{65,1},{129,65},{193,129... | collective-permute-start | bytes 1572872 | tf_op jit(solution)/shard_map/ppermute | solution.py:40
  32.9 1.9 collective-permute-start.5
  34.8 1.9 collective-permute-start.6
  36.8 3.8 %collective-permute-done.5 = bf16[512,256]{1,0:T(8,128)(2,1)S(1)} collective-permute-done((bf16[512,256]{1,0:T(8,128)(2,1)}, bf16[512,256]{1,0:T(8,128)(2,1)S(1)}, u32[]{:S(2)}, u32[]{:S(2)}) %collective-permute-start.5) | collective-permute-done | bytes 262176 | tf_op jit(solution)/shard_map/ppermute | solution.py:40
  40.5 3.5 %collective-permute-done.6 = bf16[512,256]{1,0:T(8,128)(2,1)S(1)} collective-permute-done((bf16[512,256]{1,0:T(8,128)(2,1)}, bf16[512,256]{1,0:T(8,128)(2,1)S(1)}, u32[]{:S(2)}, u32[]{:S(2)}) %collective-permute-start.6) | collective-permute-done | bytes 262176 | tf_op jit(solution)/shard_map/ppermute | solution.py:40
  44.0 0.1 pad_maximum_fusion.3
  44.1 0.0 collective-permute-done.2
  44.1 0.0 collective-permute-done.3
  44.1 10.8 %collective-permute-done.4 = bf16[2,512,256]{2,1,0:T(8,128)(2,1)S(1)} collective-permute-done((bf16[2,512,256]{2,1,0:T(8,128)(2,1)S(1)}, bf16[2,512,256]{2,1,0:T(8,128)(2,1)S(1)}, u32[]{:S(2)}, u32[]{:S(2)}) %collective-permute-start.4) | collective-permute-done | bytes 524320 | tf_op jit(solution)/shard_map/ppermute | solution.py:40
  54.9 0.3 pad_maximum_fusion.own_ref
  55.1 2.3 %collective-permute-start.10 = (bf16[4,2,512,256]{3,2,1,0:T(8,128)(2,1)S(1)}, bf16[4,2,512,256]{3,2,1,0:T(8,128)(2,1)}, u32[]{:S(2)}, u32[]{:S(2)}) collective-permute-start(bf16[4,2,512,256]{3,2,1,0:T(8,128)(2,1)S(1)} %pad_maximum_fusion.own_ref), channel_id=1, source_target_pairs={{0,32},{32,0},{1,33},{33,1},{2,34},{34,2},{3,35},{35,3},{4,36},{36... | collective-permute-start | bytes 6291464 | tf_op jit(solution)/shard_map/ppermute | solution.py:40
  57.4 2.2 %collective-permute-start.7 = (bf16[2,512,256]{2,1,0:T(8,128)(2,1)S(1)}, bf16[2,512,256]{2,1,0:T(8,128)(2,1)S(1)}, u32[]{:S(2)}, u32[]{:S(2)}) collective-permute-start(bf16[2,512,256]{2,1,0:T(8,128)(2,1)S(1)} %pad_maximum_fusion.3), channel_id=1, source_target_pairs={{0,64},{64,128},{128,192},{192,0},{1,65},{65,129},{129,193},{193,1... | collective-permute-start | bytes 1572872 | tf_op jit(solution)/shard_map/ppermute | solution.py:40
  59.7 2.6 %collective-permute-start.8 = (bf16[2,512,256]{2,1,0:T(8,128)(2,1)S(1)}, bf16[2,512,256]{2,1,0:T(8,128)(2,1)}, u32[]{:S(2)}, u32[]{:S(2)}) collective-permute-start(bf16[2,512,256]{2,1,0:T(8,128)(2,1)S(1)} %pad_maximum_fusion.3), channel_id=1, source_target_pairs={{0,128},{64,192},{128,0},{192,64},{1,129},{65,193},{129,1},{193,65... | collective-permute-start | bytes 1572872 | tf_op jit(solution)/shard_map/ppermute | solution.py:40
  62.3 3.7 %collective-permute-start.9 = (bf16[2,512,256]{2,1,0:T(8,128)(2,1)S(1)}, bf16[2,512,256]{2,1,0:T(8,128)(2,1)}, u32[]{:S(2)}, u32[]{:S(2)}) collective-permute-start(bf16[2,512,256]{2,1,0:T(8,128)(2,1)S(1)} %pad_maximum_fusion.3), channel_id=1, source_target_pairs={{0,192},{64,0},{128,64},{192,128},{1,193},{65,1},{129,65},{193,129... | collective-permute-start | bytes 1572872 | tf_op jit(solution)/shard_map/ppermute | solution.py:40
  66.0 0.1 pad_add_fusion.at_ref
  66.1 0.0 collective-permute-done.10.other_ref
  66.1 12.5 %all-gather.3.cloned.1.call-done = bf16[32,128,256]{2,1,0:T(8,128)(2,1)} async-done(((bf16[2,128,256]{2,1,0:T(8,128)(2,1)}), bf16[32,128,256]{2,1,0:T(8,128)(2,1)}) %all-gather.3.cloned.1.call-update) | async-done | bytes 2097168 | tf_op jit(solution)/shard_map/all_gather | solution.py:129
  78.5 0.0 copy-start
  78.6 1.6 copy-done
  80.1 2.4 %shard_map.46 = (f32[128,256]{1,0:T(8,128)S(1)}, f32[128,256]{1,0:T(8,128)S(1)}) custom-call(s32[3]{0:T(128)S(1)} %pad_add_fusion.at_ref, bf16[16,2,128,256]{3,2,1,0:T(8,128)(2,1)S(1)} %bitcast.23, bf16[4,2,512,256]{3,2,1,0:T(8,128)(2,1)S(1)} %pad_maximum_fusion.own_ref, bf16[4,2,512,256]{3,2,1,0:T(8,128)(2,1)} %collective-permute-done.10.other_ref), custom_call_target="tpu_custom_call" | custom-call | tf_op jit(solution)/shard_map/pallas_call | solution.py:84
  82.5 2.9 %collective-permute-start.11 = (f32[128,256]{1,0:T(8,128)S(1)}, f32[128,256]{1,0:T(8,128)S(1)}, u32[]{:S(2)}, u32[]{:S(2)}) collective-permute-start(f32[128,256]{1,0:T(8,128)S(1)} %get-tuple-element.38), channel_id=1, source_target_pairs={{0,16},{16,0},{1,17},{17,1},{2,18},{18,2},{3,19},{19,3},{4,20},{20... | collective-permute-start | bytes 393224 | tf_op jit(solution)/shard_map/ppermute | solution.py:40
  85.4 2.9 %collective-permute-done.11 = f32[128,256]{1,0:T(8,128)S(1)} collective-permute-done((f32[128,256]{1,0:T(8,128)S(1)}, f32[128,256]{1,0:T(8,128)S(1)}, u32[]{:S(2)}, u32[]{:S(2)}) %collective-permute-start.11) | collective-permute-done | bytes 131104 | tf_op jit(solution)/shard_map/ppermute | solution.py:40
  88.4 0.0 collective-permute-done.7
  88.4 0.0 collective-permute-done.8
  88.4 0.0 collective-permute-done.9
  88.4 1.5 pad_maximum_fusion.1.own_ref
  89.9 12.3 %collective-permute-start.13 = (bf16[4,2,512,256]{3,2,1,0:T(8,128)(2,1)S(1)}, bf16[4,2,512,256]{3,2,1,0:T(8,128)(2,1)S(1)}, u32[]{:S(2)}, u32[]{:S(2)}) collective-permute-start(bf16[4,2,512,256]{3,2,1,0:T(8,128)(2,1)S(1)} %pad_maximum_fusion.1.own_ref), channel_id=1, source_target_pairs={{0,32},{32,0},{1,33},{33,1},{2,34},{34,2},{3,35},{35,3},{4,36},{36... | collective-permute-start | bytes 6291464 | tf_op jit(solution)/shard_map/ppermute | solution.py:40
  102.1 5.9 %collective-permute-start.12 = (bf16[128,256]{1,0:T(8,128)(2,1)S(1)}, bf16[128,256]{1,0:T(8,128)(2,1)S(1)}, u32[]{:S(2)}, u32[]{:S(2)}) collective-permute-start(bf16[128,256]{1,0:T(8,128)(2,1)S(1)} %multiply_convert_fusion.1), channel_id=1, source_target_pairs={{0,0},{1,1},{2,32},{3,33},{4,64},{5,65},{6,96},{7,97},{8,128},{9,1... | collective-permute-start | bytes 196616 | tf_op jit(solution)/shard_map/ppermute | solution.py:40
  108.1 0.0 collective-permute-done.13.other_ref
  108.1 1.3 shard_map.47
  109.4 6.6 %collective-permute-done.12 = bf16[128,256]{1,0:T(8,128)(2,1)S(1)} collective-permute-done((bf16[128,256]{1,0:T(8,128)(2,1)S(1)}, bf16[128,256]{1,0:T(8,128)(2,1)S(1)}, u32[]{:S(2)}, u32[]{:S(2)}) %collective-permute-start.12) | collective-permute-done | bytes 65568 | tf_op jit(solution)/shard_map/ppermute | solution.py:40
  116.0 1.1 broadcast_in_dim.2
  117.1 9.6 %all-to-all-start = ((bf16[16,128,256]{2,1,0:T(8,128)(2,1)}), bf16[16,128,256]{2,1,0:T(8,128)(2,1)S(1)}, u32[]{:S(2)}, u32[]{:S(2)}) async-start(bf16[16,128,256]{2,1,0:T(8,128)(2,1)} %broadcast_in_dim.2), calls=%async_computation | async-start | bytes 2097152 | tf_op jit(solution)/shard_map/all_to_all | solution.py:18
  126.7 2.3 %collective-permute-start.14 = (f32[2,128,256]{2,1,0:T(8,128)S(1)}, f32[2,128,256]{2,1,0:T(8,128)S(1)}, u32[]{:S(2)}, u32[]{:S(2)}) collective-permute-start(f32[2,128,256]{2,1,0:T(8,128)S(1)} %get-tuple-element.46), channel_id=1, source_target_pairs={{0,0},{16,256},{256,16},{272,272},{1,1},{17,257},{257,17},{273,273... | collective-permute-start | bytes 786440 | tf_op jit(solution)/shard_map/ppermute | solution.py:40
  129.1 1.9 collective-permute-start.15
  131.0 11.0 %collective-permute-done.14 = f32[2,128,256]{2,1,0:T(8,128)S(1)} collective-permute-done((f32[2,128,256]{2,1,0:T(8,128)S(1)}, f32[2,128,256]{2,1,0:T(8,128)S(1)}, u32[]{:S(2)}, u32[]{:S(2)}) %collective-permute-start.14) | collective-permute-done | bytes 262176 | tf_op jit(solution)/shard_map/ppermute | solution.py:40
  142.0 0.0 collective-permute-done.15
  142.1 1.9 collective-permute-start.16
  144.0 1.9 collective-permute-start.17
  145.9 3.4 %collective-permute-start.18 = (bf16[2,128,256]{2,1,0:T(8,128)(2,1)S(1)}, bf16[2,128,256]{2,1,0:T(8,128)(2,1)S(1)}, u32[]{:S(2)}, u32[]{:S(2)}) collective-permute-start(bf16[2,128,256]{2,1,0:T(8,128)(2,1)S(1)} %multiply_convert_fusion), channel_id=1, source_target_pairs={{0,192},{64,0},{128,64},{192,128},{1,193},{65,1},{129,65},{193,129... | collective-permute-start | bytes 393224 | tf_op jit(solution)/shard_map/ppermute | solution.py:40
  149.3 0.0 collective-permute-done.16
  149.3 2.6 %collective-permute-done.17 = bf16[2,128,256]{2,1,0:T(8,128)(2,1)S(1)} collective-permute-done((bf16[2,128,256]{2,1,0:T(8,128)(2,1)S(1)}, bf16[2,128,256]{2,1,0:T(8,128)(2,1)S(1)}, u32[]{:S(2)}, u32[]{:S(2)}) %collective-permute-start.17) | collective-permute-done | bytes 131104 | tf_op jit(solution)/shard_map/ppermute | solution.py:40
  151.9 2.2 %collective-permute-done.18 = bf16[2,128,256]{2,1,0:T(8,128)(2,1)S(1)} collective-permute-done((bf16[2,128,256]{2,1,0:T(8,128)(2,1)S(1)}, bf16[2,128,256]{2,1,0:T(8,128)(2,1)S(1)}, u32[]{:S(2)}, u32[]{:S(2)}) %collective-permute-start.18) | collective-permute-done | bytes 131104 | tf_op jit(solution)/shard_map/ppermute | solution.py:40
  154.1 0.1 pad_maximum_fusion.4.own_ref
  154.2 4.7 %collective-permute-start.19 = (bf16[4,2,128,256]{3,2,1,0:T(8,128)(2,1)S(1)}, bf16[4,2,128,256]{3,2,1,0:T(8,128)(2,1)S(1)}, u32[]{:S(2)}, u32[]{:S(2)}) collective-permute-start(bf16[4,2,128,256]{3,2,1,0:T(8,128)(2,1)S(1)} %pad_maximum_fusion.4.own_ref), channel_id=1, source_target_pairs={{0,32},{32,0},{1,33},{33,1},{2,34},{34,2},{3,35},{35,3},{4,36},{36... | collective-permute-start | bytes 1572872 | tf_op jit(solution)/shard_map/ppermute | solution.py:40
  158.8 0.1 pad_add_fusion.2.at_ref
  158.9 1.4 collective-permute-done.19.other_ref
  160.3 16.1 %all-to-all-done.s_ref = bf16[16,128,256]{2,1,0:T(8,128)(2,1)S(1)} async-done(((bf16[16,128,256]{2,1,0:T(8,128)(2,1)}), bf16[16,128,256]{2,1,0:T(8,128)(2,1)S(1)}, u32[]{:S(2)}, u32[]{:S(2)}) %all-to-all-start) | async-done | bytes 1048608 | tf_op jit(solution)/shard_map/all_to_all | solution.py:18
  176.4 1.3 shard_map.49
  177.7 1.9 collective-permute-start.20
  179.6 1.3 shard_map.48
  180.9 12.0 %collective-permute-done.20 = f32[256,512]{1,0:T(8,128)S(1)} collective-permute-done((f32[256,512]{1,0:T(8,128)S(1)}, f32[256,512]{1,0:T(8,128)S(1)}, u32[]{:S(2)}, u32[]{:S(2)}) %collective-permute-start.20) | collective-permute-done | bytes 524320 | tf_op jit(solution)/shard_map/ppermute | solution.py:40
  192.9 0.9 add_multiply_fusion
  (2 shorter events, 0.1 us)
Async XLA Ops:
  6.5 72.0 %all-gather.3.cloned.1.call-start = ((), (), s32[]{:S(2)}) async-start(), calls=%async_computation.1 | async-start | bytes 2228224 | tf_op jit(solution)/shard_map/all_gather | solution.py:129
  8.1 14.9 %collective-permute-start = (bf16[512,256]{1,0:T(8,128)(2,1)}, bf16[512,256]{1,0:T(8,128)(2,1)S(1)}, u32[]{:S(2)}, u32[]{:S(2)}) collective-permute-start(bf16[512,256]{1,0:T(8,128)(2,1)} %param.7), channel_id=1, source_target_pairs={{0,0},{16,256},{256,16},{272,272},{1,1},{17,257},{257,17},{273,273... | collective-permute-start | bytes 786440 | tf_op jit(solution)/shard_map/ppermute | solution.py:40
  10.3 12.7 %collective-permute-start.1 = (bf16[512,256]{1,0:T(8,128)(2,1)}, bf16[512,256]{1,0:T(8,128)(2,1)S(1)}, u32[]{:S(2)}, u32[]{:S(2)}) collective-permute-start(bf16[512,256]{1,0:T(8,128)(2,1)} %param.7), channel_id=1, source_target_pairs={{0,256},{16,0},{256,272},{272,16},{1,257},{17,1},{257,273},{273,17... | collective-permute-start | bytes 786440 | tf_op jit(solution)/shard_map/ppermute | solution.py:40
  23.1 21.0 %collective-permute-start.2 = (bf16[2,512,256]{2,1,0:T(8,128)(2,1)S(1)}, bf16[2,512,256]{2,1,0:T(8,128)(2,1)S(1)}, u32[]{:S(2)}, u32[]{:S(2)}) collective-permute-start(bf16[2,512,256]{2,1,0:T(8,128)(2,1)S(1)} %pad_maximum_fusion.2), channel_id=1, source_target_pairs={{0,64},{64,128},{128,192},{192,0},{1,65},{65,129},{129,193},{193,1... | collective-permute-start | bytes 1572872 | tf_op jit(solution)/shard_map/ppermute | solution.py:40
  26.3 17.8 %collective-permute-start.3 = (bf16[2,512,256]{2,1,0:T(8,128)(2,1)S(1)}, bf16[2,512,256]{2,1,0:T(8,128)(2,1)S(1)}, u32[]{:S(2)}, u32[]{:S(2)}) collective-permute-start(bf16[2,512,256]{2,1,0:T(8,128)(2,1)S(1)} %pad_maximum_fusion.2), channel_id=1, source_target_pairs={{0,128},{64,192},{128,0},{192,64},{1,129},{65,193},{129,1},{193,65... | collective-permute-start | bytes 1572872 | tf_op jit(solution)/shard_map/ppermute | solution.py:40
  28.9 25.9 %collective-permute-start.4 = (bf16[2,512,256]{2,1,0:T(8,128)(2,1)S(1)}, bf16[2,512,256]{2,1,0:T(8,128)(2,1)S(1)}, u32[]{:S(2)}, u32[]{:S(2)}) collective-permute-start(bf16[2,512,256]{2,1,0:T(8,128)(2,1)S(1)} %pad_maximum_fusion.2), channel_id=1, source_target_pairs={{0,192},{64,0},{128,64},{192,128},{1,193},{65,1},{129,65},{193,129... | collective-permute-start | bytes 1572872 | tf_op jit(solution)/shard_map/ppermute | solution.py:40
  32.9 7.6 %collective-permute-start.5 = (bf16[512,256]{1,0:T(8,128)(2,1)}, bf16[512,256]{1,0:T(8,128)(2,1)S(1)}, u32[]{:S(2)}, u32[]{:S(2)}) collective-permute-start(bf16[512,256]{1,0:T(8,128)(2,1)} %param.6), channel_id=1, source_target_pairs={{0,0},{16,256},{256,16},{272,272},{1,1},{17,257},{257,17},{273,273... | collective-permute-start | bytes 786440 | tf_op jit(solution)/shard_map/ppermute | solution.py:40
  34.8 9.2 %collective-permute-start.6 = (bf16[512,256]{1,0:T(8,128)(2,1)}, bf16[512,256]{1,0:T(8,128)(2,1)S(1)}, u32[]{:S(2)}, u32[]{:S(2)}) collective-permute-start(bf16[512,256]{1,0:T(8,128)(2,1)} %param.6), channel_id=1, source_target_pairs={{0,256},{16,0},{256,272},{272,16},{1,257},{17,1},{257,273},{273,17... | collective-permute-start | bytes 786440 | tf_op jit(solution)/shard_map/ppermute | solution.py:40
  55.1 11.0 %collective-permute-start.10 = (bf16[4,2,512,256]{3,2,1,0:T(8,128)(2,1)S(1)}, bf16[4,2,512,256]{3,2,1,0:T(8,128)(2,1)}, u32[]{:S(2)}, u32[]{:S(2)}) collective-permute-start(bf16[4,2,512,256]{3,2,1,0:T(8,128)(2,1)S(1)} %pad_maximum_fusion.own_ref), channel_id=1, source_target_pairs={{0,32},{32,0},{1,33},{33,1},{2,34},{34,2},{3,35},{35,3},{4,36},{36... | collective-permute-start | bytes 6291464 | tf_op jit(solution)/shard_map/ppermute | solution.py:40
  57.4 31.0 %collective-permute-start.7 = (bf16[2,512,256]{2,1,0:T(8,128)(2,1)S(1)}, bf16[2,512,256]{2,1,0:T(8,128)(2,1)S(1)}, u32[]{:S(2)}, u32[]{:S(2)}) collective-permute-start(bf16[2,512,256]{2,1,0:T(8,128)(2,1)S(1)} %pad_maximum_fusion.3), channel_id=1, source_target_pairs={{0,64},{64,128},{128,192},{192,0},{1,65},{65,129},{129,193},{193,1... | collective-permute-start | bytes 1572872 | tf_op jit(solution)/shard_map/ppermute | solution.py:40
  59.7 28.7 %collective-permute-start.8 = (bf16[2,512,256]{2,1,0:T(8,128)(2,1)S(1)}, bf16[2,512,256]{2,1,0:T(8,128)(2,1)}, u32[]{:S(2)}, u32[]{:S(2)}) collective-permute-start(bf16[2,512,256]{2,1,0:T(8,128)(2,1)S(1)} %pad_maximum_fusion.3), channel_id=1, source_target_pairs={{0,128},{64,192},{128,0},{192,64},{1,129},{65,193},{129,1},{193,65... | collective-permute-start | bytes 1572872 | tf_op jit(solution)/shard_map/ppermute | solution.py:40
  62.3 26.1 %collective-permute-start.9 = (bf16[2,512,256]{2,1,0:T(8,128)(2,1)S(1)}, bf16[2,512,256]{2,1,0:T(8,128)(2,1)}, u32[]{:S(2)}, u32[]{:S(2)}) collective-permute-start(bf16[2,512,256]{2,1,0:T(8,128)(2,1)S(1)} %pad_maximum_fusion.3), channel_id=1, source_target_pairs={{0,192},{64,0},{128,64},{192,128},{1,193},{65,1},{129,65},{193,129... | collective-permute-start | bytes 1572872 | tf_op jit(solution)/shard_map/ppermute | solution.py:40
  78.5 1.6 copy-start
  82.5 5.8 %collective-permute-start.11 = (f32[128,256]{1,0:T(8,128)S(1)}, f32[128,256]{1,0:T(8,128)S(1)}, u32[]{:S(2)}, u32[]{:S(2)}) collective-permute-start(f32[128,256]{1,0:T(8,128)S(1)} %get-tuple-element.38), channel_id=1, source_target_pairs={{0,16},{16,0},{1,17},{17,1},{2,18},{18,2},{3,19},{19,3},{4,20},{20... | collective-permute-start | bytes 393224 | tf_op jit(solution)/shard_map/ppermute | solution.py:40
  89.9 18.2 %collective-permute-start.13 = (bf16[4,2,512,256]{3,2,1,0:T(8,128)(2,1)S(1)}, bf16[4,2,512,256]{3,2,1,0:T(8,128)(2,1)S(1)}, u32[]{:S(2)}, u32[]{:S(2)}) collective-permute-start(bf16[4,2,512,256]{3,2,1,0:T(8,128)(2,1)S(1)} %pad_maximum_fusion.1.own_ref), channel_id=1, source_target_pairs={{0,32},{32,0},{1,33},{33,1},{2,34},{34,2},{3,35},{35,3},{4,36},{36... | collective-permute-start | bytes 6291464 | tf_op jit(solution)/shard_map/ppermute | solution.py:40
  102.1 13.9 %collective-permute-start.12 = (bf16[128,256]{1,0:T(8,128)(2,1)S(1)}, bf16[128,256]{1,0:T(8,128)(2,1)S(1)}, u32[]{:S(2)}, u32[]{:S(2)}) collective-permute-start(bf16[128,256]{1,0:T(8,128)(2,1)S(1)} %multiply_convert_fusion.1), channel_id=1, source_target_pairs={{0,0},{1,1},{2,32},{3,33},{4,64},{5,65},{6,96},{7,97},{8,128},{9,1... | collective-permute-start | bytes 196616 | tf_op jit(solution)/shard_map/ppermute | solution.py:40
  117.1 59.3 %all-to-all-start = ((bf16[16,128,256]{2,1,0:T(8,128)(2,1)}), bf16[16,128,256]{2,1,0:T(8,128)(2,1)S(1)}, u32[]{:S(2)}, u32[]{:S(2)}) async-start(bf16[16,128,256]{2,1,0:T(8,128)(2,1)} %broadcast_in_dim.2), calls=%async_computation | async-start | bytes 2097152 | tf_op jit(solution)/shard_map/all_to_all | solution.py:18
  126.7 15.3 %collective-permute-start.14 = (f32[2,128,256]{2,1,0:T(8,128)S(1)}, f32[2,128,256]{2,1,0:T(8,128)S(1)}, u32[]{:S(2)}, u32[]{:S(2)}) collective-permute-start(f32[2,128,256]{2,1,0:T(8,128)S(1)} %get-tuple-element.46), channel_id=1, source_target_pairs={{0,0},{16,256},{256,16},{272,272},{1,1},{17,257},{257,17},{273,273... | collective-permute-start | bytes 786440 | tf_op jit(solution)/shard_map/ppermute | solution.py:40
  129.1 12.9 %collective-permute-start.15 = (f32[2,128,256]{2,1,0:T(8,128)S(1)}, f32[2,128,256]{2,1,0:T(8,128)S(1)}, u32[]{:S(2)}, u32[]{:S(2)}) collective-permute-start(f32[2,128,256]{2,1,0:T(8,128)S(1)} %get-tuple-element.47), channel_id=1, source_target_pairs={{0,256},{16,0},{256,272},{272,16},{1,257},{17,1},{257,273},{273,17... | collective-permute-start | bytes 786440 | tf_op jit(solution)/shard_map/ppermute | solution.py:40
  142.1 7.2 %collective-permute-start.16 = (bf16[2,128,256]{2,1,0:T(8,128)(2,1)S(1)}, bf16[2,128,256]{2,1,0:T(8,128)(2,1)S(1)}, u32[]{:S(2)}, u32[]{:S(2)}) collective-permute-start(bf16[2,128,256]{2,1,0:T(8,128)(2,1)S(1)} %multiply_convert_fusion), channel_id=1, source_target_pairs={{0,64},{64,128},{128,192},{192,0},{1,65},{65,129},{129,193},{193,1... | collective-permute-start | bytes 393224 | tf_op jit(solution)/shard_map/ppermute | solution.py:40
  144.0 7.9 %collective-permute-start.17 = (bf16[2,128,256]{2,1,0:T(8,128)(2,1)S(1)}, bf16[2,128,256]{2,1,0:T(8,128)(2,1)S(1)}, u32[]{:S(2)}, u32[]{:S(2)}) collective-permute-start(bf16[2,128,256]{2,1,0:T(8,128)(2,1)S(1)} %multiply_convert_fusion), channel_id=1, source_target_pairs={{0,128},{64,192},{128,0},{192,64},{1,129},{65,193},{129,1},{193,65... | collective-permute-start | bytes 393224 | tf_op jit(solution)/shard_map/ppermute | solution.py:40
  145.9 8.2 %collective-permute-start.18 = (bf16[2,128,256]{2,1,0:T(8,128)(2,1)S(1)}, bf16[2,128,256]{2,1,0:T(8,128)(2,1)S(1)}, u32[]{:S(2)}, u32[]{:S(2)}) collective-permute-start(bf16[2,128,256]{2,1,0:T(8,128)(2,1)S(1)} %multiply_convert_fusion), channel_id=1, source_target_pairs={{0,192},{64,0},{128,64},{192,128},{1,193},{65,1},{129,65},{193,129... | collective-permute-start | bytes 393224 | tf_op jit(solution)/shard_map/ppermute | solution.py:40
  154.2 6.2 %collective-permute-start.19 = (bf16[4,2,128,256]{3,2,1,0:T(8,128)(2,1)S(1)}, bf16[4,2,128,256]{3,2,1,0:T(8,128)(2,1)S(1)}, u32[]{:S(2)}, u32[]{:S(2)}) collective-permute-start(bf16[4,2,128,256]{3,2,1,0:T(8,128)(2,1)S(1)} %pad_maximum_fusion.4.own_ref), channel_id=1, source_target_pairs={{0,32},{32,0},{1,33},{33,1},{2,34},{34,2},{3,35},{35,3},{4,36},{36... | collective-permute-start | bytes 1572872 | tf_op jit(solution)/shard_map/ppermute | solution.py:40
  177.7 15.2 %collective-permute-start.20 = (f32[256,512]{1,0:T(8,128)S(1)}, f32[256,512]{1,0:T(8,128)S(1)}, u32[]{:S(2)}, u32[]{:S(2)}) collective-permute-start(f32[256,512]{1,0:T(8,128)S(1)} %shard_map.49), channel_id=1, source_target_pairs={{0,16},{16,0},{1,17},{17,1},{2,18},{18,2},{3,19},{19,3},{4,20},{20... | collective-permute-start | bytes 1572872 | tf_op jit(solution)/shard_map/ppermute | solution.py:40
Sparse Core Ops, SparseCore 0:
  9.4 69.0 all-gather.2

commit v7 on v6

--- a/solution.py
+++ b/solution.py
@@ -70,10 +70,10 @@
     for h in range(2):
         acc = jnp.zeros((256, 256), jnp.float32)
         for j in range(4):
-            at = 4 * lax.rem(y + 4 - j, 4) + h
+            at = lax.rem(y + 4 - j, 4) + 4 * h
             for act, core in ((own_ref, c), (other_ref, 1 - c)):
                 acc += lax.dot_general(
-                    act[j, k], s_ref[at + 2 * core],
+                    act[j, k], s_ref[at + 8 * core],
                     (((0,), (0,)), ((), ())), preferred_element_type=jnp.float32,
                 )
         out_ref[:, 256 * h:256 * h + 256] = acc
@@ -144,7 +144,7 @@
 
     parts = rotate(at, every, 0, both_cores(act_shifts), 1)
     grad_square, parts = lax.optimization_barrier((grad_square, parts))
-    grad_block = to_all(grad_square, ("zh", "zl"), 16)
+    grad_block = to_all(to_all(grad_square, ("zh",), 4), ("zl",), 4).reshape(16, 128, 256)
     parts = [move(parts[k], ("xh", "xl"), lambda a, p, k=k: (p ^ k, a)) for k in range(2)]
     rotated_act = parts[0] + parts[1]
     act_square = (rotated_act * rotated_act).astype(jnp.bfloat16)

time: 202 us -> 211 us (1.045)
  the two profiles are of different devices: /device:TPU:13 before, /device:TPU:1 now
where the time goes in v7:
time: 211 us; the launch traced here: 210 us
  starting transfers between devices  95.7 us (45%)
  waiting for transfers between devices  55.1 us (26%)
  blocking collectives  31.8 us (15%)
  between operations  13.7 us (6%)
  Pallas kernels  6.19 us (3%)
  other arithmetic  4.53 us (2%)
  local copies, waits for them, and re-layouts  2.73 us (1%)
    ppermute x21, starting transfers between devices, move(): return lax.ppermute(x, axes, pairs)  87.7 us
    ppermute x21, waiting for transfers between devices, move(): return lax.ppermute(x, axes, pairs)  40.8 us
    all_to_all x1, blocking collectives, to_all(): return lax.all_to_all(spread, axes, split_axis=0, concat_axis=0, tiled=True)  31.8 us
    all_gather x1, waiting for transfers between devices, on_device(): every = lax.all_gather(both, ('zh', 'zl'), axis=0, tiled=False)  14.3 us
    all_to_all x1, starting transfers between devices, to_all(): return lax.all_to_all(spread, axes, split_axis=0, concat_axis=0, tiled=True)  7.99 us
  transfers between devices with their start and end apart: 23, of which 13 were waited for; matrix products, arithmetic and copies ran while one was open for 0% of the time, Pallas kernels for 2%

profile of v7, /device:TPU:1, one launch (start us, length us, event | category | flops | bytes accessed | tf_op | source)
XLA Modules:
  0.0 209.7 jit_solution(11776524616403769312)
XLA Ops:
  6.5 0.0 all-gather.3.cloned.1.call-start
  6.5 1.5 pad_maximum_fusion.5
  8.1 0.0 all-gather.3.cloned.1.call-update
  8.1 1.6 collective-permute-start
  9.7 6.0 %collective-permute-start.1 = (bf16[512,256]{1,0:T(8,128)(2,1)}, bf16[512,256]{1,0:T(8,128)(2,1)S(1)}, u32[]{:S(2)}, u32[]{:S(2)}) collective-permute-start(bf16[512,256]{1,0:T(8,128)(2,1)} %param.7), channel_id=1, source_target_pairs={{0,256},{16,0},{256,272},{272,16},{1,257},{17,1},{257,273},{273,17... | collective-permute-start | bytes 786440 | tf_op jit(solution)/shard_map/ppermute | solution.py:40
  15.8 0.0 collective-permute-done
  15.8 3.6 %collective-permute-done.1 = bf16[512,256]{1,0:T(8,128)(2,1)S(1)} collective-permute-done((bf16[512,256]{1,0:T(8,128)(2,1)}, bf16[512,256]{1,0:T(8,128)(2,1)S(1)}, u32[]{:S(2)}, u32[]{:S(2)}) %collective-permute-start.1) | collective-permute-done | bytes 262176 | tf_op jit(solution)/shard_map/ppermute | solution.py:40
  19.4 0.1 pad_maximum_fusion.2
  19.5 4.9 %collective-permute-start.2 = (bf16[2,512,256]{2,1,0:T(8,128)(2,1)S(1)}, bf16[2,512,256]{2,1,0:T(8,128)(2,1)S(1)}, u32[]{:S(2)}, u32[]{:S(2)}) collective-permute-start(bf16[2,512,256]{2,1,0:T(8,128)(2,1)S(1)} %pad_maximum_fusion.2), channel_id=1, source_target_pairs={{0,64},{64,128},{128,192},{192,0},{1,65},{65,129},{129,193},{193,1... | collective-permute-start | bytes 1572872 | tf_op jit(solution)/shard_map/ppermute | solution.py:40
  24.4 4.5 %collective-permute-start.3 = (bf16[2,512,256]{2,1,0:T(8,128)(2,1)S(1)}, bf16[2,512,256]{2,1,0:T(8,128)(2,1)S(1)}, u32[]{:S(2)}, u32[]{:S(2)}) collective-permute-start(bf16[2,512,256]{2,1,0:T(8,128)(2,1)S(1)} %pad_maximum_fusion.2), channel_id=1, source_target_pairs={{0,128},{64,192},{128,0},{192,64},{1,129},{65,193},{129,1},{193,65... | collective-permute-start | bytes 1572872 | tf_op jit(solution)/shard_map/ppermute | solution.py:40
  28.9 3.0 %collective-permute-start.4 = (bf16[2,512,256]{2,1,0:T(8,128)(2,1)S(1)}, bf16[2,512,256]{2,1,0:T(8,128)(2,1)S(1)}, u32[]{:S(2)}, u32[]{:S(2)}) collective-permute-start(bf16[2,512,256]{2,1,0:T(8,128)(2,1)S(1)} %pad_maximum_fusion.2), channel_id=1, source_target_pairs={{0,192},{64,0},{128,64},{192,128},{1,193},{65,1},{129,65},{193,129... | collective-permute-start | bytes 1572872 | tf_op jit(solution)/shard_map/ppermute | solution.py:40
  31.9 1.6 collective-permute-start.5
  33.5 7.7 %collective-permute-start.6 = (bf16[512,256]{1,0:T(8,128)(2,1)}, bf16[512,256]{1,0:T(8,128)(2,1)S(1)}, u32[]{:S(2)}, u32[]{:S(2)}) collective-permute-start(bf16[512,256]{1,0:T(8,128)(2,1)} %param.6), channel_id=1, source_target_pairs={{0,256},{16,0},{256,272},{272,16},{1,257},{17,1},{257,273},{273,17... | collective-permute-start | bytes 786440 | tf_op jit(solution)/shard_map/ppermute | solution.py:40
  41.2 0.0 collective-permute-done.5
  41.2 3.9 %collective-permute-done.6 = bf16[512,256]{1,0:T(8,128)(2,1)S(1)} collective-permute-done((bf16[512,256]{1,0:T(8,128)(2,1)}, bf16[512,256]{1,0:T(8,128)(2,1)S(1)}, u32[]{:S(2)}, u32[]{:S(2)}) %collective-permute-start.6) | collective-permute-done | bytes 262176 | tf_op jit(solution)/shard_map/ppermute | solution.py:40
  45.1 0.1 pad_maximum_fusion.3
  45.2 0.0 collective-permute-done.2
  45.2 3.4 %collective-permute-done.3 = bf16[2,512,256]{2,1,0:T(8,128)(2,1)S(1)} collective-permute-done((bf16[2,512,256]{2,1,0:T(8,128)(2,1)S(1)}, bf16[2,512,256]{2,1,0:T(8,128)(2,1)S(1)}, u32[]{:S(2)}, u32[]{:S(2)}) %collective-permute-start.3) | collective-permute-done | bytes 524320 | tf_op jit(solution)/shard_map/ppermute | solution.py:40
  48.6 2.3 %collective-permute-done.4 = bf16[2,512,256]{2,1,0:T(8,128)(2,1)S(1)} collective-permute-done((bf16[2,512,256]{2,1,0:T(8,128)(2,1)S(1)}, bf16[2,512,256]{2,1,0:T(8,128)(2,1)S(1)}, u32[]{:S(2)}, u32[]{:S(2)}) %collective-permute-start.4) | collective-permute-done | bytes 524320 | tf_op jit(solution)/shard_map/ppermute | solution.py:40
  50.9 0.3 pad_maximum_fusion.own_ref
  51.1 3.5 %collective-permute-start.10 = (bf16[4,2,512,256]{3,2,1,0:T(8,128)(2,1)S(1)}, bf16[4,2,512,256]{3,2,1,0:T(8,128)(2,1)}, u32[]{:S(2)}, u32[]{:S(2)}) collective-permute-start(bf16[4,2,512,256]{3,2,1,0:T(8,128)(2,1)S(1)} %pad_maximum_fusion.own_ref), channel_id=1, source_target_pairs={{0,32},{32,0},{1,33},{33,1},{2,34},{34,2},{3,35},{35,3},{4,36},{36... | collective-permute-start | bytes 6291464 | tf_op jit(solution)/shard_map/ppermute | solution.py:40
  54.6 4.1 %collective-permute-start.7 = (bf16[2,512,256]{2,1,0:T(8,128)(2,1)S(1)}, bf16[2,512,256]{2,1,0:T(8,128)(2,1)S(1)}, u32[]{:S(2)}, u32[]{:S(2)}) collective-permute-start(bf16[2,512,256]{2,1,0:T(8,128)(2,1)S(1)} %pad_maximum_fusion.3), channel_id=1, source_target_pairs={{0,64},{64,128},{128,192},{192,0},{1,65},{65,129},{129,193},{193,1... | collective-permute-start | bytes 1572872 | tf_op jit(solution)/shard_map/ppermute | solution.py:40
  58.7 3.2 %collective-permute-start.8 = (bf16[2,512,256]{2,1,0:T(8,128)(2,1)S(1)}, bf16[2,512,256]{2,1,0:T(8,128)(2,1)}, u32[]{:S(2)}, u32[]{:S(2)}) collective-permute-start(bf16[2,512,256]{2,1,0:T(8,128)(2,1)S(1)} %pad_maximum_fusion.3), channel_id=1, source_target_pairs={{0,128},{64,192},{128,0},{192,64},{1,129},{65,193},{129,1},{193,65... | collective-permute-start | bytes 1572872 | tf_op jit(solution)/shard_map/ppermute | solution.py:40
  62.0 3.3 %collective-permute-start.9 = (bf16[2,512,256]{2,1,0:T(8,128)(2,1)S(1)}, bf16[2,512,256]{2,1,0:T(8,128)(2,1)}, u32[]{:S(2)}, u32[]{:S(2)}) collective-permute-start(bf16[2,512,256]{2,1,0:T(8,128)(2,1)S(1)} %pad_maximum_fusion.3), channel_id=1, source_target_pairs={{0,192},{64,0},{128,64},{192,128},{1,193},{65,1},{129,65},{193,129... | collective-permute-start | bytes 1572872 | tf_op jit(solution)/shard_map/ppermute | solution.py:40
  65.3 0.1 pad_add_fusion.at_ref
  65.4 0.0 collective-permute-done.10.other_ref
  65.4 14.3 %all-gather.3.cloned.1.call-done = bf16[32,128,256]{2,1,0:T(8,128)(2,1)} async-done(((bf16[2,128,256]{2,1,0:T(8,128)(2,1)}), bf16[32,128,256]{2,1,0:T(8,128)(2,1)}) %all-gather.3.cloned.1.call-update) | async-done | bytes 2097168 | tf_op jit(solution)/shard_map/all_gather | solution.py:129
  79.7 0.0 copy-start
  79.7 1.6 copy-done
  81.3 2.4 %shard_map.46 = (f32[128,256]{1,0:T(8,128)S(1)}, f32[128,256]{1,0:T(8,128)S(1)}) custom-call(s32[3]{0:T(128)S(1)} %pad_add_fusion.at_ref, bf16[16,2,128,256]{3,2,1,0:T(8,128)(2,1)S(1)} %bitcast.26, bf16[4,2,512,256]{3,2,1,0:T(8,128)(2,1)S(1)} %pad_maximum_fusion.own_ref, bf16[4,2,512,256]{3,2,1,0:T(8,128)(2,1)} %collective-permute-done.10.other_ref), custom_call_target="tpu_custom_call" | custom-call | tf_op jit(solution)/shard_map/pallas_call | solution.py:84
  83.7 3.0 %collective-permute-start.11 = (f32[128,256]{1,0:T(8,128)S(1)}, f32[128,256]{1,0:T(8,128)S(1)}, u32[]{:S(2)}, u32[]{:S(2)}) collective-permute-start(f32[128,256]{1,0:T(8,128)S(1)} %get-tuple-element.38), channel_id=1, source_target_pairs={{0,16},{16,0},{1,17},{17,1},{2,18},{18,2},{3,19},{19,3},{4,20},{20... | collective-permute-start | bytes 393224 | tf_op jit(solution)/shard_map/ppermute | solution.py:40
  86.7 2.7 %collective-permute-done.11 = f32[128,256]{1,0:T(8,128)S(1)} collective-permute-done((f32[128,256]{1,0:T(8,128)S(1)}, f32[128,256]{1,0:T(8,128)S(1)}, u32[]{:S(2)}, u32[]{:S(2)}) %collective-permute-start.11) | collective-permute-done | bytes 131104 | tf_op jit(solution)/shard_map/ppermute | solution.py:40
  89.4 0.0 collective-permute-done.7
  89.4 0.0 collective-permute-done.8
  89.4 0.0 collective-permute-done.9
  89.4 1.5 pad_maximum_fusion.1.own_ref
  90.9 12.1 %collective-permute-start.13 = (bf16[4,2,512,256]{3,2,1,0:T(8,128)(2,1)S(1)}, bf16[4,2,512,256]{3,2,1,0:T(8,128)(2,1)S(1)}, u32[]{:S(2)}, u32[]{:S(2)}) collective-permute-start(bf16[4,2,512,256]{3,2,1,0:T(8,128)(2,1)S(1)} %pad_maximum_fusion.1.own_ref), channel_id=1, source_target_pairs={{0,32},{32,0},{1,33},{33,1},{2,34},{34,2},{3,35},{35,3},{4,36},{36... | collective-permute-start | bytes 6291464 | tf_op jit(solution)/shard_map/ppermute | solution.py:40
  103.0 2.9 %collective-permute-start.12 = (bf16[128,256]{1,0:T(8,128)(2,1)S(1)}, bf16[128,256]{1,0:T(8,128)(2,1)S(1)}, u32[]{:S(2)}, u32[]{:S(2)}) collective-permute-start(bf16[128,256]{1,0:T(8,128)(2,1)S(1)} %multiply_convert_fusion.1), channel_id=1, source_target_pairs={{0,0},{1,1},{2,32},{3,33},{4,64},{5,65},{6,96},{7,97},{8,128},{9,1... | collective-permute-start | bytes 196616 | tf_op jit(solution)/shard_map/ppermute | solution.py:40
  105.9 0.8 collective-permute-done.13.other_ref
  106.8 1.3 shard_map.47
  108.1 1.4 collective-permute-done.12
  109.5 31.8 %all_to_all.10 = bf16[4,128,256]{2,1,0:T(8,128)(2,1)S(1)} all-to-all(bf16[4,128,256]{2,1,0:T(8,128)(2,1)S(1)} %broadcast_in_dim.4), channel_id=1, replica_groups=mesh['xh'=2,'y'=4,'c'=2,'xl'=2,'zh'=4,'zl'=4] {'zh'}, dimensions={0} | all-to-all | bytes 524288 | tf_op jit(solution)/shard_map/all_to_all | solution.py:18
  141.3 1.1 broadcast_in_dim.5
  142.4 8.0 %all-to-all-start.1 = ((bf16[4,4,128,256]{3,2,1,0:T(8,128)(2,1)}), bf16[4,4,128,256]{3,2,1,0:T(8,128)(2,1)S(1)}, u32[]{:S(2)}, u32[]{:S(2)}) async-start(bf16[4,4,128,256]{3,2,1,0:T(8,128)(2,1)} %broadcast_in_dim.5), calls=%async_computation.1 | async-start | bytes 2097152 | tf_op jit(solution)/shard_map/all_to_all | solution.py:18
  150.4 0.7 collective-permute-start.14
  151.0 7.8 %collective-permute-start.15 = (f32[2,128,256]{2,1,0:T(8,128)S(1)}, f32[2,128,256]{2,1,0:T(8,128)S(1)}, u32[]{:S(2)}, u32[]{:S(2)}) collective-permute-start(f32[2,128,256]{2,1,0:T(8,128)S(1)} %get-tuple-element.47), channel_id=1, source_target_pairs={{0,256},{16,0},{256,272},{272,16},{1,257},{17,1},{257,273},{273,17... | collective-permute-start | bytes 786440 | tf_op jit(solution)/shard_map/ppermute | solution.py:40
  158.9 0.0 collective-permute-done.14
  158.9 5.9 %collective-permute-done.15 = f32[2,128,256]{2,1,0:T(8,128)S(1)} collective-permute-done((f32[2,128,256]{2,1,0:T(8,128)S(1)}, f32[2,128,256]{2,1,0:T(8,128)S(1)}, u32[]{:S(2)}, u32[]{:S(2)}) %collective-permute-start.15) | collective-permute-done | bytes 262176 | tf_op jit(solution)/shard_map/ppermute | solution.py:40
  164.9 1.9 collective-permute-start.16
  166.8 2.7 %collective-permute-start.17 = (bf16[2,128,256]{2,1,0:T(8,128)(2,1)S(1)}, bf16[2,128,256]{2,1,0:T(8,128)(2,1)S(1)}, u32[]{:S(2)}, u32[]{:S(2)}) collective-permute-start(bf16[2,128,256]{2,1,0:T(8,128)(2,1)S(1)} %multiply_convert_fusion), channel_id=1, source_target_pairs={{0,128},{64,192},{128,0},{192,64},{1,129},{65,193},{129,1},{193,65... | collective-permute-start | bytes 393224 | tf_op jit(solution)/shard_map/ppermute | solution.py:40
  169.5 3.8 %collective-permute-start.18 = (bf16[2,128,256]{2,1,0:T(8,128)(2,1)S(1)}, bf16[2,128,256]{2,1,0:T(8,128)(2,1)S(1)}, u32[]{:S(2)}, u32[]{:S(2)}) collective-permute-start(bf16[2,128,256]{2,1,0:T(8,128)(2,1)S(1)} %multiply_convert_fusion), channel_id=1, source_target_pairs={{0,192},{64,0},{128,64},{192,128},{1,193},{65,1},{129,65},{193,129... | collective-permute-start | bytes 393224 | tf_op jit(solution)/shard_map/ppermute | solution.py:40
  173.3 0.0 collective-permute-done.16
  173.3 1.4 collective-permute-done.17
  174.7 3.1 %collective-permute-done.18 = bf16[2,128,256]{2,1,0:T(8,128)(2,1)S(1)} collective-permute-done((bf16[2,128,256]{2,1,0:T(8,128)(2,1)S(1)}, bf16[2,128,256]{2,1,0:T(8,128)(2,1)S(1)}, u32[]{:S(2)}, u32[]{:S(2)}) %collective-permute-start.18) | collective-permute-done | bytes 131104 | tf_op jit(solution)/shard_map/ppermute | solution.py:40
  177.9 0.1 pad_maximum_fusion.4.own_ref
  177.9 3.2 %collective-permute-start.19 = (bf16[4,2,128,256]{3,2,1,0:T(8,128)(2,1)S(1)}, bf16[4,2,128,256]{3,2,1,0:T(8,128)(2,1)S(1)}, u32[]{:S(2)}, u32[]{:S(2)}) collective-permute-start(bf16[4,2,128,256]{3,2,1,0:T(8,128)(2,1)S(1)} %pad_maximum_fusion.4.own_ref), channel_id=1, source_target_pairs={{0,32},{32,0},{1,33},{33,1},{2,34},{34,2},{3,35},{35,3},{4,36},{36... | collective-permute-start | bytes 1572872 | tf_op jit(solution)/shard_map/ppermute | solution.py:40
  181.2 0.1 pad_add_fusion.2.at_ref
  181.3 1.4 collective-permute-done.19.other_ref
  182.7 0.0 all-to-all-done.1
  182.7 1.3 shard_map.49
  184.0 6.0 %collective-permute-start.20 = (f32[256,512]{1,0:T(8,128)S(1)}, f32[256,512]{1,0:T(8,128)S(1)}, u32[]{:S(2)}, u32[]{:S(2)}) collective-permute-start(f32[256,512]{1,0:T(8,128)S(1)} %shard_map.49), channel_id=1, source_target_pairs={{0,16},{16,0},{1,17},{17,1},{2,18},{18,2},{3,19},{19,3},{4,20},{20... | collective-permute-start | bytes 1572872 | tf_op jit(solution)/shard_map/ppermute | solution.py:40
  190.0 1.3 shard_map.48
  191.3 10.7 %collective-permute-done.20 = f32[256,512]{1,0:T(8,128)S(1)} collective-permute-done((f32[256,512]{1,0:T(8,128)S(1)}, f32[256,512]{1,0:T(8,128)S(1)}, u32[]{:S(2)}, u32[]{:S(2)}) %collective-permute-start.20) | collective-permute-done | bytes 524320 | tf_op jit(solution)/shard_map/ppermute | solution.py:40
  202.0 0.9 add_multiply_fusion
  (3 shorter events, 0.1 us)
Async XLA Ops:
  6.5 73.2 %all-gather.3.cloned.1.call-start = ((), (), s32[]{:S(2)}) async-start(), calls=%async_computation.2 | async-start | bytes 2228224 | tf_op jit(solution)/shard_map/all_gather | solution.py:129
  8.1 7.7 %collective-permute-start = (bf16[512,256]{1,0:T(8,128)(2,1)}, bf16[512,256]{1,0:T(8,128)(2,1)S(1)}, u32[]{:S(2)}, u32[]{:S(2)}) collective-permute-start(bf16[512,256]{1,0:T(8,128)(2,1)} %param.7), channel_id=1, source_target_pairs={{0,0},{16,256},{256,16},{272,272},{1,1},{17,257},{257,17},{273,273... | collective-permute-start | bytes 786440 | tf_op jit(solution)/shard_map/ppermute | solution.py:40
  9.7 9.7 %collective-permute-start.1 = (bf16[512,256]{1,0:T(8,128)(2,1)}, bf16[512,256]{1,0:T(8,128)(2,1)S(1)}, u32[]{:S(2)}, u32[]{:S(2)}) collective-permute-start(bf16[512,256]{1,0:T(8,128)(2,1)} %param.7), channel_id=1, source_target_pairs={{0,256},{16,0},{256,272},{272,16},{1,257},{17,1},{257,273},{273,17... | collective-permute-start | bytes 786440 | tf_op jit(solution)/shard_map/ppermute | solution.py:40
  19.5 25.7 %collective-permute-start.2 = (bf16[2,512,256]{2,1,0:T(8,128)(2,1)S(1)}, bf16[2,512,256]{2,1,0:T(8,128)(2,1)S(1)}, u32[]{:S(2)}, u32[]{:S(2)}) collective-permute-start(bf16[2,512,256]{2,1,0:T(8,128)(2,1)S(1)} %pad_maximum_fusion.2), channel_id=1, source_target_pairs={{0,64},{64,128},{128,192},{192,0},{1,65},{65,129},{129,193},{193,1... | collective-permute-start | bytes 1572872 | tf_op jit(solution)/shard_map/ppermute | solution.py:40
  24.4 24.2 %collective-permute-start.3 = (bf16[2,512,256]{2,1,0:T(8,128)(2,1)S(1)}, bf16[2,512,256]{2,1,0:T(8,128)(2,1)S(1)}, u32[]{:S(2)}, u32[]{:S(2)}) collective-permute-start(bf16[2,512,256]{2,1,0:T(8,128)(2,1)S(1)} %pad_maximum_fusion.2), channel_id=1, source_target_pairs={{0,128},{64,192},{128,0},{192,64},{1,129},{65,193},{129,1},{193,65... | collective-permute-start | bytes 1572872 | tf_op jit(solution)/shard_map/ppermute | solution.py:40
  28.9 22.0 %collective-permute-start.4 = (bf16[2,512,256]{2,1,0:T(8,128)(2,1)S(1)}, bf16[2,512,256]{2,1,0:T(8,128)(2,1)S(1)}, u32[]{:S(2)}, u32[]{:S(2)}) collective-permute-start(bf16[2,512,256]{2,1,0:T(8,128)(2,1)S(1)} %pad_maximum_fusion.2), channel_id=1, source_target_pairs={{0,192},{64,0},{128,64},{192,128},{1,193},{65,1},{129,65},{193,129... | collective-permute-start | bytes 1572872 | tf_op jit(solution)/shard_map/ppermute | solution.py:40
  31.9 9.3 %collective-permute-start.5 = (bf16[512,256]{1,0:T(8,128)(2,1)}, bf16[512,256]{1,0:T(8,128)(2,1)S(1)}, u32[]{:S(2)}, u32[]{:S(2)}) collective-permute-start(bf16[512,256]{1,0:T(8,128)(2,1)} %param.6), channel_id=1, source_target_pairs={{0,0},{16,256},{256,16},{272,272},{1,1},{17,257},{257,17},{273,273... | collective-permute-start | bytes 786440 | tf_op jit(solution)/shard_map/ppermute | solution.py:40
  33.5 11.6 %collective-permute-start.6 = (bf16[512,256]{1,0:T(8,128)(2,1)}, bf16[512,256]{1,0:T(8,128)(2,1)S(1)}, u32[]{:S(2)}, u32[]{:S(2)}) collective-permute-start(bf16[512,256]{1,0:T(8,128)(2,1)} %param.6), channel_id=1, source_target_pairs={{0,256},{16,0},{256,272},{272,16},{1,257},{17,1},{257,273},{273,17... | collective-permute-start | bytes 786440 | tf_op jit(solution)/shard_map/ppermute | solution.py:40
  51.1 14.2 %collective-permute-start.10 = (bf16[4,2,512,256]{3,2,1,0:T(8,128)(2,1)S(1)}, bf16[4,2,512,256]{3,2,1,0:T(8,128)(2,1)}, u32[]{:S(2)}, u32[]{:S(2)}) collective-permute-start(bf16[4,2,512,256]{3,2,1,0:T(8,128)(2,1)S(1)} %pad_maximum_fusion.own_ref), channel_id=1, source_target_pairs={{0,32},{32,0},{1,33},{33,1},{2,34},{34,2},{3,35},{35,3},{4,36},{36... | collective-permute-start | bytes 6291464 | tf_op jit(solution)/shard_map/ppermute | solution.py:40
  54.6 34.8 %collective-permute-start.7 = (bf16[2,512,256]{2,1,0:T(8,128)(2,1)S(1)}, bf16[2,512,256]{2,1,0:T(8,128)(2,1)S(1)}, u32[]{:S(2)}, u32[]{:S(2)}) collective-permute-start(bf16[2,512,256]{2,1,0:T(8,128)(2,1)S(1)} %pad_maximum_fusion.3), channel_id=1, source_target_pairs={{0,64},{64,128},{128,192},{192,0},{1,65},{65,129},{129,193},{193,1... | collective-permute-start | bytes 1572872 | tf_op jit(solution)/shard_map/ppermute | solution.py:40
  58.7 30.7 %collective-permute-start.8 = (bf16[2,512,256]{2,1,0:T(8,128)(2,1)S(1)}, bf16[2,512,256]{2,1,0:T(8,128)(2,1)}, u32[]{:S(2)}, u32[]{:S(2)}) collective-permute-start(bf16[2,512,256]{2,1,0:T(8,128)(2,1)S(1)} %pad_maximum_fusion.3), channel_id=1, source_target_pairs={{0,128},{64,192},{128,0},{192,64},{1,129},{65,193},{129,1},{193,65... | collective-permute-start | bytes 1572872 | tf_op jit(solution)/shard_map/ppermute | solution.py:40
  62.0 27.4 %collective-permute-start.9 = (bf16[2,512,256]{2,1,0:T(8,128)(2,1)S(1)}, bf16[2,512,256]{2,1,0:T(8,128)(2,1)}, u32[]{:S(2)}, u32[]{:S(2)}) collective-permute-start(bf16[2,512,256]{2,1,0:T(8,128)(2,1)S(1)} %pad_maximum_fusion.3), channel_id=1, source_target_pairs={{0,192},{64,0},{128,64},{192,128},{1,193},{65,1},{129,65},{193,129... | collective-permute-start | bytes 1572872 | tf_op jit(solution)/shard_map/ppermute | solution.py:40
  79.7 1.6 copy-start
  83.7 5.7 %collective-permute-start.11 = (f32[128,256]{1,0:T(8,128)S(1)}, f32[128,256]{1,0:T(8,128)S(1)}, u32[]{:S(2)}, u32[]{:S(2)}) collective-permute-start(f32[128,256]{1,0:T(8,128)S(1)} %get-tuple-element.38), channel_id=1, source_target_pairs={{0,16},{16,0},{1,17},{17,1},{2,18},{18,2},{3,19},{19,3},{4,20},{20... | collective-permute-start | bytes 393224 | tf_op jit(solution)/shard_map/ppermute | solution.py:40
  90.9 15.8 %collective-permute-start.13 = (bf16[4,2,512,256]{3,2,1,0:T(8,128)(2,1)S(1)}, bf16[4,2,512,256]{3,2,1,0:T(8,128)(2,1)S(1)}, u32[]{:S(2)}, u32[]{:S(2)}) collective-permute-start(bf16[4,2,512,256]{3,2,1,0:T(8,128)(2,1)S(1)} %pad_maximum_fusion.1.own_ref), channel_id=1, source_target_pairs={{0,32},{32,0},{1,33},{33,1},{2,34},{34,2},{3,35},{35,3},{4,36},{36... | collective-permute-start | bytes 6291464 | tf_op jit(solution)/shard_map/ppermute | solution.py:40
  103.0 6.5 %collective-permute-start.12 = (bf16[128,256]{1,0:T(8,128)(2,1)S(1)}, bf16[128,256]{1,0:T(8,128)(2,1)S(1)}, u32[]{:S(2)}, u32[]{:S(2)}) collective-permute-start(bf16[128,256]{1,0:T(8,128)(2,1)S(1)} %multiply_convert_fusion.1), channel_id=1, source_target_pairs={{0,0},{1,1},{2,32},{3,33},{4,64},{5,65},{6,96},{7,97},{8,128},{9,1... | collective-permute-start | bytes 196616 | tf_op jit(solution)/shard_map/ppermute | solution.py:40
  142.4 40.3 %all-to-all-start.1 = ((bf16[4,4,128,256]{3,2,1,0:T(8,128)(2,1)}), bf16[4,4,128,256]{3,2,1,0:T(8,128)(2,1)S(1)}, u32[]{:S(2)}, u32[]{:S(2)}) async-start(bf16[4,4,128,256]{3,2,1,0:T(8,128)(2,1)} %broadcast_in_dim.5), calls=%async_computation.1 | async-start | bytes 2097152 | tf_op jit(solution)/shard_map/all_to_all | solution.py:18
  150.4 8.5 %collective-permute-start.14 = (f32[2,128,256]{2,1,0:T(8,128)S(1)}, f32[2,128,256]{2,1,0:T(8,128)S(1)}, u32[]{:S(2)}, u32[]{:S(2)}) collective-permute-start(f32[2,128,256]{2,1,0:T(8,128)S(1)} %get-tuple-element.46), channel_id=1, source_target_pairs={{0,0},{16,256},{256,16},{272,272},{1,1},{17,257},{257,17},{273,273... | collective-permute-start | bytes 786440 | tf_op jit(solution)/shard_map/ppermute | solution.py:40
  151.0 13.8 %collective-permute-start.15 = (f32[2,128,256]{2,1,0:T(8,128)S(1)}, f32[2,128,256]{2,1,0:T(8,128)S(1)}, u32[]{:S(2)}, u32[]{:S(2)}) collective-permute-start(f32[2,128,256]{2,1,0:T(8,128)S(1)} %get-tuple-element.47), channel_id=1, source_target_pairs={{0,256},{16,0},{256,272},{272,16},{1,257},{17,1},{257,273},{273,17... | collective-permute-start | bytes 786440 | tf_op jit(solution)/shard_map/ppermute | solution.py:40
  164.9 8.4 %collective-permute-start.16 = (bf16[2,128,256]{2,1,0:T(8,128)(2,1)S(1)}, bf16[2,128,256]{2,1,0:T(8,128)(2,1)S(1)}, u32[]{:S(2)}, u32[]{:S(2)}) collective-permute-start(bf16[2,128,256]{2,1,0:T(8,128)(2,1)S(1)} %multiply_convert_fusion), channel_id=1, source_target_pairs={{0,64},{64,128},{128,192},{192,0},{1,65},{65,129},{129,193},{193,1... | collective-permute-start | bytes 393224 | tf_op jit(solution)/shard_map/ppermute | solution.py:40
  166.8 7.9 %collective-permute-start.17 = (bf16[2,128,256]{2,1,0:T(8,128)(2,1)S(1)}, bf16[2,128,256]{2,1,0:T(8,128)(2,1)S(1)}, u32[]{:S(2)}, u32[]{:S(2)}) collective-permute-start(bf16[2,128,256]{2,1,0:T(8,128)(2,1)S(1)} %multiply_convert_fusion), channel_id=1, source_target_pairs={{0,128},{64,192},{128,0},{192,64},{1,129},{65,193},{129,1},{193,65... | collective-permute-start | bytes 393224 | tf_op jit(solution)/shard_map/ppermute | solution.py:40
  169.5 8.4 %collective-permute-start.18 = (bf16[2,128,256]{2,1,0:T(8,128)(2,1)S(1)}, bf16[2,128,256]{2,1,0:T(8,128)(2,1)S(1)}, u32[]{:S(2)}, u32[]{:S(2)}) collective-permute-start(bf16[2,128,256]{2,1,0:T(8,128)(2,1)S(1)} %multiply_convert_fusion), channel_id=1, source_target_pairs={{0,192},{64,0},{128,64},{192,128},{1,193},{65,1},{129,65},{193,129... | collective-permute-start | bytes 393224 | tf_op jit(solution)/shard_map/ppermute | solution.py:40
  177.9 4.8 %collective-permute-start.19 = (bf16[4,2,128,256]{3,2,1,0:T(8,128)(2,1)S(1)}, bf16[4,2,128,256]{3,2,1,0:T(8,128)(2,1)S(1)}, u32[]{:S(2)}, u32[]{:S(2)}) collective-permute-start(bf16[4,2,128,256]{3,2,1,0:T(8,128)(2,1)S(1)} %pad_maximum_fusion.4.own_ref), channel_id=1, source_target_pairs={{0,32},{32,0},{1,33},{33,1},{2,34},{34,2},{3,35},{35,3},{4,36},{36... | collective-permute-start | bytes 1572872 | tf_op jit(solution)/shard_map/ppermute | solution.py:40
  184.0 18.0 %collective-permute-start.20 = (f32[256,512]{1,0:T(8,128)S(1)}, f32[256,512]{1,0:T(8,128)S(1)}, u32[]{:S(2)}, u32[]{:S(2)}) collective-permute-start(f32[256,512]{1,0:T(8,128)S(1)} %shard_map.49), channel_id=1, source_target_pairs={{0,16},{16,0},{1,17},{17,1},{2,18},{18,2},{3,19},{19,3},{4,20},{20... | collective-permute-start | bytes 1572872 | tf_op jit(solution)/shard_map/ppermute | solution.py:40
Sparse Core Ops, SparseCore 0:
  9.4 70.2 all-gather.2

commit v8 on v7

--- a/solution.py
+++ b/solution.py
@@ -144,10 +144,12 @@
 
     parts = rotate(at, every, 0, both_cores(act_shifts), 1)
     grad_square, parts = lax.optimization_barrier((grad_square, parts))
-    grad_block = to_all(to_all(grad_square, ("zh",), 4), ("zl",), 4).reshape(16, 128, 256)
+    grad_block = to_all(grad_square, ("zh",), 4)
     parts = [move(parts[k], ("xh", "xl"), lambda a, p, k=k: (p ^ k, a)) for k in range(2)]
     rotated_act = parts[0] + parts[1]
     act_square = (rotated_act * rotated_act).astype(jnp.bfloat16)
+    grad_block, act_square = lax.optimization_barrier((grad_block, act_square))
+    grad_block = to_all(grad_block, ("zl",), 4).reshape(16, 128, 256)
     acts = both_cores(shifts(act_square))
 
     theirs = swap(correct(jnp.stack([y, c, 1 - turned]), acts, grad_block), "xl")

time: 211 us -> 201 us (0.953)
  blocking collectives: 31.8 us -> 0 us
  starting transfers between devices: 95.7 us -> 111 us
  waiting for transfers between devices: 55.1 us -> 60.6 us
    all_to_all x1 -> x0, blocking collectives: 31.8 us -> none  [to_all(): return lax.all_to_all(spread, axes, split_axis=0, concat_axis=0, tiled=True)]
    all_to_all x1 -> x2, starting transfers between devices: 7.99 us -> 21.1 us  [to_all(): return lax.all_to_all(spread, axes, split_axis=0, concat_axis=0, tiled=True)]
    all_to_all x1 -> x2, waiting for transfers between devices: 0.01 us -> 10.2 us  [to_all(): return lax.all_to_all(spread, axes, split_axis=0, concat_axis=0, tiled=True)]
    ppermute x21, waiting for transfers between devices: 40.8 us -> 36.1 us  [move(): return lax.ppermute(x, axes, pairs)]
  transfers between devices with their start and end apart: 23 -> 24, of which waited for: 13 -> 15; matrix products, arithmetic and copies ran while one was open for 0% -> 0% of each run, Pallas kernels for 2% -> 2%
where the time goes in v8:
time: 201 us; the launch traced here: 199 us
  starting transfers between devices  111 us (55%)
  waiting for transfers between devices  60.6 us (30%)
  between operations  13.7 us (7%)
  Pallas kernels  6.19 us (3%)
  other arithmetic  4.52 us (2%)
  local copies, waits for them, and re-layouts  3.4 us (2%)
    ppermute x21, starting transfers between devices, move(): return lax.ppermute(x, axes, pairs)  89.6 us
    ppermute x21, waiting for transfers between devices, move(): return lax.ppermute(x, axes, pairs)  36.1 us
    all_to_all x2, starting transfers between devices, to_all(): return lax.all_to_all(spread, axes, split_axis=0, concat_axis=0, tiled=True)  21.1 us
    all_gather x1, waiting for transfers between devices, on_device(): every = lax.all_gather(both, ('zh', 'zl'), axis=0, tiled=False)  14.3 us
    all_to_all x2, waiting for transfers between devices, to_all(): return lax.all_to_all(spread, axes, split_axis=0, concat_axis=0, tiled=True)  10.2 us
  transfers between devices with their start and end apart: 24, of which 15 were waited for; matrix products, arithmetic and copies ran while one was open for 0% of the time, Pallas kernels for 2%

profile of v8, /device:TPU:1, one launch (start us, length us, event | category | flops | bytes accessed | tf_op | source)
XLA Modules:
  0.0 199.1 jit_solution(6920040258356680118)
XLA Ops:
  6.5 1.5 pad_maximum_fusion.5
  8.1 0.0 all-gather.3.cloned.1.call-update
  8.1 1.6 collective-permute-start
  9.7 6.0 %collective-permute-start.1 = (bf16[512,256]{1,0:T(8,128)(2,1)}, bf16[512,256]{1,0:T(8,128)(2,1)S(1)}, u32[]{:S(2)}, u32[]{:S(2)}) collective-permute-start(bf16[512,256]{1,0:T(8,128)(2,1)} %param.7), channel_id=1, source_target_pairs={{0,256},{16,0},{256,272},{272,16},{1,257},{17,1},{257,273},{273,17... | collective-permute-start | bytes 786440 | tf_op jit(solution)/shard_map/ppermute | solution.py:40
  15.8 0.0 collective-permute-done
  15.8 3.6 %collective-permute-done.1 = bf16[512,256]{1,0:T(8,128)(2,1)S(1)} collective-permute-done((bf16[512,256]{1,0:T(8,128)(2,1)}, bf16[512,256]{1,0:T(8,128)(2,1)S(1)}, u32[]{:S(2)}, u32[]{:S(2)}) %collective-permute-start.1) | collective-permute-done | bytes 262176 | tf_op jit(solution)/shard_map/ppermute | solution.py:40
  19.4 0.1 pad_maximum_fusion.2
  19.5 4.9 %collective-permute-start.2 = (bf16[2,512,256]{2,1,0:T(8,128)(2,1)S(1)}, bf16[2,512,256]{2,1,0:T(8,128)(2,1)S(1)}, u32[]{:S(2)}, u32[]{:S(2)}) collective-permute-start(bf16[2,512,256]{2,1,0:T(8,128)(2,1)S(1)} %pad_maximum_fusion.2), channel_id=1, source_target_pairs={{0,64},{64,128},{128,192},{192,0},{1,65},{65,129},{129,193},{193,1... | collective-permute-start | bytes 1572872 | tf_op jit(solution)/shard_map/ppermute | solution.py:40
  24.4 4.5 %collective-permute-start.3 = (bf16[2,512,256]{2,1,0:T(8,128)(2,1)S(1)}, bf16[2,512,256]{2,1,0:T(8,128)(2,1)S(1)}, u32[]{:S(2)}, u32[]{:S(2)}) collective-permute-start(bf16[2,512,256]{2,1,0:T(8,128)(2,1)S(1)} %pad_maximum_fusion.2), channel_id=1, source_target_pairs={{0,128},{64,192},{128,0},{192,64},{1,129},{65,193},{129,1},{193,65... | collective-permute-start | bytes 1572872 | tf_op jit(solution)/shard_map/ppermute | solution.py:40
  28.9 3.0 %collective-permute-start.4 = (bf16[2,512,256]{2,1,0:T(8,128)(2,1)S(1)}, bf16[2,512,256]{2,1,0:T(8,128)(2,1)S(1)}, u32[]{:S(2)}, u32[]{:S(2)}) collective-permute-start(bf16[2,512,256]{2,1,0:T(8,128)(2,1)S(1)} %pad_maximum_fusion.2), channel_id=1, source_target_pairs={{0,192},{64,0},{128,64},{192,128},{1,193},{65,1},{129,65},{193,129... | collective-permute-start | bytes 1572872 | tf_op jit(solution)/shard_map/ppermute | solution.py:40
  31.9 1.6 collective-permute-start.5
  33.5 7.7 %collective-permute-start.6 = (bf16[512,256]{1,0:T(8,128)(2,1)}, bf16[512,256]{1,0:T(8,128)(2,1)S(1)}, u32[]{:S(2)}, u32[]{:S(2)}) collective-permute-start(bf16[512,256]{1,0:T(8,128)(2,1)} %param.6), channel_id=1, source_target_pairs={{0,256},{16,0},{256,272},{272,16},{1,257},{17,1},{257,273},{273,17... | collective-permute-start | bytes 786440 | tf_op jit(solution)/shard_map/ppermute | solution.py:40
  41.2 0.0 collective-permute-done.5
  41.2 3.9 %collective-permute-done.6 = bf16[512,256]{1,0:T(8,128)(2,1)S(1)} collective-permute-done((bf16[512,256]{1,0:T(8,128)(2,1)}, bf16[512,256]{1,0:T(8,128)(2,1)S(1)}, u32[]{:S(2)}, u32[]{:S(2)}) %collective-permute-start.6) | collective-permute-done | bytes 262176 | tf_op jit(solution)/shard_map/ppermute | solution.py:40
  45.1 0.1 pad_maximum_fusion.3
  45.2 0.0 collective-permute-done.2
  45.2 3.4 %collective-permute-done.3 = bf16[2,512,256]{2,1,0:T(8,128)(2,1)S(1)} collective-permute-done((bf16[2,512,256]{2,1,0:T(8,128)(2,1)S(1)}, bf16[2,512,256]{2,1,0:T(8,128)(2,1)S(1)}, u32[]{:S(2)}, u32[]{:S(2)}) %collective-permute-start.3) | collective-permute-done | bytes 524320 | tf_op jit(solution)/shard_map/ppermute | solution.py:40
  48.6 2.3 %collective-permute-done.4 = bf16[2,512,256]{2,1,0:T(8,128)(2,1)S(1)} collective-permute-done((bf16[2,512,256]{2,1,0:T(8,128)(2,1)S(1)}, bf16[2,512,256]{2,1,0:T(8,128)(2,1)S(1)}, u32[]{:S(2)}, u32[]{:S(2)}) %collective-permute-start.4) | collective-permute-done | bytes 524320 | tf_op jit(solution)/shard_map/ppermute | solution.py:40
  50.9 0.3 pad_maximum_fusion.own_ref
  51.1 3.5 %collective-permute-start.10 = (bf16[4,2,512,256]{3,2,1,0:T(8,128)(2,1)S(1)}, bf16[4,2,512,256]{3,2,1,0:T(8,128)(2,1)}, u32[]{:S(2)}, u32[]{:S(2)}) collective-permute-start(bf16[4,2,512,256]{3,2,1,0:T(8,128)(2,1)S(1)} %pad_maximum_fusion.own_ref), channel_id=1, source_target_pairs={{0,32},{32,0},{1,33},{33,1},{2,34},{34,2},{3,35},{35,3},{4,36},{36... | collective-permute-start | bytes 6291464 | tf_op jit(solution)/shard_map/ppermute | solution.py:40
  54.6 4.1 %collective-permute-start.7 = (bf16[2,512,256]{2,1,0:T(8,128)(2,1)S(1)}, bf16[2,512,256]{2,1,0:T(8,128)(2,1)S(1)}, u32[]{:S(2)}, u32[]{:S(2)}) collective-permute-start(bf16[2,512,256]{2,1,0:T(8,128)(2,1)S(1)} %pad_maximum_fusion.3), channel_id=1, source_target_pairs={{0,64},{64,128},{128,192},{192,0},{1,65},{65,129},{129,193},{193,1... | collective-permute-start | bytes 1572872 | tf_op jit(solution)/shard_map/ppermute | solution.py:40
  58.7 3.2 %collective-permute-start.8 = (bf16[2,512,256]{2,1,0:T(8,128)(2,1)S(1)}, bf16[2,512,256]{2,1,0:T(8,128)(2,1)}, u32[]{:S(2)}, u32[]{:S(2)}) collective-permute-start(bf16[2,512,256]{2,1,0:T(8,128)(2,1)S(1)} %pad_maximum_fusion.3), channel_id=1, source_target_pairs={{0,128},{64,192},{128,0},{192,64},{1,129},{65,193},{129,1},{193,65... | collective-permute-start | bytes 1572872 | tf_op jit(solution)/shard_map/ppermute | solution.py:40
  62.0 3.3 %collective-permute-start.9 = (bf16[2,512,256]{2,1,0:T(8,128)(2,1)S(1)}, bf16[2,512,256]{2,1,0:T(8,128)(2,1)}, u32[]{:S(2)}, u32[]{:S(2)}) collective-permute-start(bf16[2,512,256]{2,1,0:T(8,128)(2,1)S(1)} %pad_maximum_fusion.3), channel_id=1, source_target_pairs={{0,192},{64,0},{128,64},{192,128},{1,193},{65,1},{129,65},{193,129... | collective-permute-start | bytes 1572872 | tf_op jit(solution)/shard_map/ppermute | solution.py:40
  65.3 0.1 pad_add_fusion.at_ref
  65.4 0.0 collective-permute-done.10.other_ref
  65.4 14.3 %all-gather.3.cloned.1.call-done = bf16[32,128,256]{2,1,0:T(8,128)(2,1)} async-done(((bf16[2,128,256]{2,1,0:T(8,128)(2,1)}), bf16[32,128,256]{2,1,0:T(8,128)(2,1)}) %all-gather.3.cloned.1.call-update) | async-done | bytes 2097168 | tf_op jit(solution)/shard_map/all_gather | solution.py:129
  79.7 1.6 copy-done
  81.3 2.4 %shard_map.46 = (f32[128,256]{1,0:T(8,128)S(1)}, f32[128,256]{1,0:T(8,128)S(1)}) custom-call(s32[3]{0:T(128)S(1)} %pad_add_fusion.at_ref, bf16[16,2,128,256]{3,2,1,0:T(8,128)(2,1)S(1)} %bitcast.26, bf16[4,2,512,256]{3,2,1,0:T(8,128)(2,1)S(1)} %pad_maximum_fusion.own_ref, bf16[4,2,512,256]{3,2,1,0:T(8,128)(2,1)} %collective-permute-done.10.other_ref), custom_call_target="tpu_custom_call" | custom-call | tf_op jit(solution)/shard_map/pallas_call | solution.py:84
  83.7 3.0 %collective-permute-start.11 = (f32[128,256]{1,0:T(8,128)S(1)}, f32[128,256]{1,0:T(8,128)S(1)}, u32[]{:S(2)}, u32[]{:S(2)}) collective-permute-start(f32[128,256]{1,0:T(8,128)S(1)} %get-tuple-element.40), channel_id=1, source_target_pairs={{0,16},{16,0},{1,17},{17,1},{2,18},{18,2},{3,19},{19,3},{4,20},{20... | collective-permute-start | bytes 393224 | tf_op jit(solution)/shard_map/ppermute | solution.py:40
  86.7 2.7 %collective-permute-done.11 = f32[128,256]{1,0:T(8,128)S(1)} collective-permute-done((f32[128,256]{1,0:T(8,128)S(1)}, f32[128,256]{1,0:T(8,128)S(1)}, u32[]{:S(2)}, u32[]{:S(2)}) %collective-permute-start.11) | collective-permute-done | bytes 131104 | tf_op jit(solution)/shard_map/ppermute | solution.py:40
  89.4 0.0 collective-permute-done.7
  89.4 0.0 collective-permute-done.8
  89.4 0.0 collective-permute-done.9
  89.4 1.5 pad_maximum_fusion.1.own_ref
  90.9 12.1 %collective-permute-start.13 = (bf16[4,2,512,256]{3,2,1,0:T(8,128)(2,1)S(1)}, bf16[4,2,512,256]{3,2,1,0:T(8,128)(2,1)S(1)}, u32[]{:S(2)}, u32[]{:S(2)}) collective-permute-start(bf16[4,2,512,256]{3,2,1,0:T(8,128)(2,1)S(1)} %pad_maximum_fusion.1.own_ref), channel_id=1, source_target_pairs={{0,32},{32,0},{1,33},{33,1},{2,34},{34,2},{3,35},{35,3},{4,36},{36... | collective-permute-start | bytes 6291464 | tf_op jit(solution)/shard_map/ppermute | solution.py:40
  103.0 2.9 %collective-permute-start.12 = (bf16[128,256]{1,0:T(8,128)(2,1)S(1)}, bf16[128,256]{1,0:T(8,128)(2,1)S(1)}, u32[]{:S(2)}, u32[]{:S(2)}) collective-permute-start(bf16[128,256]{1,0:T(8,128)(2,1)S(1)} %multiply_convert_fusion.1), channel_id=1, source_target_pairs={{0,0},{1,1},{2,32},{3,33},{4,64},{5,65},{6,96},{7,97},{8,128},{9,1... | collective-permute-start | bytes 196616 | tf_op jit(solution)/shard_map/ppermute | solution.py:40
  105.9 0.8 collective-permute-done.13.other_ref
  106.8 1.3 shard_map.47
  108.1 1.4 collective-permute-done.12
  109.5 0.7 broadcast_in_dim.4
  110.2 16.1 %all-to-all-start = ((bf16[4,128,256]{2,1,0:T(8,128)(2,1)}), bf16[4,128,256]{2,1,0:T(8,128)(2,1)S(1)}, u32[]{:S(2)}, u32[]{:S(2)}) async-start(bf16[4,128,256]{2,1,0:T(8,128)(2,1)} %broadcast_in_dim.4), calls=%async_computation | async-start | bytes 524288 | tf_op jit(solution)/shard_map/all_to_all | solution.py:18
  126.3 0.7 collective-permute-start.14
  127.0 7.0 %collective-permute-start.15 = (f32[2,128,256]{2,1,0:T(8,128)S(1)}, f32[2,128,256]{2,1,0:T(8,128)S(1)}, u32[]{:S(2)}, u32[]{:S(2)}) collective-permute-start(f32[2,128,256]{2,1,0:T(8,128)S(1)} %get-tuple-element.50), channel_id=1, source_target_pairs={{0,256},{16,0},{256,272},{272,16},{1,257},{17,1},{257,273},{273,17... | collective-permute-start | bytes 786440 | tf_op jit(solution)/shard_map/ppermute | solution.py:40
  134.0 0.0 collective-permute-done.14
  134.0 3.3 %collective-permute-done.15 = f32[2,128,256]{2,1,0:T(8,128)S(1)} collective-permute-done((f32[2,128,256]{2,1,0:T(8,128)S(1)}, f32[2,128,256]{2,1,0:T(8,128)S(1)}, u32[]{:S(2)}, u32[]{:S(2)}) %collective-permute-start.15) | collective-permute-done | bytes 262176 | tf_op jit(solution)/shard_map/ppermute | solution.py:40
  137.3 5.4 %all-to-all-done = bf16[4,128,256]{2,1,0:T(8,128)(2,1)S(1)} async-done(((bf16[4,128,256]{2,1,0:T(8,128)(2,1)}), bf16[4,128,256]{2,1,0:T(8,128)(2,1)S(1)}, u32[]{:S(2)}, u32[]{:S(2)}) %all-to-all-start) | async-done | bytes 262176 | tf_op jit(solution)/shard_map/all_to_all | solution.py:18
  142.8 1.1 broadcast_in_dim.5
  143.9 5.0 %all-to-all-start.1 = ((bf16[4,4,128,256]{3,2,1,0:T(8,128)(2,1)}), bf16[4,4,128,256]{3,2,1,0:T(8,128)(2,1)S(1)}, u32[]{:S(2)}, u32[]{:S(2)}) async-start(bf16[4,4,128,256]{3,2,1,0:T(8,128)(2,1)} %broadcast_in_dim.5), calls=%async_computation.1 | async-start | bytes 2097152 | tf_op jit(solution)/shard_map/all_to_all | solution.py:18
  148.9 3.1 %collective-permute-start.16 = (bf16[2,128,256]{2,1,0:T(8,128)(2,1)S(1)}, bf16[2,128,256]{2,1,0:T(8,128)(2,1)S(1)}, u32[]{:S(2)}, u32[]{:S(2)}) collective-permute-start(bf16[2,128,256]{2,1,0:T(8,128)(2,1)S(1)} %multiply_convert_fusion), channel_id=1, source_target_pairs={{0,64},{64,128},{128,192},{192,0},{1,65},{65,129},{129,193},{193,1... | collective-permute-start | bytes 393224 | tf_op jit(solution)/shard_map/ppermute | solution.py:40
  152.0 1.9 collective-permute-start.17
  153.9 4.3 %collective-permute-start.18 = (bf16[2,128,256]{2,1,0:T(8,128)(2,1)S(1)}, bf16[2,128,256]{2,1,0:T(8,128)(2,1)S(1)}, u32[]{:S(2)}, u32[]{:S(2)}) collective-permute-start(bf16[2,128,256]{2,1,0:T(8,128)(2,1)S(1)} %multiply_convert_fusion), channel_id=1, source_target_pairs={{0,192},{64,0},{128,64},{192,128},{1,193},{65,1},{129,65},{193,129... | collective-permute-start | bytes 393224 | tf_op jit(solution)/shard_map/ppermute | solution.py:40
  158.2 0.0 collective-permute-done.16
  158.2 2.4 %collective-permute-done.17 = bf16[2,128,256]{2,1,0:T(8,128)(2,1)S(1)} collective-permute-done((bf16[2,128,256]{2,1,0:T(8,128)(2,1)S(1)}, bf16[2,128,256]{2,1,0:T(8,128)(2,1)S(1)}, u32[]{:S(2)}, u32[]{:S(2)}) %collective-permute-start.17) | collective-permute-done | bytes 131104 | tf_op jit(solution)/shard_map/ppermute | solution.py:40
  160.6 0.9 collective-permute-done.18
  161.5 0.1 pad_maximum_fusion.4.own_ref
  161.6 6.2 %collective-permute-start.19 = (bf16[4,2,128,256]{3,2,1,0:T(8,128)(2,1)S(1)}, bf16[4,2,128,256]{3,2,1,0:T(8,128)(2,1)S(1)}, u32[]{:S(2)}, u32[]{:S(2)}) collective-permute-start(bf16[4,2,128,256]{3,2,1,0:T(8,128)(2,1)S(1)} %pad_maximum_fusion.4.own_ref), channel_id=1, source_target_pairs={{0,32},{32,0},{1,33},{33,1},{2,34},{34,2},{3,35},{35,3},{4,36},{36... | collective-permute-start | bytes 1572872 | tf_op jit(solution)/shard_map/ppermute | solution.py:40
  167.8 0.1 pad_add_fusion.2.at_ref
  167.9 1.4 collective-permute-done.19.other_ref
  169.4 4.7 %all-to-all-done.1 = bf16[4,4,128,256]{3,2,1,0:T(8,128)(2,1)S(1)} async-done(((bf16[4,4,128,256]{3,2,1,0:T(8,128)(2,1)}), bf16[4,4,128,256]{3,2,1,0:T(8,128)(2,1)S(1)}, u32[]{:S(2)}, u32[]{:S(2)}) %all-to-all-start.1) | async-done | bytes 1048608 | tf_op jit(solution)/shard_map/all_to_all | solution.py:18
  174.1 1.3 shard_map.49
  175.3 4.8 %collective-permute-start.20 = (f32[256,512]{1,0:T(8,128)S(1)}, f32[256,512]{1,0:T(8,128)S(1)}, u32[]{:S(2)}, u32[]{:S(2)}) collective-permute-start(f32[256,512]{1,0:T(8,128)S(1)} %shard_map.49), channel_id=1, source_target_pairs={{0,16},{16,0},{1,17},{17,1},{2,18},{18,2},{3,19},{19,3},{4,20},{20... | collective-permute-start | bytes 1572872 | tf_op jit(solution)/shard_map/ppermute | solution.py:40
  180.2 1.3 shard_map.48
  181.5 9.9 %collective-permute-done.20 = f32[256,512]{1,0:T(8,128)S(1)} collective-permute-done((f32[256,512]{1,0:T(8,128)S(1)}, f32[256,512]{1,0:T(8,128)S(1)}, u32[]{:S(2)}, u32[]{:S(2)}) %collective-permute-start.20) | collective-permute-done | bytes 524320 | tf_op jit(solution)/shard_map/ppermute | solution.py:40
  191.4 0.9 add_multiply_fusion
  (4 shorter events, 0.1 us)
Async XLA Ops:
  6.5 73.2 %all-gather.3.cloned.1.call-start = ((), (), s32[]{:S(2)}) async-start(), calls=%async_computation.2 | async-start | bytes 2228224 | tf_op jit(solution)/shard_map/all_gather | solution.py:129
  8.1 7.7 %collective-permute-start = (bf16[512,256]{1,0:T(8,128)(2,1)}, bf16[512,256]{1,0:T(8,128)(2,1)S(1)}, u32[]{:S(2)}, u32[]{:S(2)}) collective-permute-start(bf16[512,256]{1,0:T(8,128)(2,1)} %param.7), channel_id=1, source_target_pairs={{0,0},{16,256},{256,16},{272,272},{1,1},{17,257},{257,17},{273,273... | collective-permute-start | bytes 786440 | tf_op jit(solution)/shard_map/ppermute | solution.py:40
  9.7 9.7 %collective-permute-start.1 = (bf16[512,256]{1,0:T(8,128)(2,1)}, bf16[512,256]{1,0:T(8,128)(2,1)S(1)}, u32[]{:S(2)}, u32[]{:S(2)}) collective-permute-start(bf16[512,256]{1,0:T(8,128)(2,1)} %param.7), channel_id=1, source_target_pairs={{0,256},{16,0},{256,272},{272,16},{1,257},{17,1},{257,273},{273,17... | collective-permute-start | bytes 786440 | tf_op jit(solution)/shard_map/ppermute | solution.py:40
  19.5 25.7 %collective-permute-start.2 = (bf16[2,512,256]{2,1,0:T(8,128)(2,1)S(1)}, bf16[2,512,256]{2,1,0:T(8,128)(2,1)S(1)}, u32[]{:S(2)}, u32[]{:S(2)}) collective-permute-start(bf16[2,512,256]{2,1,0:T(8,128)(2,1)S(1)} %pad_maximum_fusion.2), channel_id=1, source_target_pairs={{0,64},{64,128},{128,192},{192,0},{1,65},{65,129},{129,193},{193,1... | collective-permute-start | bytes 1572872 | tf_op jit(solution)/shard_map/ppermute | solution.py:40
  24.4 24.2 %collective-permute-start.3 = (bf16[2,512,256]{2,1,0:T(8,128)(2,1)S(1)}, bf16[2,512,256]{2,1,0:T(8,128)(2,1)S(1)}, u32[]{:S(2)}, u32[]{:S(2)}) collective-permute-start(bf16[2,512,256]{2,1,0:T(8,128)(2,1)S(1)} %pad_maximum_fusion.2), channel_id=1, source_target_pairs={{0,128},{64,192},{128,0},{192,64},{1,129},{65,193},{129,1},{193,65... | collective-permute-start | bytes 1572872 | tf_op jit(solution)/shard_map/ppermute | solution.py:40
  28.9 22.0 %collective-permute-start.4 = (bf16[2,512,256]{2,1,0:T(8,128)(2,1)S(1)}, bf16[2,512,256]{2,1,0:T(8,128)(2,1)S(1)}, u32[]{:S(2)}, u32[]{:S(2)}) collective-permute-start(bf16[2,512,256]{2,1,0:T(8,128)(2,1)S(1)} %pad_maximum_fusion.2), channel_id=1, source_target_pairs={{0,192},{64,0},{128,64},{192,128},{1,193},{65,1},{129,65},{193,129... | collective-permute-start | bytes 1572872 | tf_op jit(solution)/shard_map/ppermute | solution.py:40
  31.9 9.3 %collective-permute-start.5 = (bf16[512,256]{1,0:T(8,128)(2,1)}, bf16[512,256]{1,0:T(8,128)(2,1)S(1)}, u32[]{:S(2)}, u32[]{:S(2)}) collective-permute-start(bf16[512,256]{1,0:T(8,128)(2,1)} %param.6), channel_id=1, source_target_pairs={{0,0},{16,256},{256,16},{272,272},{1,1},{17,257},{257,17},{273,273... | collective-permute-start | bytes 786440 | tf_op jit(solution)/shard_map/ppermute | solution.py:40
  33.5 11.6 %collective-permute-start.6 = (bf16[512,256]{1,0:T(8,128)(2,1)}, bf16[512,256]{1,0:T(8,128)(2,1)S(1)}, u32[]{:S(2)}, u32[]{:S(2)}) collective-permute-start(bf16[512,256]{1,0:T(8,128)(2,1)} %param.6), channel_id=1, source_target_pairs={{0,256},{16,0},{256,272},{272,16},{1,257},{17,1},{257,273},{273,17... | collective-permute-start | bytes 786440 | tf_op jit(solution)/shard_map/ppermute | solution.py:40
  51.1 14.2 %collective-permute-start.10 = (bf16[4,2,512,256]{3,2,1,0:T(8,128)(2,1)S(1)}, bf16[4,2,512,256]{3,2,1,0:T(8,128)(2,1)}, u32[]{:S(2)}, u32[]{:S(2)}) collective-permute-start(bf16[4,2,512,256]{3,2,1,0:T(8,128)(2,1)S(1)} %pad_maximum_fusion.own_ref), channel_id=1, source_target_pairs={{0,32},{32,0},{1,33},{33,1},{2,34},{34,2},{3,35},{35,3},{4,36},{36... | collective-permute-start | bytes 6291464 | tf_op jit(solution)/shard_map/ppermute | solution.py:40
  54.6 34.8 %collective-permute-start.7 = (bf16[2,512,256]{2,1,0:T(8,128)(2,1)S(1)}, bf16[2,512,256]{2,1,0:T(8,128)(2,1)S(1)}, u32[]{:S(2)}, u32[]{:S(2)}) collective-permute-start(bf16[2,512,256]{2,1,0:T(8,128)(2,1)S(1)} %pad_maximum_fusion.3), channel_id=1, source_target_pairs={{0,64},{64,128},{128,192},{192,0},{1,65},{65,129},{129,193},{193,1... | collective-permute-start | bytes 1572872 | tf_op jit(solution)/shard_map/ppermute | solution.py:40
  58.7 30.7 %collective-permute-start.8 = (bf16[2,512,256]{2,1,0:T(8,128)(2,1)S(1)}, bf16[2,512,256]{2,1,0:T(8,128)(2,1)}, u32[]{:S(2)}, u32[]{:S(2)}) collective-permute-start(bf16[2,512,256]{2,1,0:T(8,128)(2,1)S(1)} %pad_maximum_fusion.3), channel_id=1, source_target_pairs={{0,128},{64,192},{128,0},{192,64},{1,129},{65,193},{129,1},{193,65... | collective-permute-start | bytes 1572872 | tf_op jit(solution)/shard_map/ppermute | solution.py:40
  62.0 27.4 %collective-permute-start.9 = (bf16[2,512,256]{2,1,0:T(8,128)(2,1)S(1)}, bf16[2,512,256]{2,1,0:T(8,128)(2,1)}, u32[]{:S(2)}, u32[]{:S(2)}) collective-permute-start(bf16[2,512,256]{2,1,0:T(8,128)(2,1)S(1)} %pad_maximum_fusion.3), channel_id=1, source_target_pairs={{0,192},{64,0},{128,64},{192,128},{1,193},{65,1},{129,65},{193,129... | collective-permute-start | bytes 1572872 | tf_op jit(solution)/shard_map/ppermute | solution.py:40
  79.7 1.6 copy-start
  83.7 5.7 %collective-permute-start.11 = (f32[128,256]{1,0:T(8,128)S(1)}, f32[128,256]{1,0:T(8,128)S(1)}, u32[]{:S(2)}, u32[]{:S(2)}) collective-permute-start(f32[128,256]{1,0:T(8,128)S(1)} %get-tuple-element.40), channel_id=1, source_target_pairs={{0,16},{16,0},{1,17},{17,1},{2,18},{18,2},{3,19},{19,3},{4,20},{20... | collective-permute-start | bytes 393224 | tf_op jit(solution)/shard_map/ppermute | solution.py:40
  90.9 15.8 %collective-permute-start.13 = (bf16[4,2,512,256]{3,2,1,0:T(8,128)(2,1)S(1)}, bf16[4,2,512,256]{3,2,1,0:T(8,128)(2,1)S(1)}, u32[]{:S(2)}, u32[]{:S(2)}) collective-permute-start(bf16[4,2,512,256]{3,2,1,0:T(8,128)(2,1)S(1)} %pad_maximum_fusion.1.own_ref), channel_id=1, source_target_pairs={{0,32},{32,0},{1,33},{33,1},{2,34},{34,2},{3,35},{35,3},{4,36},{36... | collective-permute-start | bytes 6291464 | tf_op jit(solution)/shard_map/ppermute | solution.py:40
  103.0 6.5 %collective-permute-start.12 = (bf16[128,256]{1,0:T(8,128)(2,1)S(1)}, bf16[128,256]{1,0:T(8,128)(2,1)S(1)}, u32[]{:S(2)}, u32[]{:S(2)}) collective-permute-start(bf16[128,256]{1,0:T(8,128)(2,1)S(1)} %multiply_convert_fusion.1), channel_id=1, source_target_pairs={{0,0},{1,1},{2,32},{3,33},{4,64},{5,65},{6,96},{7,97},{8,128},{9,1... | collective-permute-start | bytes 196616 | tf_op jit(solution)/shard_map/ppermute | solution.py:40
  110.2 32.6 %all-to-all-start = ((bf16[4,128,256]{2,1,0:T(8,128)(2,1)}), bf16[4,128,256]{2,1,0:T(8,128)(2,1)S(1)}, u32[]{:S(2)}, u32[]{:S(2)}) async-start(bf16[4,128,256]{2,1,0:T(8,128)(2,1)} %broadcast_in_dim.4), calls=%async_computation | async-start | bytes 524288 | tf_op jit(solution)/shard_map/all_to_all | solution.py:18
  126.3 7.7 %collective-permute-start.14 = (f32[2,128,256]{2,1,0:T(8,128)S(1)}, f32[2,128,256]{2,1,0:T(8,128)S(1)}, u32[]{:S(2)}, u32[]{:S(2)}) collective-permute-start(f32[2,128,256]{2,1,0:T(8,128)S(1)} %get-tuple-element.49), channel_id=1, source_target_pairs={{0,0},{16,256},{256,16},{272,272},{1,1},{17,257},{257,17},{273,273... | collective-permute-start | bytes 786440 | tf_op jit(solution)/shard_map/ppermute | solution.py:40
  127.0 10.3 %collective-permute-start.15 = (f32[2,128,256]{2,1,0:T(8,128)S(1)}, f32[2,128,256]{2,1,0:T(8,128)S(1)}, u32[]{:S(2)}, u32[]{:S(2)}) collective-permute-start(f32[2,128,256]{2,1,0:T(8,128)S(1)} %get-tuple-element.50), channel_id=1, source_target_pairs={{0,256},{16,0},{256,272},{272,16},{1,257},{17,1},{257,273},{273,17... | collective-permute-start | bytes 786440 | tf_op jit(solution)/shard_map/ppermute | solution.py:40
  143.9 30.2 %all-to-all-start.1 = ((bf16[4,4,128,256]{3,2,1,0:T(8,128)(2,1)}), bf16[4,4,128,256]{3,2,1,0:T(8,128)(2,1)S(1)}, u32[]{:S(2)}, u32[]{:S(2)}) async-start(bf16[4,4,128,256]{3,2,1,0:T(8,128)(2,1)} %broadcast_in_dim.5), calls=%async_computation.1 | async-start | bytes 2097152 | tf_op jit(solution)/shard_map/all_to_all | solution.py:18
  148.9 9.4 %collective-permute-start.16 = (bf16[2,128,256]{2,1,0:T(8,128)(2,1)S(1)}, bf16[2,128,256]{2,1,0:T(8,128)(2,1)S(1)}, u32[]{:S(2)}, u32[]{:S(2)}) collective-permute-start(bf16[2,128,256]{2,1,0:T(8,128)(2,1)S(1)} %multiply_convert_fusion), channel_id=1, source_target_pairs={{0,64},{64,128},{128,192},{192,0},{1,65},{65,129},{129,193},{193,1... | collective-permute-start | bytes 393224 | tf_op jit(solution)/shard_map/ppermute | solution.py:40
  152.0 8.7 %collective-permute-start.17 = (bf16[2,128,256]{2,1,0:T(8,128)(2,1)S(1)}, bf16[2,128,256]{2,1,0:T(8,128)(2,1)S(1)}, u32[]{:S(2)}, u32[]{:S(2)}) collective-permute-start(bf16[2,128,256]{2,1,0:T(8,128)(2,1)S(1)} %multiply_convert_fusion), channel_id=1, source_target_pairs={{0,128},{64,192},{128,0},{192,64},{1,129},{65,193},{129,1},{193,65... | collective-permute-start | bytes 393224 | tf_op jit(solution)/shard_map/ppermute | solution.py:40
  153.9 7.6 %collective-permute-start.18 = (bf16[2,128,256]{2,1,0:T(8,128)(2,1)S(1)}, bf16[2,128,256]{2,1,0:T(8,128)(2,1)S(1)}, u32[]{:S(2)}, u32[]{:S(2)}) collective-permute-start(bf16[2,128,256]{2,1,0:T(8,128)(2,1)S(1)} %multiply_convert_fusion), channel_id=1, source_target_pairs={{0,192},{64,0},{128,64},{192,128},{1,193},{65,1},{129,65},{193,129... | collective-permute-start | bytes 393224 | tf_op jit(solution)/shard_map/ppermute | solution.py:40
  161.6 7.8 %collective-permute-start.19 = (bf16[4,2,128,256]{3,2,1,0:T(8,128)(2,1)S(1)}, bf16[4,2,128,256]{3,2,1,0:T(8,128)(2,1)S(1)}, u32[]{:S(2)}, u32[]{:S(2)}) collective-permute-start(bf16[4,2,128,256]{3,2,1,0:T(8,128)(2,1)S(1)} %pad_maximum_fusion.4.own_ref), channel_id=1, source_target_pairs={{0,32},{32,0},{1,33},{33,1},{2,34},{34,2},{3,35},{35,3},{4,36},{36... | collective-permute-start | bytes 1572872 | tf_op jit(solution)/shard_map/ppermute | solution.py:40
  175.3 16.0 %collective-permute-start.20 = (f32[256,512]{1,0:T(8,128)S(1)}, f32[256,512]{1,0:T(8,128)S(1)}, u32[]{:S(2)}, u32[]{:S(2)}) collective-permute-start(f32[256,512]{1,0:T(8,128)S(1)} %shard_map.49), channel_id=1, source_target_pairs={{0,16},{16,0},{1,17},{17,1},{2,18},{18,2},{3,19},{19,3},{4,20},{20... | collective-permute-start | bytes 1572872 | tf_op jit(solution)/shard_map/ppermute | solution.py:40
Sparse Core Ops, SparseCore 0:
  9.4 70.2 all-gather.2

commit v9 on v8

--- a/solution.py
+++ b/solution.py
@@ -66,11 +66,11 @@
 
 
 def corrected_kernel(at_ref, own_ref, other_ref, s_ref, out_ref):
-    y, c, k = at_ref[0], at_ref[1], at_ref[2]
+    y, c, k, zh = at_ref[0], at_ref[1], at_ref[2], at_ref[3]
     for h in range(2):
         acc = jnp.zeros((256, 256), jnp.float32)
         for j in range(4):
-            at = lax.rem(y + 4 - j, 4) + 4 * h
+            at = lax.rem(zh + 4 - y + j, 4) + 4 * h
             for act, core in ((own_ref, c), (other_ref, 1 - c)):
                 acc += lax.dot_general(
                     act[j, k], s_ref[at + 8 * core],
@@ -120,7 +120,7 @@
 
 def on_device(activations, gradients, act_basis, grad_basis):
     tokens = activations.shape[0] * 16
-    xh, y, c, xl = (lax.axis_index(a) for a in ("xh", "y", "c", "xl"))
+    xh, y, c, xl, zh = (lax.axis_index(a) for a in AXES[:5])
     turned = (xh + xl) % 2
     at = jnp.stack([y, c, turned])
 
@@ -135,16 +135,20 @@
     act_shifts = shifts(act_pair)
 
     mine, theirs = rotate(at, every, 1, grad_panels, 0)
-    rotated_grad = mine + swap(theirs, "xl")
+    act_shifts, mine = lax.optimization_barrier((act_shifts, mine))
+    act_own = jnp.stack(act_shifts)
+    theirs, act_own = lax.optimization_barrier((swap(theirs, "xl"), act_own))
+    rotated_grad = mine + theirs
     grad_square = (rotated_grad * rotated_grad).astype(jnp.bfloat16)
-    act_shifts, grad_square = lax.optimization_barrier((act_shifts, grad_square))
-    grad_square = move(
-        grad_square, AXES, lambda a, b, e, p, q, r: (p, q, r // 2, a, b, 2 * e + r % 2)
-    )
+    grad_block = jnp.stack([
+        move(
+            grad_square, AXES,
+            lambda a, b, e, p, q, r, k=k: (p, q, r // 2, a, (b + k) % 4, 2 * e + r % 2),
+        )
+        for k in range(4)
+    ])
 
-    parts = rotate(at, every, 0, both_cores(act_shifts), 1)
-    grad_square, parts = lax.optimization_barrier((grad_square, parts))
-    grad_block = to_all(grad_square, ("zh",), 4)
+    parts = rotate(at, every, 0, (act_own, swap(act_own, "c")), 1)
     parts = [move(parts[k], ("xh", "xl"), lambda a, p, k=k: (p ^ k, a)) for k in range(2)]
     rotated_act = parts[0] + parts[1]
     act_square = (rotated_act * rotated_act).astype(jnp.bfloat16)
@@ -152,8 +156,8 @@
     grad_block = to_all(grad_block, ("zl",), 4).reshape(16, 128, 256)
     acts = both_cores(shifts(act_square))
 
-    theirs = swap(correct(jnp.stack([y, c, 1 - turned]), acts, grad_block), "xl")
-    mine = correct(at, acts, grad_block)
+    theirs = swap(correct(jnp.stack([y, c, 1 - turned, zh]), acts, grad_block), "xl")
+    mine = correct(jnp.stack([y, c, turned, zh]), acts, grad_block)
     return (mine + theirs) * (1.0 / tokens)
 
 

time: 201 us -> 206 us (1.025)
  the two profiles are of different devices: /device:TPU:1 before, /device:TPU:12 now
where the time goes in v9:
time: 206 us; the launch traced here: 205 us
  waiting for transfers between devices  90.5 us (44%)
  starting transfers between devices  87.5 us (42%)
  between operations  13.8 us (7%)
  Pallas kernels  6.19 us (3%)
  other arithmetic  4.64 us (2%)
  local copies, waits for them, and re-layouts  2.68 us (1%)
    ppermute x24, starting transfers between devices, move(): return lax.ppermute(x, axes, pairs)  84 us
    ppermute x24, waiting for transfers between devices, move(): return lax.ppermute(x, axes, pairs)  62.2 us
    all_gather x1, waiting for transfers between devices, on_device(): every = lax.all_gather(both, ('zh', 'zl'), axis=0, tiled=False)  20.9 us
    all_to_all x1, waiting for transfers between devices, to_all(): return lax.all_to_all(spread, axes, split_axis=0, concat_axis=0, tiled=True)  7.36 us
  transfers between devices with their start and end apart: 26, of which 13 were waited for; matrix products, arithmetic and copies ran while one was open for 1% of the time, Pallas kernels for 2%

profile of v9, /device:TPU:12, one launch (start us, length us, event | category | flops | bytes accessed | tf_op | source)
XLA Modules:
  0.0 205.2 jit_solution(17446744012370401459)
XLA Ops:
  6.5 1.5 pad_maximum_fusion.6
  8.1 0.0 all-gather.3.cloned.1.call-update
  8.1 2.4 %collective-permute-start = (bf16[512,256]{1,0:T(8,128)(2,1)}, bf16[512,256]{1,0:T(8,128)(2,1)S(1)}, u32[]{:S(2)}, u32[]{:S(2)}) collective-permute-start(bf16[512,256]{1,0:T(8,128)(2,1)} %param.7), channel_id=1, source_target_pairs={{0,0},{16,256},{256,16},{272,272},{1,1},{17,257},{257,17},{273,273... | collective-permute-start | bytes 786440 | tf_op jit(solution)/shard_map/ppermute | solution.py:40
  10.6 2.3 %collective-permute-start.1 = (bf16[512,256]{1,0:T(8,128)(2,1)}, bf16[512,256]{1,0:T(8,128)(2,1)S(1)}, u32[]{:S(2)}, u32[]{:S(2)}) collective-permute-start(bf16[512,256]{1,0:T(8,128)(2,1)} %param.7), channel_id=1, source_target_pairs={{0,256},{16,0},{256,272},{272,16},{1,257},{17,1},{257,273},{273,17... | collective-permute-start | bytes 786440 | tf_op jit(solution)/shard_map/ppermute | solution.py:40
  12.8 11.1 %collective-permute-done = bf16[512,256]{1,0:T(8,128)(2,1)S(1)} collective-permute-done((bf16[512,256]{1,0:T(8,128)(2,1)}, bf16[512,256]{1,0:T(8,128)(2,1)S(1)}, u32[]{:S(2)}, u32[]{:S(2)}) %collective-permute-start) | collective-permute-done | bytes 262176 | tf_op jit(solution)/shard_map/ppermute | solution.py:40
  23.9 0.0 collective-permute-done.1
  23.9 0.1 pad_maximum_fusion.2
  23.9 3.5 %collective-permute-start.2 = (bf16[2,512,256]{2,1,0:T(8,128)(2,1)S(1)}, bf16[2,512,256]{2,1,0:T(8,128)(2,1)S(1)}, u32[]{:S(2)}, u32[]{:S(2)}) collective-permute-start(bf16[2,512,256]{2,1,0:T(8,128)(2,1)S(1)} %pad_maximum_fusion.2), channel_id=1, source_target_pairs={{0,64},{64,128},{128,192},{192,0},{1,65},{65,129},{129,193},{193,1... | collective-permute-start | bytes 1572872 | tf_op jit(solution)/shard_map/ppermute | solution.py:40
  27.4 2.8 %collective-permute-start.3 = (bf16[2,512,256]{2,1,0:T(8,128)(2,1)S(1)}, bf16[2,512,256]{2,1,0:T(8,128)(2,1)S(1)}, u32[]{:S(2)}, u32[]{:S(2)}) collective-permute-start(bf16[2,512,256]{2,1,0:T(8,128)(2,1)S(1)} %pad_maximum_fusion.2), channel_id=1, source_target_pairs={{0,128},{64,192},{128,0},{192,64},{1,129},{65,193},{129,1},{193,65... | collective-permute-start | bytes 1572872 | tf_op jit(solution)/shard_map/ppermute | solution.py:40
  30.3 4.3 %collective-permute-start.4 = (bf16[2,512,256]{2,1,0:T(8,128)(2,1)S(1)}, bf16[2,512,256]{2,1,0:T(8,128)(2,1)S(1)}, u32[]{:S(2)}, u32[]{:S(2)}) collective-permute-start(bf16[2,512,256]{2,1,0:T(8,128)(2,1)S(1)} %pad_maximum_fusion.2), channel_id=1, source_target_pairs={{0,192},{64,0},{128,64},{192,128},{1,193},{65,1},{129,65},{193,129... | collective-permute-start | bytes 1572872 | tf_op jit(solution)/shard_map/ppermute | solution.py:40
  34.6 2.4 %collective-permute-start.5 = (bf16[512,256]{1,0:T(8,128)(2,1)}, bf16[512,256]{1,0:T(8,128)(2,1)S(1)}, u32[]{:S(2)}, u32[]{:S(2)}) collective-permute-start(bf16[512,256]{1,0:T(8,128)(2,1)} %param.6), channel_id=1, source_target_pairs={{0,0},{16,256},{256,16},{272,272},{1,1},{17,257},{257,17},{273,273... | collective-permute-start | bytes 786440 | tf_op jit(solution)/shard_map/ppermute | solution.py:40
  37.1 1.9 collective-permute-start.6
  39.0 9.7 %collective-permute-done.5 = bf16[512,256]{1,0:T(8,128)(2,1)S(1)} collective-permute-done((bf16[512,256]{1,0:T(8,128)(2,1)}, bf16[512,256]{1,0:T(8,128)(2,1)S(1)}, u32[]{:S(2)}, u32[]{:S(2)}) %collective-permute-start.5) | collective-permute-done | bytes 262176 | tf_op jit(solution)/shard_map/ppermute | solution.py:40
  48.7 0.0 collective-permute-done.6
  48.7 0.1 pad_maximum_fusion.3
  48.8 0.0 collective-permute-done.2
  48.8 0.0 collective-permute-done.3
  48.8 5.8 %collective-permute-done.4 = bf16[2,512,256]{2,1,0:T(8,128)(2,1)S(1)} collective-permute-done((bf16[2,512,256]{2,1,0:T(8,128)(2,1)S(1)}, bf16[2,512,256]{2,1,0:T(8,128)(2,1)S(1)}, u32[]{:S(2)}, u32[]{:S(2)}) %collective-permute-start.4) | collective-permute-done | bytes 524320 | tf_op jit(solution)/shard_map/ppermute | solution.py:40
  54.6 0.3 pad_maximum_fusion.own_ref
  54.8 2.0 collective-permute-start.10
  56.9 2.4 %collective-permute-start.7 = (bf16[2,512,256]{2,1,0:T(8,128)(2,1)S(1)}, bf16[2,512,256]{2,1,0:T(8,128)(2,1)S(1)}, u32[]{:S(2)}, u32[]{:S(2)}) collective-permute-start(bf16[2,512,256]{2,1,0:T(8,128)(2,1)S(1)} %pad_maximum_fusion.3), channel_id=1, source_target_pairs={{0,64},{64,128},{128,192},{192,0},{1,65},{65,129},{129,193},{193,1... | collective-permute-start | bytes 1572872 | tf_op jit(solution)/shard_map/ppermute | solution.py:40
  59.3 2.9 %collective-permute-start.8 = (bf16[2,512,256]{2,1,0:T(8,128)(2,1)S(1)}, bf16[2,512,256]{2,1,0:T(8,128)(2,1)}, u32[]{:S(2)}, u32[]{:S(2)}) collective-permute-start(bf16[2,512,256]{2,1,0:T(8,128)(2,1)S(1)} %pad_maximum_fusion.3), channel_id=1, source_target_pairs={{0,128},{64,192},{128,0},{192,64},{1,129},{65,193},{129,1},{193,65... | collective-permute-start | bytes 1572872 | tf_op jit(solution)/shard_map/ppermute | solution.py:40
  62.2 3.9 %collective-permute-start.9 = (bf16[2,512,256]{2,1,0:T(8,128)(2,1)S(1)}, bf16[2,512,256]{2,1,0:T(8,128)(2,1)}, u32[]{:S(2)}, u32[]{:S(2)}) collective-permute-start(bf16[2,512,256]{2,1,0:T(8,128)(2,1)S(1)} %pad_maximum_fusion.3), channel_id=1, source_target_pairs={{0,192},{64,0},{128,64},{192,128},{1,193},{65,1},{129,65},{193,129... | collective-permute-start | bytes 1572872 | tf_op jit(solution)/shard_map/ppermute | solution.py:40
  66.2 0.1 pad_add_fusion.1.at_ref
  66.3 20.9 %all-gather.3.cloned.1.call-done = bf16[32,128,256]{2,1,0:T(8,128)(2,1)} async-done(((bf16[2,128,256]{2,1,0:T(8,128)(2,1)}), bf16[32,128,256]{2,1,0:T(8,128)(2,1)}) %all-gather.3.cloned.1.call-update) | async-done | bytes 2097168 | tf_op jit(solution)/shard_map/all_gather | solution.py:129
  87.2 1.6 copy-done
  88.8 2.4 %shard_map.46 = (f32[128,256]{1,0:T(8,128)S(1)}, f32[128,256]{1,0:T(8,128)S(1)}) custom-call(s32[3]{0:T(128)S(1)} %pad_add_fusion.1.at_ref, bf16[16,2,128,256]{3,2,1,0:T(8,128)(2,1)S(1)} %bitcast.31, bf16[4,2,512,256]{3,2,1,0:T(8,128)(2,1)S(1)} %pad_maximum_fusion.own_ref, bf16[4,2,512,256]{3,2,1,0:T(8,128)(2,1)} %collective-permute-done.10.other_ref), custom_call_target="tpu_custom_call" | custom-call | tf_op jit(solution)/shard_map/pallas_call | solution.py:84
  91.2 0.0 collective-permute-done.7
  91.2 0.0 collective-permute-done.9
  91.2 2.9 %collective-permute-start.11 = (f32[128,256]{1,0:T(8,128)S(1)}, f32[128,256]{1,0:T(8,128)S(1)}, u32[]{:S(2)}, u32[]{:S(2)}) collective-permute-start(f32[128,256]{1,0:T(8,128)S(1)} %get-tuple-element.40), channel_id=1, source_target_pairs={{0,16},{16,0},{1,17},{17,1},{2,18},{18,2},{3,19},{19,3},{4,20},{20... | collective-permute-start | bytes 393224 | tf_op jit(solution)/shard_map/ppermute | solution.py:40
  94.1 1.5 pad_maximum_fusion.1.own_ref
  95.6 2.5 %collective-permute-done.11 = f32[128,256]{1,0:T(8,128)S(1)} collective-permute-done((f32[128,256]{1,0:T(8,128)S(1)}, f32[128,256]{1,0:T(8,128)S(1)}, u32[]{:S(2)}, u32[]{:S(2)}) %collective-permute-start.11) | collective-permute-done | bytes 131104 | tf_op jit(solution)/shard_map/ppermute | solution.py:40
  98.1 1.9 collective-permute-start.16
  100.0 4.1 %collective-permute-done.16.other_ref = bf16[4,2,512,256]{3,2,1,0:T(8,128)(2,1)S(1)} collective-permute-done((bf16[4,2,512,256]{3,2,1,0:T(8,128)(2,1)S(1)}, bf16[4,2,512,256]{3,2,1,0:T(8,128)(2,1)S(1)}, u32[]{:S(2)}, u32[]{:S(2)}) %collective-permute-start.16) | collective-permute-done | bytes 2097184 | tf_op jit(solution)/shard_map/ppermute | solution.py:40
  104.1 1.3 shard_map.47
  105.4 2.5 %collective-permute-start.17 = (f32[2,128,256]{2,1,0:T(8,128)S(1)}, f32[2,128,256]{2,1,0:T(8,128)S(1)}, u32[]{:S(2)}, u32[]{:S(2)}) collective-permute-start(f32[2,128,256]{2,1,0:T(8,128)S(1)} %get-tuple-element.47), channel_id=1, source_target_pairs={{0,0},{16,256},{256,16},{272,272},{1,1},{17,257},{257,17},{273,273... | collective-permute-start | bytes 786440 | tf_op jit(solution)/shard_map/ppermute | solution.py:40
  107.9 1.9 collective-permute-start.18
  109.8 5.8 %collective-permute-start.12 = (bf16[128,256]{1,0:T(8,128)(2,1)S(1)}, bf16[128,256]{1,0:T(8,128)(2,1)S(1)}, u32[]{:S(2)}, u32[]{:S(2)}) collective-permute-start(bf16[128,256]{1,0:T(8,128)(2,1)S(1)} %multiply_convert_fusion.1), channel_id=1, source_target_pairs={{0,0},{1,1},{2,32},{3,33},{4,64},{5,65},{6,96},{7,97},{8,128},{9,1... | collective-permute-start | bytes 196616 | tf_op jit(solution)/shard_map/ppermute | solution.py:40
  115.7 12.1 %collective-permute-start.13 = (bf16[128,256]{1,0:T(8,128)(2,1)S(1)}, bf16[128,256]{1,0:T(8,128)(2,1)S(1)}, u32[]{:S(2)}, u32[]{:S(2)}) collective-permute-start(bf16[128,256]{1,0:T(8,128)(2,1)S(1)} %multiply_convert_fusion.1), channel_id=1, source_target_pairs={{0,4},{1,5},{2,36},{3,37},{4,68},{5,69},{6,100},{7,101},{8,132},{9... | collective-permute-start | bytes 196616 | tf_op jit(solution)/shard_map/ppermute | solution.py:40
  127.8 11.4 %collective-permute-start.14 = (bf16[128,256]{1,0:T(8,128)(2,1)S(1)}, bf16[128,256]{1,0:T(8,128)(2,1)S(1)}, u32[]{:S(2)}, u32[]{:S(2)}) collective-permute-start(bf16[128,256]{1,0:T(8,128)(2,1)S(1)} %multiply_convert_fusion.1), channel_id=1, source_target_pairs={{0,8},{1,9},{2,40},{3,41},{4,72},{5,73},{6,104},{7,105},{8,136},{9... | collective-permute-start | bytes 196616 | tf_op jit(solution)/shard_map/ppermute | solution.py:40
  139.3 1.9 collective-permute-start.15
  141.2 0.0 collective-permute-done.13
  141.2 4.0 %collective-permute-done.14 = bf16[128,256]{1,0:T(8,128)(2,1)S(1)} collective-permute-done((bf16[128,256]{1,0:T(8,128)(2,1)S(1)}, bf16[128,256]{1,0:T(8,128)(2,1)S(1)}, u32[]{:S(2)}, u32[]{:S(2)}) %collective-permute-start.14) | collective-permute-done | bytes 65568 | tf_op jit(solution)/shard_map/ppermute | solution.py:40
  145.3 7.9 %collective-permute-done.15 = bf16[128,256]{1,0:T(8,128)(2,1)S(1)} collective-permute-done((bf16[128,256]{1,0:T(8,128)(2,1)S(1)}, bf16[128,256]{1,0:T(8,128)(2,1)S(1)}, u32[]{:S(2)}, u32[]{:S(2)}) %collective-permute-start.15) | collective-permute-done | bytes 65568 | tf_op jit(solution)/shard_map/ppermute | solution.py:40
  153.2 0.0 collective-permute-done.18
  153.2 1.1 broadcast_in_dim.2
  154.3 3.5 %all-to-all-start = ((bf16[4,4,128,256]{3,2,1,0:T(8,128)(2,1)}), bf16[4,4,128,256]{3,2,1,0:T(8,128)(2,1)S(1)}, u32[]{:S(2)}, u32[]{:S(2)}) async-start(bf16[4,4,128,256]{3,2,1,0:T(8,128)(2,1)} %broadcast_in_dim.2), calls=%async_computation | async-start | bytes 2097152 | tf_op jit(solution)/shard_map/all_to_all | solution.py:18
  157.8 1.9 collective-permute-start.19
  159.8 1.9 collective-permute-start.20
  161.7 3.9 %collective-permute-start.21 = (bf16[2,128,256]{2,1,0:T(8,128)(2,1)S(1)}, bf16[2,128,256]{2,1,0:T(8,128)(2,1)S(1)}, u32[]{:S(2)}, u32[]{:S(2)}) collective-permute-start(bf16[2,128,256]{2,1,0:T(8,128)(2,1)S(1)} %multiply_convert_fusion), channel_id=1, source_target_pairs={{0,192},{64,0},{128,64},{192,128},{1,193},{65,1},{129,65},{193,129... | collective-permute-start | bytes 393224 | tf_op jit(solution)/shard_map/ppermute | solution.py:40
  165.6 0.0 collective-permute-done.19
  165.6 3.2 %collective-permute-done.20 = bf16[2,128,256]{2,1,0:T(8,128)(2,1)S(1)} collective-permute-done((bf16[2,128,256]{2,1,0:T(8,128)(2,1)S(1)}, bf16[2,128,256]{2,1,0:T(8,128)(2,1)S(1)}, u32[]{:S(2)}, u32[]{:S(2)}) %collective-permute-start.20) | collective-permute-done | bytes 131104 | tf_op jit(solution)/shard_map/ppermute | solution.py:40
  168.8 1.4 collective-permute-done.21
  170.2 0.1 pad_maximum_fusion.4.own_ref
  170.3 1.9 collective-permute-start.22
  172.2 0.1 add_add_fusion.1.at_ref
  172.3 1.8 collective-permute-done.22.other_ref
  174.1 7.4 %all-to-all-done = bf16[4,4,128,256]{3,2,1,0:T(8,128)(2,1)S(1)} async-done(((bf16[4,4,128,256]{3,2,1,0:T(8,128)(2,1)}), bf16[4,4,128,256]{3,2,1,0:T(8,128)(2,1)S(1)}, u32[]{:S(2)}, u32[]{:S(2)}) %all-to-all-start) | async-done | bytes 1048608 | tf_op jit(solution)/shard_map/all_to_all | solution.py:18
  181.5 1.3 shard_map.49
  182.7 2.7 %collective-permute-start.23 = (f32[256,512]{1,0:T(8,128)S(1)}, f32[256,512]{1,0:T(8,128)S(1)}, u32[]{:S(2)}, u32[]{:S(2)}) collective-permute-start(f32[256,512]{1,0:T(8,128)S(1)} %shard_map.49), channel_id=1, source_target_pairs={{0,16},{16,0},{1,17},{17,1},{2,18},{18,2},{3,19},{19,3},{4,20},{20... | collective-permute-start | bytes 1572872 | tf_op jit(solution)/shard_map/ppermute | solution.py:40
  185.5 0.1 add_add_fusion.at_ref
  185.5 1.3 shard_map.48
  186.8 10.7 %collective-permute-done.23 = f32[256,512]{1,0:T(8,128)S(1)} collective-permute-done((f32[256,512]{1,0:T(8,128)S(1)}, f32[256,512]{1,0:T(8,128)S(1)}, u32[]{:S(2)}, u32[]{:S(2)}) %collective-permute-start.23) | collective-permute-done | bytes 524320 | tf_op jit(solution)/shard_map/ppermute | solution.py:40
  197.5 0.9 add_multiply_fusion
  (9 shorter events, 0.1 us)
Async XLA Ops:
  6.5 80.7 %all-gather.3.cloned.1.call-start = ((), (), s32[]{:S(2)}) async-start(), calls=%async_computation.1 | async-start | bytes 2228224 | tf_op jit(solution)/shard_map/all_gather | solution.py:129
  8.1 15.8 %collective-permute-start = (bf16[512,256]{1,0:T(8,128)(2,1)}, bf16[512,256]{1,0:T(8,128)(2,1)S(1)}, u32[]{:S(2)}, u32[]{:S(2)}) collective-permute-start(bf16[512,256]{1,0:T(8,128)(2,1)} %param.7), channel_id=1, source_target_pairs={{0,0},{16,256},{256,16},{272,272},{1,1},{17,257},{257,17},{273,273... | collective-permute-start | bytes 786440 | tf_op jit(solution)/shard_map/ppermute | solution.py:40
  10.6 13.3 %collective-permute-start.1 = (bf16[512,256]{1,0:T(8,128)(2,1)}, bf16[512,256]{1,0:T(8,128)(2,1)S(1)}, u32[]{:S(2)}, u32[]{:S(2)}) collective-permute-start(bf16[512,256]{1,0:T(8,128)(2,1)} %param.7), channel_id=1, source_target_pairs={{0,256},{16,0},{256,272},{272,16},{1,257},{17,1},{257,273},{273,17... | collective-permute-start | bytes 786440 | tf_op jit(solution)/shard_map/ppermute | solution.py:40
  23.9 24.8 %collective-permute-start.2 = (bf16[2,512,256]{2,1,0:T(8,128)(2,1)S(1)}, bf16[2,512,256]{2,1,0:T(8,128)(2,1)S(1)}, u32[]{:S(2)}, u32[]{:S(2)}) collective-permute-start(bf16[2,512,256]{2,1,0:T(8,128)(2,1)S(1)} %pad_maximum_fusion.2), channel_id=1, source_target_pairs={{0,64},{64,128},{128,192},{192,0},{1,65},{65,129},{129,193},{193,1... | collective-permute-start | bytes 1572872 | tf_op jit(solution)/shard_map/ppermute | solution.py:40
  27.4 21.4 %collective-permute-start.3 = (bf16[2,512,256]{2,1,0:T(8,128)(2,1)S(1)}, bf16[2,512,256]{2,1,0:T(8,128)(2,1)S(1)}, u32[]{:S(2)}, u32[]{:S(2)}) collective-permute-start(bf16[2,512,256]{2,1,0:T(8,128)(2,1)S(1)} %pad_maximum_fusion.2), channel_id=1, source_target_pairs={{0,128},{64,192},{128,0},{192,64},{1,129},{65,193},{129,1},{193,65... | collective-permute-start | bytes 1572872 | tf_op jit(solution)/shard_map/ppermute | solution.py:40
  30.3 24.3 %collective-permute-start.4 = (bf16[2,512,256]{2,1,0:T(8,128)(2,1)S(1)}, bf16[2,512,256]{2,1,0:T(8,128)(2,1)S(1)}, u32[]{:S(2)}, u32[]{:S(2)}) collective-permute-start(bf16[2,512,256]{2,1,0:T(8,128)(2,1)S(1)} %pad_maximum_fusion.2), channel_id=1, source_target_pairs={{0,192},{64,0},{128,64},{192,128},{1,193},{65,1},{129,65},{193,129... | collective-permute-start | bytes 1572872 | tf_op jit(solution)/shard_map/ppermute | solution.py:40
  34.6 14.1 %collective-permute-start.5 = (bf16[512,256]{1,0:T(8,128)(2,1)}, bf16[512,256]{1,0:T(8,128)(2,1)S(1)}, u32[]{:S(2)}, u32[]{:S(2)}) collective-permute-start(bf16[512,256]{1,0:T(8,128)(2,1)} %param.6), channel_id=1, source_target_pairs={{0,0},{16,256},{256,16},{272,272},{1,1},{17,257},{257,17},{273,273... | collective-permute-start | bytes 786440 | tf_op jit(solution)/shard_map/ppermute | solution.py:40
  37.1 11.6 %collective-permute-start.6 = (bf16[512,256]{1,0:T(8,128)(2,1)}, bf16[512,256]{1,0:T(8,128)(2,1)S(1)}, u32[]{:S(2)}, u32[]{:S(2)}) collective-permute-start(bf16[512,256]{1,0:T(8,128)(2,1)} %param.6), channel_id=1, source_target_pairs={{0,256},{16,0},{256,272},{272,16},{1,257},{17,1},{257,273},{273,17... | collective-permute-start | bytes 786440 | tf_op jit(solution)/shard_map/ppermute | solution.py:40
  54.8 11.4 %collective-permute-start.10 = (bf16[4,2,512,256]{3,2,1,0:T(8,128)(2,1)S(1)}, bf16[4,2,512,256]{3,2,1,0:T(8,128)(2,1)}, u32[]{:S(2)}, u32[]{:S(2)}) collective-permute-start(bf16[4,2,512,256]{3,2,1,0:T(8,128)(2,1)S(1)} %pad_maximum_fusion.own_ref), channel_id=1, source_target_pairs={{0,32},{32,0},{1,33},{33,1},{2,34},{34,2},{3,35},{35,3},{4,36},{36... | collective-permute-start | bytes 6291464 | tf_op jit(solution)/shard_map/ppermute | solution.py:40
  56.9 34.3 %collective-permute-start.7 = (bf16[2,512,256]{2,1,0:T(8,128)(2,1)S(1)}, bf16[2,512,256]{2,1,0:T(8,128)(2,1)S(1)}, u32[]{:S(2)}, u32[]{:S(2)}) collective-permute-start(bf16[2,512,256]{2,1,0:T(8,128)(2,1)S(1)} %pad_maximum_fusion.3), channel_id=1, source_target_pairs={{0,64},{64,128},{128,192},{192,0},{1,65},{65,129},{129,193},{193,1... | collective-permute-start | bytes 1572872 | tf_op jit(solution)/shard_map/ppermute | solution.py:40
  59.3 31.9 %collective-permute-start.8 = (bf16[2,512,256]{2,1,0:T(8,128)(2,1)S(1)}, bf16[2,512,256]{2,1,0:T(8,128)(2,1)}, u32[]{:S(2)}, u32[]{:S(2)}) collective-permute-start(bf16[2,512,256]{2,1,0:T(8,128)(2,1)S(1)} %pad_maximum_fusion.3), channel_id=1, source_target_pairs={{0,128},{64,192},{128,0},{192,64},{1,129},{65,193},{129,1},{193,65... | collective-permute-start | bytes 1572872 | tf_op jit(solution)/shard_map/ppermute | solution.py:40
  62.2 29.0 %collective-permute-start.9 = (bf16[2,512,256]{2,1,0:T(8,128)(2,1)S(1)}, bf16[2,512,256]{2,1,0:T(8,128)(2,1)}, u32[]{:S(2)}, u32[]{:S(2)}) collective-permute-start(bf16[2,512,256]{2,1,0:T(8,128)(2,1)S(1)} %pad_maximum_fusion.3), channel_id=1, source_target_pairs={{0,192},{64,0},{128,64},{192,128},{1,193},{65,1},{129,65},{193,129... | collective-permute-start | bytes 1572872 | tf_op jit(solution)/shard_map/ppermute | solution.py:40
  87.2 1.6 copy-start
  91.2 6.9 %collective-permute-start.11 = (f32[128,256]{1,0:T(8,128)S(1)}, f32[128,256]{1,0:T(8,128)S(1)}, u32[]{:S(2)}, u32[]{:S(2)}) collective-permute-start(f32[128,256]{1,0:T(8,128)S(1)} %get-tuple-element.40), channel_id=1, source_target_pairs={{0,16},{16,0},{1,17},{17,1},{2,18},{18,2},{3,19},{19,3},{4,20},{20... | collective-permute-start | bytes 393224 | tf_op jit(solution)/shard_map/ppermute | solution.py:40
  98.1 6.0 %collective-permute-start.16 = (bf16[4,2,512,256]{3,2,1,0:T(8,128)(2,1)S(1)}, bf16[4,2,512,256]{3,2,1,0:T(8,128)(2,1)S(1)}, u32[]{:S(2)}, u32[]{:S(2)}) collective-permute-start(bf16[4,2,512,256]{3,2,1,0:T(8,128)(2,1)S(1)} %pad_maximum_fusion.1.own_ref), channel_id=1, source_target_pairs={{0,32},{32,0},{1,33},{33,1},{2,34},{34,2},{3,35},{35,3},{4,36},{36... | collective-permute-start | bytes 6291464 | tf_op jit(solution)/shard_map/ppermute | solution.py:40
  105.4 47.7 %collective-permute-start.17 = (f32[2,128,256]{2,1,0:T(8,128)S(1)}, f32[2,128,256]{2,1,0:T(8,128)S(1)}, u32[]{:S(2)}, u32[]{:S(2)}) collective-permute-start(f32[2,128,256]{2,1,0:T(8,128)S(1)} %get-tuple-element.47), channel_id=1, source_target_pairs={{0,0},{16,256},{256,16},{272,272},{1,1},{17,257},{257,17},{273,273... | collective-permute-start | bytes 786440 | tf_op jit(solution)/shard_map/ppermute | solution.py:40
  107.9 45.3 %collective-permute-start.18 = (f32[2,128,256]{2,1,0:T(8,128)S(1)}, f32[2,128,256]{2,1,0:T(8,128)S(1)}, u32[]{:S(2)}, u32[]{:S(2)}) collective-permute-start(f32[2,128,256]{2,1,0:T(8,128)S(1)} %get-tuple-element.48), channel_id=1, source_target_pairs={{0,256},{16,0},{256,272},{272,16},{1,257},{17,1},{257,273},{273,17... | collective-permute-start | bytes 786440 | tf_op jit(solution)/shard_map/ppermute | solution.py:40
  109.8 29.4 %collective-permute-start.12 = (bf16[128,256]{1,0:T(8,128)(2,1)S(1)}, bf16[128,256]{1,0:T(8,128)(2,1)S(1)}, u32[]{:S(2)}, u32[]{:S(2)}) collective-permute-start(bf16[128,256]{1,0:T(8,128)(2,1)S(1)} %multiply_convert_fusion.1), channel_id=1, source_target_pairs={{0,0},{1,1},{2,32},{3,33},{4,64},{5,65},{6,96},{7,97},{8,128},{9,1... | collective-permute-start | bytes 196616 | tf_op jit(solution)/shard_map/ppermute | solution.py:40
  115.7 25.5 %collective-permute-start.13 = (bf16[128,256]{1,0:T(8,128)(2,1)S(1)}, bf16[128,256]{1,0:T(8,128)(2,1)S(1)}, u32[]{:S(2)}, u32[]{:S(2)}) collective-permute-start(bf16[128,256]{1,0:T(8,128)(2,1)S(1)} %multiply_convert_fusion.1), channel_id=1, source_target_pairs={{0,4},{1,5},{2,36},{3,37},{4,68},{5,69},{6,100},{7,101},{8,132},{9... | collective-permute-start | bytes 196616 | tf_op jit(solution)/shard_map/ppermute | solution.py:40
  127.8 17.4 %collective-permute-start.14 = (bf16[128,256]{1,0:T(8,128)(2,1)S(1)}, bf16[128,256]{1,0:T(8,128)(2,1)S(1)}, u32[]{:S(2)}, u32[]{:S(2)}) collective-permute-start(bf16[128,256]{1,0:T(8,128)(2,1)S(1)} %multiply_convert_fusion.1), channel_id=1, source_target_pairs={{0,8},{1,9},{2,40},{3,41},{4,72},{5,73},{6,104},{7,105},{8,136},{9... | collective-permute-start | bytes 196616 | tf_op jit(solution)/shard_map/ppermute | solution.py:40
  139.3 13.8 %collective-permute-start.15 = (bf16[128,256]{1,0:T(8,128)(2,1)S(1)}, bf16[128,256]{1,0:T(8,128)(2,1)S(1)}, u32[]{:S(2)}, u32[]{:S(2)}) collective-permute-start(bf16[128,256]{1,0:T(8,128)(2,1)S(1)} %multiply_convert_fusion.1), channel_id=1, source_target_pairs={{0,12},{1,13},{2,44},{3,45},{4,76},{5,77},{6,108},{7,109},{8,140},... | collective-permute-start | bytes 196616 | tf_op jit(solution)/shard_map/ppermute | solution.py:40
  154.3 27.2 %all-to-all-start = ((bf16[4,4,128,256]{3,2,1,0:T(8,128)(2,1)}), bf16[4,4,128,256]{3,2,1,0:T(8,128)(2,1)S(1)}, u32[]{:S(2)}, u32[]{:S(2)}) async-start(bf16[4,4,128,256]{3,2,1,0:T(8,128)(2,1)} %broadcast_in_dim.2), calls=%async_computation | async-start | bytes 2097152 | tf_op jit(solution)/shard_map/all_to_all | solution.py:18
  157.8 7.8 %collective-permute-start.19 = (bf16[2,128,256]{2,1,0:T(8,128)(2,1)S(1)}, bf16[2,128,256]{2,1,0:T(8,128)(2,1)S(1)}, u32[]{:S(2)}, u32[]{:S(2)}) collective-permute-start(bf16[2,128,256]{2,1,0:T(8,128)(2,1)S(1)} %multiply_convert_fusion), channel_id=1, source_target_pairs={{0,64},{64,128},{128,192},{192,0},{1,65},{65,129},{129,193},{193,1... | collective-permute-start | bytes 393224 | tf_op jit(solution)/shard_map/ppermute | solution.py:40
  159.8 9.1 %collective-permute-start.20 = (bf16[2,128,256]{2,1,0:T(8,128)(2,1)S(1)}, bf16[2,128,256]{2,1,0:T(8,128)(2,1)S(1)}, u32[]{:S(2)}, u32[]{:S(2)}) collective-permute-start(bf16[2,128,256]{2,1,0:T(8,128)(2,1)S(1)} %multiply_convert_fusion), channel_id=1, source_target_pairs={{0,128},{64,192},{128,0},{192,64},{1,129},{65,193},{129,1},{193,65... | collective-permute-start | bytes 393224 | tf_op jit(solution)/shard_map/ppermute | solution.py:40
  161.7 8.6 %collective-permute-start.21 = (bf16[2,128,256]{2,1,0:T(8,128)(2,1)S(1)}, bf16[2,128,256]{2,1,0:T(8,128)(2,1)S(1)}, u32[]{:S(2)}, u32[]{:S(2)}) collective-permute-start(bf16[2,128,256]{2,1,0:T(8,128)(2,1)S(1)} %multiply_convert_fusion), channel_id=1, source_target_pairs={{0,192},{64,0},{128,64},{192,128},{1,193},{65,1},{129,65},{193,129... | collective-permute-start | bytes 393224 | tf_op jit(solution)/shard_map/ppermute | solution.py:40
  170.3 3.8 %collective-permute-start.22 = (bf16[4,2,128,256]{3,2,1,0:T(8,128)(2,1)S(1)}, bf16[4,2,128,256]{3,2,1,0:T(8,128)(2,1)S(1)}, u32[]{:S(2)}, u32[]{:S(2)}) collective-permute-start(bf16[4,2,128,256]{3,2,1,0:T(8,128)(2,1)S(1)} %pad_maximum_fusion.4.own_ref), channel_id=1, source_target_pairs={{0,32},{32,0},{1,33},{33,1},{2,34},{34,2},{3,35},{35,3},{4,36},{36... | collective-permute-start | bytes 1572872 | tf_op jit(solution)/shard_map/ppermute | solution.py:40
  182.7 14.8 %collective-permute-start.23 = (f32[256,512]{1,0:T(8,128)S(1)}, f32[256,512]{1,0:T(8,128)S(1)}, u32[]{:S(2)}, u32[]{:S(2)}) collective-permute-start(f32[256,512]{1,0:T(8,128)S(1)} %shard_map.49), channel_id=1, source_target_pairs={{0,16},{16,0},{1,17},{17,1},{2,18},{18,2},{3,19},{19,3},{4,20},{20... | collective-permute-start | bytes 1572872 | tf_op jit(solution)/shard_map/ppermute | solution.py:40
Sparse Core Ops, SparseCore 0:
  9.4 77.7 all-gather.2

commit v10 on v6

--- a/solution.py
+++ b/solution.py
@@ -9,6 +9,7 @@
 AXES = ("xh", "y", "c", "xl", "zh", "zl")
 SIZES = (2, 4, 2, 2, 4, 4)
 VMEM = pl.BlockSpec(memory_space=pltpu.VMEM)
+HBM = pl.BlockSpec(memory_space=pltpu.HBM)
 SMEM = pl.BlockSpec(memory_space=pltpu.SMEM)
 PARAMS = pltpu.CompilerParams(vmem_limit_bytes=40 * 1024 * 1024)
 
@@ -44,18 +45,22 @@
     return jnp.dot(a, b, preferred_element_type=jnp.float32)
 
 
-def rotate_kernel(at_ref, x_ref, own_ref, other_ref, first_ref, second_ref):
+def rotate_kernel(part, at_ref, x_hbm, own_ref, other_hbm, first_ref, second_ref, x_ref, other_ref, sems):
+    copies = [
+        pltpu.make_async_copy(x_hbm.at[:, part], x_ref, sems.at[0]),
+        pltpu.make_async_copy(other_hbm, other_ref, sems.at[1]),
+    ]
+    for copy in copies:
+        copy.start()
     y, c, turned = at_ref[0], at_ref[1], at_ref[2]
-    sums = []
-    for k in range(2):
-        acc = jnp.zeros(x_ref.shape[2:], jnp.float32)
-        for j in range(4):
-            at = 4 * lax.rem(y + 4 - j, 4)
-            for h in range(2):
-                rows = slice(256 * h, 256 * h + 256)
-                acc += dot(x_ref[at + 2 * c + h, 0], own_ref[j, k, rows, :])
-                acc += dot(x_ref[at + 2 * (1 - c) + h, 0], other_ref[j, k, rows, :])
-        sums.append(acc)
+    sums = [jnp.zeros(x_ref.shape[1:], jnp.float32)] * 2
+    for copy, basis, core in ((copies[0], own_ref, c), (copies[1], other_ref, 1 - c)):
+        copy.wait()
+        for k in range(2):
+            for j in range(4):
+                at = 4 * lax.rem(y + 4 - j, 4) + 2 * core
+                for h in range(2):
+                    sums[k] += dot(x_ref[at + h], basis[j, k, 256 * h:256 * h + 256, :])
     near, far = sums
     mine, theirs = jnp.where(turned == 0, near, far), jnp.where(turned == 0, far, near)
     if len(first_ref.shape) == 2:
@@ -81,14 +86,20 @@
 
 def rotate(at, x, part, basis, paired):
     out = jax.ShapeDtypeStruct((2,) * paired + x.shape[2:], jnp.float32)
+    own, other = basis
+    x, other = (pltpu.with_memory_space_constraint(v, pltpu.HBM) for v in (x, other))
     return pl.pallas_call(
-        rotate_kernel,
-        grid=(1,),
+        functools.partial(rotate_kernel, part),
         out_shape=[out, out],
-        in_specs=[SMEM, pl.BlockSpec((16, 1) + x.shape[2:], lambda i: (0, part, 0, 0)), VMEM, VMEM],
+        in_specs=[SMEM, HBM, VMEM, HBM],
         out_specs=[VMEM, VMEM],
+        scratch_shapes=[
+            pltpu.VMEM((16,) + x.shape[2:], x.dtype),
+            pltpu.VMEM(other.shape, other.dtype),
+            pltpu.SemaphoreType.DMA((2,)),
+        ],
         compiler_params=PARAMS,
-    )(at, x, *basis)
+    )(at, x, own, other)
 
 
 def correct(at, acts, grads):
@@ -137,14 +148,13 @@
     mine, theirs = rotate(at, every, 1, grad_panels, 0)
     rotated_grad = mine + swap(theirs, "xl")
     grad_square = (rotated_grad * rotated_grad).astype(jnp.bfloat16)
-    act_shifts, grad_square = lax.optimization_barrier((act_shifts, grad_square))
     grad_square = move(
         grad_square, AXES, lambda a, b, e, p, q, r: (p, q, r // 2, a, b, 2 * e + r % 2)
     )
+    act_shifts, grad_square = lax.optimization_barrier((act_shifts, grad_square))
+    grad_block = to_all(grad_square, ("zh", "zl"), 16)
 
     parts = rotate(at, every, 0, both_cores(act_shifts), 1)
-    grad_square, parts = lax.optimization_barrier((grad_square, parts))
-    grad_block = to_all(grad_square, ("zh", "zl"), 16)
     parts = [move(parts[k], ("xh", "xl"), lambda a, p, k=k: (p ^ k, a)) for k in range(2)]
     rotated_act = parts[0] + parts[1]
     act_square = (rotated_act * rotated_act).astype(jnp.bfloat16)

time: 202 us -> 195 us (0.965)
  the two profiles are of different devices: /device:TPU:13 before, /device:TPU:1 now
where the time goes in v10:
time: 195 us
  starting transfers between devices  107 us (55%)
  waiting for transfers between devices  58.1 us (30%)
  between operations  13.7 us (7%)
  Pallas kernels  8.37 us (4%)
  other arithmetic  4.53 us (2%)
  local copies, waits for them, and re-layouts  2.44 us (1%)
    ppermute x21, starting transfers between devices, move(): return lax.ppermute(x, axes, pairs)  94.8 us
    ppermute x21, waiting for transfers between devices, move(): return lax.ppermute(x, axes, pairs)  43.8 us
    all_gather x1, waiting for transfers between devices, on_device(): every = lax.all_gather(both, ('zh', 'zl'), axis=0, tiled=False)  14.3 us
    all_to_all x1, starting transfers between devices, to_all(): return lax.all_to_all(spread, axes, split_axis=0, concat_axis=0, tiled=True)  12.6 us
    pallas_call x2, Pallas kernels, rotate(): pl.pallas_call(functools.partial(rotate_kernel, part), out_shape=[out, ou...  5.84 us
  transfers between devices with their start and end apart: 23, of which 13 were waited for; matrix products, arithmetic and copies ran while one was open for 1% of the time, Pallas kernels for 4%

profile of v10, /device:TPU:1, one launch (start us, length us, event | category | flops | bytes accessed | tf_op | source)
XLA Modules:
  0.0 194.5 jit_solution(13781978422277633667)
XLA Ops:
  6.5 0.0 all-gather.3.cloned.1.call-start
  6.5 1.5 pad_maximum_fusion.5
  8.1 0.0 all-gather.3.cloned.1.call-update
  8.1 1.6 collective-permute-start
  9.7 6.0 %collective-permute-start.1 = (bf16[512,256]{1,0:T(8,128)(2,1)}, bf16[512,256]{1,0:T(8,128)(2,1)S(1)}, u32[]{:S(2)}, u32[]{:S(2)}) collective-permute-start(bf16[512,256]{1,0:T(8,128)(2,1)} %param.7), channel_id=1, source_target_pairs={{0,256},{16,0},{256,272},{272,16},{1,257},{17,1},{257,273},{273,17... | collective-permute-start | bytes 786440 | tf_op jit(solution)/shard_map/ppermute | solution.py:41
  15.8 0.0 collective-permute-done
  15.8 3.6 %collective-permute-done.1 = bf16[512,256]{1,0:T(8,128)(2,1)S(1)} collective-permute-done((bf16[512,256]{1,0:T(8,128)(2,1)}, bf16[512,256]{1,0:T(8,128)(2,1)S(1)}, u32[]{:S(2)}, u32[]{:S(2)}) %collective-permute-start.1) | collective-permute-done | bytes 262176 | tf_op jit(solution)/shard_map/ppermute | solution.py:41
  19.4 0.1 pad_maximum_fusion.2
  19.5 4.9 %collective-permute-start.2 = (bf16[2,512,256]{2,1,0:T(8,128)(2,1)S(1)}, bf16[2,512,256]{2,1,0:T(8,128)(2,1)S(1)}, u32[]{:S(2)}, u32[]{:S(2)}) collective-permute-start(bf16[2,512,256]{2,1,0:T(8,128)(2,1)S(1)} %pad_maximum_fusion.2), channel_id=1, source_target_pairs={{0,64},{64,128},{128,192},{192,0},{1,65},{65,129},{129,193},{193,1... | collective-permute-start | bytes 1572872 | tf_op jit(solution)/shard_map/ppermute | solution.py:41
  24.4 4.5 %collective-permute-start.3 = (bf16[2,512,256]{2,1,0:T(8,128)(2,1)S(1)}, bf16[2,512,256]{2,1,0:T(8,128)(2,1)S(1)}, u32[]{:S(2)}, u32[]{:S(2)}) collective-permute-start(bf16[2,512,256]{2,1,0:T(8,128)(2,1)S(1)} %pad_maximum_fusion.2), channel_id=1, source_target_pairs={{0,128},{64,192},{128,0},{192,64},{1,129},{65,193},{129,1},{193,65... | collective-permute-start | bytes 1572872 | tf_op jit(solution)/shard_map/ppermute | solution.py:41
  28.9 3.0 %collective-permute-start.4 = (bf16[2,512,256]{2,1,0:T(8,128)(2,1)S(1)}, bf16[2,512,256]{2,1,0:T(8,128)(2,1)S(1)}, u32[]{:S(2)}, u32[]{:S(2)}) collective-permute-start(bf16[2,512,256]{2,1,0:T(8,128)(2,1)S(1)} %pad_maximum_fusion.2), channel_id=1, source_target_pairs={{0,192},{64,0},{128,64},{192,128},{1,193},{65,1},{129,65},{193,129... | collective-permute-start | bytes 1572872 | tf_op jit(solution)/shard_map/ppermute | solution.py:41
  31.9 1.6 collective-permute-start.5
  33.5 7.7 %collective-permute-start.6 = (bf16[512,256]{1,0:T(8,128)(2,1)}, bf16[512,256]{1,0:T(8,128)(2,1)S(1)}, u32[]{:S(2)}, u32[]{:S(2)}) collective-permute-start(bf16[512,256]{1,0:T(8,128)(2,1)} %param.6), channel_id=1, source_target_pairs={{0,256},{16,0},{256,272},{272,16},{1,257},{17,1},{257,273},{273,17... | collective-permute-start | bytes 786440 | tf_op jit(solution)/shard_map/ppermute | solution.py:41
  41.2 0.0 collective-permute-done.5
  41.2 3.9 %collective-permute-done.6 = bf16[512,256]{1,0:T(8,128)(2,1)S(1)} collective-permute-done((bf16[512,256]{1,0:T(8,128)(2,1)}, bf16[512,256]{1,0:T(8,128)(2,1)S(1)}, u32[]{:S(2)}, u32[]{:S(2)}) %collective-permute-start.6) | collective-permute-done | bytes 262176 | tf_op jit(solution)/shard_map/ppermute | solution.py:41
  45.1 0.1 pad_maximum_fusion.3
  45.2 0.0 collective-permute-done.2
  45.2 3.4 %collective-permute-done.3 = bf16[2,512,256]{2,1,0:T(8,128)(2,1)S(1)} collective-permute-done((bf16[2,512,256]{2,1,0:T(8,128)(2,1)S(1)}, bf16[2,512,256]{2,1,0:T(8,128)(2,1)S(1)}, u32[]{:S(2)}, u32[]{:S(2)}) %collective-permute-start.3) | collective-permute-done | bytes 524320 | tf_op jit(solution)/shard_map/ppermute | solution.py:41
  48.6 2.3 %collective-permute-done.4 = bf16[2,512,256]{2,1,0:T(8,128)(2,1)S(1)} collective-permute-done((bf16[2,512,256]{2,1,0:T(8,128)(2,1)S(1)}, bf16[2,512,256]{2,1,0:T(8,128)(2,1)S(1)}, u32[]{:S(2)}, u32[]{:S(2)}) %collective-permute-start.4) | collective-permute-done | bytes 524320 | tf_op jit(solution)/shard_map/ppermute | solution.py:41
  50.9 0.3 pad_maximum_fusion.own_ref
  51.1 3.5 %collective-permute-start.10 = (bf16[4,2,512,256]{3,2,1,0:T(8,128)(2,1)S(1)}, bf16[4,2,512,256]{3,2,1,0:T(8,128)(2,1)}, u32[]{:S(2)}, u32[]{:S(2)}) collective-permute-start(bf16[4,2,512,256]{3,2,1,0:T(8,128)(2,1)S(1)} %pad_maximum_fusion.own_ref), channel_id=1, source_target_pairs={{0,32},{32,0},{1,33},{33,1},{2,34},{34,2},{3,35},{35,3},{4,36},{36... | collective-permute-start | bytes 6291464 | tf_op jit(solution)/shard_map/ppermute | solution.py:41
  54.6 4.1 %collective-permute-start.7 = (bf16[2,512,256]{2,1,0:T(8,128)(2,1)S(1)}, bf16[2,512,256]{2,1,0:T(8,128)(2,1)S(1)}, u32[]{:S(2)}, u32[]{:S(2)}) collective-permute-start(bf16[2,512,256]{2,1,0:T(8,128)(2,1)S(1)} %pad_maximum_fusion.3), channel_id=1, source_target_pairs={{0,64},{64,128},{128,192},{192,0},{1,65},{65,129},{129,193},{193,1... | collective-permute-start | bytes 1572872 | tf_op jit(solution)/shard_map/ppermute | solution.py:41
  58.7 3.2 %collective-permute-start.8 = (bf16[2,512,256]{2,1,0:T(8,128)(2,1)S(1)}, bf16[2,512,256]{2,1,0:T(8,128)(2,1)}, u32[]{:S(2)}, u32[]{:S(2)}) collective-permute-start(bf16[2,512,256]{2,1,0:T(8,128)(2,1)S(1)} %pad_maximum_fusion.3), channel_id=1, source_target_pairs={{0,128},{64,192},{128,0},{192,64},{1,129},{65,193},{129,1},{193,65... | collective-permute-start | bytes 1572872 | tf_op jit(solution)/shard_map/ppermute | solution.py:41
  62.0 3.3 %collective-permute-start.9 = (bf16[2,512,256]{2,1,0:T(8,128)(2,1)S(1)}, bf16[2,512,256]{2,1,0:T(8,128)(2,1)}, u32[]{:S(2)}, u32[]{:S(2)}) collective-permute-start(bf16[2,512,256]{2,1,0:T(8,128)(2,1)S(1)} %pad_maximum_fusion.3), channel_id=1, source_target_pairs={{0,192},{64,0},{128,64},{192,128},{1,193},{65,1},{129,65},{193,129... | collective-permute-start | bytes 1572872 | tf_op jit(solution)/shard_map/ppermute | solution.py:41
  65.3 0.1 pad_add_fusion.at_ref
  65.4 0.0 collective-permute-done.10.other_hbm
  65.4 14.3 %all-gather.3.cloned.1.call-done = bf16[32,128,256]{2,1,0:T(8,128)(2,1)} async-done(((bf16[2,128,256]{2,1,0:T(8,128)(2,1)}), bf16[32,128,256]{2,1,0:T(8,128)(2,1)}) %all-gather.3.cloned.1.call-update) | async-done | bytes 2097168 | tf_op jit(solution)/shard_map/all_gather | solution.py:140
  79.7 2.9 %shard_map.46 = (f32[128,256]{1,0:T(8,128)S(1)}, f32[128,256]{1,0:T(8,128)S(1)}) custom-call(s32[3]{0:T(128)S(1)} %pad_add_fusion.at_ref, bf16[16,2,128,256]{3,2,1,0:T(8,128)(2,1)} %bitcast.23, bf16[4,2,512,256]{3,2,1,0:T(8,128)(2,1)S(1)} %pad_maximum_fusion.own_ref, bf16[4,2,512,256]{3,2,1,0:T(8,128)(2,1)} %collective-permute-done.10.other_hbm), custom_call_target="tpu_custom_call" | custom-call | tf_op jit(solution)/shard_map/pallas_call | solution.py:91
  82.6 3.0 %collective-permute-start.11 = (f32[128,256]{1,0:T(8,128)S(1)}, f32[128,256]{1,0:T(8,128)S(1)}, u32[]{:S(2)}, u32[]{:S(2)}) collective-permute-start(f32[128,256]{1,0:T(8,128)S(1)} %get-tuple-element.35), channel_id=1, source_target_pairs={{0,16},{16,0},{1,17},{17,1},{2,18},{18,2},{3,19},{19,3},{4,20},{20... | collective-permute-start | bytes 393224 | tf_op jit(solution)/shard_map/ppermute | solution.py:41
  85.7 2.7 %collective-permute-done.11 = f32[128,256]{1,0:T(8,128)S(1)} collective-permute-done((f32[128,256]{1,0:T(8,128)S(1)}, f32[128,256]{1,0:T(8,128)S(1)}, u32[]{:S(2)}, u32[]{:S(2)}) %collective-permute-start.11) | collective-permute-done | bytes 131104 | tf_op jit(solution)/shard_map/ppermute | solution.py:41
  88.4 13.1 %collective-permute-start.12 = (bf16[128,256]{1,0:T(8,128)(2,1)S(1)}, bf16[128,256]{1,0:T(8,128)(2,1)S(1)}, u32[]{:S(2)}, u32[]{:S(2)}) collective-permute-start(bf16[128,256]{1,0:T(8,128)(2,1)S(1)} %multiply_convert_fusion.1), channel_id=1, source_target_pairs={{0,0},{1,1},{2,32},{3,33},{4,64},{5,65},{6,96},{7,97},{8,128},{9,1... | collective-permute-start | bytes 196616 | tf_op jit(solution)/shard_map/ppermute | solution.py:41
  101.5 0.0 collective-permute-done.7
  101.5 0.0 collective-permute-done.8
  101.5 0.0 collective-permute-done.9
  101.5 2.1 %collective-permute-done.12 = bf16[128,256]{1,0:T(8,128)(2,1)S(1)} collective-permute-done((bf16[128,256]{1,0:T(8,128)(2,1)S(1)}, bf16[128,256]{1,0:T(8,128)(2,1)S(1)}, u32[]{:S(2)}, u32[]{:S(2)}) %collective-permute-start.12) | collective-permute-done | bytes 65568 | tf_op jit(solution)/shard_map/ppermute | solution.py:41
  103.6 1.1 broadcast_in_dim.2
  104.7 12.6 %all-to-all-start = ((bf16[16,128,256]{2,1,0:T(8,128)(2,1)}), bf16[16,128,256]{2,1,0:T(8,128)(2,1)S(1)}, u32[]{:S(2)}, u32[]{:S(2)}) async-start(bf16[16,128,256]{2,1,0:T(8,128)(2,1)} %broadcast_in_dim.2), calls=%async_computation | async-start | bytes 2097152 | tf_op jit(solution)/shard_map/all_to_all | solution.py:19
  117.3 1.5 pad_maximum_fusion.1.own_ref
  118.7 9.2 %collective-permute-start.13 = (bf16[4,2,512,256]{3,2,1,0:T(8,128)(2,1)S(1)}, bf16[4,2,512,256]{3,2,1,0:T(8,128)(2,1)S(1)}, u32[]{:S(2)}, u32[]{:S(2)}) collective-permute-start(bf16[4,2,512,256]{3,2,1,0:T(8,128)(2,1)S(1)} %pad_maximum_fusion.1.own_ref), channel_id=1, source_target_pairs={{0,32},{32,0},{1,33},{33,1},{2,34},{34,2},{3,35},{35,3},{4,36},{36... | collective-permute-start | bytes 6291464 | tf_op jit(solution)/shard_map/ppermute | solution.py:41
  128.0 3.8 %collective-permute-done.13.other_hbm = bf16[4,2,512,256]{3,2,1,0:T(8,128)(2,1)S(1)} collective-permute-done((bf16[4,2,512,256]{3,2,1,0:T(8,128)(2,1)S(1)}, bf16[4,2,512,256]{3,2,1,0:T(8,128)(2,1)S(1)}, u32[]{:S(2)}, u32[]{:S(2)}) %collective-permute-start.13) | collective-permute-done | bytes 2097184 | tf_op jit(solution)/shard_map/ppermute | solution.py:41
  131.7 0.0 copy-start
  131.7 1.3 copy-done
  133.1 2.9 %shard_map.47 = (f32[2,128,256]{2,1,0:T(8,128)S(1)}, f32[2,128,256]{2,1,0:T(8,128)S(1)}) custom-call(s32[3]{0:T(128)S(1)} %pad_add_fusion.at_ref, bf16[16,2,128,256]{3,2,1,0:T(8,128)(2,1)} %bitcast.24, bf16[4,2,512,256]{3,2,1,0:T(8,128)(2,1)S(1)} %pad_maximum_fusion.1.own_ref, bf16[4,2,512,256]{3,2,1,0:T(8,128)(2,1)} %copy-done), custom_call_target="tpu_custom_call" | custom-call | tf_op jit(solution)/shard_map/pallas_call | solution.py:91
  136.0 0.7 collective-permute-start.14
  136.7 7.1 %collective-permute-start.15 = (f32[2,128,256]{2,1,0:T(8,128)S(1)}, f32[2,128,256]{2,1,0:T(8,128)S(1)}, u32[]{:S(2)}, u32[]{:S(2)}) collective-permute-start(f32[2,128,256]{2,1,0:T(8,128)S(1)} %get-tuple-element.41), channel_id=1, source_target_pairs={{0,256},{16,0},{256,272},{272,16},{1,257},{17,1},{257,273},{273,17... | collective-permute-start | bytes 786440 | tf_op jit(solution)/shard_map/ppermute | solution.py:41
  143.8 0.0 collective-permute-done.14
  143.8 5.3 %collective-permute-done.15 = f32[2,128,256]{2,1,0:T(8,128)S(1)} collective-permute-done((f32[2,128,256]{2,1,0:T(8,128)S(1)}, f32[2,128,256]{2,1,0:T(8,128)S(1)}, u32[]{:S(2)}, u32[]{:S(2)}) %collective-permute-start.15) | collective-permute-done | bytes 262176 | tf_op jit(solution)/shard_map/ppermute | solution.py:41
  149.2 1.9 collective-permute-start.16
  151.1 2.8 %collective-permute-start.17 = (bf16[2,128,256]{2,1,0:T(8,128)(2,1)S(1)}, bf16[2,128,256]{2,1,0:T(8,128)(2,1)S(1)}, u32[]{:S(2)}, u32[]{:S(2)}) collective-permute-start(bf16[2,128,256]{2,1,0:T(8,128)(2,1)S(1)} %multiply_convert_fusion), channel_id=1, source_target_pairs={{0,128},{64,192},{128,0},{192,64},{1,129},{65,193},{129,1},{193,65... | collective-permute-start | bytes 393224 | tf_op jit(solution)/shard_map/ppermute | solution.py:41
  153.9 3.7 %collective-permute-start.18 = (bf16[2,128,256]{2,1,0:T(8,128)(2,1)S(1)}, bf16[2,128,256]{2,1,0:T(8,128)(2,1)S(1)}, u32[]{:S(2)}, u32[]{:S(2)}) collective-permute-start(bf16[2,128,256]{2,1,0:T(8,128)(2,1)S(1)} %multiply_convert_fusion), channel_id=1, source_target_pairs={{0,192},{64,0},{128,64},{192,128},{1,193},{65,1},{129,65},{193,129... | collective-permute-start | bytes 393224 | tf_op jit(solution)/shard_map/ppermute | solution.py:41
  157.6 0.0 collective-permute-done.16
  157.6 1.0 collective-permute-done.17
  158.7 3.5 %collective-permute-done.18 = bf16[2,128,256]{2,1,0:T(8,128)(2,1)S(1)} collective-permute-done((bf16[2,128,256]{2,1,0:T(8,128)(2,1)S(1)}, bf16[2,128,256]{2,1,0:T(8,128)(2,1)S(1)}, u32[]{:S(2)}, u32[]{:S(2)}) %collective-permute-start.18) | collective-permute-done | bytes 131104 | tf_op jit(solution)/shard_map/ppermute | solution.py:41
  162.2 0.1 pad_maximum_fusion.4.own_ref
  162.3 3.7 %collective-permute-start.19 = (bf16[4,2,128,256]{3,2,1,0:T(8,128)(2,1)S(1)}, bf16[4,2,128,256]{3,2,1,0:T(8,128)(2,1)S(1)}, u32[]{:S(2)}, u32[]{:S(2)}) collective-permute-start(bf16[4,2,128,256]{3,2,1,0:T(8,128)(2,1)S(1)} %pad_maximum_fusion.4.own_ref), channel_id=1, source_target_pairs={{0,32},{32,0},{1,33},{33,1},{2,34},{34,2},{3,35},{35,3},{4,36},{36... | collective-permute-start | bytes 1572872 | tf_op jit(solution)/shard_map/ppermute | solution.py:41
  166.0 0.1 pad_add_fusion.2.at_ref
  166.1 1.4 collective-permute-done.19.other_ref
  167.5 0.0 all-to-all-done.s_ref
  167.5 1.3 shard_map.49
  168.8 6.0 %collective-permute-start.20 = (f32[256,512]{1,0:T(8,128)S(1)}, f32[256,512]{1,0:T(8,128)S(1)}, u32[]{:S(2)}, u32[]{:S(2)}) collective-permute-start(f32[256,512]{1,0:T(8,128)S(1)} %shard_map.49), channel_id=1, source_target_pairs={{0,16},{16,0},{1,17},{17,1},{2,18},{18,2},{3,19},{19,3},{4,20},{20... | collective-permute-start | bytes 1572872 | tf_op jit(solution)/shard_map/ppermute | solution.py:41
  174.8 1.3 shard_map.48
  176.1 10.7 %collective-permute-done.20 = f32[256,512]{1,0:T(8,128)S(1)} collective-permute-done((f32[256,512]{1,0:T(8,128)S(1)}, f32[256,512]{1,0:T(8,128)S(1)}, u32[]{:S(2)}, u32[]{:S(2)}) %collective-permute-start.20) | collective-permute-done | bytes 524320 | tf_op jit(solution)/shard_map/ppermute | solution.py:41
  186.8 0.9 add_multiply_fusion
  (2 shorter events, 0.1 us)
Async XLA Ops:
  6.5 73.2 %all-gather.3.cloned.1.call-start = ((), (), s32[]{:S(2)}) async-start(), calls=%async_computation.1 | async-start | bytes 2228224 | tf_op jit(solution)/shard_map/all_gather | solution.py:140
  8.1 7.7 %collective-permute-start = (bf16[512,256]{1,0:T(8,128)(2,1)}, bf16[512,256]{1,0:T(8,128)(2,1)S(1)}, u32[]{:S(2)}, u32[]{:S(2)}) collective-permute-start(bf16[512,256]{1,0:T(8,128)(2,1)} %param.7), channel_id=1, source_target_pairs={{0,0},{16,256},{256,16},{272,272},{1,1},{17,257},{257,17},{273,273... | collective-permute-start | bytes 786440 | tf_op jit(solution)/shard_map/ppermute | solution.py:41
  9.7 9.7 %collective-permute-start.1 = (bf16[512,256]{1,0:T(8,128)(2,1)}, bf16[512,256]{1,0:T(8,128)(2,1)S(1)}, u32[]{:S(2)}, u32[]{:S(2)}) collective-permute-start(bf16[512,256]{1,0:T(8,128)(2,1)} %param.7), channel_id=1, source_target_pairs={{0,256},{16,0},{256,272},{272,16},{1,257},{17,1},{257,273},{273,17... | collective-permute-start | bytes 786440 | tf_op jit(solution)/shard_map/ppermute | solution.py:41
  19.5 25.7 %collective-permute-start.2 = (bf16[2,512,256]{2,1,0:T(8,128)(2,1)S(1)}, bf16[2,512,256]{2,1,0:T(8,128)(2,1)S(1)}, u32[]{:S(2)}, u32[]{:S(2)}) collective-permute-start(bf16[2,512,256]{2,1,0:T(8,128)(2,1)S(1)} %pad_maximum_fusion.2), channel_id=1, source_target_pairs={{0,64},{64,128},{128,192},{192,0},{1,65},{65,129},{129,193},{193,1... | collective-permute-start | bytes 1572872 | tf_op jit(solution)/shard_map/ppermute | solution.py:41
  24.4 24.2 %collective-permute-start.3 = (bf16[2,512,256]{2,1,0:T(8,128)(2,1)S(1)}, bf16[2,512,256]{2,1,0:T(8,128)(2,1)S(1)}, u32[]{:S(2)}, u32[]{:S(2)}) collective-permute-start(bf16[2,512,256]{2,1,0:T(8,128)(2,1)S(1)} %pad_maximum_fusion.2), channel_id=1, source_target_pairs={{0,128},{64,192},{128,0},{192,64},{1,129},{65,193},{129,1},{193,65... | collective-permute-start | bytes 1572872 | tf_op jit(solution)/shard_map/ppermute | solution.py:41
  28.9 22.0 %collective-permute-start.4 = (bf16[2,512,256]{2,1,0:T(8,128)(2,1)S(1)}, bf16[2,512,256]{2,1,0:T(8,128)(2,1)S(1)}, u32[]{:S(2)}, u32[]{:S(2)}) collective-permute-start(bf16[2,512,256]{2,1,0:T(8,128)(2,1)S(1)} %pad_maximum_fusion.2), channel_id=1, source_target_pairs={{0,192},{64,0},{128,64},{192,128},{1,193},{65,1},{129,65},{193,129... | collective-permute-start | bytes 1572872 | tf_op jit(solution)/shard_map/ppermute | solution.py:41
  31.9 9.3 %collective-permute-start.5 = (bf16[512,256]{1,0:T(8,128)(2,1)}, bf16[512,256]{1,0:T(8,128)(2,1)S(1)}, u32[]{:S(2)}, u32[]{:S(2)}) collective-permute-start(bf16[512,256]{1,0:T(8,128)(2,1)} %param.6), channel_id=1, source_target_pairs={{0,0},{16,256},{256,16},{272,272},{1,1},{17,257},{257,17},{273,273... | collective-permute-start | bytes 786440 | tf_op jit(solution)/shard_map/ppermute | solution.py:41
  33.5 11.6 %collective-permute-start.6 = (bf16[512,256]{1,0:T(8,128)(2,1)}, bf16[512,256]{1,0:T(8,128)(2,1)S(1)}, u32[]{:S(2)}, u32[]{:S(2)}) collective-permute-start(bf16[512,256]{1,0:T(8,128)(2,1)} %param.6), channel_id=1, source_target_pairs={{0,256},{16,0},{256,272},{272,16},{1,257},{17,1},{257,273},{273,17... | collective-permute-start | bytes 786440 | tf_op jit(solution)/shard_map/ppermute | solution.py:41
  51.1 14.2 %collective-permute-start.10 = (bf16[4,2,512,256]{3,2,1,0:T(8,128)(2,1)S(1)}, bf16[4,2,512,256]{3,2,1,0:T(8,128)(2,1)}, u32[]{:S(2)}, u32[]{:S(2)}) collective-permute-start(bf16[4,2,512,256]{3,2,1,0:T(8,128)(2,1)S(1)} %pad_maximum_fusion.own_ref), channel_id=1, source_target_pairs={{0,32},{32,0},{1,33},{33,1},{2,34},{34,2},{3,35},{35,3},{4,36},{36... | collective-permute-start | bytes 6291464 | tf_op jit(solution)/shard_map/ppermute | solution.py:41
  54.6 46.8 %collective-permute-start.7 = (bf16[2,512,256]{2,1,0:T(8,128)(2,1)S(1)}, bf16[2,512,256]{2,1,0:T(8,128)(2,1)S(1)}, u32[]{:S(2)}, u32[]{:S(2)}) collective-permute-start(bf16[2,512,256]{2,1,0:T(8,128)(2,1)S(1)} %pad_maximum_fusion.3), channel_id=1, source_target_pairs={{0,64},{64,128},{128,192},{192,0},{1,65},{65,129},{129,193},{193,1... | collective-permute-start | bytes 1572872 | tf_op jit(solution)/shard_map/ppermute | solution.py:41
  58.7 42.7 %collective-permute-start.8 = (bf16[2,512,256]{2,1,0:T(8,128)(2,1)S(1)}, bf16[2,512,256]{2,1,0:T(8,128)(2,1)}, u32[]{:S(2)}, u32[]{:S(2)}) collective-permute-start(bf16[2,512,256]{2,1,0:T(8,128)(2,1)S(1)} %pad_maximum_fusion.3), channel_id=1, source_target_pairs={{0,128},{64,192},{128,0},{192,64},{1,129},{65,193},{129,1},{193,65... | collective-permute-start | bytes 1572872 | tf_op jit(solution)/shard_map/ppermute | solution.py:41
  62.0 39.5 %collective-permute-start.9 = (bf16[2,512,256]{2,1,0:T(8,128)(2,1)S(1)}, bf16[2,512,256]{2,1,0:T(8,128)(2,1)}, u32[]{:S(2)}, u32[]{:S(2)}) collective-permute-start(bf16[2,512,256]{2,1,0:T(8,128)(2,1)S(1)} %pad_maximum_fusion.3), channel_id=1, source_target_pairs={{0,192},{64,0},{128,64},{192,128},{1,193},{65,1},{129,65},{193,129... | collective-permute-start | bytes 1572872 | tf_op jit(solution)/shard_map/ppermute | solution.py:41
  82.6 5.7 %collective-permute-start.11 = (f32[128,256]{1,0:T(8,128)S(1)}, f32[128,256]{1,0:T(8,128)S(1)}, u32[]{:S(2)}, u32[]{:S(2)}) collective-permute-start(f32[128,256]{1,0:T(8,128)S(1)} %get-tuple-element.35), channel_id=1, source_target_pairs={{0,16},{16,0},{1,17},{17,1},{2,18},{18,2},{3,19},{19,3},{4,20},{20... | collective-permute-start | bytes 393224 | tf_op jit(solution)/shard_map/ppermute | solution.py:41
  88.4 15.2 %collective-permute-start.12 = (bf16[128,256]{1,0:T(8,128)(2,1)S(1)}, bf16[128,256]{1,0:T(8,128)(2,1)S(1)}, u32[]{:S(2)}, u32[]{:S(2)}) collective-permute-start(bf16[128,256]{1,0:T(8,128)(2,1)S(1)} %multiply_convert_fusion.1), channel_id=1, source_target_pairs={{0,0},{1,1},{2,32},{3,33},{4,64},{5,65},{6,96},{7,97},{8,128},{9,1... | collective-permute-start | bytes 196616 | tf_op jit(solution)/shard_map/ppermute | solution.py:41
  104.7 62.9 %all-to-all-start = ((bf16[16,128,256]{2,1,0:T(8,128)(2,1)}), bf16[16,128,256]{2,1,0:T(8,128)(2,1)S(1)}, u32[]{:S(2)}, u32[]{:S(2)}) async-start(bf16[16,128,256]{2,1,0:T(8,128)(2,1)} %broadcast_in_dim.2), calls=%async_computation | async-start | bytes 2097152 | tf_op jit(solution)/shard_map/all_to_all | solution.py:19
  118.7 13.0 %collective-permute-start.13 = (bf16[4,2,512,256]{3,2,1,0:T(8,128)(2,1)S(1)}, bf16[4,2,512,256]{3,2,1,0:T(8,128)(2,1)S(1)}, u32[]{:S(2)}, u32[]{:S(2)}) collective-permute-start(bf16[4,2,512,256]{3,2,1,0:T(8,128)(2,1)S(1)} %pad_maximum_fusion.1.own_ref), channel_id=1, source_target_pairs={{0,32},{32,0},{1,33},{33,1},{2,34},{34,2},{3,35},{35,3},{4,36},{36... | collective-permute-start | bytes 6291464 | tf_op jit(solution)/shard_map/ppermute | solution.py:41
  131.7 1.3 copy-start
  136.0 7.8 %collective-permute-start.14 = (f32[2,128,256]{2,1,0:T(8,128)S(1)}, f32[2,128,256]{2,1,0:T(8,128)S(1)}, u32[]{:S(2)}, u32[]{:S(2)}) collective-permute-start(f32[2,128,256]{2,1,0:T(8,128)S(1)} %get-tuple-element.40), channel_id=1, source_target_pairs={{0,0},{16,256},{256,16},{272,272},{1,1},{17,257},{257,17},{273,273... | collective-permute-start | bytes 786440 | tf_op jit(solution)/shard_map/ppermute | solution.py:41
  136.7 12.5 %collective-permute-start.15 = (f32[2,128,256]{2,1,0:T(8,128)S(1)}, f32[2,128,256]{2,1,0:T(8,128)S(1)}, u32[]{:S(2)}, u32[]{:S(2)}) collective-permute-start(f32[2,128,256]{2,1,0:T(8,128)S(1)} %get-tuple-element.41), channel_id=1, source_target_pairs={{0,256},{16,0},{256,272},{272,16},{1,257},{17,1},{257,273},{273,17... | collective-permute-start | bytes 786440 | tf_op jit(solution)/shard_map/ppermute | solution.py:41
  149.2 8.4 %collective-permute-start.16 = (bf16[2,128,256]{2,1,0:T(8,128)(2,1)S(1)}, bf16[2,128,256]{2,1,0:T(8,128)(2,1)S(1)}, u32[]{:S(2)}, u32[]{:S(2)}) collective-permute-start(bf16[2,128,256]{2,1,0:T(8,128)(2,1)S(1)} %multiply_convert_fusion), channel_id=1, source_target_pairs={{0,64},{64,128},{128,192},{192,0},{1,65},{65,129},{129,193},{193,1... | collective-permute-start | bytes 393224 | tf_op jit(solution)/shard_map/ppermute | solution.py:41
  151.1 7.6 %collective-permute-start.17 = (bf16[2,128,256]{2,1,0:T(8,128)(2,1)S(1)}, bf16[2,128,256]{2,1,0:T(8,128)(2,1)S(1)}, u32[]{:S(2)}, u32[]{:S(2)}) collective-permute-start(bf16[2,128,256]{2,1,0:T(8,128)(2,1)S(1)} %multiply_convert_fusion), channel_id=1, source_target_pairs={{0,128},{64,192},{128,0},{192,64},{1,129},{65,193},{129,1},{193,65... | collective-permute-start | bytes 393224 | tf_op jit(solution)/shard_map/ppermute | solution.py:41
  153.9 8.3 %collective-permute-start.18 = (bf16[2,128,256]{2,1,0:T(8,128)(2,1)S(1)}, bf16[2,128,256]{2,1,0:T(8,128)(2,1)S(1)}, u32[]{:S(2)}, u32[]{:S(2)}) collective-permute-start(bf16[2,128,256]{2,1,0:T(8,128)(2,1)S(1)} %multiply_convert_fusion), channel_id=1, source_target_pairs={{0,192},{64,0},{128,64},{192,128},{1,193},{65,1},{129,65},{193,129... | collective-permute-start | bytes 393224 | tf_op jit(solution)/shard_map/ppermute | solution.py:41
  162.3 5.3 %collective-permute-start.19 = (bf16[4,2,128,256]{3,2,1,0:T(8,128)(2,1)S(1)}, bf16[4,2,128,256]{3,2,1,0:T(8,128)(2,1)S(1)}, u32[]{:S(2)}, u32[]{:S(2)}) collective-permute-start(bf16[4,2,128,256]{3,2,1,0:T(8,128)(2,1)S(1)} %pad_maximum_fusion.4.own_ref), channel_id=1, source_target_pairs={{0,32},{32,0},{1,33},{33,1},{2,34},{34,2},{3,35},{35,3},{4,36},{36... | collective-permute-start | bytes 1572872 | tf_op jit(solution)/shard_map/ppermute | solution.py:41
  168.8 18.0 %collective-permute-start.20 = (f32[256,512]{1,0:T(8,128)S(1)}, f32[256,512]{1,0:T(8,128)S(1)}, u32[]{:S(2)}, u32[]{:S(2)}) collective-permute-start(f32[256,512]{1,0:T(8,128)S(1)} %shard_map.49), channel_id=1, source_target_pairs={{0,16},{16,0},{1,17},{17,1},{2,18},{18,2},{3,19},{19,3},{4,20},{20... | collective-permute-start | bytes 1572872 | tf_op jit(solution)/shard_map/ppermute | solution.py:41
Sparse Core Ops, SparseCore 0:
  9.4 70.2 all-gather.2

commit v11 on v10

--- a/solution.py
+++ b/solution.py
@@ -45,17 +45,18 @@
     return jnp.dot(a, b, preferred_element_type=jnp.float32)
 
 
-def rotate_kernel(part, at_ref, x_hbm, own_ref, other_hbm, first_ref, second_ref, x_ref, other_ref, sems):
-    copies = [
-        pltpu.make_async_copy(x_hbm.at[:, part], x_ref, sems.at[0]),
-        pltpu.make_async_copy(other_hbm, other_ref, sems.at[1]),
-    ]
+def rotate_kernel(part, at_ref, x_hbm, own_ref, other_hbm, first_ref, second_ref, x_ref, sems, *held):
+    copies = [pltpu.make_async_copy(x_hbm.at[:, part], x_ref, sems.at[0])]
+    other_ref = held[0] if held else other_hbm
+    if held:
+        copies.append(pltpu.make_async_copy(other_hbm, other_ref, sems.at[1]))
     for copy in copies:
         copy.start()
     y, c, turned = at_ref[0], at_ref[1], at_ref[2]
     sums = [jnp.zeros(x_ref.shape[1:], jnp.float32)] * 2
-    for copy, basis, core in ((copies[0], own_ref, c), (copies[1], other_ref, 1 - c)):
-        copy.wait()
+    for half, basis, core in ((0, own_ref, c), (1, other_ref, 1 - c)):
+        if half < len(copies):
+            copies[half].wait()
         for k in range(2):
             for j in range(4):
                 at = 4 * lax.rem(y + 4 - j, 4) + 2 * core
@@ -75,10 +76,10 @@
     for h in range(2):
         acc = jnp.zeros((256, 256), jnp.float32)
         for j in range(4):
-            at = 4 * lax.rem(y + 4 - j, 4) + h
+            at = lax.rem(y + 4 - j, 4) + 4 * h
             for act, core in ((own_ref, c), (other_ref, 1 - c)):
                 acc += lax.dot_general(
-                    act[j, k], s_ref[at + 2 * core],
+                    act[j, k], s_ref[at + 8 * core],
                     (((0,), (0,)), ((), ())), preferred_element_type=jnp.float32,
                 )
         out_ref[:, 256 * h:256 * h + 256] = acc
@@ -87,17 +88,18 @@
 def rotate(at, x, part, basis, paired):
     out = jax.ShapeDtypeStruct((2,) * paired + x.shape[2:], jnp.float32)
     own, other = basis
-    x, other = (pltpu.with_memory_space_constraint(v, pltpu.HBM) for v in (x, other))
+    x = pltpu.with_memory_space_constraint(x, pltpu.HBM)
+    if not paired:
+        other = pltpu.with_memory_space_constraint(other, pltpu.HBM)
     return pl.pallas_call(
         functools.partial(rotate_kernel, part),
         out_shape=[out, out],
-        in_specs=[SMEM, HBM, VMEM, HBM],
+        in_specs=[SMEM, HBM, VMEM, VMEM if paired else HBM],
         out_specs=[VMEM, VMEM],
         scratch_shapes=[
             pltpu.VMEM((16,) + x.shape[2:], x.dtype),
-            pltpu.VMEM(other.shape, other.dtype),
             pltpu.SemaphoreType.DMA((2,)),
-        ],
+        ] + [pltpu.VMEM(other.shape, other.dtype)] * (1 - paired),
         compiler_params=PARAMS,
     )(at, x, own, other)
 
@@ -140,10 +142,9 @@
     every = lax.all_gather(both, ("zh", "zl"), axis=0, tiled=False)
     grad_pair = cross(grad_basis)
     act_basis, grad_pair = lax.optimization_barrier((act_basis, grad_pair))
-    grad_shifts, act_pair = lax.optimization_barrier((shifts(grad_pair), cross(act_basis)))
-    grad_panels = both_cores(grad_shifts)
-    act_pair, grad_own = lax.optimization_barrier((act_pair, grad_panels[0]))
-    act_shifts = shifts(act_pair)
+    grad_panels = both_cores(shifts(grad_pair))
+    act_shifts, grad_own = lax.optimization_barrier((shifts(cross(act_basis)), grad_panels[0]))
+    grad_panels = (grad_own, grad_panels[1])
 
     mine, theirs = rotate(at, every, 1, grad_panels, 0)
     rotated_grad = mine + swap(theirs, "xl")
@@ -151,13 +152,15 @@
     grad_square = move(
         grad_square, AXES, lambda a, b, e, p, q, r: (p, q, r // 2, a, b, 2 * e + r % 2)
     )
-    act_shifts, grad_square = lax.optimization_barrier((act_shifts, grad_square))
-    grad_block = to_all(grad_square, ("zh", "zl"), 16)
 
     parts = rotate(at, every, 0, both_cores(act_shifts), 1)
+    grad_square, parts = lax.optimization_barrier((grad_square, parts))
+    grad_block = to_all(grad_square, ("zh",), 4)
     parts = [move(parts[k], ("xh", "xl"), lambda a, p, k=k: (p ^ k, a)) for k in range(2)]
     rotated_act = parts[0] + parts[1]
     act_square = (rotated_act * rotated_act).astype(jnp.bfloat16)
+    grad_block, act_square = lax.optimization_barrier((grad_block, act_square))
+    grad_block = to_all(grad_block, ("zl",), 4).reshape(16, 128, 256)
     acts = both_cores(shifts(act_square))
 
     theirs = swap(correct(jnp.stack([y, c, 1 - turned]), acts, grad_block), "xl")

time: 195 us -> 204 us (1.046)
  starting transfers between devices: 107 us -> 122 us
  waiting for transfers between devices: 58.1 us -> 50.1 us
    all_to_all x1 -> x2, starting transfers between devices: 12.6 us -> 30.3 us  [to_all(): return lax.all_to_all(spread, axes, split_axis=0, concat_axis=0, tiled=True)]
    all_gather x1, waiting for transfers between devices: 14.3 us -> 0.99 us  [on_device(): every = lax.all_gather(both, ('zh', 'zl'), axis=0, tiled=False)]
    all_to_all x1 -> x2, waiting for transfers between devices: 0.01 us -> 9.2 us  [to_all(): return lax.all_to_all(spread, axes, split_axis=0, concat_axis=0, tiled=True)]
    ppermute x21, waiting for transfers between devices: 43.8 us -> 39.9 us  [move(): return lax.ppermute(x, axes, pairs)]
    ppermute x21, starting transfers between devices: 94.8 us -> 91.5 us  [move(): return lax.ppermute(x, axes, pairs)]
  transfers between devices with their start and end apart: 23 -> 24, of which waited for: 13 -> 14; matrix products, arithmetic and copies ran while one was open for 1% -> 1% of each run, Pallas kernels for 4% -> 4%
where the time goes in v11:
time: 204 us; the launch traced here: 202 us
  starting transfers between devices  122 us (60%)
  waiting for transfers between devices  50.1 us (25%)
  between operations  13.7 us (7%)
  Pallas kernels  10.1 us (5%)
  other arithmetic  4.69 us (2%)
    ppermute x21, starting transfers between devices, move(): return lax.ppermute(x, axes, pairs)  91.5 us
    ppermute x21, waiting for transfers between devices, move(): return lax.ppermute(x, axes, pairs)  39.9 us
    all_to_all x2, starting transfers between devices, to_all(): return lax.all_to_all(spread, axes, split_axis=0, concat_axis=0, tiled=True)  30.3 us
    all_to_all x2, waiting for transfers between devices, to_all(): return lax.all_to_all(spread, axes, split_axis=0, concat_axis=0, tiled=True)  9.2 us
    pallas_call x2, Pallas kernels, rotate(): pl.pallas_call(functools.partial(rotate_kernel, part), out_shape=[out, ou...  7.54 us
  transfers between devices with their start and end apart: 24, of which 14 were waited for; matrix products, arithmetic and copies ran while one was open for 1% of the time, Pallas kernels for 4%

profile of v11, /device:TPU:1, one launch (start us, length us, event | category | flops | bytes accessed | tf_op | source)
XLA Modules:
  0.0 202.2 jit_solution(13972702790436741166)
XLA Ops:
  6.5 0.0 all-gather.3.cloned.1.call-start
  6.5 1.5 pad_maximum_fusion.5
  8.1 0.0 all-gather.3.cloned.1.call-update
  8.1 5.5 %collective-permute-start.1 = (bf16[512,256]{1,0:T(8,128)(2,1)}, bf16[512,256]{1,0:T(8,128)(2,1)S(1)}, u32[]{:S(2)}, u32[]{:S(2)}) collective-permute-start(bf16[512,256]{1,0:T(8,128)(2,1)} %param.7), channel_id=1, source_target_pairs={{0,256},{16,0},{256,272},{272,16},{1,257},{17,1},{257,273},{273,17... | collective-permute-start | bytes 786440 | tf_op jit(solution)/shard_map/ppermute | solution.py:41
  13.6 1.6 collective-permute-start
  15.2 2.0 collective-permute-done.1
  17.2 0.0 collective-permute-done
  17.2 0.1 pad_maximum_fusion.2
  17.3 6.3 %collective-permute-start.9 = (bf16[2,512,256]{2,1,0:T(8,128)(2,1)S(1)}, bf16[2,512,256]{2,1,0:T(8,128)(2,1)S(1)}, u32[]{:S(2)}, u32[]{:S(2)}) collective-permute-start(bf16[2,512,256]{2,1,0:T(8,128)(2,1)S(1)} %pad_maximum_fusion.2), channel_id=1, source_target_pairs={{0,192},{64,0},{128,64},{192,128},{1,193},{65,1},{129,65},{193,129... | collective-permute-start | bytes 1572872 | tf_op jit(solution)/shard_map/ppermute | solution.py:41
  23.6 2.3 %collective-permute-start.8 = (bf16[2,512,256]{2,1,0:T(8,128)(2,1)S(1)}, bf16[2,512,256]{2,1,0:T(8,128)(2,1)S(1)}, u32[]{:S(2)}, u32[]{:S(2)}) collective-permute-start(bf16[2,512,256]{2,1,0:T(8,128)(2,1)S(1)} %pad_maximum_fusion.2), channel_id=1, source_target_pairs={{0,128},{64,192},{128,0},{192,64},{1,129},{65,193},{129,1},{193,65... | collective-permute-start | bytes 1572872 | tf_op jit(solution)/shard_map/ppermute | solution.py:41
  25.9 2.6 %collective-permute-start.7 = (bf16[2,512,256]{2,1,0:T(8,128)(2,1)S(1)}, bf16[2,512,256]{2,1,0:T(8,128)(2,1)S(1)}, u32[]{:S(2)}, u32[]{:S(2)}) collective-permute-start(bf16[2,512,256]{2,1,0:T(8,128)(2,1)S(1)} %pad_maximum_fusion.2), channel_id=1, source_target_pairs={{0,64},{64,128},{128,192},{192,0},{1,65},{65,129},{129,193},{193,1... | collective-permute-start | bytes 1572872 | tf_op jit(solution)/shard_map/ppermute | solution.py:41
  28.5 12.1 %collective-permute-start.3 = (bf16[512,256]{1,0:T(8,128)(2,1)}, bf16[512,256]{1,0:T(8,128)(2,1)S(1)}, u32[]{:S(2)}, u32[]{:S(2)}) collective-permute-start(bf16[512,256]{1,0:T(8,128)(2,1)} %param.6), channel_id=1, source_target_pairs={{0,256},{16,0},{256,272},{272,16},{1,257},{17,1},{257,273},{273,17... | collective-permute-start | bytes 786440 | tf_op jit(solution)/shard_map/ppermute | solution.py:41
  40.6 1.6 collective-permute-start.2
  42.2 3.0 %collective-permute-done.3 = bf16[512,256]{1,0:T(8,128)(2,1)S(1)} collective-permute-done((bf16[512,256]{1,0:T(8,128)(2,1)}, bf16[512,256]{1,0:T(8,128)(2,1)S(1)}, u32[]{:S(2)}, u32[]{:S(2)}) %collective-permute-start.3) | collective-permute-done | bytes 262176 | tf_op jit(solution)/shard_map/ppermute | solution.py:41
  45.2 0.0 collective-permute-done.2
  45.2 0.1 pad_maximum_fusion.3
  45.3 3.5 %collective-permute-start.4 = (bf16[2,512,256]{2,1,0:T(8,128)(2,1)S(1)}, bf16[2,512,256]{2,1,0:T(8,128)(2,1)S(1)}, u32[]{:S(2)}, u32[]{:S(2)}) collective-permute-start(bf16[2,512,256]{2,1,0:T(8,128)(2,1)S(1)} %pad_maximum_fusion.3), channel_id=1, source_target_pairs={{0,64},{64,128},{128,192},{192,0},{1,65},{65,129},{129,193},{193,1... | collective-permute-start | bytes 1572872 | tf_op jit(solution)/shard_map/ppermute | solution.py:41
  48.8 3.5 %collective-permute-start.5 = (bf16[2,512,256]{2,1,0:T(8,128)(2,1)S(1)}, bf16[2,512,256]{2,1,0:T(8,128)(2,1)S(1)}, u32[]{:S(2)}, u32[]{:S(2)}) collective-permute-start(bf16[2,512,256]{2,1,0:T(8,128)(2,1)S(1)} %pad_maximum_fusion.3), channel_id=1, source_target_pairs={{0,128},{64,192},{128,0},{192,64},{1,129},{65,193},{129,1},{193,65... | collective-permute-start | bytes 1572872 | tf_op jit(solution)/shard_map/ppermute | solution.py:41
  52.3 0.0 collective-permute-done.9
  52.3 3.0 %collective-permute-start.6 = (bf16[2,512,256]{2,1,0:T(8,128)(2,1)S(1)}, bf16[2,512,256]{2,1,0:T(8,128)(2,1)S(1)}, u32[]{:S(2)}, u32[]{:S(2)}) collective-permute-start(bf16[2,512,256]{2,1,0:T(8,128)(2,1)S(1)} %pad_maximum_fusion.3), channel_id=1, source_target_pairs={{0,192},{64,0},{128,64},{192,128},{1,193},{65,1},{129,65},{193,129... | collective-permute-start | bytes 1572872 | tf_op jit(solution)/shard_map/ppermute | solution.py:41
  55.3 0.0 collective-permute-done.8
  55.3 0.0 collective-permute-done.7
  55.4 1.6 pad_maximum_fusion.own_ref
  57.0 4.7 %collective-permute-start.10 = (bf16[4,2,512,256]{3,2,1,0:T(8,128)(2,1)}, bf16[4,2,512,256]{3,2,1,0:T(8,128)(2,1)}, u32[]{:S(2)}, u32[]{:S(2)}) collective-permute-start(bf16[4,2,512,256]{3,2,1,0:T(8,128)(2,1)} %pad_maximum_fusion.own_ref), channel_id=1, source_target_pairs={{0,32},{32,0},{1,33},{33,1},{2,34},{34,2},{3,35},{35,3},{4,36},{36... | collective-permute-start | bytes 6291464 | tf_op jit(solution)/shard_map/ppermute | solution.py:41
  61.7 0.5 collective-permute-done.4
  62.2 10.3 %collective-permute-done.5 = bf16[2,512,256]{2,1,0:T(8,128)(2,1)S(1)} collective-permute-done((bf16[2,512,256]{2,1,0:T(8,128)(2,1)S(1)}, bf16[2,512,256]{2,1,0:T(8,128)(2,1)S(1)}, u32[]{:S(2)}, u32[]{:S(2)}) %collective-permute-start.5) | collective-permute-done | bytes 524320 | tf_op jit(solution)/shard_map/ppermute | solution.py:41
  72.6 2.4 %collective-permute-done.6 = bf16[2,512,256]{2,1,0:T(8,128)(2,1)S(1)} collective-permute-done((bf16[2,512,256]{2,1,0:T(8,128)(2,1)S(1)}, bf16[2,512,256]{2,1,0:T(8,128)(2,1)S(1)}, u32[]{:S(2)}, u32[]{:S(2)}) %collective-permute-start.6) | collective-permute-done | bytes 524320 | tf_op jit(solution)/shard_map/ppermute | solution.py:41
  74.9 0.3 pad_maximum_fusion.1.own_ref
  75.2 3.5 %collective-permute-start.13 = (bf16[4,2,512,256]{3,2,1,0:T(8,128)(2,1)S(1)}, bf16[4,2,512,256]{3,2,1,0:T(8,128)(2,1)}, u32[]{:S(2)}, u32[]{:S(2)}) collective-permute-start(bf16[4,2,512,256]{3,2,1,0:T(8,128)(2,1)S(1)} %pad_maximum_fusion.1.own_ref), channel_id=1, source_target_pairs={{0,32},{32,0},{1,33},{33,1},{2,34},{34,2},{3,35},{35,3},{4,36},{36... | collective-permute-start | bytes 6291464 | tf_op jit(solution)/shard_map/ppermute | solution.py:41
  78.7 0.1 pad_add_fusion.at_ref
  78.8 0.0 collective-permute-done.10.other_hbm
  78.8 1.0 all-gather.3.cloned.1.call-done
  79.8 4.0 %shard_map.46 = (f32[128,256]{1,0:T(8,128)S(1)}, f32[128,256]{1,0:T(8,128)S(1)}) custom-call(s32[3]{0:T(128)S(1)} %pad_add_fusion.at_ref, bf16[16,2,128,256]{3,2,1,0:T(8,128)(2,1)} %bitcast.26, bf16[4,2,512,256]{3,2,1,0:T(8,128)(2,1)} %pad_maximum_fusion.own_ref, bf16[4,2,512,256]{3,2,1,0:T(8,128)(2,1)} %collective-permute-done.10.other_hbm), custom_call_target="tpu_custom_call" | custom-call | tf_op jit(solution)/shard_map/pallas_call | solution.py:94
  83.8 10.4 %collective-permute-start.11 = (f32[128,256]{1,0:T(8,128)S(1)}, f32[128,256]{1,0:T(8,128)S(1)}, u32[]{:S(2)}, u32[]{:S(2)}) collective-permute-start(f32[128,256]{1,0:T(8,128)S(1)} %get-tuple-element.29), channel_id=1, source_target_pairs={{0,16},{16,0},{1,17},{17,1},{2,18},{18,2},{3,19},{19,3},{4,20},{20... | collective-permute-start | bytes 393224 | tf_op jit(solution)/shard_map/ppermute | solution.py:41
  94.2 2.3 %collective-permute-done.11 = f32[128,256]{1,0:T(8,128)S(1)} collective-permute-done((f32[128,256]{1,0:T(8,128)S(1)}, f32[128,256]{1,0:T(8,128)S(1)}, u32[]{:S(2)}, u32[]{:S(2)}) %collective-permute-start.11) | collective-permute-done | bytes 131104 | tf_op jit(solution)/shard_map/ppermute | solution.py:41
  96.6 6.8 %collective-permute-start.12 = (bf16[128,256]{1,0:T(8,128)(2,1)S(1)}, bf16[128,256]{1,0:T(8,128)(2,1)S(1)}, u32[]{:S(2)}, u32[]{:S(2)}) collective-permute-start(bf16[128,256]{1,0:T(8,128)(2,1)S(1)} %multiply_convert_fusion.1), channel_id=1, source_target_pairs={{0,0},{1,1},{2,32},{3,33},{4,64},{5,65},{6,96},{7,97},{8,128},{9,1... | collective-permute-start | bytes 196616 | tf_op jit(solution)/shard_map/ppermute | solution.py:41
  103.3 0.0 collective-permute-done.13.other_hbm
  103.3 3.6 %shard_map.47 = (f32[2,128,256]{2,1,0:T(8,128)S(1)}, f32[2,128,256]{2,1,0:T(8,128)S(1)}) custom-call(s32[3]{0:T(128)S(1)} %pad_add_fusion.at_ref, bf16[16,2,128,256]{3,2,1,0:T(8,128)(2,1)} %bitcast.27, bf16[4,2,512,256]{3,2,1,0:T(8,128)(2,1)S(1)} %pad_maximum_fusion.1.own_ref, bf16[4,2,512,256]{3,2,1,0:T(8,128)(2,1)} %collective-permute-done.13.other_hbm), custom_call_target="tpu_custom_call" | custom-call | tf_op jit(solution)/shard_map/pallas_call | solution.py:94
  106.9 0.0 collective-permute-done.12
  106.9 0.7 broadcast_in_dim.4
  107.6 21.4 %all-to-all-start = ((bf16[4,128,256]{2,1,0:T(8,128)(2,1)}), bf16[4,128,256]{2,1,0:T(8,128)(2,1)S(1)}, u32[]{:S(2)}, u32[]{:S(2)}) async-start(bf16[4,128,256]{2,1,0:T(8,128)(2,1)} %broadcast_in_dim.4), calls=%async_computation | async-start | bytes 524288 | tf_op jit(solution)/shard_map/all_to_all | solution.py:19
  129.1 0.7 collective-permute-start.14
  129.7 7.0 %collective-permute-start.15 = (f32[2,128,256]{2,1,0:T(8,128)S(1)}, f32[2,128,256]{2,1,0:T(8,128)S(1)}, u32[]{:S(2)}, u32[]{:S(2)}) collective-permute-start(f32[2,128,256]{2,1,0:T(8,128)S(1)} %get-tuple-element.38), channel_id=1, source_target_pairs={{0,256},{16,0},{256,272},{272,16},{1,257},{17,1},{257,273},{273,17... | collective-permute-start | bytes 786440 | tf_op jit(solution)/shard_map/ppermute | solution.py:41
  136.7 0.0 collective-permute-done.14
  136.7 3.4 %collective-permute-done.15 = f32[2,128,256]{2,1,0:T(8,128)S(1)} collective-permute-done((f32[2,128,256]{2,1,0:T(8,128)S(1)}, f32[2,128,256]{2,1,0:T(8,128)S(1)}, u32[]{:S(2)}, u32[]{:S(2)}) %collective-permute-start.15) | collective-permute-done | bytes 262176 | tf_op jit(solution)/shard_map/ppermute | solution.py:41
  140.2 3.3 %all-to-all-done = bf16[4,128,256]{2,1,0:T(8,128)(2,1)S(1)} async-done(((bf16[4,128,256]{2,1,0:T(8,128)(2,1)}), bf16[4,128,256]{2,1,0:T(8,128)(2,1)S(1)}, u32[]{:S(2)}, u32[]{:S(2)}) %all-to-all-start) | async-done | bytes 262176 | tf_op jit(solution)/shard_map/all_to_all | solution.py:19
  143.5 1.1 broadcast_in_dim.5
  144.6 8.9 %all-to-all-start.1 = ((bf16[4,4,128,256]{3,2,1,0:T(8,128)(2,1)}), bf16[4,4,128,256]{3,2,1,0:T(8,128)(2,1)S(1)}, u32[]{:S(2)}, u32[]{:S(2)}) async-start(bf16[4,4,128,256]{3,2,1,0:T(8,128)(2,1)} %broadcast_in_dim.5), calls=%async_computation.1 | async-start | bytes 2097152 | tf_op jit(solution)/shard_map/all_to_all | solution.py:19
  153.4 1.9 collective-permute-start.18
  155.4 4.3 %collective-permute-start.17 = (bf16[2,128,256]{2,1,0:T(8,128)(2,1)S(1)}, bf16[2,128,256]{2,1,0:T(8,128)(2,1)S(1)}, u32[]{:S(2)}, u32[]{:S(2)}) collective-permute-start(bf16[2,128,256]{2,1,0:T(8,128)(2,1)S(1)} %multiply_convert_fusion), channel_id=1, source_target_pairs={{0,128},{64,192},{128,0},{192,64},{1,129},{65,193},{129,1},{193,65... | collective-permute-start | bytes 393224 | tf_op jit(solution)/shard_map/ppermute | solution.py:41
  159.7 1.9 collective-permute-start.16
  161.6 0.0 collective-permute-done.18
  161.6 1.1 collective-permute-done.17
  162.7 3.9 %collective-permute-done.16 = bf16[2,128,256]{2,1,0:T(8,128)(2,1)S(1)} collective-permute-done((bf16[2,128,256]{2,1,0:T(8,128)(2,1)S(1)}, bf16[2,128,256]{2,1,0:T(8,128)(2,1)S(1)}, u32[]{:S(2)}, u32[]{:S(2)}) %collective-permute-start.16) | collective-permute-done | bytes 131104 | tf_op jit(solution)/shard_map/ppermute | solution.py:41
  166.6 0.1 pad_maximum_fusion.4.own_ref
  166.7 4.5 %collective-permute-start.19 = (bf16[4,2,128,256]{3,2,1,0:T(8,128)(2,1)S(1)}, bf16[4,2,128,256]{3,2,1,0:T(8,128)(2,1)S(1)}, u32[]{:S(2)}, u32[]{:S(2)}) collective-permute-start(bf16[4,2,128,256]{3,2,1,0:T(8,128)(2,1)S(1)} %pad_maximum_fusion.4.own_ref), channel_id=1, source_target_pairs={{0,32},{32,0},{1,33},{33,1},{2,34},{34,2},{3,35},{35,3},{4,36},{36... | collective-permute-start | bytes 1572872 | tf_op jit(solution)/shard_map/ppermute | solution.py:41
  171.2 0.1 pad_add_fusion.2.at_ref
  171.3 1.4 collective-permute-done.19.other_ref
  172.7 5.9 %all-to-all-done.1 = bf16[4,4,128,256]{3,2,1,0:T(8,128)(2,1)S(1)} async-done(((bf16[4,4,128,256]{3,2,1,0:T(8,128)(2,1)}), bf16[4,4,128,256]{3,2,1,0:T(8,128)(2,1)S(1)}, u32[]{:S(2)}, u32[]{:S(2)}) %all-to-all-start.1) | async-done | bytes 1048608 | tf_op jit(solution)/shard_map/all_to_all | solution.py:19
  178.7 1.3 shard_map.49
  179.9 3.8 %collective-permute-start.20 = (f32[256,512]{1,0:T(8,128)S(1)}, f32[256,512]{1,0:T(8,128)S(1)}, u32[]{:S(2)}, u32[]{:S(2)}) collective-permute-start(f32[256,512]{1,0:T(8,128)S(1)} %shard_map.49), channel_id=1, source_target_pairs={{0,16},{16,0},{1,17},{17,1},{2,18},{18,2},{3,19},{19,3},{4,20},{20... | collective-permute-start | bytes 1572872 | tf_op jit(solution)/shard_map/ppermute | solution.py:41
  183.7 1.3 shard_map.48
  185.0 9.5 %collective-permute-done.20 = f32[256,512]{1,0:T(8,128)S(1)} collective-permute-done((f32[256,512]{1,0:T(8,128)S(1)}, f32[256,512]{1,0:T(8,128)S(1)}, u32[]{:S(2)}, u32[]{:S(2)}) %collective-permute-start.20) | collective-permute-done | bytes 524320 | tf_op jit(solution)/shard_map/ppermute | solution.py:41
  194.5 0.9 add_multiply_fusion
  (2 shorter events, 0.1 us)
Async XLA Ops:
  6.5 73.2 %all-gather.3.cloned.1.call-start = ((), (), s32[]{:S(2)}) async-start(), calls=%async_computation.2 | async-start | bytes 2228224 | tf_op jit(solution)/shard_map/all_gather | solution.py:142
  8.1 9.1 %collective-permute-start.1 = (bf16[512,256]{1,0:T(8,128)(2,1)}, bf16[512,256]{1,0:T(8,128)(2,1)S(1)}, u32[]{:S(2)}, u32[]{:S(2)}) collective-permute-start(bf16[512,256]{1,0:T(8,128)(2,1)} %param.7), channel_id=1, source_target_pairs={{0,256},{16,0},{256,272},{272,16},{1,257},{17,1},{257,273},{273,17... | collective-permute-start | bytes 786440 | tf_op jit(solution)/shard_map/ppermute | solution.py:41
  13.6 3.6 %collective-permute-start = (bf16[512,256]{1,0:T(8,128)(2,1)}, bf16[512,256]{1,0:T(8,128)(2,1)S(1)}, u32[]{:S(2)}, u32[]{:S(2)}) collective-permute-start(bf16[512,256]{1,0:T(8,128)(2,1)} %param.7), channel_id=1, source_target_pairs={{0,0},{16,256},{256,16},{272,272},{1,1},{17,257},{257,17},{273,273... | collective-permute-start | bytes 786440 | tf_op jit(solution)/shard_map/ppermute | solution.py:41
  17.3 35.0 %collective-permute-start.9 = (bf16[2,512,256]{2,1,0:T(8,128)(2,1)S(1)}, bf16[2,512,256]{2,1,0:T(8,128)(2,1)S(1)}, u32[]{:S(2)}, u32[]{:S(2)}) collective-permute-start(bf16[2,512,256]{2,1,0:T(8,128)(2,1)S(1)} %pad_maximum_fusion.2), channel_id=1, source_target_pairs={{0,192},{64,0},{128,64},{192,128},{1,193},{65,1},{129,65},{193,129... | collective-permute-start | bytes 1572872 | tf_op jit(solution)/shard_map/ppermute | solution.py:41
  23.6 31.7 %collective-permute-start.8 = (bf16[2,512,256]{2,1,0:T(8,128)(2,1)S(1)}, bf16[2,512,256]{2,1,0:T(8,128)(2,1)S(1)}, u32[]{:S(2)}, u32[]{:S(2)}) collective-permute-start(bf16[2,512,256]{2,1,0:T(8,128)(2,1)S(1)} %pad_maximum_fusion.2), channel_id=1, source_target_pairs={{0,128},{64,192},{128,0},{192,64},{1,129},{65,193},{129,1},{193,65... | collective-permute-start | bytes 1572872 | tf_op jit(solution)/shard_map/ppermute | solution.py:41
  25.9 29.5 %collective-permute-start.7 = (bf16[2,512,256]{2,1,0:T(8,128)(2,1)S(1)}, bf16[2,512,256]{2,1,0:T(8,128)(2,1)S(1)}, u32[]{:S(2)}, u32[]{:S(2)}) collective-permute-start(bf16[2,512,256]{2,1,0:T(8,128)(2,1)S(1)} %pad_maximum_fusion.2), channel_id=1, source_target_pairs={{0,64},{64,128},{128,192},{192,0},{1,65},{65,129},{129,193},{193,1... | collective-permute-start | bytes 1572872 | tf_op jit(solution)/shard_map/ppermute | solution.py:41
  28.5 16.7 %collective-permute-start.3 = (bf16[512,256]{1,0:T(8,128)(2,1)}, bf16[512,256]{1,0:T(8,128)(2,1)S(1)}, u32[]{:S(2)}, u32[]{:S(2)}) collective-permute-start(bf16[512,256]{1,0:T(8,128)(2,1)} %param.6), channel_id=1, source_target_pairs={{0,256},{16,0},{256,272},{272,16},{1,257},{17,1},{257,273},{273,17... | collective-permute-start | bytes 786440 | tf_op jit(solution)/shard_map/ppermute | solution.py:41
  40.6 4.6 %collective-permute-start.2 = (bf16[512,256]{1,0:T(8,128)(2,1)}, bf16[512,256]{1,0:T(8,128)(2,1)S(1)}, u32[]{:S(2)}, u32[]{:S(2)}) collective-permute-start(bf16[512,256]{1,0:T(8,128)(2,1)} %param.6), channel_id=1, source_target_pairs={{0,0},{16,256},{256,16},{272,272},{1,1},{17,257},{257,17},{273,273... | collective-permute-start | bytes 786440 | tf_op jit(solution)/shard_map/ppermute | solution.py:41
  45.3 16.9 %collective-permute-start.4 = (bf16[2,512,256]{2,1,0:T(8,128)(2,1)S(1)}, bf16[2,512,256]{2,1,0:T(8,128)(2,1)S(1)}, u32[]{:S(2)}, u32[]{:S(2)}) collective-permute-start(bf16[2,512,256]{2,1,0:T(8,128)(2,1)S(1)} %pad_maximum_fusion.3), channel_id=1, source_target_pairs={{0,64},{64,128},{128,192},{192,0},{1,65},{65,129},{129,193},{193,1... | collective-permute-start | bytes 1572872 | tf_op jit(solution)/shard_map/ppermute | solution.py:41
  48.8 23.8 %collective-permute-start.5 = (bf16[2,512,256]{2,1,0:T(8,128)(2,1)S(1)}, bf16[2,512,256]{2,1,0:T(8,128)(2,1)S(1)}, u32[]{:S(2)}, u32[]{:S(2)}) collective-permute-start(bf16[2,512,256]{2,1,0:T(8,128)(2,1)S(1)} %pad_maximum_fusion.3), channel_id=1, source_target_pairs={{0,128},{64,192},{128,0},{192,64},{1,129},{65,193},{129,1},{193,65... | collective-permute-start | bytes 1572872 | tf_op jit(solution)/shard_map/ppermute | solution.py:41
  52.3 22.6 %collective-permute-start.6 = (bf16[2,512,256]{2,1,0:T(8,128)(2,1)S(1)}, bf16[2,512,256]{2,1,0:T(8,128)(2,1)S(1)}, u32[]{:S(2)}, u32[]{:S(2)}) collective-permute-start(bf16[2,512,256]{2,1,0:T(8,128)(2,1)S(1)} %pad_maximum_fusion.3), channel_id=1, source_target_pairs={{0,192},{64,0},{128,64},{192,128},{1,193},{65,1},{129,65},{193,129... | collective-permute-start | bytes 1572872 | tf_op jit(solution)/shard_map/ppermute | solution.py:41
  57.0 21.8 %collective-permute-start.10 = (bf16[4,2,512,256]{3,2,1,0:T(8,128)(2,1)}, bf16[4,2,512,256]{3,2,1,0:T(8,128)(2,1)}, u32[]{:S(2)}, u32[]{:S(2)}) collective-permute-start(bf16[4,2,512,256]{3,2,1,0:T(8,128)(2,1)} %pad_maximum_fusion.own_ref), channel_id=1, source_target_pairs={{0,32},{32,0},{1,33},{33,1},{2,34},{34,2},{3,35},{35,3},{4,36},{36... | collective-permute-start | bytes 6291464 | tf_op jit(solution)/shard_map/ppermute | solution.py:41
  75.2 28.1 %collective-permute-start.13 = (bf16[4,2,512,256]{3,2,1,0:T(8,128)(2,1)S(1)}, bf16[4,2,512,256]{3,2,1,0:T(8,128)(2,1)}, u32[]{:S(2)}, u32[]{:S(2)}) collective-permute-start(bf16[4,2,512,256]{3,2,1,0:T(8,128)(2,1)S(1)} %pad_maximum_fusion.1.own_ref), channel_id=1, source_target_pairs={{0,32},{32,0},{1,33},{33,1},{2,34},{34,2},{3,35},{35,3},{4,36},{36... | collective-permute-start | bytes 6291464 | tf_op jit(solution)/shard_map/ppermute | solution.py:41
  83.8 12.8 %collective-permute-start.11 = (f32[128,256]{1,0:T(8,128)S(1)}, f32[128,256]{1,0:T(8,128)S(1)}, u32[]{:S(2)}, u32[]{:S(2)}) collective-permute-start(f32[128,256]{1,0:T(8,128)S(1)} %get-tuple-element.29), channel_id=1, source_target_pairs={{0,16},{16,0},{1,17},{17,1},{2,18},{18,2},{3,19},{19,3},{4,20},{20... | collective-permute-start | bytes 393224 | tf_op jit(solution)/shard_map/ppermute | solution.py:41
  96.6 10.4 %collective-permute-start.12 = (bf16[128,256]{1,0:T(8,128)(2,1)S(1)}, bf16[128,256]{1,0:T(8,128)(2,1)S(1)}, u32[]{:S(2)}, u32[]{:S(2)}) collective-permute-start(bf16[128,256]{1,0:T(8,128)(2,1)S(1)} %multiply_convert_fusion.1), channel_id=1, source_target_pairs={{0,0},{1,1},{2,32},{3,33},{4,64},{5,65},{6,96},{7,97},{8,128},{9,1... | collective-permute-start | bytes 196616 | tf_op jit(solution)/shard_map/ppermute | solution.py:41
  107.6 35.8 %all-to-all-start = ((bf16[4,128,256]{2,1,0:T(8,128)(2,1)}), bf16[4,128,256]{2,1,0:T(8,128)(2,1)S(1)}, u32[]{:S(2)}, u32[]{:S(2)}) async-start(bf16[4,128,256]{2,1,0:T(8,128)(2,1)} %broadcast_in_dim.4), calls=%async_computation | async-start | bytes 524288 | tf_op jit(solution)/shard_map/all_to_all | solution.py:19
  129.1 7.7 %collective-permute-start.14 = (f32[2,128,256]{2,1,0:T(8,128)S(1)}, f32[2,128,256]{2,1,0:T(8,128)S(1)}, u32[]{:S(2)}, u32[]{:S(2)}) collective-permute-start(f32[2,128,256]{2,1,0:T(8,128)S(1)} %get-tuple-element.37), channel_id=1, source_target_pairs={{0,0},{16,256},{256,16},{272,272},{1,1},{17,257},{257,17},{273,273... | collective-permute-start | bytes 786440 | tf_op jit(solution)/shard_map/ppermute | solution.py:41
  129.7 10.4 %collective-permute-start.15 = (f32[2,128,256]{2,1,0:T(8,128)S(1)}, f32[2,128,256]{2,1,0:T(8,128)S(1)}, u32[]{:S(2)}, u32[]{:S(2)}) collective-permute-start(f32[2,128,256]{2,1,0:T(8,128)S(1)} %get-tuple-element.38), channel_id=1, source_target_pairs={{0,256},{16,0},{256,272},{272,16},{1,257},{17,1},{257,273},{273,17... | collective-permute-start | bytes 786440 | tf_op jit(solution)/shard_map/ppermute | solution.py:41
  144.6 34.1 %all-to-all-start.1 = ((bf16[4,4,128,256]{3,2,1,0:T(8,128)(2,1)}), bf16[4,4,128,256]{3,2,1,0:T(8,128)(2,1)S(1)}, u32[]{:S(2)}, u32[]{:S(2)}) async-start(bf16[4,4,128,256]{3,2,1,0:T(8,128)(2,1)} %broadcast_in_dim.5), calls=%async_computation.1 | async-start | bytes 2097152 | tf_op jit(solution)/shard_map/all_to_all | solution.py:19
  153.4 8.2 %collective-permute-start.18 = (bf16[2,128,256]{2,1,0:T(8,128)(2,1)S(1)}, bf16[2,128,256]{2,1,0:T(8,128)(2,1)S(1)}, u32[]{:S(2)}, u32[]{:S(2)}) collective-permute-start(bf16[2,128,256]{2,1,0:T(8,128)(2,1)S(1)} %multiply_convert_fusion), channel_id=1, source_target_pairs={{0,192},{64,0},{128,64},{192,128},{1,193},{65,1},{129,65},{193,129... | collective-permute-start | bytes 393224 | tf_op jit(solution)/shard_map/ppermute | solution.py:41
  155.4 7.4 %collective-permute-start.17 = (bf16[2,128,256]{2,1,0:T(8,128)(2,1)S(1)}, bf16[2,128,256]{2,1,0:T(8,128)(2,1)S(1)}, u32[]{:S(2)}, u32[]{:S(2)}) collective-permute-start(bf16[2,128,256]{2,1,0:T(8,128)(2,1)S(1)} %multiply_convert_fusion), channel_id=1, source_target_pairs={{0,128},{64,192},{128,0},{192,64},{1,129},{65,193},{129,1},{193,65... | collective-permute-start | bytes 393224 | tf_op jit(solution)/shard_map/ppermute | solution.py:41
  159.7 6.9 %collective-permute-start.16 = (bf16[2,128,256]{2,1,0:T(8,128)(2,1)S(1)}, bf16[2,128,256]{2,1,0:T(8,128)(2,1)S(1)}, u32[]{:S(2)}, u32[]{:S(2)}) collective-permute-start(bf16[2,128,256]{2,1,0:T(8,128)(2,1)S(1)} %multiply_convert_fusion), channel_id=1, source_target_pairs={{0,64},{64,128},{128,192},{192,0},{1,65},{65,129},{129,193},{193,1... | collective-permute-start | bytes 393224 | tf_op jit(solution)/shard_map/ppermute | solution.py:41
  166.7 6.1 %collective-permute-start.19 = (bf16[4,2,128,256]{3,2,1,0:T(8,128)(2,1)S(1)}, bf16[4,2,128,256]{3,2,1,0:T(8,128)(2,1)S(1)}, u32[]{:S(2)}, u32[]{:S(2)}) collective-permute-start(bf16[4,2,128,256]{3,2,1,0:T(8,128)(2,1)S(1)} %pad_maximum_fusion.4.own_ref), channel_id=1, source_target_pairs={{0,32},{32,0},{1,33},{33,1},{2,34},{34,2},{3,35},{35,3},{4,36},{36... | collective-permute-start | bytes 1572872 | tf_op jit(solution)/shard_map/ppermute | solution.py:41
  179.9 14.5 %collective-permute-start.20 = (f32[256,512]{1,0:T(8,128)S(1)}, f32[256,512]{1,0:T(8,128)S(1)}, u32[]{:S(2)}, u32[]{:S(2)}) collective-permute-start(f32[256,512]{1,0:T(8,128)S(1)} %shard_map.49), channel_id=1, source_target_pairs={{0,16},{16,0},{1,17},{17,1},{2,18},{18,2},{3,19},{19,3},{4,20},{20... | collective-permute-start | bytes 1572872 | tf_op jit(solution)/shard_map/ppermute | solution.py:41
Sparse Core Ops, SparseCore 0:
  9.4 70.2 all-gather.2

commit v12 on v11

--- a/solution.py
+++ b/solution.py
@@ -74,15 +74,15 @@
 def corrected_kernel(at_ref, own_ref, other_ref, s_ref, out_ref):
     y, c, k = at_ref[0], at_ref[1], at_ref[2]
     for h in range(2):
-        acc = jnp.zeros((256, 256), jnp.float32)
+        acc = jnp.zeros((256, 128), jnp.float32)
         for j in range(4):
-            at = lax.rem(y + 4 - j, 4) + 4 * h
+            at = 4 * lax.rem(y + 4 - j, 4) + h
             for act, core in ((own_ref, c), (other_ref, 1 - c)):
                 acc += lax.dot_general(
-                    act[j, k], s_ref[at + 8 * core],
+                    act[j, k], s_ref[at + 2 * core],
                     (((0,), (0,)), ((), ())), preferred_element_type=jnp.float32,
                 )
-        out_ref[:, 256 * h:256 * h + 256] = acc
+        out_ref[:, 128 * h:128 * h + 128] = acc
 
 
 def rotate(at, x, part, basis, paired):
@@ -107,7 +107,7 @@
 def correct(at, acts, grads):
     return pl.pallas_call(
         corrected_kernel,
-        out_shape=jax.ShapeDtypeStruct((256, 512), jnp.float32),
+        out_shape=jax.ShapeDtypeStruct((256, 256), jnp.float32),
         in_specs=[SMEM] + [VMEM] * 3,
         out_specs=VMEM,
         compiler_params=PARAMS,
@@ -142,30 +142,35 @@
     every = lax.all_gather(both, ("zh", "zl"), axis=0, tiled=False)
     grad_pair = cross(grad_basis)
     act_basis, grad_pair = lax.optimization_barrier((act_basis, grad_pair))
-    grad_panels = both_cores(shifts(grad_pair))
-    act_shifts, grad_own = lax.optimization_barrier((shifts(cross(act_basis)), grad_panels[0]))
-    grad_panels = (grad_own, grad_panels[1])
+    grad_shifts, act_pair = lax.optimization_barrier((shifts(grad_pair), cross(act_basis)))
+    grad_panels = both_cores(grad_shifts)
+    act_pair, grad_own = lax.optimization_barrier((act_pair, grad_panels[0]))
+    act_shifts = shifts(act_pair)
 
     mine, theirs = rotate(at, every, 1, grad_panels, 0)
     rotated_grad = mine + swap(theirs, "xl")
     grad_square = (rotated_grad * rotated_grad).astype(jnp.bfloat16)
+    act_shifts, grad_square = lax.optimization_barrier((act_shifts, grad_square))
     grad_square = move(
         grad_square, AXES, lambda a, b, e, p, q, r: (p, q, r // 2, a, b, 2 * e + r % 2)
     )
 
     parts = rotate(at, every, 0, both_cores(act_shifts), 1)
     grad_square, parts = lax.optimization_barrier((grad_square, parts))
-    grad_block = to_all(grad_square, ("zh",), 4)
+    first = to_all(grad_square[:, :128], ("zh", "zl"), 16)
     parts = [move(parts[k], ("xh", "xl"), lambda a, p, k=k: (p ^ k, a)) for k in range(2)]
     rotated_act = parts[0] + parts[1]
     act_square = (rotated_act * rotated_act).astype(jnp.bfloat16)
-    grad_block, act_square = lax.optimization_barrier((grad_block, act_square))
-    grad_block = to_all(grad_block, ("zl",), 4).reshape(16, 128, 256)
+    second, act_square = lax.optimization_barrier((grad_square[:, 128:], act_square))
+    second = to_all(second, ("zh", "zl"), 16)
     acts = both_cores(shifts(act_square))
 
-    theirs = swap(correct(jnp.stack([y, c, 1 - turned]), acts, grad_block), "xl")
-    mine = correct(at, acts, grad_block)
-    return (mine + theirs) * (1.0 / tokens)
+    halves = []
+    for grads in (first, second):
+        theirs = swap(correct(jnp.stack([y, c, 1 - turned]), acts, grads), "xl")
+        halves.append((correct(at, acts, grads) + theirs) * (1.0 / tokens))
+    low, high = halves
+    return jnp.concatenate([low[:, :128], high[:, :128], low[:, 128:], high[:, 128:]], axis=1)
 
 
 def solution(mesh):

time: 204 us -> 209 us (1.025)
  the two profiles are of different devices: /device:TPU:1 before, /device:TPU:2 now
where the time goes in v12:
time: 209 us; the launch traced here: 208 us
  starting transfers between devices  94.8 us (45%)
  waiting for transfers between devices  83.4 us (40%)
  between operations  13.7 us (7%)
  Pallas kernels  9.49 us (5%)
  other arithmetic  4.74 us (2%)
    ppermute x22, starting transfers between devices, move(): return lax.ppermute(x, axes, pairs)  68.6 us
    ppermute x22, waiting for transfers between devices, move(): return lax.ppermute(x, axes, pairs)  44 us
    all_to_all x2, starting transfers between devices, to_all(): return lax.all_to_all(spread, axes, split_axis=0, concat_axis=0, tiled=True)  26.3 us
    all_gather x1, waiting for transfers between devices, on_device(): every = lax.all_gather(both, ('zh', 'zl'), axis=0, tiled=False)  20.7 us
    all_to_all x2, waiting for transfers between devices, to_all(): return lax.all_to_all(spread, axes, split_axis=0, concat_axis=0, tiled=True)  18.7 us
    pallas_call x2, Pallas kernels, rotate(): pl.pallas_call(functools.partial(rotate_kernel, part), out_shape=[out, ou...  5.45 us
  transfers between devices with their start and end apart: 25, of which 14 were waited for; matrix products, arithmetic and copies ran while one was open for 0% of the time, Pallas kernels for 5%

profile of v12, /device:TPU:2, one launch (start us, length us, event | category | flops | bytes accessed | tf_op | source)
XLA Modules:
  0.0 208.1 jit_solution(10871634995587940877)
XLA Ops:
  6.5 1.5 pad_maximum_fusion.6
  8.1 0.0 all-gather.3.cloned.1.call-update
  8.1 3.4 %collective-permute-start = (bf16[512,256]{1,0:T(8,128)(2,1)}, bf16[512,256]{1,0:T(8,128)(2,1)S(1)}, u32[]{:S(2)}, u32[]{:S(2)}) collective-permute-start(bf16[512,256]{1,0:T(8,128)(2,1)} %param.7), channel_id=1, source_target_pairs={{0,0},{16,256},{256,16},{272,272},{1,1},{17,257},{257,17},{273,273... | collective-permute-start | bytes 786440 | tf_op jit(solution)/shard_map/ppermute | solution.py:41
  11.5 6.0 %collective-permute-start.1 = (bf16[512,256]{1,0:T(8,128)(2,1)}, bf16[512,256]{1,0:T(8,128)(2,1)S(1)}, u32[]{:S(2)}, u32[]{:S(2)}) collective-permute-start(bf16[512,256]{1,0:T(8,128)(2,1)} %param.7), channel_id=1, source_target_pairs={{0,256},{16,0},{256,272},{272,16},{1,257},{17,1},{257,273},{273,17... | collective-permute-start | bytes 786440 | tf_op jit(solution)/shard_map/ppermute | solution.py:41
  17.5 6.3 %collective-permute-done = bf16[512,256]{1,0:T(8,128)(2,1)S(1)} collective-permute-done((bf16[512,256]{1,0:T(8,128)(2,1)}, bf16[512,256]{1,0:T(8,128)(2,1)S(1)}, u32[]{:S(2)}, u32[]{:S(2)}) %collective-permute-start) | collective-permute-done | bytes 262176 | tf_op jit(solution)/shard_map/ppermute | solution.py:41
  23.9 0.0 collective-permute-done.1
  23.9 0.1 pad_maximum_fusion.2
  23.9 3.5 %collective-permute-start.2 = (bf16[2,512,256]{2,1,0:T(8,128)(2,1)S(1)}, bf16[2,512,256]{2,1,0:T(8,128)(2,1)S(1)}, u32[]{:S(2)}, u32[]{:S(2)}) collective-permute-start(bf16[2,512,256]{2,1,0:T(8,128)(2,1)S(1)} %pad_maximum_fusion.2), channel_id=1, source_target_pairs={{0,64},{64,128},{128,192},{192,0},{1,65},{65,129},{129,193},{193,1... | collective-permute-start | bytes 1572872 | tf_op jit(solution)/shard_map/ppermute | solution.py:41
  27.4 4.8 %collective-permute-start.3 = (bf16[2,512,256]{2,1,0:T(8,128)(2,1)S(1)}, bf16[2,512,256]{2,1,0:T(8,128)(2,1)S(1)}, u32[]{:S(2)}, u32[]{:S(2)}) collective-permute-start(bf16[2,512,256]{2,1,0:T(8,128)(2,1)S(1)} %pad_maximum_fusion.2), channel_id=1, source_target_pairs={{0,128},{64,192},{128,0},{192,64},{1,129},{65,193},{129,1},{193,65... | collective-permute-start | bytes 1572872 | tf_op jit(solution)/shard_map/ppermute | solution.py:41
  32.2 3.3 %collective-permute-start.4 = (bf16[2,512,256]{2,1,0:T(8,128)(2,1)S(1)}, bf16[2,512,256]{2,1,0:T(8,128)(2,1)S(1)}, u32[]{:S(2)}, u32[]{:S(2)}) collective-permute-start(bf16[2,512,256]{2,1,0:T(8,128)(2,1)S(1)} %pad_maximum_fusion.2), channel_id=1, source_target_pairs={{0,192},{64,0},{128,64},{192,128},{1,193},{65,1},{129,65},{193,129... | collective-permute-start | bytes 1572872 | tf_op jit(solution)/shard_map/ppermute | solution.py:41
  35.5 3.4 %collective-permute-start.5 = (bf16[512,256]{1,0:T(8,128)(2,1)}, bf16[512,256]{1,0:T(8,128)(2,1)S(1)}, u32[]{:S(2)}, u32[]{:S(2)}) collective-permute-start(bf16[512,256]{1,0:T(8,128)(2,1)} %param.6), channel_id=1, source_target_pairs={{0,0},{16,256},{256,16},{272,272},{1,1},{17,257},{257,17},{273,273... | collective-permute-start | bytes 786440 | tf_op jit(solution)/shard_map/ppermute | solution.py:41
  38.9 1.9 collective-permute-start.6
  40.8 8.8 %collective-permute-done.5 = bf16[512,256]{1,0:T(8,128)(2,1)S(1)} collective-permute-done((bf16[512,256]{1,0:T(8,128)(2,1)}, bf16[512,256]{1,0:T(8,128)(2,1)S(1)}, u32[]{:S(2)}, u32[]{:S(2)}) %collective-permute-start.5) | collective-permute-done | bytes 262176 | tf_op jit(solution)/shard_map/ppermute | solution.py:41
  49.6 0.0 collective-permute-done.6
  49.6 0.1 pad_maximum_fusion.3
  49.7 0.0 collective-permute-done.2
  49.7 1.6 collective-permute-done.3
  51.3 1.4 collective-permute-done.4
  52.6 0.3 pad_maximum_fusion.own_ref
  52.9 1.9 collective-permute-start.10
  54.8 4.5 %collective-permute-start.7 = (bf16[2,512,256]{2,1,0:T(8,128)(2,1)S(1)}, bf16[2,512,256]{2,1,0:T(8,128)(2,1)}, u32[]{:S(2)}, u32[]{:S(2)}) collective-permute-start(bf16[2,512,256]{2,1,0:T(8,128)(2,1)S(1)} %pad_maximum_fusion.3), channel_id=1, source_target_pairs={{0,64},{64,128},{128,192},{192,0},{1,65},{65,129},{129,193},{193,1... | collective-permute-start | bytes 1572872 | tf_op jit(solution)/shard_map/ppermute | solution.py:41
  59.4 3.4 %collective-permute-start.8 = (bf16[2,512,256]{2,1,0:T(8,128)(2,1)S(1)}, bf16[2,512,256]{2,1,0:T(8,128)(2,1)}, u32[]{:S(2)}, u32[]{:S(2)}) collective-permute-start(bf16[2,512,256]{2,1,0:T(8,128)(2,1)S(1)} %pad_maximum_fusion.3), channel_id=1, source_target_pairs={{0,128},{64,192},{128,0},{192,64},{1,129},{65,193},{129,1},{193,65... | collective-permute-start | bytes 1572872 | tf_op jit(solution)/shard_map/ppermute | solution.py:41
  62.8 3.6 %collective-permute-start.9 = (bf16[2,512,256]{2,1,0:T(8,128)(2,1)S(1)}, bf16[2,512,256]{2,1,0:T(8,128)(2,1)}, u32[]{:S(2)}, u32[]{:S(2)}) collective-permute-start(bf16[2,512,256]{2,1,0:T(8,128)(2,1)S(1)} %pad_maximum_fusion.3), channel_id=1, source_target_pairs={{0,192},{64,0},{128,64},{192,128},{1,193},{65,1},{129,65},{193,129... | collective-permute-start | bytes 1572872 | tf_op jit(solution)/shard_map/ppermute | solution.py:41
  66.4 0.1 pad_add_fusion.at_ref
  66.4 0.0 collective-permute-done.10.other_hbm
  66.4 20.7 %all-gather.3.cloned.1.call-done = bf16[32,128,256]{2,1,0:T(8,128)(2,1)} async-done(((bf16[2,128,256]{2,1,0:T(8,128)(2,1)}), bf16[32,128,256]{2,1,0:T(8,128)(2,1)}) %all-gather.3.cloned.1.call-update) | async-done | bytes 2097168 | tf_op jit(solution)/shard_map/all_gather | solution.py:142
  87.1 2.9 %shard_map.46 = (f32[128,256]{1,0:T(8,128)S(1)}, f32[128,256]{1,0:T(8,128)S(1)}) custom-call(s32[3]{0:T(128)S(1)} %pad_add_fusion.at_ref, bf16[16,2,128,256]{3,2,1,0:T(8,128)(2,1)} %bitcast.23, bf16[4,2,512,256]{3,2,1,0:T(8,128)(2,1)S(1)} %pad_maximum_fusion.own_ref, bf16[4,2,512,256]{3,2,1,0:T(8,128)(2,1)} %collective-permute-done.10.other_hbm), custom_call_target="tpu_custom_call" | custom-call | tf_op jit(solution)/shard_map/pallas_call | solution.py:94
  90.1 2.6 %collective-permute-start.11 = (f32[128,256]{1,0:T(8,128)S(1)}, f32[128,256]{1,0:T(8,128)S(1)}, u32[]{:S(2)}, u32[]{:S(2)}) collective-permute-start(f32[128,256]{1,0:T(8,128)S(1)} %get-tuple-element.40), channel_id=1, source_target_pairs={{0,16},{16,0},{1,17},{17,1},{2,18},{18,2},{3,19},{19,3},{4,20},{20... | collective-permute-start | bytes 393224 | tf_op jit(solution)/shard_map/ppermute | solution.py:41
  92.7 4.3 %collective-permute-done.11 = f32[128,256]{1,0:T(8,128)S(1)} collective-permute-done((f32[128,256]{1,0:T(8,128)S(1)}, f32[128,256]{1,0:T(8,128)S(1)}, u32[]{:S(2)}, u32[]{:S(2)}) %collective-permute-start.11) | collective-permute-done | bytes 131104 | tf_op jit(solution)/shard_map/ppermute | solution.py:41
  97.0 0.0 collective-permute-done.8
  97.0 0.0 collective-permute-done.9
  97.0 1.6 pad_maximum_fusion.1.own_ref
  98.6 1.9 collective-permute-start.13
  100.5 3.4 %collective-permute-start.12 = (bf16[128,256]{1,0:T(8,128)(2,1)S(1)}, bf16[128,256]{1,0:T(8,128)(2,1)S(1)}, u32[]{:S(2)}, u32[]{:S(2)}) collective-permute-start(bf16[128,256]{1,0:T(8,128)(2,1)S(1)} %multiply_convert_fusion.1), channel_id=1, source_target_pairs={{0,0},{1,1},{2,32},{3,33},{4,64},{5,65},{6,96},{7,97},{8,128},{9,1... | collective-permute-start | bytes 196616 | tf_op jit(solution)/shard_map/ppermute | solution.py:41
  104.0 0.7 collective-permute-done.13.other_hbm
  104.7 2.5 %shard_map.47 = (f32[2,128,256]{2,1,0:T(8,128)S(1)}, f32[2,128,256]{2,1,0:T(8,128)S(1)}) custom-call(s32[3]{0:T(128)S(1)} %pad_add_fusion.at_ref, bf16[16,2,128,256]{3,2,1,0:T(8,128)(2,1)} %bitcast.24, bf16[4,2,512,256]{3,2,1,0:T(8,128)(2,1)S(1)} %pad_maximum_fusion.1.own_ref, bf16[4,2,512,256]{3,2,1,0:T(8,128)(2,1)S(1)} %collective-permute-done.13.other_hbm), custom_call_target="tpu_custom_call" | custom-call | tf_op jit(solution)/shard_map/pallas_call | solution.py:94
  107.2 0.9 broadcast_in_dim.4
  108.1 19.3 %all-to-all-start = ((bf16[16,128,128]{2,1,0:T(8,128)(2,1)}), bf16[16,128,128]{2,1,0:T(8,128)(2,1)S(1)}, u32[]{:S(2)}, u32[]{:S(2)}) async-start(bf16[16,128,128]{2,1,0:T(8,128)(2,1)} %broadcast_in_dim.4), calls=%async_computation | async-start | bytes 1048576 | tf_op jit(solution)/shard_map/all_to_all | solution.py:19
  127.5 3.4 %collective-permute-start.14 = (f32[2,128,256]{2,1,0:T(8,128)S(1)}, f32[2,128,256]{2,1,0:T(8,128)S(1)}, u32[]{:S(2)}, u32[]{:S(2)}) collective-permute-start(f32[2,128,256]{2,1,0:T(8,128)S(1)} %get-tuple-element.49), channel_id=1, source_target_pairs={{0,0},{16,256},{256,16},{272,272},{1,1},{17,257},{257,17},{273,273... | collective-permute-start | bytes 786440 | tf_op jit(solution)/shard_map/ppermute | solution.py:41
  130.8 1.9 collective-permute-start.15
  132.8 8.9 %collective-permute-done.14 = f32[2,128,256]{2,1,0:T(8,128)S(1)} collective-permute-done((f32[2,128,256]{2,1,0:T(8,128)S(1)}, f32[2,128,256]{2,1,0:T(8,128)S(1)}, u32[]{:S(2)}, u32[]{:S(2)}) %collective-permute-start.14) | collective-permute-done | bytes 262176 | tf_op jit(solution)/shard_map/ppermute | solution.py:41
  141.7 0.0 collective-permute-done.15
  141.7 13.1 %all-to-all-done.s_ref = bf16[16,128,128]{2,1,0:T(8,128)(2,1)S(1)} async-done(((bf16[16,128,128]{2,1,0:T(8,128)(2,1)}), bf16[16,128,128]{2,1,0:T(8,128)(2,1)S(1)}, u32[]{:S(2)}, u32[]{:S(2)}) %all-to-all-start) | async-done | bytes 524320 | tf_op jit(solution)/shard_map/all_to_all | solution.py:19
  154.8 0.9 broadcast_in_dim.5
  155.7 7.0 %all-to-all-start.1 = ((bf16[16,128,128]{2,1,0:T(8,128)(2,1)}), bf16[16,128,128]{2,1,0:T(8,128)(2,1)S(1)}, u32[]{:S(2)}, u32[]{:S(2)}) async-start(bf16[16,128,128]{2,1,0:T(8,128)(2,1)} %broadcast_in_dim.5), calls=%async_computation.1 | async-start | bytes 1048576 | tf_op jit(solution)/shard_map/all_to_all | solution.py:19
  162.7 2.4 %collective-permute-start.16 = (bf16[2,128,256]{2,1,0:T(8,128)(2,1)S(1)}, bf16[2,128,256]{2,1,0:T(8,128)(2,1)S(1)}, u32[]{:S(2)}, u32[]{:S(2)}) collective-permute-start(bf16[2,128,256]{2,1,0:T(8,128)(2,1)S(1)} %multiply_convert_fusion), channel_id=1, source_target_pairs={{0,64},{64,128},{128,192},{192,0},{1,65},{65,129},{129,193},{193,1... | collective-permute-start | bytes 393224 | tf_op jit(solution)/shard_map/ppermute | solution.py:41
  165.1 5.7 %collective-permute-start.17 = (bf16[2,128,256]{2,1,0:T(8,128)(2,1)S(1)}, bf16[2,128,256]{2,1,0:T(8,128)(2,1)S(1)}, u32[]{:S(2)}, u32[]{:S(2)}) collective-permute-start(bf16[2,128,256]{2,1,0:T(8,128)(2,1)S(1)} %multiply_convert_fusion), channel_id=1, source_target_pairs={{0,128},{64,192},{128,0},{192,64},{1,129},{65,193},{129,1},{193,65... | collective-permute-start | bytes 393224 | tf_op jit(solution)/shard_map/ppermute | solution.py:41
  170.7 1.9 collective-permute-start.18
  172.7 1.9 collective-permute-done.17
  174.5 3.0 %collective-permute-done.18 = bf16[2,128,256]{2,1,0:T(8,128)(2,1)S(1)} collective-permute-done((bf16[2,128,256]{2,1,0:T(8,128)(2,1)S(1)}, bf16[2,128,256]{2,1,0:T(8,128)(2,1)S(1)}, u32[]{:S(2)}, u32[]{:S(2)}) %collective-permute-start.18) | collective-permute-done | bytes 131104 | tf_op jit(solution)/shard_map/ppermute | solution.py:41
  177.6 0.1 pad_maximum_fusion.4.own_ref
  177.7 1.9 collective-permute-start.19
  179.6 0.1 pad_add_fusion.2.at_ref
  179.7 1.8 collective-permute-done.19.other_ref
  181.5 1.0 shard_map.49
  182.5 1.9 collective-permute-start.20
  184.4 1.0 shard_map.48
  185.4 5.6 %all-to-all-done.1.s_ref = bf16[16,128,128]{2,1,0:T(8,128)(2,1)S(1)} async-done(((bf16[16,128,128]{2,1,0:T(8,128)(2,1)}), bf16[16,128,128]{2,1,0:T(8,128)(2,1)S(1)}, u32[]{:S(2)}, u32[]{:S(2)}) %all-to-all-start.1) | async-done | bytes 524320 | tf_op jit(solution)/shard_map/all_to_all | solution.py:19
  191.1 1.0 shard_map.51
  192.1 1.9 collective-permute-start.21
  194.0 0.1 add_multiply_fusion.1
  194.1 1.0 shard_map.50
  195.1 5.2 %collective-permute-done.21 = f32[256,256]{1,0:T(8,128)S(1)} collective-permute-done((f32[256,256]{1,0:T(8,128)S(1)}, f32[256,256]{1,0:T(8,128)S(1)}, u32[]{:S(2)}, u32[]{:S(2)}) %collective-permute-start.21) | collective-permute-done | bytes 262176 | tf_op jit(solution)/shard_map/ppermute | solution.py:41
  200.4 0.9 pad_maximum_fusion.5
  (11 shorter events, 0.1 us)
Async XLA Ops:
  6.5 80.6 %all-gather.3.cloned.1.call-start = ((), (), s32[]{:S(2)}) async-start(), calls=%async_computation.2 | async-start | bytes 2228224 | tf_op jit(solution)/shard_map/all_gather | solution.py:142
  8.1 15.8 %collective-permute-start = (bf16[512,256]{1,0:T(8,128)(2,1)}, bf16[512,256]{1,0:T(8,128)(2,1)S(1)}, u32[]{:S(2)}, u32[]{:S(2)}) collective-permute-start(bf16[512,256]{1,0:T(8,128)(2,1)} %param.7), channel_id=1, source_target_pairs={{0,0},{16,256},{256,16},{272,272},{1,1},{17,257},{257,17},{273,273... | collective-permute-start | bytes 786440 | tf_op jit(solution)/shard_map/ppermute | solution.py:41
  11.5 12.4 %collective-permute-start.1 = (bf16[512,256]{1,0:T(8,128)(2,1)}, bf16[512,256]{1,0:T(8,128)(2,1)S(1)}, u32[]{:S(2)}, u32[]{:S(2)}) collective-permute-start(bf16[512,256]{1,0:T(8,128)(2,1)} %param.7), channel_id=1, source_target_pairs={{0,256},{16,0},{256,272},{272,16},{1,257},{17,1},{257,273},{273,17... | collective-permute-start | bytes 786440 | tf_op jit(solution)/shard_map/ppermute | solution.py:41
  23.9 25.7 %collective-permute-start.2 = (bf16[2,512,256]{2,1,0:T(8,128)(2,1)S(1)}, bf16[2,512,256]{2,1,0:T(8,128)(2,1)S(1)}, u32[]{:S(2)}, u32[]{:S(2)}) collective-permute-start(bf16[2,512,256]{2,1,0:T(8,128)(2,1)S(1)} %pad_maximum_fusion.2), channel_id=1, source_target_pairs={{0,64},{64,128},{128,192},{192,0},{1,65},{65,129},{129,193},{193,1... | collective-permute-start | bytes 1572872 | tf_op jit(solution)/shard_map/ppermute | solution.py:41
  27.4 23.9 %collective-permute-start.3 = (bf16[2,512,256]{2,1,0:T(8,128)(2,1)S(1)}, bf16[2,512,256]{2,1,0:T(8,128)(2,1)S(1)}, u32[]{:S(2)}, u32[]{:S(2)}) collective-permute-start(bf16[2,512,256]{2,1,0:T(8,128)(2,1)S(1)} %pad_maximum_fusion.2), channel_id=1, source_target_pairs={{0,128},{64,192},{128,0},{192,64},{1,129},{65,193},{129,1},{193,65... | collective-permute-start | bytes 1572872 | tf_op jit(solution)/shard_map/ppermute | solution.py:41
  32.2 20.4 %collective-permute-start.4 = (bf16[2,512,256]{2,1,0:T(8,128)(2,1)S(1)}, bf16[2,512,256]{2,1,0:T(8,128)(2,1)S(1)}, u32[]{:S(2)}, u32[]{:S(2)}) collective-permute-start(bf16[2,512,256]{2,1,0:T(8,128)(2,1)S(1)} %pad_maximum_fusion.2), channel_id=1, source_target_pairs={{0,192},{64,0},{128,64},{192,128},{1,193},{65,1},{129,65},{193,129... | collective-permute-start | bytes 1572872 | tf_op jit(solution)/shard_map/ppermute | solution.py:41
  35.5 14.1 %collective-permute-start.5 = (bf16[512,256]{1,0:T(8,128)(2,1)}, bf16[512,256]{1,0:T(8,128)(2,1)S(1)}, u32[]{:S(2)}, u32[]{:S(2)}) collective-permute-start(bf16[512,256]{1,0:T(8,128)(2,1)} %param.6), channel_id=1, source_target_pairs={{0,0},{16,256},{256,16},{272,272},{1,1},{17,257},{257,17},{273,273... | collective-permute-start | bytes 786440 | tf_op jit(solution)/shard_map/ppermute | solution.py:41
  38.9 10.7 %collective-permute-start.6 = (bf16[512,256]{1,0:T(8,128)(2,1)}, bf16[512,256]{1,0:T(8,128)(2,1)S(1)}, u32[]{:S(2)}, u32[]{:S(2)}) collective-permute-start(bf16[512,256]{1,0:T(8,128)(2,1)} %param.6), channel_id=1, source_target_pairs={{0,256},{16,0},{256,272},{272,16},{1,257},{17,1},{257,273},{273,17... | collective-permute-start | bytes 786440 | tf_op jit(solution)/shard_map/ppermute | solution.py:41
  52.9 13.5 %collective-permute-start.10 = (bf16[4,2,512,256]{3,2,1,0:T(8,128)(2,1)S(1)}, bf16[4,2,512,256]{3,2,1,0:T(8,128)(2,1)}, u32[]{:S(2)}, u32[]{:S(2)}) collective-permute-start(bf16[4,2,512,256]{3,2,1,0:T(8,128)(2,1)S(1)} %pad_maximum_fusion.own_ref), channel_id=1, source_target_pairs={{0,32},{32,0},{1,33},{33,1},{2,34},{34,2},{3,35},{35,3},{4,36},{36... | collective-permute-start | bytes 6291464 | tf_op jit(solution)/shard_map/ppermute | solution.py:41
  54.8 42.1 %collective-permute-start.7 = (bf16[2,512,256]{2,1,0:T(8,128)(2,1)S(1)}, bf16[2,512,256]{2,1,0:T(8,128)(2,1)}, u32[]{:S(2)}, u32[]{:S(2)}) collective-permute-start(bf16[2,512,256]{2,1,0:T(8,128)(2,1)S(1)} %pad_maximum_fusion.3), channel_id=1, source_target_pairs={{0,64},{64,128},{128,192},{192,0},{1,65},{65,129},{129,193},{193,1... | collective-permute-start | bytes 1572872 | tf_op jit(solution)/shard_map/ppermute | solution.py:41
  59.4 37.6 %collective-permute-start.8 = (bf16[2,512,256]{2,1,0:T(8,128)(2,1)S(1)}, bf16[2,512,256]{2,1,0:T(8,128)(2,1)}, u32[]{:S(2)}, u32[]{:S(2)}) collective-permute-start(bf16[2,512,256]{2,1,0:T(8,128)(2,1)S(1)} %pad_maximum_fusion.3), channel_id=1, source_target_pairs={{0,128},{64,192},{128,0},{192,64},{1,129},{65,193},{129,1},{193,65... | collective-permute-start | bytes 1572872 | tf_op jit(solution)/shard_map/ppermute | solution.py:41
  62.8 34.2 %collective-permute-start.9 = (bf16[2,512,256]{2,1,0:T(8,128)(2,1)S(1)}, bf16[2,512,256]{2,1,0:T(8,128)(2,1)}, u32[]{:S(2)}, u32[]{:S(2)}) collective-permute-start(bf16[2,512,256]{2,1,0:T(8,128)(2,1)S(1)} %pad_maximum_fusion.3), channel_id=1, source_target_pairs={{0,192},{64,0},{128,64},{192,128},{1,193},{65,1},{129,65},{193,129... | collective-permute-start | bytes 1572872 | tf_op jit(solution)/shard_map/ppermute | solution.py:41
  90.1 6.9 %collective-permute-start.11 = (f32[128,256]{1,0:T(8,128)S(1)}, f32[128,256]{1,0:T(8,128)S(1)}, u32[]{:S(2)}, u32[]{:S(2)}) collective-permute-start(f32[128,256]{1,0:T(8,128)S(1)} %get-tuple-element.40), channel_id=1, source_target_pairs={{0,16},{16,0},{1,17},{17,1},{2,18},{18,2},{3,19},{19,3},{4,20},{20... | collective-permute-start | bytes 393224 | tf_op jit(solution)/shard_map/ppermute | solution.py:41
  98.6 6.1 %collective-permute-start.13 = (bf16[4,2,512,256]{3,2,1,0:T(8,128)(2,1)S(1)}, bf16[4,2,512,256]{3,2,1,0:T(8,128)(2,1)S(1)}, u32[]{:S(2)}, u32[]{:S(2)}) collective-permute-start(bf16[4,2,512,256]{3,2,1,0:T(8,128)(2,1)S(1)} %pad_maximum_fusion.1.own_ref), channel_id=1, source_target_pairs={{0,32},{32,0},{1,33},{33,1},{2,34},{34,2},{3,35},{35,3},{4,36},{36... | collective-permute-start | bytes 6291464 | tf_op jit(solution)/shard_map/ppermute | solution.py:41
  100.5 6.7 %collective-permute-start.12 = (bf16[128,256]{1,0:T(8,128)(2,1)S(1)}, bf16[128,256]{1,0:T(8,128)(2,1)S(1)}, u32[]{:S(2)}, u32[]{:S(2)}) collective-permute-start(bf16[128,256]{1,0:T(8,128)(2,1)S(1)} %multiply_convert_fusion.1), channel_id=1, source_target_pairs={{0,0},{1,1},{2,32},{3,33},{4,64},{5,65},{6,96},{7,97},{8,128},{9,1... | collective-permute-start | bytes 196616 | tf_op jit(solution)/shard_map/ppermute | solution.py:41
  108.1 46.7 %all-to-all-start = ((bf16[16,128,128]{2,1,0:T(8,128)(2,1)}), bf16[16,128,128]{2,1,0:T(8,128)(2,1)S(1)}, u32[]{:S(2)}, u32[]{:S(2)}) async-start(bf16[16,128,128]{2,1,0:T(8,128)(2,1)} %broadcast_in_dim.4), calls=%async_computation | async-start | bytes 1048576 | tf_op jit(solution)/shard_map/all_to_all | solution.py:19
  127.5 14.2 %collective-permute-start.14 = (f32[2,128,256]{2,1,0:T(8,128)S(1)}, f32[2,128,256]{2,1,0:T(8,128)S(1)}, u32[]{:S(2)}, u32[]{:S(2)}) collective-permute-start(f32[2,128,256]{2,1,0:T(8,128)S(1)} %get-tuple-element.49), channel_id=1, source_target_pairs={{0,0},{16,256},{256,16},{272,272},{1,1},{17,257},{257,17},{273,273... | collective-permute-start | bytes 786440 | tf_op jit(solution)/shard_map/ppermute | solution.py:41
  130.8 10.9 %collective-permute-start.15 = (f32[2,128,256]{2,1,0:T(8,128)S(1)}, f32[2,128,256]{2,1,0:T(8,128)S(1)}, u32[]{:S(2)}, u32[]{:S(2)}) collective-permute-start(f32[2,128,256]{2,1,0:T(8,128)S(1)} %get-tuple-element.50), channel_id=1, source_target_pairs={{0,256},{16,0},{256,272},{272,16},{1,257},{17,1},{257,273},{273,17... | collective-permute-start | bytes 786440 | tf_op jit(solution)/shard_map/ppermute | solution.py:41
  155.7 35.3 %all-to-all-start.1 = ((bf16[16,128,128]{2,1,0:T(8,128)(2,1)}), bf16[16,128,128]{2,1,0:T(8,128)(2,1)S(1)}, u32[]{:S(2)}, u32[]{:S(2)}) async-start(bf16[16,128,128]{2,1,0:T(8,128)(2,1)} %broadcast_in_dim.5), calls=%async_computation.1 | async-start | bytes 1048576 | tf_op jit(solution)/shard_map/all_to_all | solution.py:19
  162.7 10.0 %collective-permute-start.16 = (bf16[2,128,256]{2,1,0:T(8,128)(2,1)S(1)}, bf16[2,128,256]{2,1,0:T(8,128)(2,1)S(1)}, u32[]{:S(2)}, u32[]{:S(2)}) collective-permute-start(bf16[2,128,256]{2,1,0:T(8,128)(2,1)S(1)} %multiply_convert_fusion), channel_id=1, source_target_pairs={{0,64},{64,128},{128,192},{192,0},{1,65},{65,129},{129,193},{193,1... | collective-permute-start | bytes 393224 | tf_op jit(solution)/shard_map/ppermute | solution.py:41
  165.1 9.5 %collective-permute-start.17 = (bf16[2,128,256]{2,1,0:T(8,128)(2,1)S(1)}, bf16[2,128,256]{2,1,0:T(8,128)(2,1)S(1)}, u32[]{:S(2)}, u32[]{:S(2)}) collective-permute-start(bf16[2,128,256]{2,1,0:T(8,128)(2,1)S(1)} %multiply_convert_fusion), channel_id=1, source_target_pairs={{0,128},{64,192},{128,0},{192,64},{1,129},{65,193},{129,1},{193,65... | collective-permute-start | bytes 393224 | tf_op jit(solution)/shard_map/ppermute | solution.py:41
  170.7 6.9 %collective-permute-start.18 = (bf16[2,128,256]{2,1,0:T(8,128)(2,1)S(1)}, bf16[2,128,256]{2,1,0:T(8,128)(2,1)S(1)}, u32[]{:S(2)}, u32[]{:S(2)}) collective-permute-start(bf16[2,128,256]{2,1,0:T(8,128)(2,1)S(1)} %multiply_convert_fusion), channel_id=1, source_target_pairs={{0,192},{64,0},{128,64},{192,128},{1,193},{65,1},{129,65},{193,129... | collective-permute-start | bytes 393224 | tf_op jit(solution)/shard_map/ppermute | solution.py:41
  177.7 3.8 %collective-permute-start.19 = (bf16[4,2,128,256]{3,2,1,0:T(8,128)(2,1)S(1)}, bf16[4,2,128,256]{3,2,1,0:T(8,128)(2,1)S(1)}, u32[]{:S(2)}, u32[]{:S(2)}) collective-permute-start(bf16[4,2,128,256]{3,2,1,0:T(8,128)(2,1)S(1)} %pad_maximum_fusion.4.own_ref), channel_id=1, source_target_pairs={{0,32},{32,0},{1,33},{33,1},{2,34},{34,2},{3,35},{35,3},{4,36},{36... | collective-permute-start | bytes 1572872 | tf_op jit(solution)/shard_map/ppermute | solution.py:41
  182.5 11.5 %collective-permute-start.20 = (f32[256,256]{1,0:T(8,128)S(1)}, f32[256,256]{1,0:T(8,128)S(1)}, u32[]{:S(2)}, u32[]{:S(2)}) collective-permute-start(f32[256,256]{1,0:T(8,128)S(1)} %shard_map.49), channel_id=1, source_target_pairs={{0,16},{16,0},{1,17},{17,1},{2,18},{18,2},{3,19},{19,3},{4,20},{20... | collective-permute-start | bytes 786440 | tf_op jit(solution)/shard_map/ppermute | solution.py:41
  192.1 8.3 %collective-permute-start.21 = (f32[256,256]{1,0:T(8,128)S(1)}, f32[256,256]{1,0:T(8,128)S(1)}, u32[]{:S(2)}, u32[]{:S(2)}) collective-permute-start(f32[256,256]{1,0:T(8,128)S(1)} %shard_map.51), channel_id=1, source_target_pairs={{0,16},{16,0},{1,17},{17,1},{2,18},{18,2},{3,19},{19,3},{4,20},{20... | collective-permute-start | bytes 786440 | tf_op jit(solution)/shard_map/ppermute | solution.py:41
Sparse Core Ops, SparseCore 0:
  9.4 77.6 all-gather.2

commit v13 on v11

--- a/solution.py
+++ b/solution.py
@@ -142,9 +142,10 @@
     every = lax.all_gather(both, ("zh", "zl"), axis=0, tiled=False)
     grad_pair = cross(grad_basis)
     act_basis, grad_pair = lax.optimization_barrier((act_basis, grad_pair))
-    grad_panels = both_cores(shifts(grad_pair))
-    act_shifts, grad_own = lax.optimization_barrier((shifts(cross(act_basis)), grad_panels[0]))
-    grad_panels = (grad_own, grad_panels[1])
+    grad_shifts, act_pair = lax.optimization_barrier((shifts(grad_pair), cross(act_basis)))
+    grad_panels = both_cores(grad_shifts)
+    act_pair, grad_own = lax.optimization_barrier((act_pair, grad_panels[0]))
+    act_shifts = shifts(act_pair)
 
     mine, theirs = rotate(at, every, 1, grad_panels, 0)
     rotated_grad = mine + swap(theirs, "xl")
@@ -152,10 +153,10 @@
     grad_square = move(
         grad_square, AXES, lambda a, b, e, p, q, r: (p, q, r // 2, a, b, 2 * e + r % 2)
     )
+    act_shifts, grad_square = lax.optimization_barrier((act_shifts, grad_square))
+    grad_block = to_all(grad_square, ("zh",), 4)
 
     parts = rotate(at, every, 0, both_cores(act_shifts), 1)
-    grad_square, parts = lax.optimization_barrier((grad_square, parts))
-    grad_block = to_all(grad_square, ("zh",), 4)
     parts = [move(parts[k], ("xh", "xl"), lambda a, p, k=k: (p ^ k, a)) for k in range(2)]
     rotated_act = parts[0] + parts[1]
     act_square = (rotated_act * rotated_act).astype(jnp.bfloat16)

time: 204 us -> 201 us (0.985)
  starting transfers between devices: 122 us -> 109 us
  waiting for transfers between devices: 50.1 us -> 61.5 us
    all_gather x1, waiting for transfers between devices: 0.99 us -> 14.3 us  [on_device(): every = lax.all_gather(both, ('zh', 'zl'), axis=0, tiled=False)]
    all_to_all x2, starting transfers between devices: 30.3 us -> 23 us  [to_all(): return lax.all_to_all(spread, axes, split_axis=0, concat_axis=0, tiled=True)]
    ppermute x21, starting transfers between devices: 91.5 us -> 86 us  [move(): return lax.ppermute(x, axes, pairs)]
where the time goes in v13:
time: 201 us; the launch traced here: 200 us
  starting transfers between devices  109 us (54%)
  waiting for transfers between devices  61.5 us (31%)
  between operations  13.7 us (7%)
  Pallas kernels  9 us (4%)
  other arithmetic  4.52 us (2%)
    ppermute x21, starting transfers between devices, move(): return lax.ppermute(x, axes, pairs)  86 us
    ppermute x21, waiting for transfers between devices, move(): return lax.ppermute(x, axes, pairs)  38.9 us
    all_to_all x2, starting transfers between devices, to_all(): return lax.all_to_all(spread, axes, split_axis=0, concat_axis=0, tiled=True)  23 us
    all_gather x1, waiting for transfers between devices, on_device(): every = lax.all_gather(both, ('zh', 'zl'), axis=0, tiled=False)  14.3 us
    all_to_all x2, waiting for transfers between devices, to_all(): return lax.all_to_all(spread, axes, split_axis=0, concat_axis=0, tiled=True)  8.3 us
    pallas_call x2, Pallas kernels, rotate(): pl.pallas_call(functools.partial(rotate_kernel, part), out_shape=[out, ou...  6.48 us
  transfers between devices with their start and end apart: 24, of which 14 were waited for; matrix products, arithmetic and copies ran while one was open for 1% of the time, Pallas kernels for 4%

profile of v13, /device:TPU:1, one launch (start us, length us, event | category | flops | bytes accessed | tf_op | source)
XLA Modules:
  0.0 199.6 jit_solution(1363636328940068887)
XLA Ops:
  6.5 0.0 all-gather.3.cloned.1.call-start
  6.5 1.5 pad_maximum_fusion.5
  8.1 0.0 all-gather.3.cloned.1.call-update
  8.1 1.6 collective-permute-start
  9.7 6.0 %collective-permute-start.1 = (bf16[512,256]{1,0:T(8,128)(2,1)}, bf16[512,256]{1,0:T(8,128)(2,1)S(1)}, u32[]{:S(2)}, u32[]{:S(2)}) collective-permute-start(bf16[512,256]{1,0:T(8,128)(2,1)} %param.7), channel_id=1, source_target_pairs={{0,256},{16,0},{256,272},{272,16},{1,257},{17,1},{257,273},{273,17... | collective-permute-start | bytes 786440 | tf_op jit(solution)/shard_map/ppermute | solution.py:41
  15.8 0.0 collective-permute-done
  15.8 3.6 %collective-permute-done.1 = bf16[512,256]{1,0:T(8,128)(2,1)S(1)} collective-permute-done((bf16[512,256]{1,0:T(8,128)(2,1)}, bf16[512,256]{1,0:T(8,128)(2,1)S(1)}, u32[]{:S(2)}, u32[]{:S(2)}) %collective-permute-start.1) | collective-permute-done | bytes 262176 | tf_op jit(solution)/shard_map/ppermute | solution.py:41
  19.4 0.1 pad_maximum_fusion.2
  19.5 4.9 %collective-permute-start.2 = (bf16[2,512,256]{2,1,0:T(8,128)(2,1)S(1)}, bf16[2,512,256]{2,1,0:T(8,128)(2,1)S(1)}, u32[]{:S(2)}, u32[]{:S(2)}) collective-permute-start(bf16[2,512,256]{2,1,0:T(8,128)(2,1)S(1)} %pad_maximum_fusion.2), channel_id=1, source_target_pairs={{0,64},{64,128},{128,192},{192,0},{1,65},{65,129},{129,193},{193,1... | collective-permute-start | bytes 1572872 | tf_op jit(solution)/shard_map/ppermute | solution.py:41
  24.4 4.5 %collective-permute-start.3 = (bf16[2,512,256]{2,1,0:T(8,128)(2,1)S(1)}, bf16[2,512,256]{2,1,0:T(8,128)(2,1)S(1)}, u32[]{:S(2)}, u32[]{:S(2)}) collective-permute-start(bf16[2,512,256]{2,1,0:T(8,128)(2,1)S(1)} %pad_maximum_fusion.2), channel_id=1, source_target_pairs={{0,128},{64,192},{128,0},{192,64},{1,129},{65,193},{129,1},{193,65... | collective-permute-start | bytes 1572872 | tf_op jit(solution)/shard_map/ppermute | solution.py:41
  28.9 3.0 %collective-permute-start.4 = (bf16[2,512,256]{2,1,0:T(8,128)(2,1)S(1)}, bf16[2,512,256]{2,1,0:T(8,128)(2,1)S(1)}, u32[]{:S(2)}, u32[]{:S(2)}) collective-permute-start(bf16[2,512,256]{2,1,0:T(8,128)(2,1)S(1)} %pad_maximum_fusion.2), channel_id=1, source_target_pairs={{0,192},{64,0},{128,64},{192,128},{1,193},{65,1},{129,65},{193,129... | collective-permute-start | bytes 1572872 | tf_op jit(solution)/shard_map/ppermute | solution.py:41
  31.9 1.6 collective-permute-start.5
  33.5 7.7 %collective-permute-start.6 = (bf16[512,256]{1,0:T(8,128)(2,1)}, bf16[512,256]{1,0:T(8,128)(2,1)S(1)}, u32[]{:S(2)}, u32[]{:S(2)}) collective-permute-start(bf16[512,256]{1,0:T(8,128)(2,1)} %param.6), channel_id=1, source_target_pairs={{0,256},{16,0},{256,272},{272,16},{1,257},{17,1},{257,273},{273,17... | collective-permute-start | bytes 786440 | tf_op jit(solution)/shard_map/ppermute | solution.py:41
  41.2 0.0 collective-permute-done.5
  41.2 3.9 %collective-permute-done.6 = bf16[512,256]{1,0:T(8,128)(2,1)S(1)} collective-permute-done((bf16[512,256]{1,0:T(8,128)(2,1)}, bf16[512,256]{1,0:T(8,128)(2,1)S(1)}, u32[]{:S(2)}, u32[]{:S(2)}) %collective-permute-start.6) | collective-permute-done | bytes 262176 | tf_op jit(solution)/shard_map/ppermute | solution.py:41
  45.1 0.1 pad_maximum_fusion.3
  45.2 0.0 collective-permute-done.2
  45.2 3.4 %collective-permute-done.3 = bf16[2,512,256]{2,1,0:T(8,128)(2,1)S(1)} collective-permute-done((bf16[2,512,256]{2,1,0:T(8,128)(2,1)S(1)}, bf16[2,512,256]{2,1,0:T(8,128)(2,1)S(1)}, u32[]{:S(2)}, u32[]{:S(2)}) %collective-permute-start.3) | collective-permute-done | bytes 524320 | tf_op jit(solution)/shard_map/ppermute | solution.py:41
  48.6 2.3 %collective-permute-done.4 = bf16[2,512,256]{2,1,0:T(8,128)(2,1)S(1)} collective-permute-done((bf16[2,512,256]{2,1,0:T(8,128)(2,1)S(1)}, bf16[2,512,256]{2,1,0:T(8,128)(2,1)S(1)}, u32[]{:S(2)}, u32[]{:S(2)}) %collective-permute-start.4) | collective-permute-done | bytes 524320 | tf_op jit(solution)/shard_map/ppermute | solution.py:41
  50.9 0.3 pad_maximum_fusion.own_ref
  51.1 3.5 %collective-permute-start.10 = (bf16[4,2,512,256]{3,2,1,0:T(8,128)(2,1)S(1)}, bf16[4,2,512,256]{3,2,1,0:T(8,128)(2,1)}, u32[]{:S(2)}, u32[]{:S(2)}) collective-permute-start(bf16[4,2,512,256]{3,2,1,0:T(8,128)(2,1)S(1)} %pad_maximum_fusion.own_ref), channel_id=1, source_target_pairs={{0,32},{32,0},{1,33},{33,1},{2,34},{34,2},{3,35},{35,3},{4,36},{36... | collective-permute-start | bytes 6291464 | tf_op jit(solution)/shard_map/ppermute | solution.py:41
  54.6 4.1 %collective-permute-start.7 = (bf16[2,512,256]{2,1,0:T(8,128)(2,1)S(1)}, bf16[2,512,256]{2,1,0:T(8,128)(2,1)S(1)}, u32[]{:S(2)}, u32[]{:S(2)}) collective-permute-start(bf16[2,512,256]{2,1,0:T(8,128)(2,1)S(1)} %pad_maximum_fusion.3), channel_id=1, source_target_pairs={{0,64},{64,128},{128,192},{192,0},{1,65},{65,129},{129,193},{193,1... | collective-permute-start | bytes 1572872 | tf_op jit(solution)/shard_map/ppermute | solution.py:41
  58.7 3.2 %collective-permute-start.8 = (bf16[2,512,256]{2,1,0:T(8,128)(2,1)S(1)}, bf16[2,512,256]{2,1,0:T(8,128)(2,1)}, u32[]{:S(2)}, u32[]{:S(2)}) collective-permute-start(bf16[2,512,256]{2,1,0:T(8,128)(2,1)S(1)} %pad_maximum_fusion.3), channel_id=1, source_target_pairs={{0,128},{64,192},{128,0},{192,64},{1,129},{65,193},{129,1},{193,65... | collective-permute-start | bytes 1572872 | tf_op jit(solution)/shard_map/ppermute | solution.py:41
  62.0 3.3 %collective-permute-start.9 = (bf16[2,512,256]{2,1,0:T(8,128)(2,1)S(1)}, bf16[2,512,256]{2,1,0:T(8,128)(2,1)}, u32[]{:S(2)}, u32[]{:S(2)}) collective-permute-start(bf16[2,512,256]{2,1,0:T(8,128)(2,1)S(1)} %pad_maximum_fusion.3), channel_id=1, source_target_pairs={{0,192},{64,0},{128,64},{192,128},{1,193},{65,1},{129,65},{193,129... | collective-permute-start | bytes 1572872 | tf_op jit(solution)/shard_map/ppermute | solution.py:41
  65.3 0.1 pad_add_fusion.at_ref
  65.4 0.0 collective-permute-done.10.other_hbm
  65.4 14.3 %all-gather.3.cloned.1.call-done = bf16[32,128,256]{2,1,0:T(8,128)(2,1)} async-done(((bf16[2,128,256]{2,1,0:T(8,128)(2,1)}), bf16[32,128,256]{2,1,0:T(8,128)(2,1)}) %all-gather.3.cloned.1.call-update) | async-done | bytes 2097168 | tf_op jit(solution)/shard_map/all_gather | solution.py:142
  79.7 2.9 %shard_map.46 = (f32[128,256]{1,0:T(8,128)S(1)}, f32[128,256]{1,0:T(8,128)S(1)}) custom-call(s32[3]{0:T(128)S(1)} %pad_add_fusion.at_ref, bf16[16,2,128,256]{3,2,1,0:T(8,128)(2,1)} %bitcast.26, bf16[4,2,512,256]{3,2,1,0:T(8,128)(2,1)S(1)} %pad_maximum_fusion.own_ref, bf16[4,2,512,256]{3,2,1,0:T(8,128)(2,1)} %collective-permute-done.10.other_hbm), custom_call_target="tpu_custom_call" | custom-call | tf_op jit(solution)/shard_map/pallas_call | solution.py:94
  82.6 3.0 %collective-permute-start.11 = (f32[128,256]{1,0:T(8,128)S(1)}, f32[128,256]{1,0:T(8,128)S(1)}, u32[]{:S(2)}, u32[]{:S(2)}) collective-permute-start(f32[128,256]{1,0:T(8,128)S(1)} %get-tuple-element.37), channel_id=1, source_target_pairs={{0,16},{16,0},{1,17},{17,1},{2,18},{18,2},{3,19},{19,3},{4,20},{20... | collective-permute-start | bytes 393224 | tf_op jit(solution)/shard_map/ppermute | solution.py:41
  85.7 2.7 %collective-permute-done.11 = f32[128,256]{1,0:T(8,128)S(1)} collective-permute-done((f32[128,256]{1,0:T(8,128)S(1)}, f32[128,256]{1,0:T(8,128)S(1)}, u32[]{:S(2)}, u32[]{:S(2)}) %collective-permute-start.11) | collective-permute-done | bytes 131104 | tf_op jit(solution)/shard_map/ppermute | solution.py:41
  88.4 13.1 %collective-permute-start.12 = (bf16[128,256]{1,0:T(8,128)(2,1)S(1)}, bf16[128,256]{1,0:T(8,128)(2,1)S(1)}, u32[]{:S(2)}, u32[]{:S(2)}) collective-permute-start(bf16[128,256]{1,0:T(8,128)(2,1)S(1)} %multiply_convert_fusion.1), channel_id=1, source_target_pairs={{0,0},{1,1},{2,32},{3,33},{4,64},{5,65},{6,96},{7,97},{8,128},{9,1... | collective-permute-start | bytes 196616 | tf_op jit(solution)/shard_map/ppermute | solution.py:41
  101.5 0.0 collective-permute-done.7
  101.5 0.0 collective-permute-done.8
  101.5 0.0 collective-permute-done.9
  101.5 2.1 %collective-permute-done.12 = bf16[128,256]{1,0:T(8,128)(2,1)S(1)} collective-permute-done((bf16[128,256]{1,0:T(8,128)(2,1)S(1)}, bf16[128,256]{1,0:T(8,128)(2,1)S(1)}, u32[]{:S(2)}, u32[]{:S(2)}) %collective-permute-start.12) | collective-permute-done | bytes 65568 | tf_op jit(solution)/shard_map/ppermute | solution.py:41
  103.6 1.5 pad_maximum_fusion.1.own_ref
  105.0 1.9 collective-permute-start.13
  106.9 0.7 broadcast_in_dim.4
  107.7 19.5 %all-to-all-start = ((bf16[4,128,256]{2,1,0:T(8,128)(2,1)}), bf16[4,128,256]{2,1,0:T(8,128)(2,1)S(1)}, u32[]{:S(2)}, u32[]{:S(2)}) async-start(bf16[4,128,256]{2,1,0:T(8,128)(2,1)} %broadcast_in_dim.4), calls=%async_computation | async-start | bytes 524288 | tf_op jit(solution)/shard_map/all_to_all | solution.py:19
  127.2 0.0 collective-permute-done.13.other_hbm
  127.2 3.6 %shard_map.47 = (f32[2,128,256]{2,1,0:T(8,128)S(1)}, f32[2,128,256]{2,1,0:T(8,128)S(1)}) custom-call(s32[3]{0:T(128)S(1)} %pad_add_fusion.at_ref, bf16[16,2,128,256]{3,2,1,0:T(8,128)(2,1)} %bitcast.27, bf16[4,2,512,256]{3,2,1,0:T(8,128)(2,1)S(1)} %pad_maximum_fusion.1.own_ref, bf16[4,2,512,256]{3,2,1,0:T(8,128)(2,1)} %collective-permute-done.13.other_hbm), custom_call_target="tpu_custom_call" | custom-call | tf_op jit(solution)/shard_map/pallas_call | solution.py:94
  130.8 0.7 collective-permute-start.14
  131.4 7.1 %collective-permute-start.15 = (f32[2,128,256]{2,1,0:T(8,128)S(1)}, f32[2,128,256]{2,1,0:T(8,128)S(1)}, u32[]{:S(2)}, u32[]{:S(2)}) collective-permute-start(f32[2,128,256]{2,1,0:T(8,128)S(1)} %get-tuple-element.44), channel_id=1, source_target_pairs={{0,256},{16,0},{256,272},{272,16},{1,257},{17,1},{257,273},{273,17... | collective-permute-start | bytes 786440 | tf_op jit(solution)/shard_map/ppermute | solution.py:41
  138.6 0.0 collective-permute-done.14
  138.6 5.4 %collective-permute-done.15 = f32[2,128,256]{2,1,0:T(8,128)S(1)} collective-permute-done((f32[2,128,256]{2,1,0:T(8,128)S(1)}, f32[2,128,256]{2,1,0:T(8,128)S(1)}, u32[]{:S(2)}, u32[]{:S(2)}) %collective-permute-start.15) | collective-permute-done | bytes 262176 | tf_op jit(solution)/shard_map/ppermute | solution.py:41
  144.0 1.2 all-to-all-done
  145.3 1.1 broadcast_in_dim.5
  146.4 3.5 %all-to-all-start.1 = ((bf16[4,4,128,256]{3,2,1,0:T(8,128)(2,1)}), bf16[4,4,128,256]{3,2,1,0:T(8,128)(2,1)S(1)}, u32[]{:S(2)}, u32[]{:S(2)}) async-start(bf16[4,4,128,256]{3,2,1,0:T(8,128)(2,1)} %broadcast_in_dim.5), calls=%async_computation.1 | async-start | bytes 2097152 | tf_op jit(solution)/shard_map/all_to_all | solution.py:19
  149.9 1.9 collective-permute-start.16
  151.8 1.9 collective-permute-start.17
  153.7 4.6 %collective-permute-start.18 = (bf16[2,128,256]{2,1,0:T(8,128)(2,1)S(1)}, bf16[2,128,256]{2,1,0:T(8,128)(2,1)S(1)}, u32[]{:S(2)}, u32[]{:S(2)}) collective-permute-start(bf16[2,128,256]{2,1,0:T(8,128)(2,1)S(1)} %multiply_convert_fusion), channel_id=1, source_target_pairs={{0,192},{64,0},{128,64},{192,128},{1,193},{65,1},{129,65},{193,129... | collective-permute-start | bytes 393224 | tf_op jit(solution)/shard_map/ppermute | solution.py:41
  158.3 0.0 collective-permute-done.16
  158.3 0.9 collective-permute-done.17
  159.2 3.7 %collective-permute-done.18 = bf16[2,128,256]{2,1,0:T(8,128)(2,1)S(1)} collective-permute-done((bf16[2,128,256]{2,1,0:T(8,128)(2,1)S(1)}, bf16[2,128,256]{2,1,0:T(8,128)(2,1)S(1)}, u32[]{:S(2)}, u32[]{:S(2)}) %collective-permute-start.18) | collective-permute-done | bytes 131104 | tf_op jit(solution)/shard_map/ppermute | solution.py:41
  162.9 0.1 pad_maximum_fusion.4.own_ref
  163.0 3.5 %collective-permute-start.19 = (bf16[4,2,128,256]{3,2,1,0:T(8,128)(2,1)S(1)}, bf16[4,2,128,256]{3,2,1,0:T(8,128)(2,1)S(1)}, u32[]{:S(2)}, u32[]{:S(2)}) collective-permute-start(bf16[4,2,128,256]{3,2,1,0:T(8,128)(2,1)S(1)} %pad_maximum_fusion.4.own_ref), channel_id=1, source_target_pairs={{0,32},{32,0},{1,33},{33,1},{2,34},{34,2},{3,35},{35,3},{4,36},{36... | collective-permute-start | bytes 1572872 | tf_op jit(solution)/shard_map/ppermute | solution.py:41
  166.5 0.1 pad_add_fusion.2.at_ref
  166.6 1.4 collective-permute-done.19.other_ref
  168.0 7.1 %all-to-all-done.1 = bf16[4,4,128,256]{3,2,1,0:T(8,128)(2,1)S(1)} async-done(((bf16[4,4,128,256]{3,2,1,0:T(8,128)(2,1)}), bf16[4,4,128,256]{3,2,1,0:T(8,128)(2,1)S(1)}, u32[]{:S(2)}, u32[]{:S(2)}) %all-to-all-start.1) | async-done | bytes 1048608 | tf_op jit(solution)/shard_map/all_to_all | solution.py:19
  175.1 1.3 shard_map.49
  176.3 4.8 %collective-permute-start.20 = (f32[256,512]{1,0:T(8,128)S(1)}, f32[256,512]{1,0:T(8,128)S(1)}, u32[]{:S(2)}, u32[]{:S(2)}) collective-permute-start(f32[256,512]{1,0:T(8,128)S(1)} %shard_map.49), channel_id=1, source_target_pairs={{0,16},{16,0},{1,17},{17,1},{2,18},{18,2},{3,19},{19,3},{4,20},{20... | collective-permute-start | bytes 1572872 | tf_op jit(solution)/shard_map/ppermute | solution.py:41
  181.1 1.3 shard_map.48
  182.4 9.5 %collective-permute-done.20 = f32[256,512]{1,0:T(8,128)S(1)} collective-permute-done((f32[256,512]{1,0:T(8,128)S(1)}, f32[256,512]{1,0:T(8,128)S(1)}, u32[]{:S(2)}, u32[]{:S(2)}) %collective-permute-start.20) | collective-permute-done | bytes 524320 | tf_op jit(solution)/shard_map/ppermute | solution.py:41
  191.9 0.9 add_multiply_fusion
  (2 shorter events, 0.1 us)
Async XLA Ops:
  6.5 73.2 %all-gather.3.cloned.1.call-start = ((), (), s32[]{:S(2)}) async-start(), calls=%async_computation.2 | async-start | bytes 2228224 | tf_op jit(solution)/shard_map/all_gather | solution.py:142
  8.1 7.7 %collective-permute-start = (bf16[512,256]{1,0:T(8,128)(2,1)}, bf16[512,256]{1,0:T(8,128)(2,1)S(1)}, u32[]{:S(2)}, u32[]{:S(2)}) collective-permute-start(bf16[512,256]{1,0:T(8,128)(2,1)} %param.7), channel_id=1, source_target_pairs={{0,0},{16,256},{256,16},{272,272},{1,1},{17,257},{257,17},{273,273... | collective-permute-start | bytes 786440 | tf_op jit(solution)/shard_map/ppermute | solution.py:41
  9.7 9.7 %collective-permute-start.1 = (bf16[512,256]{1,0:T(8,128)(2,1)}, bf16[512,256]{1,0:T(8,128)(2,1)S(1)}, u32[]{:S(2)}, u32[]{:S(2)}) collective-permute-start(bf16[512,256]{1,0:T(8,128)(2,1)} %param.7), channel_id=1, source_target_pairs={{0,256},{16,0},{256,272},{272,16},{1,257},{17,1},{257,273},{273,17... | collective-permute-start | bytes 786440 | tf_op jit(solution)/shard_map/ppermute | solution.py:41
  19.5 25.7 %collective-permute-start.2 = (bf16[2,512,256]{2,1,0:T(8,128)(2,1)S(1)}, bf16[2,512,256]{2,1,0:T(8,128)(2,1)S(1)}, u32[]{:S(2)}, u32[]{:S(2)}) collective-permute-start(bf16[2,512,256]{2,1,0:T(8,128)(2,1)S(1)} %pad_maximum_fusion.2), channel_id=1, source_target_pairs={{0,64},{64,128},{128,192},{192,0},{1,65},{65,129},{129,193},{193,1... | collective-permute-start | bytes 1572872 | tf_op jit(solution)/shard_map/ppermute | solution.py:41
  24.4 24.2 %collective-permute-start.3 = (bf16[2,512,256]{2,1,0:T(8,128)(2,1)S(1)}, bf16[2,512,256]{2,1,0:T(8,128)(2,1)S(1)}, u32[]{:S(2)}, u32[]{:S(2)}) collective-permute-start(bf16[2,512,256]{2,1,0:T(8,128)(2,1)S(1)} %pad_maximum_fusion.2), channel_id=1, source_target_pairs={{0,128},{64,192},{128,0},{192,64},{1,129},{65,193},{129,1},{193,65... | collective-permute-start | bytes 1572872 | tf_op jit(solution)/shard_map/ppermute | solution.py:41
  28.9 22.0 %collective-permute-start.4 = (bf16[2,512,256]{2,1,0:T(8,128)(2,1)S(1)}, bf16[2,512,256]{2,1,0:T(8,128)(2,1)S(1)}, u32[]{:S(2)}, u32[]{:S(2)}) collective-permute-start(bf16[2,512,256]{2,1,0:T(8,128)(2,1)S(1)} %pad_maximum_fusion.2), channel_id=1, source_target_pairs={{0,192},{64,0},{128,64},{192,128},{1,193},{65,1},{129,65},{193,129... | collective-permute-start | bytes 1572872 | tf_op jit(solution)/shard_map/ppermute | solution.py:41
  31.9 9.3 %collective-permute-start.5 = (bf16[512,256]{1,0:T(8,128)(2,1)}, bf16[512,256]{1,0:T(8,128)(2,1)S(1)}, u32[]{:S(2)}, u32[]{:S(2)}) collective-permute-start(bf16[512,256]{1,0:T(8,128)(2,1)} %param.6), channel_id=1, source_target_pairs={{0,0},{16,256},{256,16},{272,272},{1,1},{17,257},{257,17},{273,273... | collective-permute-start | bytes 786440 | tf_op jit(solution)/shard_map/ppermute | solution.py:41
  33.5 11.6 %collective-permute-start.6 = (bf16[512,256]{1,0:T(8,128)(2,1)}, bf16[512,256]{1,0:T(8,128)(2,1)S(1)}, u32[]{:S(2)}, u32[]{:S(2)}) collective-permute-start(bf16[512,256]{1,0:T(8,128)(2,1)} %param.6), channel_id=1, source_target_pairs={{0,256},{16,0},{256,272},{272,16},{1,257},{17,1},{257,273},{273,17... | collective-permute-start | bytes 786440 | tf_op jit(solution)/shard_map/ppermute | solution.py:41
  51.1 14.2 %collective-permute-start.10 = (bf16[4,2,512,256]{3,2,1,0:T(8,128)(2,1)S(1)}, bf16[4,2,512,256]{3,2,1,0:T(8,128)(2,1)}, u32[]{:S(2)}, u32[]{:S(2)}) collective-permute-start(bf16[4,2,512,256]{3,2,1,0:T(8,128)(2,1)S(1)} %pad_maximum_fusion.own_ref), channel_id=1, source_target_pairs={{0,32},{32,0},{1,33},{33,1},{2,34},{34,2},{3,35},{35,3},{4,36},{36... | collective-permute-start | bytes 6291464 | tf_op jit(solution)/shard_map/ppermute | solution.py:41
  54.6 46.8 %collective-permute-start.7 = (bf16[2,512,256]{2,1,0:T(8,128)(2,1)S(1)}, bf16[2,512,256]{2,1,0:T(8,128)(2,1)S(1)}, u32[]{:S(2)}, u32[]{:S(2)}) collective-permute-start(bf16[2,512,256]{2,1,0:T(8,128)(2,1)S(1)} %pad_maximum_fusion.3), channel_id=1, source_target_pairs={{0,64},{64,128},{128,192},{192,0},{1,65},{65,129},{129,193},{193,1... | collective-permute-start | bytes 1572872 | tf_op jit(solution)/shard_map/ppermute | solution.py:41
  58.7 42.7 %collective-permute-start.8 = (bf16[2,512,256]{2,1,0:T(8,128)(2,1)S(1)}, bf16[2,512,256]{2,1,0:T(8,128)(2,1)}, u32[]{:S(2)}, u32[]{:S(2)}) collective-permute-start(bf16[2,512,256]{2,1,0:T(8,128)(2,1)S(1)} %pad_maximum_fusion.3), channel_id=1, source_target_pairs={{0,128},{64,192},{128,0},{192,64},{1,129},{65,193},{129,1},{193,65... | collective-permute-start | bytes 1572872 | tf_op jit(solution)/shard_map/ppermute | solution.py:41
  62.0 39.5 %collective-permute-start.9 = (bf16[2,512,256]{2,1,0:T(8,128)(2,1)S(1)}, bf16[2,512,256]{2,1,0:T(8,128)(2,1)}, u32[]{:S(2)}, u32[]{:S(2)}) collective-permute-start(bf16[2,512,256]{2,1,0:T(8,128)(2,1)S(1)} %pad_maximum_fusion.3), channel_id=1, source_target_pairs={{0,192},{64,0},{128,64},{192,128},{1,193},{65,1},{129,65},{193,129... | collective-permute-start | bytes 1572872 | tf_op jit(solution)/shard_map/ppermute | solution.py:41
  82.6 5.7 %collective-permute-start.11 = (f32[128,256]{1,0:T(8,128)S(1)}, f32[128,256]{1,0:T(8,128)S(1)}, u32[]{:S(2)}, u32[]{:S(2)}) collective-permute-start(f32[128,256]{1,0:T(8,128)S(1)} %get-tuple-element.37), channel_id=1, source_target_pairs={{0,16},{16,0},{1,17},{17,1},{2,18},{18,2},{3,19},{19,3},{4,20},{20... | collective-permute-start | bytes 393224 | tf_op jit(solution)/shard_map/ppermute | solution.py:41
  88.4 15.2 %collective-permute-start.12 = (bf16[128,256]{1,0:T(8,128)(2,1)S(1)}, bf16[128,256]{1,0:T(8,128)(2,1)S(1)}, u32[]{:S(2)}, u32[]{:S(2)}) collective-permute-start(bf16[128,256]{1,0:T(8,128)(2,1)S(1)} %multiply_convert_fusion.1), channel_id=1, source_target_pairs={{0,0},{1,1},{2,32},{3,33},{4,64},{5,65},{6,96},{7,97},{8,128},{9,1... | collective-permute-start | bytes 196616 | tf_op jit(solution)/shard_map/ppermute | solution.py:41
  105.0 22.2 %collective-permute-start.13 = (bf16[4,2,512,256]{3,2,1,0:T(8,128)(2,1)S(1)}, bf16[4,2,512,256]{3,2,1,0:T(8,128)(2,1)}, u32[]{:S(2)}, u32[]{:S(2)}) collective-permute-start(bf16[4,2,512,256]{3,2,1,0:T(8,128)(2,1)S(1)} %pad_maximum_fusion.1.own_ref), channel_id=1, source_target_pairs={{0,32},{32,0},{1,33},{33,1},{2,34},{34,2},{3,35},{35,3},{4,36},{36... | collective-permute-start | bytes 6291464 | tf_op jit(solution)/shard_map/ppermute | solution.py:41
  107.7 37.6 %all-to-all-start = ((bf16[4,128,256]{2,1,0:T(8,128)(2,1)}), bf16[4,128,256]{2,1,0:T(8,128)(2,1)S(1)}, u32[]{:S(2)}, u32[]{:S(2)}) async-start(bf16[4,128,256]{2,1,0:T(8,128)(2,1)} %broadcast_in_dim.4), calls=%async_computation | async-start | bytes 524288 | tf_op jit(solution)/shard_map/all_to_all | solution.py:19
  130.8 7.8 %collective-permute-start.14 = (f32[2,128,256]{2,1,0:T(8,128)S(1)}, f32[2,128,256]{2,1,0:T(8,128)S(1)}, u32[]{:S(2)}, u32[]{:S(2)}) collective-permute-start(f32[2,128,256]{2,1,0:T(8,128)S(1)} %get-tuple-element.43), channel_id=1, source_target_pairs={{0,0},{16,256},{256,16},{272,272},{1,1},{17,257},{257,17},{273,273... | collective-permute-start | bytes 786440 | tf_op jit(solution)/shard_map/ppermute | solution.py:41
  131.4 12.6 %collective-permute-start.15 = (f32[2,128,256]{2,1,0:T(8,128)S(1)}, f32[2,128,256]{2,1,0:T(8,128)S(1)}, u32[]{:S(2)}, u32[]{:S(2)}) collective-permute-start(f32[2,128,256]{2,1,0:T(8,128)S(1)} %get-tuple-element.44), channel_id=1, source_target_pairs={{0,256},{16,0},{256,272},{272,16},{1,257},{17,1},{257,273},{273,17... | collective-permute-start | bytes 786440 | tf_op jit(solution)/shard_map/ppermute | solution.py:41
  146.4 28.7 %all-to-all-start.1 = ((bf16[4,4,128,256]{3,2,1,0:T(8,128)(2,1)}), bf16[4,4,128,256]{3,2,1,0:T(8,128)(2,1)S(1)}, u32[]{:S(2)}, u32[]{:S(2)}) async-start(bf16[4,4,128,256]{3,2,1,0:T(8,128)(2,1)} %broadcast_in_dim.5), calls=%async_computation.1 | async-start | bytes 2097152 | tf_op jit(solution)/shard_map/all_to_all | solution.py:19
  149.9 8.4 %collective-permute-start.16 = (bf16[2,128,256]{2,1,0:T(8,128)(2,1)S(1)}, bf16[2,128,256]{2,1,0:T(8,128)(2,1)S(1)}, u32[]{:S(2)}, u32[]{:S(2)}) collective-permute-start(bf16[2,128,256]{2,1,0:T(8,128)(2,1)S(1)} %multiply_convert_fusion), channel_id=1, source_target_pairs={{0,64},{64,128},{128,192},{192,0},{1,65},{65,129},{129,193},{193,1... | collective-permute-start | bytes 393224 | tf_op jit(solution)/shard_map/ppermute | solution.py:41
  151.8 7.4 %collective-permute-start.17 = (bf16[2,128,256]{2,1,0:T(8,128)(2,1)S(1)}, bf16[2,128,256]{2,1,0:T(8,128)(2,1)S(1)}, u32[]{:S(2)}, u32[]{:S(2)}) collective-permute-start(bf16[2,128,256]{2,1,0:T(8,128)(2,1)S(1)} %multiply_convert_fusion), channel_id=1, source_target_pairs={{0,128},{64,192},{128,0},{192,64},{1,129},{65,193},{129,1},{193,65... | collective-permute-start | bytes 393224 | tf_op jit(solution)/shard_map/ppermute | solution.py:41
  153.7 9.2 %collective-permute-start.18 = (bf16[2,128,256]{2,1,0:T(8,128)(2,1)S(1)}, bf16[2,128,256]{2,1,0:T(8,128)(2,1)S(1)}, u32[]{:S(2)}, u32[]{:S(2)}) collective-permute-start(bf16[2,128,256]{2,1,0:T(8,128)(2,1)S(1)} %multiply_convert_fusion), channel_id=1, source_target_pairs={{0,192},{64,0},{128,64},{192,128},{1,193},{65,1},{129,65},{193,129... | collective-permute-start | bytes 393224 | tf_op jit(solution)/shard_map/ppermute | solution.py:41
  163.0 5.0 %collective-permute-start.19 = (bf16[4,2,128,256]{3,2,1,0:T(8,128)(2,1)S(1)}, bf16[4,2,128,256]{3,2,1,0:T(8,128)(2,1)S(1)}, u32[]{:S(2)}, u32[]{:S(2)}) collective-permute-start(bf16[4,2,128,256]{3,2,1,0:T(8,128)(2,1)S(1)} %pad_maximum_fusion.4.own_ref), channel_id=1, source_target_pairs={{0,32},{32,0},{1,33},{33,1},{2,34},{34,2},{3,35},{35,3},{4,36},{36... | collective-permute-start | bytes 1572872 | tf_op jit(solution)/shard_map/ppermute | solution.py:41
  176.3 15.5 %collective-permute-start.20 = (f32[256,512]{1,0:T(8,128)S(1)}, f32[256,512]{1,0:T(8,128)S(1)}, u32[]{:S(2)}, u32[]{:S(2)}) collective-permute-start(f32[256,512]{1,0:T(8,128)S(1)} %shard_map.49), channel_id=1, source_target_pairs={{0,16},{16,0},{1,17},{17,1},{2,18},{18,2},{3,19},{19,3},{4,20},{20... | collective-permute-start | bytes 1572872 | tf_op jit(solution)/shard_map/ppermute | solution.py:41
Sparse Core Ops, SparseCore 0:
  9.4 70.2 all-gather.2

commit v14 on v13

--- a/solution.py
+++ b/solution.py
@@ -76,10 +76,10 @@
     for h in range(2):
         acc = jnp.zeros((256, 256), jnp.float32)
         for j in range(4):
-            at = lax.rem(y + 4 - j, 4) + 4 * h
+            at = 4 * lax.rem(y + 4 - j, 4) + h
             for act, core in ((own_ref, c), (other_ref, 1 - c)):
                 acc += lax.dot_general(
-                    act[j, k], s_ref[at + 8 * core],
+                    act[j, k], s_ref[at + 2 * core],
                     (((0,), (0,)), ((), ())), preferred_element_type=jnp.float32,
                 )
         out_ref[:, 256 * h:256 * h + 256] = acc
@@ -154,14 +154,12 @@
         grad_square, AXES, lambda a, b, e, p, q, r: (p, q, r // 2, a, b, 2 * e + r % 2)
     )
     act_shifts, grad_square = lax.optimization_barrier((act_shifts, grad_square))
-    grad_block = to_all(grad_square, ("zh",), 4)
+    grad_block = to_all(grad_square, ("zh", "zl"), 16)
 
     parts = rotate(at, every, 0, both_cores(act_shifts), 1)
     parts = [move(parts[k], ("xh", "xl"), lambda a, p, k=k: (p ^ k, a)) for k in range(2)]
     rotated_act = parts[0] + parts[1]
     act_square = (rotated_act * rotated_act).astype(jnp.bfloat16)
-    grad_block, act_square = lax.optimization_barrier((grad_block, act_square))
-    grad_block = to_all(grad_block, ("zl",), 4).reshape(16, 128, 256)
     acts = both_cores(shifts(act_square))
 
     theirs = swap(correct(jnp.stack([y, c, 1 - turned]), acts, grad_block), "xl")

time: 201 us -> 193 us (0.960)
  waiting for transfers between devices: 61.5 us -> 57.5 us
    all_to_all x2 -> x1, starting transfers between devices: 23 us -> 12.6 us  [to_all(): return lax.all_to_all(spread, axes, split_axis=0, concat_axis=0, tiled=True)]
    ppermute x21, starting transfers between devices: 86 us -> 94.8 us  [move(): return lax.ppermute(x, axes, pairs)]
    all_to_all x2 -> x1, waiting for transfers between devices: 8.3 us -> 0.01 us  [to_all(): return lax.all_to_all(spread, axes, split_axis=0, concat_axis=0, tiled=True)]
    ppermute x21, waiting for transfers between devices: 38.9 us -> 43.2 us  [move(): return lax.ppermute(x, axes, pairs)]
  transfers between devices with their start and end apart: 24 -> 23, of which waited for: 14 -> 13; matrix products, arithmetic and copies ran while one was open for 1% -> 1% of each run, Pallas kernels for 4% -> 3%
where the time goes in v14:
time: 193 us; the launch traced here: 192 us
  starting transfers between devices  107 us (55%)
  waiting for transfers between devices  57.5 us (30%)
  between operations  13.7 us (7%)
  Pallas kernels  7.98 us (4%)
  other arithmetic  4.53 us (2%)
    ppermute x21, starting transfers between devices, move(): return lax.ppermute(x, axes, pairs)  94.8 us
    ppermute x21, waiting for transfers between devices, move(): return lax.ppermute(x, axes, pairs)  43.2 us
    all_gather x1, waiting for transfers between devices, on_device(): every = lax.all_gather(both, ('zh', 'zl'), axis=0, tiled=False)  14.3 us
    all_to_all x1, starting transfers between devices, to_all(): return lax.all_to_all(spread, axes, split_axis=0, concat_axis=0, tiled=True)  12.6 us
    pallas_call x2, Pallas kernels, rotate(): pl.pallas_call(functools.partial(rotate_kernel, part), out_shape=[out, ou...  5.45 us
  transfers between devices with their start and end apart: 23, of which 13 were waited for; matrix products, arithmetic and copies ran while one was open for 1% of the time, Pallas kernels for 3%

profile of v14, /device:TPU:1, one launch (start us, length us, event | category | flops | bytes accessed | tf_op | source)
XLA Modules:
  0.0 192.2 jit_solution(2935998748120389458)
XLA Ops:
  6.5 0.0 all-gather.3.cloned.1.call-start
  6.5 1.5 pad_maximum_fusion.5
  8.1 0.0 all-gather.3.cloned.1.call-update
  8.1 1.6 collective-permute-start
  9.7 6.0 %collective-permute-start.1 = (bf16[512,256]{1,0:T(8,128)(2,1)}, bf16[512,256]{1,0:T(8,128)(2,1)S(1)}, u32[]{:S(2)}, u32[]{:S(2)}) collective-permute-start(bf16[512,256]{1,0:T(8,128)(2,1)} %param.7), channel_id=1, source_target_pairs={{0,256},{16,0},{256,272},{272,16},{1,257},{17,1},{257,273},{273,17... | collective-permute-start | bytes 786440 | tf_op jit(solution)/shard_map/ppermute | solution.py:41
  15.8 0.0 collective-permute-done
  15.8 3.6 %collective-permute-done.1 = bf16[512,256]{1,0:T(8,128)(2,1)S(1)} collective-permute-done((bf16[512,256]{1,0:T(8,128)(2,1)}, bf16[512,256]{1,0:T(8,128)(2,1)S(1)}, u32[]{:S(2)}, u32[]{:S(2)}) %collective-permute-start.1) | collective-permute-done | bytes 262176 | tf_op jit(solution)/shard_map/ppermute | solution.py:41
  19.4 0.1 pad_maximum_fusion.2
  19.5 4.9 %collective-permute-start.2 = (bf16[2,512,256]{2,1,0:T(8,128)(2,1)S(1)}, bf16[2,512,256]{2,1,0:T(8,128)(2,1)S(1)}, u32[]{:S(2)}, u32[]{:S(2)}) collective-permute-start(bf16[2,512,256]{2,1,0:T(8,128)(2,1)S(1)} %pad_maximum_fusion.2), channel_id=1, source_target_pairs={{0,64},{64,128},{128,192},{192,0},{1,65},{65,129},{129,193},{193,1... | collective-permute-start | bytes 1572872 | tf_op jit(solution)/shard_map/ppermute | solution.py:41
  24.4 4.5 %collective-permute-start.3 = (bf16[2,512,256]{2,1,0:T(8,128)(2,1)S(1)}, bf16[2,512,256]{2,1,0:T(8,128)(2,1)S(1)}, u32[]{:S(2)}, u32[]{:S(2)}) collective-permute-start(bf16[2,512,256]{2,1,0:T(8,128)(2,1)S(1)} %pad_maximum_fusion.2), channel_id=1, source_target_pairs={{0,128},{64,192},{128,0},{192,64},{1,129},{65,193},{129,1},{193,65... | collective-permute-start | bytes 1572872 | tf_op jit(solution)/shard_map/ppermute | solution.py:41
  28.9 3.0 %collective-permute-start.4 = (bf16[2,512,256]{2,1,0:T(8,128)(2,1)S(1)}, bf16[2,512,256]{2,1,0:T(8,128)(2,1)S(1)}, u32[]{:S(2)}, u32[]{:S(2)}) collective-permute-start(bf16[2,512,256]{2,1,0:T(8,128)(2,1)S(1)} %pad_maximum_fusion.2), channel_id=1, source_target_pairs={{0,192},{64,0},{128,64},{192,128},{1,193},{65,1},{129,65},{193,129... | collective-permute-start | bytes 1572872 | tf_op jit(solution)/shard_map/ppermute | solution.py:41
  31.9 1.6 collective-permute-start.5
  33.5 7.7 %collective-permute-start.6 = (bf16[512,256]{1,0:T(8,128)(2,1)}, bf16[512,256]{1,0:T(8,128)(2,1)S(1)}, u32[]{:S(2)}, u32[]{:S(2)}) collective-permute-start(bf16[512,256]{1,0:T(8,128)(2,1)} %param.6), channel_id=1, source_target_pairs={{0,256},{16,0},{256,272},{272,16},{1,257},{17,1},{257,273},{273,17... | collective-permute-start | bytes 786440 | tf_op jit(solution)/shard_map/ppermute | solution.py:41
  41.2 0.0 collective-permute-done.5
  41.2 3.9 %collective-permute-done.6 = bf16[512,256]{1,0:T(8,128)(2,1)S(1)} collective-permute-done((bf16[512,256]{1,0:T(8,128)(2,1)}, bf16[512,256]{1,0:T(8,128)(2,1)S(1)}, u32[]{:S(2)}, u32[]{:S(2)}) %collective-permute-start.6) | collective-permute-done | bytes 262176 | tf_op jit(solution)/shard_map/ppermute | solution.py:41
  45.1 0.1 pad_maximum_fusion.3
  45.2 0.0 collective-permute-done.2
  45.2 3.4 %collective-permute-done.3 = bf16[2,512,256]{2,1,0:T(8,128)(2,1)S(1)} collective-permute-done((bf16[2,512,256]{2,1,0:T(8,128)(2,1)S(1)}, bf16[2,512,256]{2,1,0:T(8,128)(2,1)S(1)}, u32[]{:S(2)}, u32[]{:S(2)}) %collective-permute-start.3) | collective-permute-done | bytes 524320 | tf_op jit(solution)/shard_map/ppermute | solution.py:41
  48.6 2.3 %collective-permute-done.4 = bf16[2,512,256]{2,1,0:T(8,128)(2,1)S(1)} collective-permute-done((bf16[2,512,256]{2,1,0:T(8,128)(2,1)S(1)}, bf16[2,512,256]{2,1,0:T(8,128)(2,1)S(1)}, u32[]{:S(2)}, u32[]{:S(2)}) %collective-permute-start.4) | collective-permute-done | bytes 524320 | tf_op jit(solution)/shard_map/ppermute | solution.py:41
  50.9 0.3 pad_maximum_fusion.own_ref
  51.1 3.5 %collective-permute-start.10 = (bf16[4,2,512,256]{3,2,1,0:T(8,128)(2,1)S(1)}, bf16[4,2,512,256]{3,2,1,0:T(8,128)(2,1)}, u32[]{:S(2)}, u32[]{:S(2)}) collective-permute-start(bf16[4,2,512,256]{3,2,1,0:T(8,128)(2,1)S(1)} %pad_maximum_fusion.own_ref), channel_id=1, source_target_pairs={{0,32},{32,0},{1,33},{33,1},{2,34},{34,2},{3,35},{35,3},{4,36},{36... | collective-permute-start | bytes 6291464 | tf_op jit(solution)/shard_map/ppermute | solution.py:41
  54.6 4.1 %collective-permute-start.7 = (bf16[2,512,256]{2,1,0:T(8,128)(2,1)S(1)}, bf16[2,512,256]{2,1,0:T(8,128)(2,1)S(1)}, u32[]{:S(2)}, u32[]{:S(2)}) collective-permute-start(bf16[2,512,256]{2,1,0:T(8,128)(2,1)S(1)} %pad_maximum_fusion.3), channel_id=1, source_target_pairs={{0,64},{64,128},{128,192},{192,0},{1,65},{65,129},{129,193},{193,1... | collective-permute-start | bytes 1572872 | tf_op jit(solution)/shard_map/ppermute | solution.py:41
  58.7 3.2 %collective-permute-start.8 = (bf16[2,512,256]{2,1,0:T(8,128)(2,1)S(1)}, bf16[2,512,256]{2,1,0:T(8,128)(2,1)}, u32[]{:S(2)}, u32[]{:S(2)}) collective-permute-start(bf16[2,512,256]{2,1,0:T(8,128)(2,1)S(1)} %pad_maximum_fusion.3), channel_id=1, source_target_pairs={{0,128},{64,192},{128,0},{192,64},{1,129},{65,193},{129,1},{193,65... | collective-permute-start | bytes 1572872 | tf_op jit(solution)/shard_map/ppermute | solution.py:41
  62.0 3.3 %collective-permute-start.9 = (bf16[2,512,256]{2,1,0:T(8,128)(2,1)S(1)}, bf16[2,512,256]{2,1,0:T(8,128)(2,1)}, u32[]{:S(2)}, u32[]{:S(2)}) collective-permute-start(bf16[2,512,256]{2,1,0:T(8,128)(2,1)S(1)} %pad_maximum_fusion.3), channel_id=1, source_target_pairs={{0,192},{64,0},{128,64},{192,128},{1,193},{65,1},{129,65},{193,129... | collective-permute-start | bytes 1572872 | tf_op jit(solution)/shard_map/ppermute | solution.py:41
  65.3 0.1 pad_add_fusion.at_ref
  65.4 0.0 collective-permute-done.10.other_hbm
  65.4 14.3 %all-gather.3.cloned.1.call-done = bf16[32,128,256]{2,1,0:T(8,128)(2,1)} async-done(((bf16[2,128,256]{2,1,0:T(8,128)(2,1)}), bf16[32,128,256]{2,1,0:T(8,128)(2,1)}) %all-gather.3.cloned.1.call-update) | async-done | bytes 2097168 | tf_op jit(solution)/shard_map/all_gather | solution.py:142
  79.7 2.9 %shard_map.46 = (f32[128,256]{1,0:T(8,128)S(1)}, f32[128,256]{1,0:T(8,128)S(1)}) custom-call(s32[3]{0:T(128)S(1)} %pad_add_fusion.at_ref, bf16[16,2,128,256]{3,2,1,0:T(8,128)(2,1)} %bitcast.23, bf16[4,2,512,256]{3,2,1,0:T(8,128)(2,1)S(1)} %pad_maximum_fusion.own_ref, bf16[4,2,512,256]{3,2,1,0:T(8,128)(2,1)} %collective-permute-done.10.other_hbm), custom_call_target="tpu_custom_call" | custom-call | tf_op jit(solution)/shard_map/pallas_call | solution.py:94
  82.6 3.0 %collective-permute-start.11 = (f32[128,256]{1,0:T(8,128)S(1)}, f32[128,256]{1,0:T(8,128)S(1)}, u32[]{:S(2)}, u32[]{:S(2)}) collective-permute-start(f32[128,256]{1,0:T(8,128)S(1)} %get-tuple-element.35), channel_id=1, source_target_pairs={{0,16},{16,0},{1,17},{17,1},{2,18},{18,2},{3,19},{19,3},{4,20},{20... | collective-permute-start | bytes 393224 | tf_op jit(solution)/shard_map/ppermute | solution.py:41
  85.7 2.7 %collective-permute-done.11 = f32[128,256]{1,0:T(8,128)S(1)} collective-permute-done((f32[128,256]{1,0:T(8,128)S(1)}, f32[128,256]{1,0:T(8,128)S(1)}, u32[]{:S(2)}, u32[]{:S(2)}) %collective-permute-start.11) | collective-permute-done | bytes 131104 | tf_op jit(solution)/shard_map/ppermute | solution.py:41
  88.4 13.1 %collective-permute-start.12 = (bf16[128,256]{1,0:T(8,128)(2,1)S(1)}, bf16[128,256]{1,0:T(8,128)(2,1)S(1)}, u32[]{:S(2)}, u32[]{:S(2)}) collective-permute-start(bf16[128,256]{1,0:T(8,128)(2,1)S(1)} %multiply_convert_fusion.1), channel_id=1, source_target_pairs={{0,0},{1,1},{2,32},{3,33},{4,64},{5,65},{6,96},{7,97},{8,128},{9,1... | collective-permute-start | bytes 196616 | tf_op jit(solution)/shard_map/ppermute | solution.py:41
  101.5 0.0 collective-permute-done.7
  101.5 0.0 collective-permute-done.8
  101.5 0.0 collective-permute-done.9
  101.5 2.1 %collective-permute-done.12 = bf16[128,256]{1,0:T(8,128)(2,1)S(1)} collective-permute-done((bf16[128,256]{1,0:T(8,128)(2,1)S(1)}, bf16[128,256]{1,0:T(8,128)(2,1)S(1)}, u32[]{:S(2)}, u32[]{:S(2)}) %collective-permute-start.12) | collective-permute-done | bytes 65568 | tf_op jit(solution)/shard_map/ppermute | solution.py:41
  103.6 1.1 broadcast_in_dim.2
  104.7 12.6 %all-to-all-start = ((bf16[16,128,256]{2,1,0:T(8,128)(2,1)}), bf16[16,128,256]{2,1,0:T(8,128)(2,1)S(1)}, u32[]{:S(2)}, u32[]{:S(2)}) async-start(bf16[16,128,256]{2,1,0:T(8,128)(2,1)} %broadcast_in_dim.2), calls=%async_computation | async-start | bytes 2097152 | tf_op jit(solution)/shard_map/all_to_all | solution.py:19
  117.3 1.5 pad_maximum_fusion.1.own_ref
  118.7 9.2 %collective-permute-start.13 = (bf16[4,2,512,256]{3,2,1,0:T(8,128)(2,1)S(1)}, bf16[4,2,512,256]{3,2,1,0:T(8,128)(2,1)S(1)}, u32[]{:S(2)}, u32[]{:S(2)}) collective-permute-start(bf16[4,2,512,256]{3,2,1,0:T(8,128)(2,1)S(1)} %pad_maximum_fusion.1.own_ref), channel_id=1, source_target_pairs={{0,32},{32,0},{1,33},{33,1},{2,34},{34,2},{3,35},{35,3},{4,36},{36... | collective-permute-start | bytes 6291464 | tf_op jit(solution)/shard_map/ppermute | solution.py:41
  128.0 3.8 %collective-permute-done.13.other_hbm = bf16[4,2,512,256]{3,2,1,0:T(8,128)(2,1)S(1)} collective-permute-done((bf16[4,2,512,256]{3,2,1,0:T(8,128)(2,1)S(1)}, bf16[4,2,512,256]{3,2,1,0:T(8,128)(2,1)S(1)}, u32[]{:S(2)}, u32[]{:S(2)}) %collective-permute-start.13) | collective-permute-done | bytes 2097184 | tf_op jit(solution)/shard_map/ppermute | solution.py:41
  131.7 2.5 %shard_map.47 = (f32[2,128,256]{2,1,0:T(8,128)S(1)}, f32[2,128,256]{2,1,0:T(8,128)S(1)}) custom-call(s32[3]{0:T(128)S(1)} %pad_add_fusion.at_ref, bf16[16,2,128,256]{3,2,1,0:T(8,128)(2,1)} %bitcast.24, bf16[4,2,512,256]{3,2,1,0:T(8,128)(2,1)S(1)} %pad_maximum_fusion.1.own_ref, bf16[4,2,512,256]{3,2,1,0:T(8,128)(2,1)S(1)} %collective-permute-done.13.other_hbm), custom_call_target="tpu_custom_call" | custom-call | tf_op jit(solution)/shard_map/pallas_call | solution.py:94
  134.3 0.7 collective-permute-start.14
  134.9 7.1 %collective-permute-start.15 = (f32[2,128,256]{2,1,0:T(8,128)S(1)}, f32[2,128,256]{2,1,0:T(8,128)S(1)}, u32[]{:S(2)}, u32[]{:S(2)}) collective-permute-start(f32[2,128,256]{2,1,0:T(8,128)S(1)} %get-tuple-element.41), channel_id=1, source_target_pairs={{0,256},{16,0},{256,272},{272,16},{1,257},{17,1},{257,273},{273,17... | collective-permute-start | bytes 786440 | tf_op jit(solution)/shard_map/ppermute | solution.py:41
  142.1 0.0 collective-permute-done.14
  142.1 5.3 %collective-permute-done.15 = f32[2,128,256]{2,1,0:T(8,128)S(1)} collective-permute-done((f32[2,128,256]{2,1,0:T(8,128)S(1)}, f32[2,128,256]{2,1,0:T(8,128)S(1)}, u32[]{:S(2)}, u32[]{:S(2)}) %collective-permute-start.15) | collective-permute-done | bytes 262176 | tf_op jit(solution)/shard_map/ppermute | solution.py:41
  147.4 1.9 collective-permute-start.16
  149.4 2.8 %collective-permute-start.17 = (bf16[2,128,256]{2,1,0:T(8,128)(2,1)S(1)}, bf16[2,128,256]{2,1,0:T(8,128)(2,1)S(1)}, u32[]{:S(2)}, u32[]{:S(2)}) collective-permute-start(bf16[2,128,256]{2,1,0:T(8,128)(2,1)S(1)} %multiply_convert_fusion), channel_id=1, source_target_pairs={{0,128},{64,192},{128,0},{192,64},{1,129},{65,193},{129,1},{193,65... | collective-permute-start | bytes 393224 | tf_op jit(solution)/shard_map/ppermute | solution.py:41
  152.2 3.7 %collective-permute-start.18 = (bf16[2,128,256]{2,1,0:T(8,128)(2,1)S(1)}, bf16[2,128,256]{2,1,0:T(8,128)(2,1)S(1)}, u32[]{:S(2)}, u32[]{:S(2)}) collective-permute-start(bf16[2,128,256]{2,1,0:T(8,128)(2,1)S(1)} %multiply_convert_fusion), channel_id=1, source_target_pairs={{0,192},{64,0},{128,64},{192,128},{1,193},{65,1},{129,65},{193,129... | collective-permute-start | bytes 393224 | tf_op jit(solution)/shard_map/ppermute | solution.py:41
  155.9 0.0 collective-permute-done.16
  155.9 1.0 collective-permute-done.17
  156.9 3.5 %collective-permute-done.18 = bf16[2,128,256]{2,1,0:T(8,128)(2,1)S(1)} collective-permute-done((bf16[2,128,256]{2,1,0:T(8,128)(2,1)S(1)}, bf16[2,128,256]{2,1,0:T(8,128)(2,1)S(1)}, u32[]{:S(2)}, u32[]{:S(2)}) %collective-permute-start.18) | collective-permute-done | bytes 131104 | tf_op jit(solution)/shard_map/ppermute | solution.py:41
  160.4 0.1 pad_maximum_fusion.4.own_ref
  160.5 3.8 %collective-permute-start.19 = (bf16[4,2,128,256]{3,2,1,0:T(8,128)(2,1)S(1)}, bf16[4,2,128,256]{3,2,1,0:T(8,128)(2,1)S(1)}, u32[]{:S(2)}, u32[]{:S(2)}) collective-permute-start(bf16[4,2,128,256]{3,2,1,0:T(8,128)(2,1)S(1)} %pad_maximum_fusion.4.own_ref), channel_id=1, source_target_pairs={{0,32},{32,0},{1,33},{33,1},{2,34},{34,2},{3,35},{35,3},{4,36},{36... | collective-permute-start | bytes 1572872 | tf_op jit(solution)/shard_map/ppermute | solution.py:41
  164.3 0.1 pad_add_fusion.2.at_ref
  164.4 1.4 collective-permute-done.19.other_ref
  165.8 0.0 all-to-all-done.s_ref
  165.8 1.3 shard_map.49
  167.1 6.0 %collective-permute-start.20 = (f32[256,512]{1,0:T(8,128)S(1)}, f32[256,512]{1,0:T(8,128)S(1)}, u32[]{:S(2)}, u32[]{:S(2)}) collective-permute-start(f32[256,512]{1,0:T(8,128)S(1)} %shard_map.49), channel_id=1, source_target_pairs={{0,16},{16,0},{1,17},{17,1},{2,18},{18,2},{3,19},{19,3},{4,20},{20... | collective-permute-start | bytes 1572872 | tf_op jit(solution)/shard_map/ppermute | solution.py:41
  173.1 1.3 shard_map.48
  174.3 10.1 %collective-permute-done.20 = f32[256,512]{1,0:T(8,128)S(1)} collective-permute-done((f32[256,512]{1,0:T(8,128)S(1)}, f32[256,512]{1,0:T(8,128)S(1)}, u32[]{:S(2)}, u32[]{:S(2)}) %collective-permute-start.20) | collective-permute-done | bytes 524320 | tf_op jit(solution)/shard_map/ppermute | solution.py:41
  184.5 0.9 add_multiply_fusion
  (2 shorter events, 0.1 us)
Async XLA Ops:
  6.5 73.2 %all-gather.3.cloned.1.call-start = ((), (), s32[]{:S(2)}) async-start(), calls=%async_computation.1 | async-start | bytes 2228224 | tf_op jit(solution)/shard_map/all_gather | solution.py:142
  8.1 7.7 %collective-permute-start = (bf16[512,256]{1,0:T(8,128)(2,1)}, bf16[512,256]{1,0:T(8,128)(2,1)S(1)}, u32[]{:S(2)}, u32[]{:S(2)}) collective-permute-start(bf16[512,256]{1,0:T(8,128)(2,1)} %param.7), channel_id=1, source_target_pairs={{0,0},{16,256},{256,16},{272,272},{1,1},{17,257},{257,17},{273,273... | collective-permute-start | bytes 786440 | tf_op jit(solution)/shard_map/ppermute | solution.py:41
  9.7 9.7 %collective-permute-start.1 = (bf16[512,256]{1,0:T(8,128)(2,1)}, bf16[512,256]{1,0:T(8,128)(2,1)S(1)}, u32[]{:S(2)}, u32[]{:S(2)}) collective-permute-start(bf16[512,256]{1,0:T(8,128)(2,1)} %param.7), channel_id=1, source_target_pairs={{0,256},{16,0},{256,272},{272,16},{1,257},{17,1},{257,273},{273,17... | collective-permute-start | bytes 786440 | tf_op jit(solution)/shard_map/ppermute | solution.py:41
  19.5 25.7 %collective-permute-start.2 = (bf16[2,512,256]{2,1,0:T(8,128)(2,1)S(1)}, bf16[2,512,256]{2,1,0:T(8,128)(2,1)S(1)}, u32[]{:S(2)}, u32[]{:S(2)}) collective-permute-start(bf16[2,512,256]{2,1,0:T(8,128)(2,1)S(1)} %pad_maximum_fusion.2), channel_id=1, source_target_pairs={{0,64},{64,128},{128,192},{192,0},{1,65},{65,129},{129,193},{193,1... | collective-permute-start | bytes 1572872 | tf_op jit(solution)/shard_map/ppermute | solution.py:41
  24.4 24.2 %collective-permute-start.3 = (bf16[2,512,256]{2,1,0:T(8,128)(2,1)S(1)}, bf16[2,512,256]{2,1,0:T(8,128)(2,1)S(1)}, u32[]{:S(2)}, u32[]{:S(2)}) collective-permute-start(bf16[2,512,256]{2,1,0:T(8,128)(2,1)S(1)} %pad_maximum_fusion.2), channel_id=1, source_target_pairs={{0,128},{64,192},{128,0},{192,64},{1,129},{65,193},{129,1},{193,65... | collective-permute-start | bytes 1572872 | tf_op jit(solution)/shard_map/ppermute | solution.py:41
  28.9 22.0 %collective-permute-start.4 = (bf16[2,512,256]{2,1,0:T(8,128)(2,1)S(1)}, bf16[2,512,256]{2,1,0:T(8,128)(2,1)S(1)}, u32[]{:S(2)}, u32[]{:S(2)}) collective-permute-start(bf16[2,512,256]{2,1,0:T(8,128)(2,1)S(1)} %pad_maximum_fusion.2), channel_id=1, source_target_pairs={{0,192},{64,0},{128,64},{192,128},{1,193},{65,1},{129,65},{193,129... | collective-permute-start | bytes 1572872 | tf_op jit(solution)/shard_map/ppermute | solution.py:41
  31.9 9.3 %collective-permute-start.5 = (bf16[512,256]{1,0:T(8,128)(2,1)}, bf16[512,256]{1,0:T(8,128)(2,1)S(1)}, u32[]{:S(2)}, u32[]{:S(2)}) collective-permute-start(bf16[512,256]{1,0:T(8,128)(2,1)} %param.6), channel_id=1, source_target_pairs={{0,0},{16,256},{256,16},{272,272},{1,1},{17,257},{257,17},{273,273... | collective-permute-start | bytes 786440 | tf_op jit(solution)/shard_map/ppermute | solution.py:41
  33.5 11.6 %collective-permute-start.6 = (bf16[512,256]{1,0:T(8,128)(2,1)}, bf16[512,256]{1,0:T(8,128)(2,1)S(1)}, u32[]{:S(2)}, u32[]{:S(2)}) collective-permute-start(bf16[512,256]{1,0:T(8,128)(2,1)} %param.6), channel_id=1, source_target_pairs={{0,256},{16,0},{256,272},{272,16},{1,257},{17,1},{257,273},{273,17... | collective-permute-start | bytes 786440 | tf_op jit(solution)/shard_map/ppermute | solution.py:41
  51.1 14.2 %collective-permute-start.10 = (bf16[4,2,512,256]{3,2,1,0:T(8,128)(2,1)S(1)}, bf16[4,2,512,256]{3,2,1,0:T(8,128)(2,1)}, u32[]{:S(2)}, u32[]{:S(2)}) collective-permute-start(bf16[4,2,512,256]{3,2,1,0:T(8,128)(2,1)S(1)} %pad_maximum_fusion.own_ref), channel_id=1, source_target_pairs={{0,32},{32,0},{1,33},{33,1},{2,34},{34,2},{3,35},{35,3},{4,36},{36... | collective-permute-start | bytes 6291464 | tf_op jit(solution)/shard_map/ppermute | solution.py:41
  54.6 46.8 %collective-permute-start.7 = (bf16[2,512,256]{2,1,0:T(8,128)(2,1)S(1)}, bf16[2,512,256]{2,1,0:T(8,128)(2,1)S(1)}, u32[]{:S(2)}, u32[]{:S(2)}) collective-permute-start(bf16[2,512,256]{2,1,0:T(8,128)(2,1)S(1)} %pad_maximum_fusion.3), channel_id=1, source_target_pairs={{0,64},{64,128},{128,192},{192,0},{1,65},{65,129},{129,193},{193,1... | collective-permute-start | bytes 1572872 | tf_op jit(solution)/shard_map/ppermute | solution.py:41
  58.7 42.7 %collective-permute-start.8 = (bf16[2,512,256]{2,1,0:T(8,128)(2,1)S(1)}, bf16[2,512,256]{2,1,0:T(8,128)(2,1)}, u32[]{:S(2)}, u32[]{:S(2)}) collective-permute-start(bf16[2,512,256]{2,1,0:T(8,128)(2,1)S(1)} %pad_maximum_fusion.3), channel_id=1, source_target_pairs={{0,128},{64,192},{128,0},{192,64},{1,129},{65,193},{129,1},{193,65... | collective-permute-start | bytes 1572872 | tf_op jit(solution)/shard_map/ppermute | solution.py:41
  62.0 39.5 %collective-permute-start.9 = (bf16[2,512,256]{2,1,0:T(8,128)(2,1)S(1)}, bf16[2,512,256]{2,1,0:T(8,128)(2,1)}, u32[]{:S(2)}, u32[]{:S(2)}) collective-permute-start(bf16[2,512,256]{2,1,0:T(8,128)(2,1)S(1)} %pad_maximum_fusion.3), channel_id=1, source_target_pairs={{0,192},{64,0},{128,64},{192,128},{1,193},{65,1},{129,65},{193,129... | collective-permute-start | bytes 1572872 | tf_op jit(solution)/shard_map/ppermute | solution.py:41
  82.6 5.7 %collective-permute-start.11 = (f32[128,256]{1,0:T(8,128)S(1)}, f32[128,256]{1,0:T(8,128)S(1)}, u32[]{:S(2)}, u32[]{:S(2)}) collective-permute-start(f32[128,256]{1,0:T(8,128)S(1)} %get-tuple-element.35), channel_id=1, source_target_pairs={{0,16},{16,0},{1,17},{17,1},{2,18},{18,2},{3,19},{19,3},{4,20},{20... | collective-permute-start | bytes 393224 | tf_op jit(solution)/shard_map/ppermute | solution.py:41
  88.4 15.2 %collective-permute-start.12 = (bf16[128,256]{1,0:T(8,128)(2,1)S(1)}, bf16[128,256]{1,0:T(8,128)(2,1)S(1)}, u32[]{:S(2)}, u32[]{:S(2)}) collective-permute-start(bf16[128,256]{1,0:T(8,128)(2,1)S(1)} %multiply_convert_fusion.1), channel_id=1, source_target_pairs={{0,0},{1,1},{2,32},{3,33},{4,64},{5,65},{6,96},{7,97},{8,128},{9,1... | collective-permute-start | bytes 196616 | tf_op jit(solution)/shard_map/ppermute | solution.py:41
  104.7 61.1 %all-to-all-start = ((bf16[16,128,256]{2,1,0:T(8,128)(2,1)}), bf16[16,128,256]{2,1,0:T(8,128)(2,1)S(1)}, u32[]{:S(2)}, u32[]{:S(2)}) async-start(bf16[16,128,256]{2,1,0:T(8,128)(2,1)} %broadcast_in_dim.2), calls=%async_computation | async-start | bytes 2097152 | tf_op jit(solution)/shard_map/all_to_all | solution.py:19
  118.7 13.0 %collective-permute-start.13 = (bf16[4,2,512,256]{3,2,1,0:T(8,128)(2,1)S(1)}, bf16[4,2,512,256]{3,2,1,0:T(8,128)(2,1)S(1)}, u32[]{:S(2)}, u32[]{:S(2)}) collective-permute-start(bf16[4,2,512,256]{3,2,1,0:T(8,128)(2,1)S(1)} %pad_maximum_fusion.1.own_ref), channel_id=1, source_target_pairs={{0,32},{32,0},{1,33},{33,1},{2,34},{34,2},{3,35},{35,3},{4,36},{36... | collective-permute-start | bytes 6291464 | tf_op jit(solution)/shard_map/ppermute | solution.py:41
  134.3 7.8 %collective-permute-start.14 = (f32[2,128,256]{2,1,0:T(8,128)S(1)}, f32[2,128,256]{2,1,0:T(8,128)S(1)}, u32[]{:S(2)}, u32[]{:S(2)}) collective-permute-start(f32[2,128,256]{2,1,0:T(8,128)S(1)} %get-tuple-element.40), channel_id=1, source_target_pairs={{0,0},{16,256},{256,16},{272,272},{1,1},{17,257},{257,17},{273,273... | collective-permute-start | bytes 786440 | tf_op jit(solution)/shard_map/ppermute | solution.py:41
  134.9 12.5 %collective-permute-start.15 = (f32[2,128,256]{2,1,0:T(8,128)S(1)}, f32[2,128,256]{2,1,0:T(8,128)S(1)}, u32[]{:S(2)}, u32[]{:S(2)}) collective-permute-start(f32[2,128,256]{2,1,0:T(8,128)S(1)} %get-tuple-element.41), channel_id=1, source_target_pairs={{0,256},{16,0},{256,272},{272,16},{1,257},{17,1},{257,273},{273,17... | collective-permute-start | bytes 786440 | tf_op jit(solution)/shard_map/ppermute | solution.py:41
  147.4 8.4 %collective-permute-start.16 = (bf16[2,128,256]{2,1,0:T(8,128)(2,1)S(1)}, bf16[2,128,256]{2,1,0:T(8,128)(2,1)S(1)}, u32[]{:S(2)}, u32[]{:S(2)}) collective-permute-start(bf16[2,128,256]{2,1,0:T(8,128)(2,1)S(1)} %multiply_convert_fusion), channel_id=1, source_target_pairs={{0,64},{64,128},{128,192},{192,0},{1,65},{65,129},{129,193},{193,1... | collective-permute-start | bytes 393224 | tf_op jit(solution)/shard_map/ppermute | solution.py:41
  149.4 7.6 %collective-permute-start.17 = (bf16[2,128,256]{2,1,0:T(8,128)(2,1)S(1)}, bf16[2,128,256]{2,1,0:T(8,128)(2,1)S(1)}, u32[]{:S(2)}, u32[]{:S(2)}) collective-permute-start(bf16[2,128,256]{2,1,0:T(8,128)(2,1)S(1)} %multiply_convert_fusion), channel_id=1, source_target_pairs={{0,128},{64,192},{128,0},{192,64},{1,129},{65,193},{129,1},{193,65... | collective-permute-start | bytes 393224 | tf_op jit(solution)/shard_map/ppermute | solution.py:41
  152.2 8.3 %collective-permute-start.18 = (bf16[2,128,256]{2,1,0:T(8,128)(2,1)S(1)}, bf16[2,128,256]{2,1,0:T(8,128)(2,1)S(1)}, u32[]{:S(2)}, u32[]{:S(2)}) collective-permute-start(bf16[2,128,256]{2,1,0:T(8,128)(2,1)S(1)} %multiply_convert_fusion), channel_id=1, source_target_pairs={{0,192},{64,0},{128,64},{192,128},{1,193},{65,1},{129,65},{193,129... | collective-permute-start | bytes 393224 | tf_op jit(solution)/shard_map/ppermute | solution.py:41
  160.5 5.3 %collective-permute-start.19 = (bf16[4,2,128,256]{3,2,1,0:T(8,128)(2,1)S(1)}, bf16[4,2,128,256]{3,2,1,0:T(8,128)(2,1)S(1)}, u32[]{:S(2)}, u32[]{:S(2)}) collective-permute-start(bf16[4,2,128,256]{3,2,1,0:T(8,128)(2,1)S(1)} %pad_maximum_fusion.4.own_ref), channel_id=1, source_target_pairs={{0,32},{32,0},{1,33},{33,1},{2,34},{34,2},{3,35},{35,3},{4,36},{36... | collective-permute-start | bytes 1572872 | tf_op jit(solution)/shard_map/ppermute | solution.py:41
  167.1 17.4 %collective-permute-start.20 = (f32[256,512]{1,0:T(8,128)S(1)}, f32[256,512]{1,0:T(8,128)S(1)}, u32[]{:S(2)}, u32[]{:S(2)}) collective-permute-start(f32[256,512]{1,0:T(8,128)S(1)} %shard_map.49), channel_id=1, source_target_pairs={{0,16},{16,0},{1,17},{17,1},{2,18},{18,2},{3,19},{19,3},{4,20},{20... | collective-permute-start | bytes 1572872 | tf_op jit(solution)/shard_map/ppermute | solution.py:41
Sparse Core Ops, SparseCore 0:
  9.4 70.2 all-gather.2

commit v15 on v14

--- a/solution.py
+++ b/solution.py
@@ -144,7 +144,6 @@
     act_basis, grad_pair = lax.optimization_barrier((act_basis, grad_pair))
     grad_shifts, act_pair = lax.optimization_barrier((shifts(grad_pair), cross(act_basis)))
     grad_panels = both_cores(grad_shifts)
-    act_pair, grad_own = lax.optimization_barrier((act_pair, grad_panels[0]))
     act_shifts = shifts(act_pair)
 
     mine, theirs = rotate(at, every, 1, grad_panels, 0)

time: 193 us -> 193 us (level)
  no operation moved by 1% of the time
where the time goes in v15:
time: 193 us; the launch traced here: 192 us
  starting transfers between devices  107 us (55%)
  waiting for transfers between devices  57.5 us (30%)
  between operations  13.7 us (7%)
  Pallas kernels  7.98 us (4%)
  other arithmetic  4.53 us (2%)
    ppermute x21, starting transfers between devices, move(): return lax.ppermute(x, axes, pairs)  94.8 us
    ppermute x21, waiting for transfers between devices, move(): return lax.ppermute(x, axes, pairs)  43.2 us
    all_gather x1, waiting for transfers between devices, on_device(): every = lax.all_gather(both, ('zh', 'zl'), axis=0, tiled=False)  14.3 us
    all_to_all x1, starting transfers between devices, to_all(): return lax.all_to_all(spread, axes, split_axis=0, concat_axis=0, tiled=True)  12.6 us
    pallas_call x2, Pallas kernels, rotate(): pl.pallas_call(functools.partial(rotate_kernel, part), out_shape=[out, ou...  5.45 us
  transfers between devices with their start and end apart: 23, of which 13 were waited for; matrix products, arithmetic and copies ran while one was open for 1% of the time, Pallas kernels for 3%

profile of v15, /device:TPU:1, one launch (start us, length us, event | category | flops | bytes accessed | tf_op | source)
XLA Modules:
  0.0 192.2 jit_solution(2935998748120389458)
XLA Ops:
  6.5 0.0 all-gather.3.cloned.1.call-start
  6.5 1.5 pad_maximum_fusion.5
  8.1 0.0 all-gather.3.cloned.1.call-update
  8.1 1.6 collective-permute-start
  9.7 6.0 %collective-permute-start.1 = (bf16[512,256]{1,0:T(8,128)(2,1)}, bf16[512,256]{1,0:T(8,128)(2,1)S(1)}, u32[]{:S(2)}, u32[]{:S(2)}) collective-permute-start(bf16[512,256]{1,0:T(8,128)(2,1)} %param.7), channel_id=1, source_target_pairs={{0,256},{16,0},{256,272},{272,16},{1,257},{17,1},{257,273},{273,17... | collective-permute-start | bytes 786440 | tf_op jit(solution)/shard_map/ppermute | solution.py:41
  15.8 0.0 collective-permute-done
  15.8 3.6 %collective-permute-done.1 = bf16[512,256]{1,0:T(8,128)(2,1)S(1)} collective-permute-done((bf16[512,256]{1,0:T(8,128)(2,1)}, bf16[512,256]{1,0:T(8,128)(2,1)S(1)}, u32[]{:S(2)}, u32[]{:S(2)}) %collective-permute-start.1) | collective-permute-done | bytes 262176 | tf_op jit(solution)/shard_map/ppermute | solution.py:41
  19.4 0.1 pad_maximum_fusion.2
  19.5 4.9 %collective-permute-start.2 = (bf16[2,512,256]{2,1,0:T(8,128)(2,1)S(1)}, bf16[2,512,256]{2,1,0:T(8,128)(2,1)S(1)}, u32[]{:S(2)}, u32[]{:S(2)}) collective-permute-start(bf16[2,512,256]{2,1,0:T(8,128)(2,1)S(1)} %pad_maximum_fusion.2), channel_id=1, source_target_pairs={{0,64},{64,128},{128,192},{192,0},{1,65},{65,129},{129,193},{193,1... | collective-permute-start | bytes 1572872 | tf_op jit(solution)/shard_map/ppermute | solution.py:41
  24.4 4.5 %collective-permute-start.3 = (bf16[2,512,256]{2,1,0:T(8,128)(2,1)S(1)}, bf16[2,512,256]{2,1,0:T(8,128)(2,1)S(1)}, u32[]{:S(2)}, u32[]{:S(2)}) collective-permute-start(bf16[2,512,256]{2,1,0:T(8,128)(2,1)S(1)} %pad_maximum_fusion.2), channel_id=1, source_target_pairs={{0,128},{64,192},{128,0},{192,64},{1,129},{65,193},{129,1},{193,65... | collective-permute-start | bytes 1572872 | tf_op jit(solution)/shard_map/ppermute | solution.py:41
  28.9 3.0 %collective-permute-start.4 = (bf16[2,512,256]{2,1,0:T(8,128)(2,1)S(1)}, bf16[2,512,256]{2,1,0:T(8,128)(2,1)S(1)}, u32[]{:S(2)}, u32[]{:S(2)}) collective-permute-start(bf16[2,512,256]{2,1,0:T(8,128)(2,1)S(1)} %pad_maximum_fusion.2), channel_id=1, source_target_pairs={{0,192},{64,0},{128,64},{192,128},{1,193},{65,1},{129,65},{193,129... | collective-permute-start | bytes 1572872 | tf_op jit(solution)/shard_map/ppermute | solution.py:41
  31.9 1.6 collective-permute-start.5
  33.5 7.7 %collective-permute-start.6 = (bf16[512,256]{1,0:T(8,128)(2,1)}, bf16[512,256]{1,0:T(8,128)(2,1)S(1)}, u32[]{:S(2)}, u32[]{:S(2)}) collective-permute-start(bf16[512,256]{1,0:T(8,128)(2,1)} %param.6), channel_id=1, source_target_pairs={{0,256},{16,0},{256,272},{272,16},{1,257},{17,1},{257,273},{273,17... | collective-permute-start | bytes 786440 | tf_op jit(solution)/shard_map/ppermute | solution.py:41
  41.2 0.0 collective-permute-done.5
  41.2 3.9 %collective-permute-done.6 = bf16[512,256]{1,0:T(8,128)(2,1)S(1)} collective-permute-done((bf16[512,256]{1,0:T(8,128)(2,1)}, bf16[512,256]{1,0:T(8,128)(2,1)S(1)}, u32[]{:S(2)}, u32[]{:S(2)}) %collective-permute-start.6) | collective-permute-done | bytes 262176 | tf_op jit(solution)/shard_map/ppermute | solution.py:41
  45.1 0.1 pad_maximum_fusion.3
  45.2 0.0 collective-permute-done.2
  45.2 3.4 %collective-permute-done.3 = bf16[2,512,256]{2,1,0:T(8,128)(2,1)S(1)} collective-permute-done((bf16[2,512,256]{2,1,0:T(8,128)(2,1)S(1)}, bf16[2,512,256]{2,1,0:T(8,128)(2,1)S(1)}, u32[]{:S(2)}, u32[]{:S(2)}) %collective-permute-start.3) | collective-permute-done | bytes 524320 | tf_op jit(solution)/shard_map/ppermute | solution.py:41
  48.6 2.3 %collective-permute-done.4 = bf16[2,512,256]{2,1,0:T(8,128)(2,1)S(1)} collective-permute-done((bf16[2,512,256]{2,1,0:T(8,128)(2,1)S(1)}, bf16[2,512,256]{2,1,0:T(8,128)(2,1)S(1)}, u32[]{:S(2)}, u32[]{:S(2)}) %collective-permute-start.4) | collective-permute-done | bytes 524320 | tf_op jit(solution)/shard_map/ppermute | solution.py:41
  50.9 0.3 pad_maximum_fusion.own_ref
  51.1 3.5 %collective-permute-start.10 = (bf16[4,2,512,256]{3,2,1,0:T(8,128)(2,1)S(1)}, bf16[4,2,512,256]{3,2,1,0:T(8,128)(2,1)}, u32[]{:S(2)}, u32[]{:S(2)}) collective-permute-start(bf16[4,2,512,256]{3,2,1,0:T(8,128)(2,1)S(1)} %pad_maximum_fusion.own_ref), channel_id=1, source_target_pairs={{0,32},{32,0},{1,33},{33,1},{2,34},{34,2},{3,35},{35,3},{4,36},{36... | collective-permute-start | bytes 6291464 | tf_op jit(solution)/shard_map/ppermute | solution.py:41
  54.6 4.1 %collective-permute-start.7 = (bf16[2,512,256]{2,1,0:T(8,128)(2,1)S(1)}, bf16[2,512,256]{2,1,0:T(8,128)(2,1)S(1)}, u32[]{:S(2)}, u32[]{:S(2)}) collective-permute-start(bf16[2,512,256]{2,1,0:T(8,128)(2,1)S(1)} %pad_maximum_fusion.3), channel_id=1, source_target_pairs={{0,64},{64,128},{128,192},{192,0},{1,65},{65,129},{129,193},{193,1... | collective-permute-start | bytes 1572872 | tf_op jit(solution)/shard_map/ppermute | solution.py:41
  58.7 3.2 %collective-permute-start.8 = (bf16[2,512,256]{2,1,0:T(8,128)(2,1)S(1)}, bf16[2,512,256]{2,1,0:T(8,128)(2,1)}, u32[]{:S(2)}, u32[]{:S(2)}) collective-permute-start(bf16[2,512,256]{2,1,0:T(8,128)(2,1)S(1)} %pad_maximum_fusion.3), channel_id=1, source_target_pairs={{0,128},{64,192},{128,0},{192,64},{1,129},{65,193},{129,1},{193,65... | collective-permute-start | bytes 1572872 | tf_op jit(solution)/shard_map/ppermute | solution.py:41
  62.0 3.3 %collective-permute-start.9 = (bf16[2,512,256]{2,1,0:T(8,128)(2,1)S(1)}, bf16[2,512,256]{2,1,0:T(8,128)(2,1)}, u32[]{:S(2)}, u32[]{:S(2)}) collective-permute-start(bf16[2,512,256]{2,1,0:T(8,128)(2,1)S(1)} %pad_maximum_fusion.3), channel_id=1, source_target_pairs={{0,192},{64,0},{128,64},{192,128},{1,193},{65,1},{129,65},{193,129... | collective-permute-start | bytes 1572872 | tf_op jit(solution)/shard_map/ppermute | solution.py:41
  65.3 0.1 pad_add_fusion.at_ref
  65.4 0.0 collective-permute-done.10.other_hbm
  65.4 14.3 %all-gather.3.cloned.1.call-done = bf16[32,128,256]{2,1,0:T(8,128)(2,1)} async-done(((bf16[2,128,256]{2,1,0:T(8,128)(2,1)}), bf16[32,128,256]{2,1,0:T(8,128)(2,1)}) %all-gather.3.cloned.1.call-update) | async-done | bytes 2097168 | tf_op jit(solution)/shard_map/all_gather | solution.py:142
  79.7 2.9 %shard_map.46 = (f32[128,256]{1,0:T(8,128)S(1)}, f32[128,256]{1,0:T(8,128)S(1)}) custom-call(s32[3]{0:T(128)S(1)} %pad_add_fusion.at_ref, bf16[16,2,128,256]{3,2,1,0:T(8,128)(2,1)} %bitcast.23, bf16[4,2,512,256]{3,2,1,0:T(8,128)(2,1)S(1)} %pad_maximum_fusion.own_ref, bf16[4,2,512,256]{3,2,1,0:T(8,128)(2,1)} %collective-permute-done.10.other_hbm), custom_call_target="tpu_custom_call" | custom-call | tf_op jit(solution)/shard_map/pallas_call | solution.py:94
  82.6 3.0 %collective-permute-start.11 = (f32[128,256]{1,0:T(8,128)S(1)}, f32[128,256]{1,0:T(8,128)S(1)}, u32[]{:S(2)}, u32[]{:S(2)}) collective-permute-start(f32[128,256]{1,0:T(8,128)S(1)} %get-tuple-element.33), channel_id=1, source_target_pairs={{0,16},{16,0},{1,17},{17,1},{2,18},{18,2},{3,19},{19,3},{4,20},{20... | collective-permute-start | bytes 393224 | tf_op jit(solution)/shard_map/ppermute | solution.py:41
  85.7 2.7 %collective-permute-done.11 = f32[128,256]{1,0:T(8,128)S(1)} collective-permute-done((f32[128,256]{1,0:T(8,128)S(1)}, f32[128,256]{1,0:T(8,128)S(1)}, u32[]{:S(2)}, u32[]{:S(2)}) %collective-permute-start.11) | collective-permute-done | bytes 131104 | tf_op jit(solution)/shard_map/ppermute | solution.py:41
  88.4 13.1 %collective-permute-start.12 = (bf16[128,256]{1,0:T(8,128)(2,1)S(1)}, bf16[128,256]{1,0:T(8,128)(2,1)S(1)}, u32[]{:S(2)}, u32[]{:S(2)}) collective-permute-start(bf16[128,256]{1,0:T(8,128)(2,1)S(1)} %multiply_convert_fusion.1), channel_id=1, source_target_pairs={{0,0},{1,1},{2,32},{3,33},{4,64},{5,65},{6,96},{7,97},{8,128},{9,1... | collective-permute-start | bytes 196616 | tf_op jit(solution)/shard_map/ppermute | solution.py:41
  101.5 0.0 collective-permute-done.7
  101.5 0.0 collective-permute-done.8
  101.5 0.0 collective-permute-done.9
  101.5 2.1 %collective-permute-done.12 = bf16[128,256]{1,0:T(8,128)(2,1)S(1)} collective-permute-done((bf16[128,256]{1,0:T(8,128)(2,1)S(1)}, bf16[128,256]{1,0:T(8,128)(2,1)S(1)}, u32[]{:S(2)}, u32[]{:S(2)}) %collective-permute-start.12) | collective-permute-done | bytes 65568 | tf_op jit(solution)/shard_map/ppermute | solution.py:41
  103.6 1.1 broadcast_in_dim.2
  104.7 12.6 %all-to-all-start = ((bf16[16,128,256]{2,1,0:T(8,128)(2,1)}), bf16[16,128,256]{2,1,0:T(8,128)(2,1)S(1)}, u32[]{:S(2)}, u32[]{:S(2)}) async-start(bf16[16,128,256]{2,1,0:T(8,128)(2,1)} %broadcast_in_dim.2), calls=%async_computation | async-start | bytes 2097152 | tf_op jit(solution)/shard_map/all_to_all | solution.py:19
  117.3 1.5 pad_maximum_fusion.1.own_ref
  118.7 9.2 %collective-permute-start.13 = (bf16[4,2,512,256]{3,2,1,0:T(8,128)(2,1)S(1)}, bf16[4,2,512,256]{3,2,1,0:T(8,128)(2,1)S(1)}, u32[]{:S(2)}, u32[]{:S(2)}) collective-permute-start(bf16[4,2,512,256]{3,2,1,0:T(8,128)(2,1)S(1)} %pad_maximum_fusion.1.own_ref), channel_id=1, source_target_pairs={{0,32},{32,0},{1,33},{33,1},{2,34},{34,2},{3,35},{35,3},{4,36},{36... | collective-permute-start | bytes 6291464 | tf_op jit(solution)/shard_map/ppermute | solution.py:41
  128.0 3.8 %collective-permute-done.13.other_hbm = bf16[4,2,512,256]{3,2,1,0:T(8,128)(2,1)S(1)} collective-permute-done((bf16[4,2,512,256]{3,2,1,0:T(8,128)(2,1)S(1)}, bf16[4,2,512,256]{3,2,1,0:T(8,128)(2,1)S(1)}, u32[]{:S(2)}, u32[]{:S(2)}) %collective-permute-start.13) | collective-permute-done | bytes 2097184 | tf_op jit(solution)/shard_map/ppermute | solution.py:41
  131.7 2.5 %shard_map.47 = (f32[2,128,256]{2,1,0:T(8,128)S(1)}, f32[2,128,256]{2,1,0:T(8,128)S(1)}) custom-call(s32[3]{0:T(128)S(1)} %pad_add_fusion.at_ref, bf16[16,2,128,256]{3,2,1,0:T(8,128)(2,1)} %bitcast.24, bf16[4,2,512,256]{3,2,1,0:T(8,128)(2,1)S(1)} %pad_maximum_fusion.1.own_ref, bf16[4,2,512,256]{3,2,1,0:T(8,128)(2,1)S(1)} %collective-permute-done.13.other_hbm), custom_call_target="tpu_custom_call" | custom-call | tf_op jit(solution)/shard_map/pallas_call | solution.py:94
  134.3 0.7 collective-permute-start.14
  134.9 7.1 %collective-permute-start.15 = (f32[2,128,256]{2,1,0:T(8,128)S(1)}, f32[2,128,256]{2,1,0:T(8,128)S(1)}, u32[]{:S(2)}, u32[]{:S(2)}) collective-permute-start(f32[2,128,256]{2,1,0:T(8,128)S(1)} %get-tuple-element.39), channel_id=1, source_target_pairs={{0,256},{16,0},{256,272},{272,16},{1,257},{17,1},{257,273},{273,17... | collective-permute-start | bytes 786440 | tf_op jit(solution)/shard_map/ppermute | solution.py:41
  142.1 0.0 collective-permute-done.14
  142.1 5.3 %collective-permute-done.15 = f32[2,128,256]{2,1,0:T(8,128)S(1)} collective-permute-done((f32[2,128,256]{2,1,0:T(8,128)S(1)}, f32[2,128,256]{2,1,0:T(8,128)S(1)}, u32[]{:S(2)}, u32[]{:S(2)}) %collective-permute-start.15) | collective-permute-done | bytes 262176 | tf_op jit(solution)/shard_map/ppermute | solution.py:41
  147.4 1.9 collective-permute-start.16
  149.4 2.8 %collective-permute-start.17 = (bf16[2,128,256]{2,1,0:T(8,128)(2,1)S(1)}, bf16[2,128,256]{2,1,0:T(8,128)(2,1)S(1)}, u32[]{:S(2)}, u32[]{:S(2)}) collective-permute-start(bf16[2,128,256]{2,1,0:T(8,128)(2,1)S(1)} %multiply_convert_fusion), channel_id=1, source_target_pairs={{0,128},{64,192},{128,0},{192,64},{1,129},{65,193},{129,1},{193,65... | collective-permute-start | bytes 393224 | tf_op jit(solution)/shard_map/ppermute | solution.py:41
  152.2 3.7 %collective-permute-start.18 = (bf16[2,128,256]{2,1,0:T(8,128)(2,1)S(1)}, bf16[2,128,256]{2,1,0:T(8,128)(2,1)S(1)}, u32[]{:S(2)}, u32[]{:S(2)}) collective-permute-start(bf16[2,128,256]{2,1,0:T(8,128)(2,1)S(1)} %multiply_convert_fusion), channel_id=1, source_target_pairs={{0,192},{64,0},{128,64},{192,128},{1,193},{65,1},{129,65},{193,129... | collective-permute-start | bytes 393224 | tf_op jit(solution)/shard_map/ppermute | solution.py:41
  155.9 0.0 collective-permute-done.16
  155.9 1.0 collective-permute-done.17
  156.9 3.5 %collective-permute-done.18 = bf16[2,128,256]{2,1,0:T(8,128)(2,1)S(1)} collective-permute-done((bf16[2,128,256]{2,1,0:T(8,128)(2,1)S(1)}, bf16[2,128,256]{2,1,0:T(8,128)(2,1)S(1)}, u32[]{:S(2)}, u32[]{:S(2)}) %collective-permute-start.18) | collective-permute-done | bytes 131104 | tf_op jit(solution)/shard_map/ppermute | solution.py:41
  160.4 0.1 pad_maximum_fusion.4.own_ref
  160.5 3.8 %collective-permute-start.19 = (bf16[4,2,128,256]{3,2,1,0:T(8,128)(2,1)S(1)}, bf16[4,2,128,256]{3,2,1,0:T(8,128)(2,1)S(1)}, u32[]{:S(2)}, u32[]{:S(2)}) collective-permute-start(bf16[4,2,128,256]{3,2,1,0:T(8,128)(2,1)S(1)} %pad_maximum_fusion.4.own_ref), channel_id=1, source_target_pairs={{0,32},{32,0},{1,33},{33,1},{2,34},{34,2},{3,35},{35,3},{4,36},{36... | collective-permute-start | bytes 1572872 | tf_op jit(solution)/shard_map/ppermute | solution.py:41
  164.3 0.1 pad_add_fusion.2.at_ref
  164.4 1.4 collective-permute-done.19.other_ref
  165.8 0.0 all-to-all-done.s_ref
  165.8 1.3 shard_map.49
  167.1 6.0 %collective-permute-start.20 = (f32[256,512]{1,0:T(8,128)S(1)}, f32[256,512]{1,0:T(8,128)S(1)}, u32[]{:S(2)}, u32[]{:S(2)}) collective-permute-start(f32[256,512]{1,0:T(8,128)S(1)} %shard_map.49), channel_id=1, source_target_pairs={{0,16},{16,0},{1,17},{17,1},{2,18},{18,2},{3,19},{19,3},{4,20},{20... | collective-permute-start | bytes 1572872 | tf_op jit(solution)/shard_map/ppermute | solution.py:41
  173.1 1.3 shard_map.48
  174.3 10.1 %collective-permute-done.20 = f32[256,512]{1,0:T(8,128)S(1)} collective-permute-done((f32[256,512]{1,0:T(8,128)S(1)}, f32[256,512]{1,0:T(8,128)S(1)}, u32[]{:S(2)}, u32[]{:S(2)}) %collective-permute-start.20) | collective-permute-done | bytes 524320 | tf_op jit(solution)/shard_map/ppermute | solution.py:41
  184.5 0.9 add_multiply_fusion
  (2 shorter events, 0.1 us)
Async XLA Ops:
  6.5 73.2 %all-gather.3.cloned.1.call-start = ((), (), s32[]{:S(2)}) async-start(), calls=%async_computation.1 | async-start | bytes 2228224 | tf_op jit(solution)/shard_map/all_gather | solution.py:142
  8.1 7.7 %collective-permute-start = (bf16[512,256]{1,0:T(8,128)(2,1)}, bf16[512,256]{1,0:T(8,128)(2,1)S(1)}, u32[]{:S(2)}, u32[]{:S(2)}) collective-permute-start(bf16[512,256]{1,0:T(8,128)(2,1)} %param.7), channel_id=1, source_target_pairs={{0,0},{16,256},{256,16},{272,272},{1,1},{17,257},{257,17},{273,273... | collective-permute-start | bytes 786440 | tf_op jit(solution)/shard_map/ppermute | solution.py:41
  9.7 9.7 %collective-permute-start.1 = (bf16[512,256]{1,0:T(8,128)(2,1)}, bf16[512,256]{1,0:T(8,128)(2,1)S(1)}, u32[]{:S(2)}, u32[]{:S(2)}) collective-permute-start(bf16[512,256]{1,0:T(8,128)(2,1)} %param.7), channel_id=1, source_target_pairs={{0,256},{16,0},{256,272},{272,16},{1,257},{17,1},{257,273},{273,17... | collective-permute-start | bytes 786440 | tf_op jit(solution)/shard_map/ppermute | solution.py:41
  19.5 25.7 %collective-permute-start.2 = (bf16[2,512,256]{2,1,0:T(8,128)(2,1)S(1)}, bf16[2,512,256]{2,1,0:T(8,128)(2,1)S(1)}, u32[]{:S(2)}, u32[]{:S(2)}) collective-permute-start(bf16[2,512,256]{2,1,0:T(8,128)(2,1)S(1)} %pad_maximum_fusion.2), channel_id=1, source_target_pairs={{0,64},{64,128},{128,192},{192,0},{1,65},{65,129},{129,193},{193,1... | collective-permute-start | bytes 1572872 | tf_op jit(solution)/shard_map/ppermute | solution.py:41
  24.4 24.2 %collective-permute-start.3 = (bf16[2,512,256]{2,1,0:T(8,128)(2,1)S(1)}, bf16[2,512,256]{2,1,0:T(8,128)(2,1)S(1)}, u32[]{:S(2)}, u32[]{:S(2)}) collective-permute-start(bf16[2,512,256]{2,1,0:T(8,128)(2,1)S(1)} %pad_maximum_fusion.2), channel_id=1, source_target_pairs={{0,128},{64,192},{128,0},{192,64},{1,129},{65,193},{129,1},{193,65... | collective-permute-start | bytes 1572872 | tf_op jit(solution)/shard_map/ppermute | solution.py:41
  28.9 22.0 %collective-permute-start.4 = (bf16[2,512,256]{2,1,0:T(8,128)(2,1)S(1)}, bf16[2,512,256]{2,1,0:T(8,128)(2,1)S(1)}, u32[]{:S(2)}, u32[]{:S(2)}) collective-permute-start(bf16[2,512,256]{2,1,0:T(8,128)(2,1)S(1)} %pad_maximum_fusion.2), channel_id=1, source_target_pairs={{0,192},{64,0},{128,64},{192,128},{1,193},{65,1},{129,65},{193,129... | collective-permute-start | bytes 1572872 | tf_op jit(solution)/shard_map/ppermute | solution.py:41
  31.9 9.3 %collective-permute-start.5 = (bf16[512,256]{1,0:T(8,128)(2,1)}, bf16[512,256]{1,0:T(8,128)(2,1)S(1)}, u32[]{:S(2)}, u32[]{:S(2)}) collective-permute-start(bf16[512,256]{1,0:T(8,128)(2,1)} %param.6), channel_id=1, source_target_pairs={{0,0},{16,256},{256,16},{272,272},{1,1},{17,257},{257,17},{273,273... | collective-permute-start | bytes 786440 | tf_op jit(solution)/shard_map/ppermute | solution.py:41
  33.5 11.6 %collective-permute-start.6 = (bf16[512,256]{1,0:T(8,128)(2,1)}, bf16[512,256]{1,0:T(8,128)(2,1)S(1)}, u32[]{:S(2)}, u32[]{:S(2)}) collective-permute-start(bf16[512,256]{1,0:T(8,128)(2,1)} %param.6), channel_id=1, source_target_pairs={{0,256},{16,0},{256,272},{272,16},{1,257},{17,1},{257,273},{273,17... | collective-permute-start | bytes 786440 | tf_op jit(solution)/shard_map/ppermute | solution.py:41
  51.1 14.2 %collective-permute-start.10 = (bf16[4,2,512,256]{3,2,1,0:T(8,128)(2,1)S(1)}, bf16[4,2,512,256]{3,2,1,0:T(8,128)(2,1)}, u32[]{:S(2)}, u32[]{:S(2)}) collective-permute-start(bf16[4,2,512,256]{3,2,1,0:T(8,128)(2,1)S(1)} %pad_maximum_fusion.own_ref), channel_id=1, source_target_pairs={{0,32},{32,0},{1,33},{33,1},{2,34},{34,2},{3,35},{35,3},{4,36},{36... | collective-permute-start | bytes 6291464 | tf_op jit(solution)/shard_map/ppermute | solution.py:41
  54.6 46.8 %collective-permute-start.7 = (bf16[2,512,256]{2,1,0:T(8,128)(2,1)S(1)}, bf16[2,512,256]{2,1,0:T(8,128)(2,1)S(1)}, u32[]{:S(2)}, u32[]{:S(2)}) collective-permute-start(bf16[2,512,256]{2,1,0:T(8,128)(2,1)S(1)} %pad_maximum_fusion.3), channel_id=1, source_target_pairs={{0,64},{64,128},{128,192},{192,0},{1,65},{65,129},{129,193},{193,1... | collective-permute-start | bytes 1572872 | tf_op jit(solution)/shard_map/ppermute | solution.py:41
  58.7 42.7 %collective-permute-start.8 = (bf16[2,512,256]{2,1,0:T(8,128)(2,1)S(1)}, bf16[2,512,256]{2,1,0:T(8,128)(2,1)}, u32[]{:S(2)}, u32[]{:S(2)}) collective-permute-start(bf16[2,512,256]{2,1,0:T(8,128)(2,1)S(1)} %pad_maximum_fusion.3), channel_id=1, source_target_pairs={{0,128},{64,192},{128,0},{192,64},{1,129},{65,193},{129,1},{193,65... | collective-permute-start | bytes 1572872 | tf_op jit(solution)/shard_map/ppermute | solution.py:41
  62.0 39.5 %collective-permute-start.9 = (bf16[2,512,256]{2,1,0:T(8,128)(2,1)S(1)}, bf16[2,512,256]{2,1,0:T(8,128)(2,1)}, u32[]{:S(2)}, u32[]{:S(2)}) collective-permute-start(bf16[2,512,256]{2,1,0:T(8,128)(2,1)S(1)} %pad_maximum_fusion.3), channel_id=1, source_target_pairs={{0,192},{64,0},{128,64},{192,128},{1,193},{65,1},{129,65},{193,129... | collective-permute-start | bytes 1572872 | tf_op jit(solution)/shard_map/ppermute | solution.py:41
  82.6 5.7 %collective-permute-start.11 = (f32[128,256]{1,0:T(8,128)S(1)}, f32[128,256]{1,0:T(8,128)S(1)}, u32[]{:S(2)}, u32[]{:S(2)}) collective-permute-start(f32[128,256]{1,0:T(8,128)S(1)} %get-tuple-element.33), channel_id=1, source_target_pairs={{0,16},{16,0},{1,17},{17,1},{2,18},{18,2},{3,19},{19,3},{4,20},{20... | collective-permute-start | bytes 393224 | tf_op jit(solution)/shard_map/ppermute | solution.py:41
  88.4 15.2 %collective-permute-start.12 = (bf16[128,256]{1,0:T(8,128)(2,1)S(1)}, bf16[128,256]{1,0:T(8,128)(2,1)S(1)}, u32[]{:S(2)}, u32[]{:S(2)}) collective-permute-start(bf16[128,256]{1,0:T(8,128)(2,1)S(1)} %multiply_convert_fusion.1), channel_id=1, source_target_pairs={{0,0},{1,1},{2,32},{3,33},{4,64},{5,65},{6,96},{7,97},{8,128},{9,1... | collective-permute-start | bytes 196616 | tf_op jit(solution)/shard_map/ppermute | solution.py:41
  104.7 61.1 %all-to-all-start = ((bf16[16,128,256]{2,1,0:T(8,128)(2,1)}), bf16[16,128,256]{2,1,0:T(8,128)(2,1)S(1)}, u32[]{:S(2)}, u32[]{:S(2)}) async-start(bf16[16,128,256]{2,1,0:T(8,128)(2,1)} %broadcast_in_dim.2), calls=%async_computation | async-start | bytes 2097152 | tf_op jit(solution)/shard_map/all_to_all | solution.py:19
  118.7 13.0 %collective-permute-start.13 = (bf16[4,2,512,256]{3,2,1,0:T(8,128)(2,1)S(1)}, bf16[4,2,512,256]{3,2,1,0:T(8,128)(2,1)S(1)}, u32[]{:S(2)}, u32[]{:S(2)}) collective-permute-start(bf16[4,2,512,256]{3,2,1,0:T(8,128)(2,1)S(1)} %pad_maximum_fusion.1.own_ref), channel_id=1, source_target_pairs={{0,32},{32,0},{1,33},{33,1},{2,34},{34,2},{3,35},{35,3},{4,36},{36... | collective-permute-start | bytes 6291464 | tf_op jit(solution)/shard_map/ppermute | solution.py:41
  134.3 7.8 %collective-permute-start.14 = (f32[2,128,256]{2,1,0:T(8,128)S(1)}, f32[2,128,256]{2,1,0:T(8,128)S(1)}, u32[]{:S(2)}, u32[]{:S(2)}) collective-permute-start(f32[2,128,256]{2,1,0:T(8,128)S(1)} %get-tuple-element.38), channel_id=1, source_target_pairs={{0,0},{16,256},{256,16},{272,272},{1,1},{17,257},{257,17},{273,273... | collective-permute-start | bytes 786440 | tf_op jit(solution)/shard_map/ppermute | solution.py:41
  134.9 12.5 %collective-permute-start.15 = (f32[2,128,256]{2,1,0:T(8,128)S(1)}, f32[2,128,256]{2,1,0:T(8,128)S(1)}, u32[]{:S(2)}, u32[]{:S(2)}) collective-permute-start(f32[2,128,256]{2,1,0:T(8,128)S(1)} %get-tuple-element.39), channel_id=1, source_target_pairs={{0,256},{16,0},{256,272},{272,16},{1,257},{17,1},{257,273},{273,17... | collective-permute-start | bytes 786440 | tf_op jit(solution)/shard_map/ppermute | solution.py:41
  147.4 8.4 %collective-permute-start.16 = (bf16[2,128,256]{2,1,0:T(8,128)(2,1)S(1)}, bf16[2,128,256]{2,1,0:T(8,128)(2,1)S(1)}, u32[]{:S(2)}, u32[]{:S(2)}) collective-permute-start(bf16[2,128,256]{2,1,0:T(8,128)(2,1)S(1)} %multiply_convert_fusion), channel_id=1, source_target_pairs={{0,64},{64,128},{128,192},{192,0},{1,65},{65,129},{129,193},{193,1... | collective-permute-start | bytes 393224 | tf_op jit(solution)/shard_map/ppermute | solution.py:41
  149.4 7.6 %collective-permute-start.17 = (bf16[2,128,256]{2,1,0:T(8,128)(2,1)S(1)}, bf16[2,128,256]{2,1,0:T(8,128)(2,1)S(1)}, u32[]{:S(2)}, u32[]{:S(2)}) collective-permute-start(bf16[2,128,256]{2,1,0:T(8,128)(2,1)S(1)} %multiply_convert_fusion), channel_id=1, source_target_pairs={{0,128},{64,192},{128,0},{192,64},{1,129},{65,193},{129,1},{193,65... | collective-permute-start | bytes 393224 | tf_op jit(solution)/shard_map/ppermute | solution.py:41
  152.2 8.3 %collective-permute-start.18 = (bf16[2,128,256]{2,1,0:T(8,128)(2,1)S(1)}, bf16[2,128,256]{2,1,0:T(8,128)(2,1)S(1)}, u32[]{:S(2)}, u32[]{:S(2)}) collective-permute-start(bf16[2,128,256]{2,1,0:T(8,128)(2,1)S(1)} %multiply_convert_fusion), channel_id=1, source_target_pairs={{0,192},{64,0},{128,64},{192,128},{1,193},{65,1},{129,65},{193,129... | collective-permute-start | bytes 393224 | tf_op jit(solution)/shard_map/ppermute | solution.py:41
  160.5 5.3 %collective-permute-start.19 = (bf16[4,2,128,256]{3,2,1,0:T(8,128)(2,1)S(1)}, bf16[4,2,128,256]{3,2,1,0:T(8,128)(2,1)S(1)}, u32[]{:S(2)}, u32[]{:S(2)}) collective-permute-start(bf16[4,2,128,256]{3,2,1,0:T(8,128)(2,1)S(1)} %pad_maximum_fusion.4.own_ref), channel_id=1, source_target_pairs={{0,32},{32,0},{1,33},{33,1},{2,34},{34,2},{3,35},{35,3},{4,36},{36... | collective-permute-start | bytes 1572872 | tf_op jit(solution)/shard_map/ppermute | solution.py:41
  167.1 17.4 %collective-permute-start.20 = (f32[256,512]{1,0:T(8,128)S(1)}, f32[256,512]{1,0:T(8,128)S(1)}, u32[]{:S(2)}, u32[]{:S(2)}) collective-permute-start(f32[256,512]{1,0:T(8,128)S(1)} %shard_map.49), channel_id=1, source_target_pairs={{0,16},{16,0},{1,17},{17,1},{2,18},{18,2},{3,19},{19,3},{4,20},{20... | collective-permute-start | bytes 1572872 | tf_op jit(solution)/shard_map/ppermute | solution.py:41
Sparse Core Ops, SparseCore 0:
  9.4 70.2 all-gather.2
